TPU v7x, 32 devices: a whole 2x2x4 slice. The times are simulated.
32 devices in a mesh: dp: 8 (over z, y), tensor: 4 (over x, core).
Axes of the slice: x: 2, y: 2, z: 4, core: 2. Of those that a mesh axis runs over, the one named last changes fastest.
Arguments:
- inputs: bfloat16 [4096, 512], P('dp'), may hold values from -6 to 6
- query_weight: bfloat16 [512, 512], P(None, 'tensor'), may hold values from -0.25 to 0.25
- key_weight: bfloat16 [512, 512], P(None, 'tensor'), may hold values from -0.25 to 0.25
- value_weight: bfloat16 [512, 512], P(None, 'tensor'), may hold values from -0.25 to 0.25
- query_bias: float32 [512], P('tensor'), may hold values from -3 to 3
- value_bias: float32 [512], P('tensor'), may hold values from -3 to 3
- position_bias: float32 [49, 16], P(None, 'tensor'), may hold values from -4 to 4
- proj_weight: bfloat16 [512, 512], P('tensor'), may hold values from -0.5 to 0.5
- proj_bias: float32 [512], replicated, may hold values from -2 to 2
- norm1_gain: float32 [512], replicated, may hold values from 0.5 to 1.5
- norm1_shift: float32 [512], replicated, may hold values from -2 to 2
- norm2_gain: float32 [512], replicated, may hold values from 0.5 to 1.5
- norm2_shift: float32 [512], replicated, may hold values from -2 to 2
- up_weight: bfloat16 [512, 2048], P(None, 'tensor'), may hold values from -0.25 to 0.25
- up_bias: float32 [2048], P('tensor'), may hold values from -2 to 2
- down_weight: bfloat16 [2048, 512], P('tensor'), may hold values from -0.25 to 0.25
- down_bias: float32 [512], replicated, may hold values from -2 to 2
- segment_ids: int32 [8, 512], P('dp'), may hold values from 0 to 3, never falling along the last dimension, each value on 1 to 256 neighbouring positions
- valid_mask: int32 [8, 512], P('dp'), may hold values 0 or 1
- position_index: int32 [16, 16], replicated, may hold values from 0 to 48
- out_cotangent: bfloat16 [4096, 512], P('dp'), may hold values from -6 to 6
Outputs:
- layer_out: float32 [4096, 512], P('dp')
- input_grad: float32 [4096, 512], P('dp')
- query_weight_grad: float32 [512, 512], P(None, 'tensor')
- key_weight_grad: float32 [512, 512], P(None, 'tensor')
- value_weight_grad: float32 [512, 512], P(None, 'tensor')
- query_bias_grad: float32 [512], P('tensor')
- value_bias_grad: float32 [512], P('tensor')
- position_bias_grad: float32 [49, 16], P(None, 'tensor')
- proj_weight_grad: float32 [512, 512], P('tensor')
- proj_bias_grad: float32 [512], replicated
- norm1_gain_grad: float32 [512], replicated
- norm1_shift_grad: float32 [512], replicated
- norm2_gain_grad: float32 [512], replicated
- norm2_shift_grad: float32 [512], replicated
- up_weight_grad: float32 [512, 2048], P(None, 'tensor')
- up_bias_grad: float32 [2048], P('tensor')
- down_weight_grad: float32 [2048, 512], P('tensor')
- down_bias_grad: float32 [512], replicated
Inputs may be any that keep to these rules, and one draw needn't show every extreme that they name: `segment_ids`: within each grid the clip numbers never fall, and each clip has 1 to 256 patches.
All inputs are finite; a program needn't handle non-finite values. No bound on the sum of `valid_mask` on one device may be relied on, other than what follows from the above.
Results may differ from a plain program's by a relative error of at most 0.012.
Values may be sent and summed in bfloat16 or wider, within the bound.
No kernel may reach another device: no remote copies, remote signals or barrier semaphores. Data moves between devices by JAX's collectives and lax.ppermute only.
A program may use at most 64 MiB of HBM per device.

v0:
```python
import jax
import jax.numpy as jnp
from jax import lax
from jax.sharding import PartitionSpec as P

HD = 32
GH = 64
GW = 8
WS = 4


NEG_FILL = -1e30


def normalize(value):
    centre = value - jnp.mean(value, axis=-1, keepdims=True)
    spread = jnp.mean(centre * centre, axis=-1, keepdims=True)
    inverse = lax.rsqrt(spread + 1e-06)
    return (centre * inverse, inverse)


def norm_back(grad_out, normed, inverse, gain):
    scaled = grad_out * gain
    first_mean = jnp.mean(scaled, axis=-1, keepdims=True)
    second_mean = jnp.mean(scaled * normed, axis=-1, keepdims=True)
    return inverse * (scaled - first_mean - normed * second_mean)


def to_windows(field):
    grids = field.shape[0] // (GH * GW)
    chans = field.shape[-1]
    shaped = field.reshape(grids, GH // WS, WS, GW // WS, WS, chans)
    return shaped.transpose(0, 1, 3, 2, 4, 5).reshape(-1, WS * WS, chans)


def from_windows(field):
    chans = field.shape[-1]
    grids = field.shape[0] // (GH // WS * (GW // WS))
    shaped = field.reshape(grids, GH // WS, GW // WS, WS, WS, chans)
    return shaped.transpose(0, 1, 3, 2, 4, 5).reshape(-1, chans)


def matmul(left, right):
    return jnp.dot(left, right, preferred_element_type=jnp.float32)


def gelu_fn(value):
    return jax.nn.gelu(value, approximate=True)


def tensor_reduce(col_grads, row_grads, small_grads):
    return (col_grads, row_grads, small_grads)


def shards(
    inputs,
    query_weight,
    key_weight,
    value_weight,
    query_bias,
    value_bias,
    position_bias,
    proj_weight,
    proj_bias,
    norm1_gain,
    norm1_shift,
    norm2_gain,
    norm2_shift,
    up_weight,
    up_bias,
    down_weight,
    down_bias,
    segment_ids,
    valid_mask,
    position_index,
    out_cotangent,
):
    window = WS * WS
    factor = HD ** (-0.5)
    width = inputs.shape[1]
    x_rows = to_windows(inputs).reshape(-1, width)
    cot_rows = to_windows(out_cotangent).reshape(-1, width)
    seg_rows = to_windows(segment_ids.reshape(-1, 1)).reshape(-1)
    valid_rows = to_windows(valid_mask.reshape(-1, 1)).reshape(-1)
    wq, wk, wv, w_up = (query_weight, key_weight, value_weight, up_weight)
    w_proj, w_down = (proj_weight, down_weight)
    b_query, b_value, b_up, rel_bias = (query_bias, value_bias, up_bias, position_bias)
    local_heads = wq.shape[1] // HD
    xfull = x_rows.astype(jnp.float32)
    normed1, inverse1 = normalize(xfull)
    first = (normed1 * norm1_gain + norm1_shift).astype(jnp.bfloat16)
    query = (matmul(first, wq) + b_query).astype(jnp.bfloat16)
    key = matmul(first, wk).astype(jnp.bfloat16)
    value = (matmul(first, wv) + b_value).astype(jnp.bfloat16)
    qwin = query.reshape(-1, window, local_heads, HD)
    kwin = key.reshape(-1, window, local_heads, HD)
    vwin = value.reshape(-1, window, local_heads, HD)
    offsets = lax.broadcasted_iota(jnp.int32, (window * window, rel_bias.shape[0]), 1)
    onehot = (position_index.reshape(-1, 1) == offsets).astype(jnp.float32)
    bias = jnp.dot(onehot, rel_bias, precision=lax.Precision.HIGHEST)
    bias = bias.reshape(window, window, local_heads).transpose(2, 0, 1)
    segwin = seg_rows.reshape(-1, window)
    validwin = valid_rows.reshape(-1, window)
    selfs = jnp.eye(window, dtype=jnp.int32) > 0
    allowed = (segwin[:, :, None] == segwin[:, None, :]) & (
        (validwin[:, None, :] > 0) | selfs[None]
    )
    scores = (
        jnp.einsum("wqhd,wkhd->whqk", qwin, kwin, preferred_element_type=jnp.float32) * factor
        + bias[None]
    )
    scores = jnp.where(allowed[:, None], scores, NEG_FILL)
    top = jnp.max(scores, axis=-1, keepdims=True)
    expo = jnp.exp(scores - top)
    probs = expo / jnp.sum(expo, axis=-1, keepdims=True)
    probs_low = probs.astype(jnp.bfloat16)
    attended = jnp.einsum("whqk,wkhd->wqhd", probs_low, vwin, preferred_element_type=jnp.float32)
    attended = attended.reshape(-1, local_heads * HD).astype(jnp.bfloat16)
    attn_out = lax.psum(matmul(attended, w_proj), "tensor")
    mid = xfull + attn_out + proj_bias
    normed2, inverse2 = normalize(mid)
    second = (normed2 * norm2_gain + norm2_shift).astype(jnp.bfloat16)
    pre = matmul(second, w_up) + b_up
    hidden_full, gelu_pull = jax.vjp(gelu_fn, pre)
    hidden = hidden_full.astype(jnp.bfloat16)
    mlp_out = lax.psum(matmul(hidden, w_down).astype(jnp.bfloat16), "tensor").astype(jnp.float32)
    layer_rows = mid + mlp_out + down_bias
    grad_out = cot_rows.astype(jnp.float32)
    down_bias_grad = jnp.sum(grad_out, axis=0)
    grad_mlp = grad_out.astype(jnp.bfloat16)
    down_weight_grad = matmul(hidden.T, grad_mlp)
    grad_hidden = matmul(grad_mlp, w_down.T)
    grad_pre = gelu_pull(grad_hidden)[0].astype(jnp.bfloat16)
    up_bias_grad = jnp.sum(grad_pre.astype(jnp.float32), axis=0)
    up_weight_grad = matmul(second.T, grad_pre)
    grad_second = lax.psum(matmul(grad_pre, w_up.T), "tensor")
    norm2_gain_grad = jnp.sum(grad_second * normed2, axis=0)
    norm2_shift_grad = jnp.sum(grad_second, axis=0)
    grad_mid = grad_out + norm_back(grad_second, normed2, inverse2, norm2_gain)
    proj_bias_grad = jnp.sum(grad_mid, axis=0)
    grad_proj = grad_mid.astype(jnp.bfloat16)
    proj_weight_grad = matmul(attended.T, grad_proj)
    grad_att = matmul(grad_proj, w_proj.T).astype(jnp.bfloat16)
    gwin = grad_att.reshape(-1, window, local_heads, HD)
    grad_probs = jnp.einsum("wqhd,wkhd->whqk", gwin, vwin, preferred_element_type=jnp.float32)
    grad_value = jnp.einsum(
        "whqk,wqhd->wkhd", probs_low, gwin, preferred_element_type=jnp.float32
    ).astype(jnp.bfloat16)
    grad_scores = probs * (grad_probs - jnp.sum(probs * grad_probs, axis=-1, keepdims=True))
    grad_scores = grad_scores.astype(jnp.bfloat16)
    grad_query = (
        factor
        * jnp.einsum("whqk,wkhd->wqhd", grad_scores, kwin, preferred_element_type=jnp.float32)
    ).astype(jnp.bfloat16)
    grad_key = (
        factor
        * jnp.einsum("whqk,wqhd->wkhd", grad_scores, qwin, preferred_element_type=jnp.float32)
    ).astype(jnp.bfloat16)
    score_total = jnp.sum(grad_scores.astype(jnp.float32), axis=0)
    score_total = score_total.transpose(1, 2, 0).reshape(window * window, local_heads)
    position_bias_grad = jnp.dot(onehot.T, score_total, precision=lax.Precision.HIGHEST)
    query_rows = grad_query.reshape(-1, local_heads * HD)
    key_rows = grad_key.reshape(-1, local_heads * HD)
    value_rows = grad_value.reshape(-1, local_heads * HD)
    query_bias_grad = jnp.sum(query_rows.astype(jnp.float32), axis=0)
    value_bias_grad = jnp.sum(value_rows.astype(jnp.float32), axis=0)
    query_weight_grad = matmul(first.T, query_rows)
    key_weight_grad = matmul(first.T, key_rows)
    value_weight_grad = matmul(first.T, value_rows)
    first_part = matmul(query_rows, wq.T) + matmul(key_rows, wk.T) + matmul(value_rows, wv.T)
    grad_first = lax.psum(first_part, "tensor")
    norm1_gain_grad = jnp.sum(grad_first * normed1, axis=0)
    norm1_shift_grad = jnp.sum(grad_first, axis=0)
    grad_rows_out = grad_mid + norm_back(grad_first, normed1, inverse1, norm1_gain)
    (
        (wq_part, wk_part, wv_part, rel_part, w1_part),
        (bq_part, bv_part, wo_part, b1_part, w2_part),
        (bo_part, g1_part, s1_part, b2_part, g2_part, s2_part),
    ) = tensor_reduce(
        (query_weight_grad, key_weight_grad, value_weight_grad, position_bias_grad, up_weight_grad),
        (query_bias_grad, value_bias_grad, proj_weight_grad, up_bias_grad, down_weight_grad),
        (
            proj_bias_grad,
            norm1_gain_grad,
            norm1_shift_grad,
            down_bias_grad,
            norm2_gain_grad,
            norm2_shift_grad,
        ),
    )
    every = lax.psum(
        (
            wq_part,
            wk_part,
            wv_part,
            bq_part,
            bv_part,
            rel_part,
            wo_part,
            bo_part,
            g1_part,
            s1_part,
            w1_part,
            b1_part,
            w2_part,
            b2_part,
            g2_part,
            s2_part,
        ),
        "dp",
    )
    early_set = every[:10]
    late_set = every[10:]
    layer_out = from_windows(layer_rows.reshape(-1, window, width))
    input_grad = from_windows(grad_rows_out.reshape(-1, window, width))
    (
        wq_total,
        wk_total,
        wv_total,
        bq_total,
        bv_total,
        rel_total,
        wo_total,
        bo_total,
        g1_total,
        s1_total,
    ) = early_set
    w1_total, b1_total, w2_total, b2_total, g2_total, s2_total = late_set
    return (
        layer_out,
        input_grad,
        wq_total,
        wk_total,
        wv_total,
        bq_total,
        bv_total,
        rel_total,
        wo_total,
        bo_total,
        g1_total,
        s1_total,
        g2_total,
        s2_total,
        w1_total,
        b1_total,
        w2_total,
        b2_total,
    )


def solution(mesh):
    return jax.shard_map(
        shards,
        mesh=mesh,
        in_specs=(
            P("dp", None),
            P(None, "tensor"),
            P(None, "tensor"),
            P(None, "tensor"),
            P("tensor"),
            P("tensor"),
            P(None, "tensor"),
            P("tensor", None),
            P(),
            P(),
            P(),
            P(),
            P(),
            P(None, "tensor"),
            P("tensor"),
            P("tensor", None),
            P(),
            P("dp", None),
            P("dp", None),
            P(),
            P("dp", None),
        ),
        out_specs=(
            P("dp", None),
            P("dp", None),
            P(None, "tensor"),
            P(None, "tensor"),
            P(None, "tensor"),
            P("tensor"),
            P("tensor"),
            P(None, "tensor"),
            P("tensor", None),
            P(),
            P(),
            P(),
            P(),
            P(),
            P(None, "tensor"),
            P("tensor"),
            P("tensor", None),
            P(),
        ),
        check_vma=False,
    )
```

profile of v0, /device:TPU:0, one launch (start us, length us, event | category | flops | bytes accessed | tf_op | source)
XLA Modules:
  0.0 360.2 jit_solution(3782836094382820206)
XLA Ops:
  7.8 1.4 reshape.268
  10.1 1.1 copy.158
  15.8 1.6 reshape.266
  20.2 2.0 reshape.254
  22.2 1.6 fusion.12
  23.8 1.1 reshape.255
  25.0 1.0 reshape.256
  26.8 2.8 fusion.44
  29.6 1.8 fusion.9
  32.5 1.2 fusion.49
  33.8 1.2 reshape.259
  35.0 1.1 copy.159
  36.1 1.2 reshape_reshape.16
  37.3 1.2 add_convert_fusion
  38.6 1.2 convert_element_type.153
  39.8 1.4 fusion.50
  41.3 31.5 %all-reduce.8.cloned.1.call-done = f32[512,512]{1,0:T(8,128)} async-done(((f32[512,512]{1,0:T(8,128)}), f32[512,512]{1,0:T(8,128)}) %all-reduce.8.cloned.1.call-update) | async-done | bytes 1048592 | tf_op jit(solution)/shard_map/psum | solution.py:119
  72.7 1.4 fusion.43
  75.4 1.7 convert_reduce_fusion.1
  77.2 1.6 fusion.38
  78.7 1.4 fusion.51
  80.2 2.7 convolution_convert_fusion.1
  82.9 2.7 fusion.40
  85.9 30.9 %all-reduce.12.cloned.1.call-done = f32[512,512]{1,0:T(8,128)} async-done(((f32[512,512]{1,0:T(8,128)}), f32[512,512]{1,0:T(8,128)}) %all-reduce.12.cloned.1.call-update) | async-done | bytes 1048592 | tf_op jit(solution)/shard_map/psum | solution.py:136
  116.8 1.7 multiply_reduce_fusion
  118.6 34.2 %all-reduce.10.cloned.1.call-done = bf16[512,512]{1,0:T(8,128)(2,1)} async-done(((bf16[512,512]{1,0:T(8,128)(2,1)}), bf16[512,512]{1,0:T(8,128)(2,1)}) %all-reduce.10.cloned.1.call-update) | async-done | bytes 524304 | tf_op jit(solution)/shard_map/psum | solution.py:126
  152.8 3.0 fusion.42
  157.0 1.0 reshape.260
  158.1 2.9 convert_reduce_fusion.3
  165.7 1.3 copy.115
  168.2 1.0 fusion.54
  170.1 1.3 convolution_add_fusion
  171.5 1.0 fusion.53
  172.6 1.0 fusion.55
  174.6 1.0 copy-done.4
  176.6 2.5 reshape_reshape.15
  179.2 2.3 copy.105
  181.5 2.6 reshape.258
  184.3 23.4 %all-reduce.14.cloned.1.call-done = f32[512,512]{1,0:T(8,128)} async-done(((f32[512,512]{1,0:T(8,128)}), f32[512,512]{1,0:T(8,128)}) %all-reduce.14.cloned.1.call-update) | async-done | bytes 1048592 | tf_op jit(solution)/shard_map/psum | solution.py:171
  207.8 1.8 multiply_reduce_fusion.1
  209.6 1.3 multiply_add_fusion
  211.0 1.5 reshape_reshape.17
  212.6 1.3 reshape.264
  214.6 39.6 %all-reduce = (f32[128]{0:T(128)}, f32[128]{0:T(128)}, f32[49,4]{0,1:T(4,128)}, f32[512]{0:T(512)}, f32[512]{0:T(512)}, /*index=5*/f32[512]{0:T(512)}, f32[512]{...) all-reduce(f32[128]{0:T(128)S(1)} %reduce_sum.195, ...), channel_id=1, replica_groups=mesh['dp'=8,'tensor'=4] {'dp'}, use_global_device_ids=true, to_apply=%region_19.20 | all-reduce | flops 4036 | bytes 32288 | tf_op jit(solution)/shard_map/psum | solution.py:191
  254.2 91.6 %all-reduce.16.cloned.1.call-done = (f32[512,128]{1,0:T(8,128)}, f32[512,128]{1,0:T(8,128)}, f32[512,128]{1,0:T(8,128)}, f32[128,512]{1,0:T(8,128)}, f32[512,512]{1,0:T(8,128)}, /*index=5*/f32[512,512]{1,0:T(8,128)}) async-done(((f32[512,128]{1,0:T(8,128)}, f32[512,128]{1,0:T(8,128)}, f32[512,128]{1,0:T(8,128)}, f32[128,512]{1,0:T(8,128)}, f32[512,512]{1,0:T(8,128)}, /*index=5*/f32[512,512]{1,0:T(8,128)}), ...) | async-done | bytes 3145744 | tf_op jit(solution)/shard_map/psum | solution.py:191
  345.9 1.8 copy.170
  347.6 1.7 copy.171
  351.1 1.0 copy.174
  (180 shorter events, 26.7 us)
Async XLA Ops:
  7.2 67.3 %copy-start = (bf16[512,512]{1,0:T(8,128)(2,1)S(1)}, bf16[512,512]{1,0:T(8,128)(2,1)}, u32[]{:S(2)}) copy-start(bf16[512,512]{1,0:T(8,128)(2,1)} %param.34) | copy-start | bytes 1572868
  7.2 65.5 %all-reduce.8.cloned.1.call-start = ((), (), s32[]{:S(2)}) async-start(), calls=%async_computation | async-start | bytes 2097152 | tf_op jit(solution)/shard_map/psum | solution.py:119
  9.6 7.8 %copy-start.33 = (f32[512]{0:T(512)}, f32[512]{0:T(512)S(1)}, u32[]{:S(2)}) copy-start(f32[512]{0:T(512)S(1)} %div.35) | copy-start | bytes 6148
  10.1 1.1 copy-start.48
  10.1 1.2 copy-start.43
  13.5 1.2 copy-start.51
  15.8 1.6 copy-start.35
  15.8 1.6 copy-start.31
  15.8 1.6 copy-start.40
  20.2 2.0 copy-start.19
  25.0 4.6 %copy-start.8 = (bf16[32,16,4,32]{3,2,1,0:T(4,128)(2,1)}, bf16[32,16,4,32]{3,2,1,0:T(4,128)(2,1)S(1)}, u32[]{:S(2)}) copy-start(bf16[32,16,4,32]{3,2,1,0:T(4,128)(2,1)S(1)} %reshape.255) | copy-start | bytes 393220
  25.0 1.1 copy-start.39
  25.0 1.0 copy-start.42
  29.6 1.8 copy-start.29
  33.8 83.0 %all-reduce.12.cloned.1.call-start = ((), (), s32[]{:S(2)}) async-start(), calls=%async_computation.2 | async-start | bytes 2097152 | tf_op jit(solution)/shard_map/psum | solution.py:136
  35.0 1.1 copy-start.3
  36.1 1.2 copy-start.32
  36.1 1.2 copy-start.41
  37.3 2.5 copy-start.5
  38.6 1.2 copy-start.25
  39.8 32.9 %copy-start.44 = (f32[512]{0:T(512)S(1)}, f32[512]{0:T(512)}, u32[]{:S(2)}) copy-start(f32[512]{0:T(512)} %param.29) | copy-start | bytes 6148
  74.2 1.2 copy-start.14
  74.2 1.2 copy-start.56
  75.4 1.8 copy-start.6
  77.1 1.6 copy-start.57
  77.2 1.6 copy-start.10
  80.2 72.6 %all-reduce.10.cloned.1.call-start = ((), (), s32[]{:S(2)}) async-start(), calls=%async_computation.1 | async-start | bytes 1048576 | tf_op jit(solution)/shard_map/psum | solution.py:126
  85.7 122.1 %all-reduce.14.cloned.1.call-start = ((), (), s32[]{:S(2)}) async-start(), calls=%async_computation.3 | async-start | bytes 2097152 | tf_op jit(solution)/shard_map/psum | solution.py:171
  118.6 34.2 %copy-start.46 = (f32[512]{0:T(512)S(1)}, f32[512]{0:T(512)}, u32[]{:S(2)}) copy-start(f32[512]{0:T(512)} %param.37) | copy-start | bytes 6148
  155.8 1.0 copy-start.1
  155.8 2.3 copy-start.11
  157.0 1.1 copy-start.30
  158.1 2.9 copy-start.17
  158.1 2.9 copy-start.18
  161.5 1.0 copy-start.9
  162.6 1.0 copy-start.16
  168.2 1.1 copy-start.22
  171.5 2.1 copy-start.2
  171.5 174.4 %all-reduce.16.cloned.1.call-start = ((), (), s32[]{:S(2)}) async-start(), calls=%async_computation.4 | async-start | bytes 6291456 | tf_op jit(solution)/shard_map/psum | solution.py:191
  174.6 1.0 copy-start.4
  181.5 2.6 copy-start.53
  184.1 23.7 %copy-start.34 = (f32[512]{0:T(512)S(1)}, f32[512]{0:T(512)}, u32[]{:S(2)}) copy-start(f32[512]{0:T(512)} %copy-done.33) | copy-start | bytes 6148
  184.1 23.7 %copy-start.36 = (f32[512]{0:T(512)S(1)}, f32[512]{0:T(512)}, u32[]{:S(2)}) copy-start(f32[512]{0:T(512)} %copy-done.35) | copy-start | bytes 6148
  207.8 1.8 copy-start.7
  345.9 3.4 copy-start.27
  345.9 5.2 %copy-start.13 = (f32[512,512]{1,0:T(8,128)S(1)}, f32[512,512]{1,0:T(8,128)}, u32[]{:S(2)}) copy-start(f32[512,512]{1,0:T(8,128)} %get-tuple-element.76) | copy-start | bytes 3145732
  349.3 1.0 copy-start.26
  351.1 1.6 copy-start.12
  (15 other events, 12.4 us)
Sparse Core Ops, SparseCore 0:
  33.9 38.7 all-reduce.7
  80.3 36.4 all-reduce.11
  119.2 33.5 all-reduce.9
  171.6 36.1 all-reduce.13
  213.6 132.1 all-reduce.15
where the time goes:
time: 362 us; the launch traced here: 360 us
  waiting for transfers between devices  212 us (59%)
  local copies, waits for them, and re-layouts  47.8 us (13%)
  blocking collectives  39.6 us (11%)
  matrix products  31.7 us (9%)
  other arithmetic  14.5 us (4%)
  between operations  14.4 us (4%)
    psum x1, waiting for transfers between devices, shards(): lax.psum((wq_part, wk_part, wv_part, bq_part, bv_part, rel_part, wo_part,...  91.6 us
    psum x1, blocking collectives, shards(): lax.psum((wq_part, wk_part, wv_part, bq_part, bv_part, rel_part, wo_part,...  39.6 us
    psum x1, waiting for transfers between devices, shards(): lax.psum(matmul(hidden, w_down).astype(jnp.bfloat16), 'tensor')  34.2 us
    psum x1, waiting for transfers between devices, shards(): attn_out = lax.psum(matmul(attended, w_proj), 'tensor')  31.5 us
    psum x1, waiting for transfers between devices, shards(): grad_second = lax.psum(matmul(grad_pre, w_up.T), 'tensor')  30.9 us
    psum x1, waiting for transfers between devices, shards(): grad_first = lax.psum(first_part, 'tensor')  23.4 us
    dot_general x18, matrix products, matmul(): return jnp.dot(left, right, preferred_element_type=jnp.float32)  22 us
    unnamed x123, local copies, waits for them, and re-layouts  17.8 us
  transfers between devices with their start and end apart: 5, of which 5 were waited for; matrix products, arithmetic and copies ran while one was open for 9% of the time, Pallas kernels for 0%

commit v1 on v0

v1 whole, which is shorter than its diff:
```python
import jax
import jax.numpy as jnp
from jax import lax
from jax.experimental import pallas as pl
from jax.experimental.pallas import tpu as pltpu
from jax.sharding import PartitionSpec as P

HD = 32
GW = 8
WS = 4
WIN = WS * WS
BLOCK = 128
NEG_FILL = -1e30
BF = jnp.bfloat16
F32 = jnp.float32
EXACT = lax.Precision.HIGHEST
VMEM_BYTES = 24 * 1024 * 1024


def dot(left, right):
    return jnp.dot(left, right, preferred_element_type=F32)


def dot_nt(left, right):
    return lax.dot_general(left, right, (((1,), (1,)), ((), ())), preferred_element_type=F32)


def dot_tn(left, right):
    return lax.dot_general(left, right, (((0,), (0,)), ((), ())), preferred_element_type=F32)


def normalize(value):
    centre = value - jnp.mean(value, axis=-1, keepdims=True)
    spread = jnp.mean(centre * centre, axis=-1, keepdims=True)
    inverse = lax.rsqrt(spread + 1e-06)
    return centre * inverse, inverse


def norm_back(grad_out, normed, inverse, gain):
    scaled = grad_out * gain
    first_mean = jnp.mean(scaled, axis=-1, keepdims=True)
    second_mean = jnp.mean(scaled * normed, axis=-1, keepdims=True)
    return inverse * (scaled - first_mean - normed * second_mean)


def row(ref):
    return ref[...].reshape(1, -1)


def iota(shape, axis):
    return lax.broadcasted_iota(jnp.int32, shape, axis)


def place(token):
    return (token // GW) % WS * WS + token % WS


def window(token):
    return token // (GW * WS) * (GW // WS) + token % GW // WS


def head_mask(head):
    return iota((BLOCK, BLOCK), 1) // HD == head


def attend_kernel(
    rel, seg, valid, pidx, x, wq, wk, wv, bq, bv, g1, s1, att, first, q, k, v, probs
):
    tokens = x.shape[0]
    heads = wq.shape[1] // HD
    blocks = tokens // BLOCK
    for b in range(blocks):
        rows = pl.ds(b * BLOCK, BLOCK)
        normed, _ = normalize(x[rows, :].astype(F32))
        first[rows, :] = (normed * row(g1) + row(s1)).astype(BF)
    q[...] = (dot(first[...], wq[...]) + row(bq)).astype(BF)
    k[...] = dot(first[...], wk[...]).astype(BF)
    v[...] = (dot(first[...], wv[...]) + row(bv)).astype(BF)
    spread = (place(iota((BLOCK, WIN), 0)) == iota((BLOCK, WIN), 1)).astype(F32)
    index = pidx[...]
    biases = [jnp.zeros((WIN, WIN), F32) for _ in range(heads)]
    for o in range(rel.shape[0]):
        hit = index == o
        biases = [jnp.where(hit, rel[o, h], biases[h]) for h in range(heads)]
    biases = [
        lax.dot_general(
            jnp.dot(spread, bias, precision=EXACT, preferred_element_type=F32),
            spread,
            (((1,), (1,)), ((), ())),
            precision=EXACT,
            preferred_element_type=F32,
        )
        for bias in biases
    ]
    query_at, key_at = iota((BLOCK, BLOCK), 0), iota((BLOCK, BLOCK), 1)
    near = window(query_at) == window(key_at)
    selfs = query_at == key_at
    factor = HD ** (-0.5)
    for b in range(blocks):
        rows = pl.ds(b * BLOCK, BLOCK)
        seg_keys = jnp.broadcast_to(seg[:, rows].astype(F32), (BLOCK, BLOCK))
        valid_keys = jnp.broadcast_to(valid[:, rows], (BLOCK, BLOCK)) > 0
        allowed = near & (seg_keys == seg_keys.T) & (valid_keys | selfs)
        qb, kb, vb = q[rows, :], k[rows, :], v[rows, :]
        total = jnp.zeros((BLOCK, BLOCK), F32)
        for h in range(heads):
            mine = head_mask(h)
            kh = jnp.where(mine, kb, jnp.zeros_like(kb))
            vh = jnp.where(mine, vb, jnp.zeros_like(vb))
            scores = dot_nt(qb, kh) * factor + biases[h]
            scores = jnp.where(allowed, scores, NEG_FILL)
            expo = jnp.exp(scores - jnp.max(scores, axis=-1, keepdims=True))
            prob = expo * (1.0 / jnp.sum(expo, axis=-1, keepdims=True))
            probs[b * heads + h] = prob
            total = total + dot(prob.astype(BF), vh)
        att[rows, :] = total.astype(BF)


def mlp_kernel(
    spot, x, cot, a0, a1, a2, a3, p0, p1, p2, p3, bo, g2, s2, w1, b1, w2,
    mid, second, hidden, gpre, keep, send, att_all, wo_all,
):
    me = spot[0]
    width = a0.shape[1]
    for j, (a, p) in enumerate(((a0, p0), (a1, p1), (a2, p2), (a3, p3))):
        here = pl.ds(pl.multiple_of((me ^ j) * width, width), width)
        att_all[:, here] = a[...]
        wo_all[here, :] = p[...]
    tokens = x.shape[0]
    half = tokens // 2
    curve = (2.0 / jnp.pi) ** 0.5
    for i in range(2):
        rows = pl.ds(i * half, half)
        value = x[rows, :].astype(F32) + dot(att_all[rows, :], wo_all[...]) + row(bo)
        mid[rows, :] = value
        normed, _ = normalize(value)
        second[rows, :] = (normed * row(g2) + row(s2)).astype(BF)
        pre = dot(second[rows, :], w1[...]) + row(b1)
        square = pre * pre
        bend = jnp.tanh(curve * (pre + 0.044715 * (pre * square)))
        upper = 0.5 * (1.0 + bend)
        hidden[rows, :] = (pre * upper).astype(BF)
        slope = upper + 0.5 * pre * (1.0 - bend * bend) * (curve * (1.0 + 0.134145 * square))
        gpre[rows, :] = (dot_nt(cot[rows, :], w2[...]) * slope).astype(BF)
    core = me % 2
    mine = pl.ds(pl.multiple_of(core * half, half), half)
    other = pl.ds(pl.multiple_of((1 - core) * half, half), half)
    send[...] = dot_nt(gpre[other, :], w1[...]).astype(BF)
    keep[...] = dot_nt(gpre[mine, :], w1[...])


def mlp_grad_kernel(
    spot, cot, second, hidden, gpre, w2, w1_grad, w2_grad, keep, send, small
):
    core = spot[0] % 2
    half = cot.shape[0] // 2
    mine = pl.ds(pl.multiple_of(core * half, half), half)
    other = pl.ds(pl.multiple_of((1 - core) * half, half), half)
    w2_grad[...] = dot_tn(hidden[...], cot[...]).astype(BF)
    w1_grad[...] = dot_tn(second[...], gpre[...]).astype(BF)
    send[...] = dot(hidden[other, :], w2[...]).astype(BF)
    keep[...] = dot(hidden[mine, :], w2[...])
    small[...] = jnp.zeros_like(small)
    small[0:1, :] = jnp.sum(gpre[...].astype(F32), axis=0, keepdims=True)
    small[1:2, :] = jnp.sum(cot[...].astype(F32), axis=0, keepdims=True)


def attend_back_kernel(
    spot, pidx, s2a, s2b, cot, mid, x, g2, att, wo, q, k, v, probs, first, wq, wk, wv,
    gmid, pay, keep, send, small, gsec, gproj, gatt, gq, gk, gv,
):
    core = spot[0] % 2
    tokens = x.shape[0]
    half = tokens // 2
    heads = wq.shape[1] // HD
    blocks = tokens // BLOCK
    mine = pl.ds(pl.multiple_of(core * half, half), half)
    other = pl.ds(pl.multiple_of((1 - core) * half, half), half)
    gsec[mine, :] = s2a[...].astype(F32)
    gsec[other, :] = s2b[...].astype(F32)
    width = x.shape[1]
    gain_sum = jnp.zeros((1, width), F32)
    shift_sum = jnp.zeros((1, width), F32)
    proj_sum = jnp.zeros((1, width), F32)
    for b in range(blocks):
        rows = pl.ds(b * BLOCK, BLOCK)
        grad = gsec[rows, :]
        normed, inverse = normalize(mid[rows, :])
        gain_sum += jnp.sum(grad * normed, axis=0, keepdims=True)
        shift_sum += jnp.sum(grad, axis=0, keepdims=True)
        value = cot[rows, :].astype(F32) + norm_back(grad, normed, inverse, row(g2))
        gmid[rows, :] = value
        proj_sum += jnp.sum(value, axis=0, keepdims=True)
        gproj[rows, :] = value.astype(BF)
    gatt[...] = dot_nt(gproj[...], wo[...]).astype(BF)
    factor = HD ** (-0.5)
    score_sums = [jnp.zeros((BLOCK, BLOCK), F32) for _ in range(heads)]
    for b in range(blocks):
        rows = pl.ds(b * BLOCK, BLOCK)
        qb, kb, vb, gb = q[rows, :], k[rows, :], v[rows, :], gatt[rows, :]
        sum_q = jnp.zeros((BLOCK, BLOCK), F32)
        sum_k = jnp.zeros((BLOCK, BLOCK), F32)
        sum_v = jnp.zeros((BLOCK, BLOCK), F32)
        for h in range(heads):
            own = head_mask(h)
            zero = jnp.zeros_like(qb)
            prob = probs[b * heads + h]
            grad = dot_nt(gb, jnp.where(own, vb, zero))
            sum_v += dot_tn(prob.astype(BF), jnp.where(own, gb, zero))
            inner = jnp.sum(prob * grad, axis=-1, keepdims=True)
            gscore = (prob * (grad - inner)).astype(BF)
            sum_q += dot(gscore, jnp.where(own, kb, zero))
            sum_k += dot_tn(gscore, jnp.where(own, qb, zero))
            score_sums[h] += gscore.astype(F32)
        gq[rows, :] = (factor * sum_q).astype(BF)
        gk[rows, :] = (factor * sum_k).astype(BF)
        gv[rows, :] = sum_v.astype(BF)
    span = wq.shape[1]
    for j, part in enumerate((gq, gk, gv)):
        grads = dot_tn(first[...], part[...]).astype(BF)
        for i in range(width // span):
            pay[j * span:(j + 1) * span, i * span:(i + 1) * span] = grads[i * span:(i + 1) * span]
    pay[3 * span:4 * span, :] = dot_tn(att[...], gproj[...]).astype(BF)
    norm1_gain = jnp.zeros((1, width), F32)
    norm1_shift = jnp.zeros((1, width), F32)
    for part, where in ((0, mine), (1, other)):
        grads = (
            dot_nt(gq[where, :], wq[...])
            + dot_nt(gk[where, :], wk[...])
            + dot_nt(gv[where, :], wv[...])
        )
        normed, _ = normalize(x[where, :].astype(F32))
        norm1_gain += jnp.sum(grads * normed, axis=0, keepdims=True)
        norm1_shift += jnp.sum(grads, axis=0, keepdims=True)
        if part == 0:
            keep[0:half, :] = grads
        else:
            send[0:half, :] = grads.astype(BF)
    tail = keep.shape[0] - half
    which = iota((tail, width), 0)
    sums = jnp.where(which == 0, norm1_gain, jnp.where(which == 1, norm1_shift, 0.0))
    keep[half:, :] = sums
    send[half:, :] = sums.astype(BF)
    at = place(iota((BLOCK, WIN), 0)) == iota((BLOCK, WIN), 1)
    fold = at.astype(F32)
    lanes = heads * WIN
    folded = jnp.zeros((WIN, lanes), F32)
    for h in range(heads):
        lane = iota((BLOCK, lanes), 1)
        lay = ((place(iota((BLOCK, lanes), 0)) == lane % WIN) & (lane // WIN == h)).astype(F32)
        once = lax.dot_general(
            fold, score_sums[h], (((0,), (0,)), ((), ())),
            precision=EXACT, preferred_element_type=F32,
        )
        folded += jnp.dot(once, lay, precision=EXACT, preferred_element_type=F32)
    index = jnp.concatenate([pidx[...]] * heads, axis=1)
    slots = 64
    slot = iota((slots, lanes), 0)
    by_offset = jnp.zeros((slots, lanes), F32)
    for o in range(49):
        total = jnp.sum(jnp.where(index == o, folded, 0.0), axis=0, keepdims=True)
        by_offset = jnp.where(slot == o, total, by_offset)
    pick = (iota((8, lanes), 1) // WIN == iota((8, lanes), 0)).astype(F32)
    offsets = lax.dot_general(
        pick, by_offset, (((1,), (1,)), ((), ())), precision=EXACT, preferred_element_type=F32
    )
    small[...] = jnp.zeros_like(small)
    small[0:1, :] = gain_sum
    small[1:2, :] = shift_sum
    small[2:3, :] = proj_sum
    small[3:4, 0:span] = jnp.sum(gq[...].astype(F32), axis=0, keepdims=True)
    small[3:4, span:2 * span] = jnp.sum(gv[...].astype(F32), axis=0, keepdims=True)
    small[8:16, 0:slots] = offsets


def finish_kernel(spot, s4a, s4b, m4a, m4b, gmid, x, g1, mid, b2, layer_out, input_grad):
    core = spot[0] % 2
    half = x.shape[0] // 2
    for part, (gref, mref) in enumerate(((s4a, m4a), (s4b, m4b))):
        start = core if part == 0 else 1 - core
        where = pl.ds(pl.multiple_of(start * half, half), half)
        normed, inverse = normalize(x[where, :].astype(F32))
        grad = gref[0:half, :].astype(F32)
        input_grad[where, :] = gmid[where, :] + norm_back(grad, normed, inverse, row(g1))
        layer_out[where, :] = mid[where, :] + mref[...].astype(F32) + row(b2)


def call(kernel, outs, args, scalars, scratch=(), flops=0):
    in_specs = [
        pl.BlockSpec(memory_space=pltpu.SMEM if i in scalars else pltpu.VMEM)
        for i in range(len(args))
    ]
    shapes = [jax.ShapeDtypeStruct(shape, dtype) for shape, dtype in outs]
    moved = sum(a.size * a.dtype.itemsize for a in list(args) + shapes)
    return pl.pallas_call(
        kernel,
        out_shape=shapes,
        in_specs=in_specs,
        out_specs=[pl.BlockSpec(memory_space=pltpu.VMEM)] * len(shapes),
        scratch_shapes=[pltpu.VMEM(shape, dtype) for shape, dtype in scratch],
        compiler_params=pltpu.CompilerParams(vmem_limit_bytes=VMEM_BYTES),
        cost_estimate=pl.CostEstimate(flops=flops, bytes_accessed=moved, transcendentals=0),
    )(*args)


def swap(value, axis, bit, size):
    return lax.ppermute(value, axis, [(i, i ^ bit) for i in range(size)])


def shards(
    inputs,
    query_weight,
    key_weight,
    value_weight,
    query_bias,
    value_bias,
    position_bias,
    proj_weight,
    proj_bias,
    norm1_gain,
    norm1_shift,
    norm2_gain,
    norm2_shift,
    up_weight,
    up_bias,
    down_weight,
    down_bias,
    segment_ids,
    valid_mask,
    position_index,
    out_cotangent,
    dp,
    tensor,
):
    tokens, width = inputs.shape
    half = tokens // 2
    span = query_weight.shape[1]
    units = up_weight.shape[1]
    heads = span // HD
    blocks = tokens // BLOCK
    me = lax.axis_index("tensor")
    spot = me.astype(jnp.int32).reshape(1)
    mate = lax.axis_index("dp")
    seg = segment_ids.reshape(1, tokens)
    valid = valid_mask.reshape(1, tokens)

    wo_x = swap(proj_weight, "tensor", 2, tensor)
    wo_c = swap(proj_weight, "tensor", 1, tensor)
    wo_d = swap(wo_x, "tensor", 1, tensor)

    att, first, q, k, v, probs = call(
        attend_kernel,
        [
            ((tokens, span), BF), ((tokens, width), BF), ((tokens, span), BF),
            ((tokens, span), BF), ((tokens, span), BF), ((blocks * heads, BLOCK, BLOCK), F32),
        ],
        [
            position_bias, seg, valid, position_index, inputs, query_weight, key_weight,
            value_weight, query_bias, value_bias, norm1_gain, norm1_shift,
        ],
        (0,),
        flops=2 * tokens * width * 3 * span,
    )
    att_x = swap(att, "tensor", 2, tensor)
    att_c = swap(att, "tensor", 1, tensor)
    att_d = swap(att_x, "tensor", 1, tensor)

    mid, second, hidden, gpre, keep3, send3 = call(
        mlp_kernel,
        [
            ((tokens, width), F32), ((tokens, width), BF), ((tokens, units), BF),
            ((tokens, units), BF), ((half, width), F32), ((half, width), BF),
        ],
        [
            spot, inputs, out_cotangent, att, att_c, att_x, att_d, proj_weight, wo_c, wo_x, wo_d,
            proj_bias, norm2_gain, norm2_shift, up_weight, up_bias, down_weight,
        ],
        (0,),
        scratch=[((tokens, tensor * span), BF), ((tensor * span, width), BF)],
        flops=2 * tokens * width * 4 * units,
    )

    def fold(value, other):
        return (value.astype(F32) + other.astype(F32)).astype(BF)

    pair3 = fold(keep3, swap(send3, "tensor", 1, tensor))
    sum3 = fold(pair3, swap(pair3, "tensor", 2, tensor))
    rest3 = swap(sum3, "tensor", 1, tensor)

    w1_pay, w2_pay, keep2, send2, small_a = call(
        mlp_grad_kernel,
        [
            ((width, units), BF), ((units, width), BF), ((half, width), F32),
            ((half, width), BF), ((8, width), F32),
        ],
        [spot, out_cotangent, second, hidden, gpre, down_weight],
        (0,),
        flops=2 * tokens * width * 3 * units,
    )

    gmid, pay, keep4, send4, small_b = call(
        attend_back_kernel,
        [
            ((tokens, width), F32), ((4 * span, width), BF), ((half + 16, width), F32),
            ((half + 16, width), BF), ((16, width), F32),
        ],
        [
            spot, position_index, sum3, rest3, out_cotangent, mid, inputs, norm2_gain, att,
            proj_weight, q, k, v, probs, first, query_weight, key_weight, value_weight,
        ],
        (0,),
        scratch=[
            ((tokens, width), F32), ((tokens, width), BF), ((tokens, span), BF),
            ((tokens, span), BF), ((tokens, span), BF), ((tokens, span), BF),
        ],
        flops=2 * tokens * width * 8 * span,
    )

    keep4 = jnp.concatenate([keep4, keep2])
    send4 = jnp.concatenate([send4, send2])
    pair4 = fold(keep4, swap(send4, "tensor", 1, tensor))
    sum4 = fold(pair4, swap(pair4, "tensor", 2, tensor))
    rest4 = swap(sum4, "tensor", 1, tensor)

    bits = [1 << i for i in range(dp.bit_length() - 1)]

    def scatter(value):
        for bit in bits:
            part = value.shape[0] // 2
            flag = (mate // bit) % 2
            own = lax.dynamic_slice_in_dim(value, flag * part, part)
            away = lax.dynamic_slice_in_dim(value, (1 - flag) * part, part)
            value = fold(own, swap(away, "dp", bit, dp))
        return value

    def join(bit, own, other):
        flag = (mate // bit) % 2
        return jnp.where(
            flag == 0, jnp.concatenate([own, other]), jnp.concatenate([other, own])
        )

    def gather(value, extra=None):
        for bit in reversed(bits):
            if extra is None:
                value = join(bit, value, swap(value, "dp", bit, dp))
            else:
                rows = value.shape[0]
                come = swap(jnp.concatenate([value, extra]), "dp", bit, dp)
                value = join(bit, value, come[:rows])
                extra = fold(extra, come[rows:])
        return value if extra is None else (value, extra)

    mlp_total = gather(scatter(jnp.concatenate([w1_pay, w2_pay])))
    w1_total = mlp_total[:width].astype(F32)
    w2_total = mlp_total[width:].astype(F32)

    small = jnp.concatenate([small_a.astype(BF), small_b.astype(BF), sum4[half:half + 8]])
    att_total, small = gather(scatter(pay), small)
    att_total = att_total.astype(F32)
    small = small.astype(F32)

    def unfold(block):
        return jnp.concatenate([block[:, i * span:(i + 1) * span] for i in range(width // span)])

    wq_total = unfold(att_total[:span])
    wk_total = unfold(att_total[span:2 * span])
    wv_total = unfold(att_total[2 * span:3 * span])
    wo_total = att_total[3 * span:]
    b1_total, b2_total = small[0], small[1]
    g2_total, s2_total, bo_total = small[8], small[9], small[10]
    bq_total, bv_total = small[11, :span], small[11, span:2 * span]
    rel_total = small[16:16 + heads, :position_bias.shape[0]].T
    g1_total, s1_total = small[24], small[25]

    layer_out, input_grad = call(
        finish_kernel,
        [((tokens, width), F32), ((tokens, width), F32)],
        [
            spot, sum4[:half], rest4[:half], sum4[half + 16:], rest4[half + 16:], gmid, inputs,
            norm1_gain, mid, down_bias,
        ],
        (0,),
        flops=tokens * width,
    )
    return (
        layer_out,
        input_grad,
        wq_total,
        wk_total,
        wv_total,
        bq_total,
        bv_total,
        rel_total,
        wo_total,
        bo_total,
        g1_total,
        s1_total,
        g2_total,
        s2_total,
        w1_total,
        b1_total,
        w2_total,
        b2_total,
    )


def solution(mesh):
    dp, tensor = mesh.shape["dp"], mesh.shape["tensor"]

    def body(*args):
        return shards(*args, dp=dp, tensor=tensor)

    column, line, whole = P(None, "tensor"), P("tensor"), P()
    return jax.shard_map(
        body,
        mesh=mesh,
        in_specs=(
            P("dp", None),
            column,
            column,
            column,
            line,
            line,
            column,
            P("tensor", None),
            whole,
            whole,
            whole,
            whole,
            whole,
            column,
            line,
            P("tensor", None),
            whole,
            P("dp", None),
            P("dp", None),
            whole,
            P("dp", None),
        ),
        out_specs=(
            P("dp", None),
            P("dp", None),
            column,
            column,
            column,
            line,
            line,
            column,
            P("tensor", None),
            whole,
            whole,
            whole,
            whole,
            whole,
            column,
            line,
            P("tensor", None),
            whole,
        ),
        check_vma=False,
    )
```

time: 362 us -> 136 us (0.38)
  waiting for transfers between devices: 212 us -> 50.3 us
  blocking collectives: 39.6 us -> 0 us
  matrix products: 31.7 us -> 0 us
  Pallas kernels: 0 us -> 16.2 us
  starting transfers between devices: 0.39 us -> 16.2 us
  between operations: 14.4 us -> 1.1 us
  local copies, waits for them, and re-layouts: 47.8 us -> 38.6 us
    psum x5 -> x0, waiting for transfers between devices: 212 us -> none  [the longest x1 91.6 us: shards(): lax.psum((wq_part, wk_part, wv_part, bq_part, bv_part, rel_part, wo_part,...]
    ppermute x0 -> x24, waiting for transfers between devices: none -> 50.3 us  [swap(): return lax.ppermute(value, axis, [(i, i ^ bit) for i in range(size)])]
    psum x1 -> x0, blocking collectives: 39.6 us -> none  [shards(): lax.psum((wq_part, wk_part, wv_part, bq_part, bv_part, rel_part, wo_part,...]
    dot_general x25 -> x0, matrix products: 28.9 us -> none  [the longest x18 22 us: matmul(): return jnp.dot(left, right, preferred_element_type=jnp.float32)]
    pallas_call x0 -> x5, Pallas kernels: none -> 16.2 us  [call(): pl.pallas_call(kernel, out_shape=shapes, in_specs=in_specs, out_specs=[pl...]
    ppermute x0 -> x24, starting transfers between devices: none -> 16.2 us  [swap(): return lax.ppermute(value, axis, [(i, i ^ bit) for i in range(size)])]
    unnamed x123 -> x112, local copies, waits for them, and re-layouts: 17.8 us -> 33.6 us
    reshape x14 -> x0, local copies, waits for them, and re-layouts: 13 us -> none  [the longest x2 3.92 us: from_windows(): return shaped.transpose(0, 1, 3, 2, 4, 5).reshape(-1, chans)]
  transfers between devices with their start and end apart: 5 -> 24, of which waited for: 5 -> 12; matrix products, arithmetic and copies ran while one was open for 9% -> 10% of each run, Pallas kernels for 0% -> 9%
where the time goes in v1:
time: 136 us; the launch traced here: 135 us
  waiting for transfers between devices  50.3 us (37%)
  local copies, waits for them, and re-layouts  38.6 us (28%)
  starting transfers between devices  16.2 us (12%)
  Pallas kernels  16.2 us (12%)
  other arithmetic  12.8 us (9%)
    ppermute x24, waiting for transfers between devices, swap(): return lax.ppermute(value, axis, [(i, i ^ bit) for i in range(size)])  50.3 us
    unnamed x112, local copies, waits for them, and re-layouts  33.6 us
    pallas_call x5, Pallas kernels, call(): pl.pallas_call(kernel, out_shape=shapes, in_specs=in_specs, out_specs=[pl...  16.2 us
    ppermute x24, starting transfers between devices, swap(): return lax.ppermute(value, axis, [(i, i ^ bit) for i in range(size)])  16.2 us
    convert_element_type x12, other arithmetic, fold(): return (value.astype(F32) + other.astype(F32)).astype(BF)  6.73 us
  transfers between devices with their start and end apart: 24, of which 12 were waited for; matrix products, arithmetic and copies ran while one was open for 10% of the time, Pallas kernels for 9%

profile of v1, /device:TPU:0, one launch (start us, length us, event | category | flops | bytes accessed | tf_op | source)
XLA Modules:
  0.0 135.2 jit_solution(2062899592559468508)
XLA Ops:
  0.7 3.0 %collective-permute-start.4 = (bf16[128,512]{1,0:T(8,128)(2,1)}, bf16[128,512]{1,0:T(8,128)(2,1)S(1)}, u32[]{:S(2)}, u32[]{:S(2)}) collective-permute-start(bf16[128,512]{1,0:T(8,128)(2,1)} %wo.1), channel_id=1, source_target_pairs={{0,2},{1,3},{2,0},{3,1},{4,6},{5,7},{6,4},{7,5},{8,10},{9,11},{10,... | collective-permute-start | bytes 393224 | tf_op jit(solution)/shard_map/ppermute | solution.py:307
  4.4 1.0 copy-done
  5.5 0.9 copy-done.12
  6.4 0.9 copy-done.14
  7.3 0.9 copy-done.16
  12.9 4.6 %shard_map.340 = (bf16[512,128]{1,0:T(8,128)(2,1)S(1)}, bf16[512,512]{1,0:T(8,128)(2,1)S(1)}, bf16[512,128]{1,0:T(8,128)(2,1)S(1)}, bf16[512,128]{1,0:T(8,128)(2...) custom-call(f32[49,4]{1,0:T(8,128)S(1)} %copy.39.rel, s32[1,512]{1,0:T(1,128)S(1)} %copy-done.38, ...), custom_call_target="tpu_custom_call" | custom-call | flops 201326592 | bytes 3025680 | tf_op jit(solution)/shard_map/pallas_call | solution.py:295
  20.9 4.4 %collective-permute-done.1.a2 = bf16[512,128]{1,0:T(8,128)(2,1)S(1)} collective-permute-done((bf16[512,128]{1,0:T(8,128)(2,1)S(1)}, bf16[512,128]{1,0:T(8,128)(2,1)S(1)}, u32[]{:S(2)}, u32[]{:S(2)}) %collective-permute-start.1) | collective-permute-done | bytes 131104 | tf_op jit(solution)/shard_map/ppermute | solution.py:307
  27.3 1.0 copy-done.1
  28.4 1.0 copy-done.5
  29.4 0.9 copy-done.22
  31.0 1.0 copy-done.44
  32.0 1.0 copy-done.45
  33.1 0.9 copy-done.47
  34.0 0.9 copy-done.49
  36.9 2.4 %shard_map.341 = (f32[512,512]{1,0:T(8,128)S(1)}, bf16[512,512]{1,0:T(8,128)(2,1)S(1)}, bf16[512,512]{1,0:T(8,128)(2,1)S(1)}, bf16[512,512]{1,0:T(8,128)(2,1)S(1...) custom-call(s32[1]{0:T(128)} %bitcast.spot, bf16[512,512]{1,0:T(8,128)(2,1)S(1)} %copy-done.1, ...), custom_call_target="tpu_custom_call" | custom-call | flops 1073741824 | bytes 6561796 | tf_op jit(solution)/shard_map/pallas_call | solution.py:295
  39.3 1.0 shard_map.343
  42.2 1.5 %collective-permute-start.18 = (bf16[512,512]{1,0:T(8,128)(2,1)}, bf16[512,512]{1,0:T(8,128)(2,1)}, u32[]{:S(2)}, u32[]{:S(2)}) collective-permute-start(bf16[512,512]{1,0:T(8,128)(2,1)} %constant_dynamic-slice_fusion.2), channel_id=1, source_target_pairs={{0,4},{4,0},{8,12},{12,8},{16,20},{20,16},{24,28},{28,24},{1,5},{5... | collective-permute-start | bytes 1572872 | tf_op jit(solution)/shard_map/ppermute | solution.py:307
  43.7 1.5 %collective-permute-done.6 = bf16[256,512]{1,0:T(8,128)(2,1)S(1)} collective-permute-done((bf16[256,512]{1,0:T(8,128)(2,1)S(1)}, bf16[256,512]{1,0:T(8,128)(2,1)S(1)}, u32[]{:S(2)}, u32[]{:S(2)}) %collective-permute-start.6) | collective-permute-done | bytes 262176 | tf_op jit(solution)/shard_map/ppermute | solution.py:307
  46.5 9.9 %collective-permute-done.18 = bf16[512,512]{1,0:T(8,128)(2,1)} collective-permute-done((bf16[512,512]{1,0:T(8,128)(2,1)}, bf16[512,512]{1,0:T(8,128)(2,1)}, u32[]{:S(2)}, u32[]{:S(2)}) %collective-permute-start.18) | collective-permute-done | bytes 524320 | tf_op jit(solution)/shard_map/ppermute | solution.py:307
  56.4 1.2 add_convert_fusion.1
  58.4 1.6 %collective-permute-start.19 = (bf16[256,512]{1,0:T(8,128)(2,1)}, bf16[256,512]{1,0:T(8,128)(2,1)}, u32[]{:S(2)}, u32[]{:S(2)}) collective-permute-start(bf16[256,512]{1,0:T(8,128)(2,1)} %constant_dynamic-slice_fusion.1), channel_id=1, source_target_pairs={{0,8},{4,12},{8,0},{12,4},{16,24},{20,28},{24,16},{28,20},{1,9},{5... | collective-permute-start | bytes 786440 | tf_op jit(solution)/shard_map/ppermute | solution.py:307
  60.0 1.1 add_convert_fusion.4.s2a
  61.2 5.1 %collective-permute-done.19 = bf16[256,512]{1,0:T(8,128)(2,1)} collective-permute-done((bf16[256,512]{1,0:T(8,128)(2,1)}, bf16[256,512]{1,0:T(8,128)(2,1)}, u32[]{:S(2)}, u32[]{:S(2)}) %collective-permute-start.19) | collective-permute-done | bytes 262176 | tf_op jit(solution)/shard_map/ppermute | solution.py:307
  66.3 1.0 add_convert_fusion.2
  67.3 2.7 %collective-permute-start.20 = (bf16[128,512]{1,0:T(8,128)(2,1)S(1)}, bf16[128,512]{1,0:T(8,128)(2,1)S(1)}, u32[]{:S(2)}, u32[]{:S(2)}) collective-permute-start(bf16[128,512]{1,0:T(8,128)(2,1)S(1)} %constant_dynamic-slice_fusion), channel_id=1, source_target_pairs={{0,16},{4,20},{8,24},{12,28},{16,0},{20,4},{24,8},{28,12},{1,17},{... | collective-permute-start | bytes 393224 | tf_op jit(solution)/shard_map/ppermute | solution.py:307
  70.0 1.0 copy-done.7
  71.1 1.0 copy-done.9
  72.1 0.9 copy-done.17
  73.0 0.9 copy-done.23
  73.9 0.9 copy-done.25
  74.8 0.9 copy-done.27
  75.7 0.9 copy-done.29
  77.5 6.1 %shard_map.342 = (f32[512,512]{1,0:T(8,128)S(1)}, bf16[512,512]{1,0:T(8,128)(2,1)S(1)}, f32[272,512]{1,0:T(8,128)S(1)}, bf16[272,512]{1,0:T(8,128)(2,1)S(1)}, f32[16,512]{1,0:T(8,128)S(1)}) custom-call(s32[1]{0:T(128)} %bitcast.spot, s32[16,16]{1,0:T(8,128)S(1)} %copy-done.33, bf16[256,512]{1,0:T(8,128)(2,1)S(1)} %add_convert_fusion.4.s2a, ...), custom_call_target="tpu_custom_call" | custom-call | flops 536870912 | bytes 7687172 | tf_op jit(solution)/shard_map/pallas_call | solution.py:295
  83.6 1.0 copy-done.3
  86.1 1.5 %collective-permute-start.12 = (bf16[256,512]{1,0:T(8,128)(2,1)}, bf16[256,512]{1,0:T(8,128)(2,1)}, u32[]{:S(2)}, u32[]{:S(2)}) collective-permute-start(bf16[256,512]{1,0:T(8,128)(2,1)} %constant_dynamic-slice_fusion.5), channel_id=1, source_target_pairs={{0,4},{4,0},{8,12},{12,8},{16,20},{20,16},{24,28},{28,24},{1,5},{5... | collective-permute-start | bytes 786440 | tf_op jit(solution)/shard_map/ppermute | solution.py:307
  89.1 6.2 %collective-permute-done.21 = bf16[128,512]{1,0:T(8,128)(2,1)} collective-permute-done((bf16[128,512]{1,0:T(8,128)(2,1)S(1)}, bf16[128,512]{1,0:T(8,128)(2,1)}, u32[]{:S(2)}, u32[]{:S(2)}) %collective-permute-start.21) | collective-permute-done | bytes 131104 | tf_op jit(solution)/shard_map/ppermute | solution.py:307
  95.3 1.1 maximum_select_fusion.4
  96.7 1.0 add_convert_fusion.3
  97.8 1.8 %collective-permute-start.13 = (bf16[128,512]{1,0:T(8,128)(2,1)S(1)}, bf16[128,512]{1,0:T(8,128)(2,1)S(1)}, u32[]{:S(2)}, u32[]{:S(2)}) collective-permute-start(bf16[128,512]{1,0:T(8,128)(2,1)S(1)} %constant_dynamic-slice_fusion.4), channel_id=1, source_target_pairs={{0,8},{4,12},{8,0},{12,4},{16,24},{20,28},{24,16},{28,20},{1,9},{5... | collective-permute-start | bytes 393224 | tf_op jit(solution)/shard_map/ppermute | solution.py:307
  99.6 1.2 fusion
  101.4 3.5 %collective-permute-done.13 = bf16[128,512]{1,0:T(8,128)(2,1)S(1)} collective-permute-done((bf16[128,512]{1,0:T(8,128)(2,1)S(1)}, bf16[128,512]{1,0:T(8,128)(2,1)S(1)}, u32[]{:S(2)}, u32[]{:S(2)}) %collective-permute-start.13) | collective-permute-done | bytes 131104 | tf_op jit(solution)/shard_map/ppermute | solution.py:307
  105.9 6.4 %collective-permute-done.14 = bf16[64,512]{1,0:T(8,128)(2,1)S(1)} collective-permute-done((bf16[64,512]{1,0:T(8,128)(2,1)S(1)}, bf16[64,512]{1,0:T(8,128)(2,1)S(1)}, u32[]{:S(2)}, u32[]{:S(2)}) %collective-permute-start.14) | collective-permute-done | bytes 65568 | tf_op jit(solution)/shard_map/ppermute | solution.py:307
  112.7 1.9 %collective-permute-done.23 = bf16[512,512]{1,0:T(8,128)(2,1)S(1)} collective-permute-done((bf16[512,512]{1,0:T(8,128)(2,1)S(1)}, bf16[512,512]{1,0:T(8,128)(2,1)S(1)}, u32[]{:S(2)}, u32[]{:S(2)}) %collective-permute-start.23) | collective-permute-done | bytes 524320 | tf_op jit(solution)/shard_map/ppermute | solution.py:307
  115.1 3.4 %collective-permute-done.15 = bf16[96,512]{1,0:T(8,128)(2,1)S(1)} collective-permute-done((bf16[96,512]{1,0:T(8,128)(2,1)S(1)}, bf16[96,512]{1,0:T(8,128)(2,1)S(1)}, u32[]{:S(2)}, u32[]{:S(2)}) %collective-permute-start.15) | collective-permute-done | bytes 98336 | tf_op jit(solution)/shard_map/ppermute | solution.py:307
  118.6 1.6 %slice_convert_fusion = (f32[512,512]{1,0:T(8,128)}, f32[512,512]{1,0:T(8,128)}) fusion(bf16[1024,512]{1,0:T(8,128)(2,1)S(1)} %maximum_select_fusion), kind=kLoop, calls=%fused_computation.6 | loop fusion | flops 524288 | bytes 3145728 | tf_op jit(solution)/shard_map/convert_element_type | solution.py:455
  120.2 3.7 %collective-permute-done.16 = bf16[160,512]{1,0:T(8,128)(2,1)S(1)} collective-permute-done((bf16[160,512]{1,0:T(8,128)(2,1)S(1)}, bf16[160,512]{1,0:T(8,128)(2,1)S(1)}, u32[]{:S(2)}, u32[]{:S(2)}) %collective-permute-start.16) | collective-permute-done | bytes 163872 | tf_op jit(solution)/shard_map/ppermute | solution.py:307
  125.3 2.1 %shard_map.344 = (f32[512,512]{1,0:T(8,128)}, f32[512,512]{1,0:T(8,128)}) custom-call(s32[1]{0:T(128)} %bitcast.spot, bf16[256,512]{1,0:T(8,128)(2,1)S(1)} %get-tuple-element.83.s4a, bf16[256,512]{1,0:T(8,128)(2,1)S(1)} %get-tuple-element.81.s4b, bf16[256,512]{1,0:T(8,128)(2,1)S(1)} %get-tuple-element.82.m4a, bf16[256,512]{1,0:T(8,128)(2,1)S(1)} %get-tuple-element.80.m4b, ...), custom_call_target="tpu_custom_call" | custom-call | flops 262144 | bytes 5771268 | tf_op jit(solution)/shard_map/pallas_call | solution.py:295
  127.4 3.5 %collective-permute-done.17 = bf16[288,512]{1,0:T(8,128)(2,1)S(1)} collective-permute-done((bf16[288,512]{1,0:T(8,128)(2,1)S(1)}, bf16[288,512]{1,0:T(8,128)(2,1)S(1)}, u32[]{:S(2)}, u32[]{:S(2)}) %collective-permute-start.17) | collective-permute-done | bytes 294944 | tf_op jit(solution)/shard_map/ppermute | solution.py:307
  (163 shorter events, 29.7 us)
Async XLA Ops:
  0.7 20.2 %collective-permute-start.4 = (bf16[128,512]{1,0:T(8,128)(2,1)}, bf16[128,512]{1,0:T(8,128)(2,1)S(1)}, u32[]{:S(2)}, u32[]{:S(2)}) collective-permute-start(bf16[128,512]{1,0:T(8,128)(2,1)} %wo.1), channel_id=1, source_target_pairs={{0,2},{1,3},{2,0},{3,1},{4,6},{5,7},{6,4},{7,5},{8,10},{9,11},{10,... | collective-permute-start | bytes 393224 | tf_op jit(solution)/shard_map/ppermute | solution.py:307
  4.4 1.0 copy-start
  20.3 19.0 %copy-start.24 = (bf16[512,128]{1,0:T(8,128)(2,1)}, bf16[512,128]{1,0:T(8,128)(2,1)S(1)}, u32[]{:S(2)}) copy-start(bf16[512,128]{1,0:T(8,128)(2,1)S(1)} %get-tuple-element.42.a0.att) | copy-start | bytes 393220
  20.3 5.0 %collective-permute-start.1 = (bf16[512,128]{1,0:T(8,128)(2,1)S(1)}, bf16[512,128]{1,0:T(8,128)(2,1)S(1)}, u32[]{:S(2)}, u32[]{:S(2)}) collective-permute-start(bf16[512,128]{1,0:T(8,128)(2,1)S(1)} %get-tuple-element.42.a0.att), channel_id=1, source_target_pairs={{0,2},{1,3},{2,0},{3,1},{4,6},{5,7},{6,4},{7,5},{8,10},{9,11},{10,... | collective-permute-start | bytes 393224 | tf_op jit(solution)/shard_map/ppermute | solution.py:307
  20.4 5.0 %collective-permute-start.3 = (bf16[128,512]{1,0:T(8,128)(2,1)}, bf16[128,512]{1,0:T(8,128)(2,1)S(1)}, u32[]{:S(2)}, u32[]{:S(2)}) collective-permute-start(bf16[128,512]{1,0:T(8,128)(2,1)} %wo.1), channel_id=1, source_target_pairs={{0,1},{1,0},{2,3},{3,2},{4,5},{5,4},{6,7},{7,6},{8,9},{9,8},{10,11... | collective-permute-start | bytes 393224 | tf_op jit(solution)/shard_map/ppermute | solution.py:307
  20.4 5.0 %collective-permute-start = (bf16[512,128]{1,0:T(8,128)(2,1)S(1)}, bf16[512,128]{1,0:T(8,128)(2,1)S(1)}, u32[]{:S(2)}, u32[]{:S(2)}) collective-permute-start(bf16[512,128]{1,0:T(8,128)(2,1)S(1)} %get-tuple-element.42.a0.att), channel_id=1, source_target_pairs={{0,1},{1,0},{2,3},{3,2},{4,5},{5,4},{6,7},{7,6},{8,9},{9,8},{10,11... | collective-permute-start | bytes 393224 | tf_op jit(solution)/shard_map/ppermute | solution.py:307
  20.9 4.5 %collective-permute-start.5 = (bf16[128,512]{1,0:T(8,128)(2,1)S(1)}, bf16[128,512]{1,0:T(8,128)(2,1)S(1)}, u32[]{:S(2)}, u32[]{:S(2)}) collective-permute-start(bf16[128,512]{1,0:T(8,128)(2,1)S(1)} %collective-permute-done.4.p2), channel_id=1, source_target_pairs={{0,1},{1,0},{2,3},{3,2},{4,5},{5,4},{6,7},{7,6},{8,9},{9,8},{10,11... | collective-permute-start | bytes 393224 | tf_op jit(solution)/shard_map/ppermute | solution.py:307
  25.3 1.3 collective-permute-start.2
  27.3 1.0 copy-start.1
  28.4 1.0 copy-start.5
  31.0 1.0 copy-start.44
  32.0 1.0 copy-start.45
  33.1 0.9 copy-start.47
  36.9 2.4 %copy-start.6 = (bf16[512,512]{1,0:T(8,128)(2,1)S(1)}, bf16[512,512]{1,0:T(8,128)(2,1)}, u32[]{:S(2)}) copy-start(bf16[512,512]{1,0:T(8,128)(2,1)} %cot.5) | copy-start | bytes 1572868
  41.3 2.4 %copy-start.53 = (bf16[1024,512]{1,0:T(8,128)(2,1)}, bf16[1024,512]{1,0:T(8,128)(2,1)S(1)}, u32[]{:S(2)}) copy-start(bf16[1024,512]{1,0:T(8,128)(2,1)S(1)} %constant_dynamic-update-slice_fusion) | copy-start | bytes 3145732
  42.2 14.3 %collective-permute-start.18 = (bf16[512,512]{1,0:T(8,128)(2,1)}, bf16[512,512]{1,0:T(8,128)(2,1)}, u32[]{:S(2)}, u32[]{:S(2)}) collective-permute-start(bf16[512,512]{1,0:T(8,128)(2,1)} %constant_dynamic-slice_fusion.2), channel_id=1, source_target_pairs={{0,4},{4,0},{8,12},{12,8},{16,20},{20,16},{24,28},{28,24},{1,5},{5... | collective-permute-start | bytes 1572872 | tf_op jit(solution)/shard_map/ppermute | solution.py:307
  43.7 1.5 %collective-permute-start.6 = (bf16[256,512]{1,0:T(8,128)(2,1)S(1)}, bf16[256,512]{1,0:T(8,128)(2,1)S(1)}, u32[]{:S(2)}, u32[]{:S(2)}) collective-permute-start(bf16[256,512]{1,0:T(8,128)(2,1)S(1)} %get-tuple-element.44), channel_id=1, source_target_pairs={{0,1},{1,0},{2,3},{3,2},{4,5},{5,4},{6,7},{7,6},{8,9},{9,8},{10,11... | collective-permute-start | bytes 786440 | tf_op jit(solution)/shard_map/ppermute | solution.py:307
  43.7 12.8 %copy-start.54 = (bf16[1024,512]{1,0:T(8,128)(2,1)S(1)}, bf16[1024,512]{1,0:T(8,128)(2,1)}, u32[]{:S(2)}) copy-start(bf16[1024,512]{1,0:T(8,128)(2,1)} %copy-done.53) | copy-start | bytes 3145732
  46.0 14.0 %collective-permute-start.7 = (bf16[256,512]{1,0:T(8,128)(2,1)}, bf16[256,512]{1,0:T(8,128)(2,1)}, u32[]{:S(2)}, u32[]{:S(2)}) collective-permute-start(bf16[256,512]{1,0:T(8,128)(2,1)} %add_convert_fusion.5), channel_id=1, source_target_pairs={{0,2},{1,3},{2,0},{3,1},{4,6},{5,7},{6,4},{7,5},{8,10},{9,11},{10,... | collective-permute-start | bytes 786440 | tf_op jit(solution)/shard_map/ppermute | solution.py:307
  58.4 11.6 %copy-start.2 = (bf16[512,512]{1,0:T(8,128)(2,1)S(1)}, bf16[512,512]{1,0:T(8,128)(2,1)}, u32[]{:S(2)}) copy-start(bf16[512,512]{1,0:T(8,128)(2,1)} %x.7) | copy-start | bytes 1572868
  58.4 11.6 %copy-start.13 = (bf16[512,128]{1,0:T(8,128)(2,1)S(1)}, bf16[512,128]{1,0:T(8,128)(2,1)}, u32[]{:S(2)}) copy-start(bf16[512,128]{1,0:T(8,128)(2,1)} %wq.3) | copy-start | bytes 393220
  58.4 11.6 %copy-start.15 = (bf16[512,128]{1,0:T(8,128)(2,1)S(1)}, bf16[512,128]{1,0:T(8,128)(2,1)}, u32[]{:S(2)}) copy-start(bf16[512,128]{1,0:T(8,128)(2,1)} %wk.3) | copy-start | bytes 393220
  58.4 11.6 %copy-start.33 = (s32[16,16]{1,0:T(8,128)S(1)}, s32[16,16]{1,0:T(8,128)}, u32[]{:S(2)}) copy-start(s32[16,16]{1,0:T(8,128)} %pidx.3) | copy-start | bytes 3076
  58.4 11.7 %copy-start.37 = (f32[512]{0:T(512)S(1)}, f32[512]{0:T(512)}, u32[]{:S(2)}) copy-start(f32[512]{0:T(512)} %g2.3) | copy-start | bytes 6148
  58.4 7.9 %collective-permute-start.19 = (bf16[256,512]{1,0:T(8,128)(2,1)}, bf16[256,512]{1,0:T(8,128)(2,1)}, u32[]{:S(2)}, u32[]{:S(2)}) collective-permute-start(bf16[256,512]{1,0:T(8,128)(2,1)} %constant_dynamic-slice_fusion.1), channel_id=1, source_target_pairs={{0,8},{4,12},{8,0},{12,4},{16,24},{20,28},{24,16},{28,20},{1,9},{5... | collective-permute-start | bytes 786440 | tf_op jit(solution)/shard_map/ppermute | solution.py:307
  61.1 8.9 %collective-permute-start.8 = (bf16[256,512]{1,0:T(8,128)(2,1)S(1)}, bf16[256,512]{1,0:T(8,128)(2,1)S(1)}, u32[]{:S(2)}, u32[]{:S(2)}) collective-permute-start(bf16[256,512]{1,0:T(8,128)(2,1)S(1)} %add_convert_fusion.4.s2a), channel_id=1, source_target_pairs={{0,1},{1,0},{2,3},{3,2},{4,5},{5,4},{6,7},{7,6},{8,9},{9,8},{10,11... | collective-permute-start | bytes 786440 | tf_op jit(solution)/shard_map/ppermute | solution.py:307
  67.3 20.3 %collective-permute-start.20 = (bf16[128,512]{1,0:T(8,128)(2,1)S(1)}, bf16[128,512]{1,0:T(8,128)(2,1)S(1)}, u32[]{:S(2)}, u32[]{:S(2)}) collective-permute-start(bf16[128,512]{1,0:T(8,128)(2,1)S(1)} %constant_dynamic-slice_fusion), channel_id=1, source_target_pairs={{0,16},{4,20},{8,24},{12,28},{16,0},{20,4},{24,8},{28,12},{1,17},{... | collective-permute-start | bytes 393224 | tf_op jit(solution)/shard_map/ppermute | solution.py:307
  70.0 1.0 copy-start.7
  71.1 1.0 copy-start.9
  83.6 1.0 copy-start.3
  84.6 3.7 %copy-start.21 = (bf16[256,512]{1,0:T(8,128)(2,1)S(1)}, bf16[256,512]{1,0:T(8,128)(2,1)}, u32[]{:S(2)}) copy-start(bf16[256,512]{1,0:T(8,128)(2,1)} %copy-done.20) | copy-start | bytes 786436
  86.1 10.6 %copy-start.11 = (bf16[512,512]{1,0:T(8,128)(2,1)S(1)}, bf16[512,512]{1,0:T(8,128)(2,1)}, u32[]{:S(2)}) copy-start(bf16[512,512]{1,0:T(8,128)(2,1)} %copy-done.10) | copy-start | bytes 1572868
  86.1 10.6 %collective-permute-start.12 = (bf16[256,512]{1,0:T(8,128)(2,1)}, bf16[256,512]{1,0:T(8,128)(2,1)}, u32[]{:S(2)}, u32[]{:S(2)}) collective-permute-start(bf16[256,512]{1,0:T(8,128)(2,1)} %constant_dynamic-slice_fusion.5), channel_id=1, source_target_pairs={{0,4},{4,0},{8,12},{12,8},{16,20},{20,16},{24,28},{28,24},{1,5},{5... | collective-permute-start | bytes 786440 | tf_op jit(solution)/shard_map/ppermute | solution.py:307
  87.9 7.4 %collective-permute-start.21 = (bf16[128,512]{1,0:T(8,128)(2,1)S(1)}, bf16[128,512]{1,0:T(8,128)(2,1)}, u32[]{:S(2)}, u32[]{:S(2)}) collective-permute-start(bf16[128,512]{1,0:T(8,128)(2,1)S(1)} %add_convert_fusion.6), channel_id=1, source_target_pairs={{0,16},{4,20},{8,24},{12,28},{16,0},{20,4},{24,8},{28,12},{1,17},{... | collective-permute-start | bytes 393224 | tf_op jit(solution)/shard_map/ppermute | solution.py:307
  89.1 10.5 %copy-start.19 = (f32[256,512]{1,0:T(8,128)S(1)}, f32[256,512]{1,0:T(8,128)}, u32[]{:S(2)}) copy-start(f32[256,512]{1,0:T(8,128)} %copy-done.18) | copy-start | bytes 1572868
  89.1 10.5 %collective-permute-start.9 = (bf16[528,512]{1,0:T(8,128)(2,1)}, bf16[528,512]{1,0:T(8,128)(2,1)}, u32[]{:S(2)}, u32[]{:S(2)}) collective-permute-start(bf16[528,512]{1,0:T(8,128)(2,1)} %pad_maximum_fusion), channel_id=1, source_target_pairs={{0,1},{1,0},{2,3},{3,2},{4,5},{5,4},{6,7},{7,6},{8,9},{9,8},{10,11... | collective-permute-start | bytes 1622024 | tf_op jit(solution)/shard_map/ppermute | solution.py:307
  96.4 8.8 %collective-permute-start.22 = (bf16[256,512]{1,0:T(8,128)(2,1)S(1)}, bf16[256,512]{1,0:T(8,128)(2,1)S(1)}, u32[]{:S(2)}, u32[]{:S(2)}) collective-permute-start(bf16[256,512]{1,0:T(8,128)(2,1)S(1)} %maximum_select_fusion.4), channel_id=1, source_target_pairs={{0,8},{4,12},{8,0},{12,4},{16,24},{20,28},{24,16},{28,20},{1,9},{5... | collective-permute-start | bytes 786440 | tf_op jit(solution)/shard_map/ppermute | solution.py:307
  97.8 7.2 %collective-permute-start.13 = (bf16[128,512]{1,0:T(8,128)(2,1)S(1)}, bf16[128,512]{1,0:T(8,128)(2,1)S(1)}, u32[]{:S(2)}, u32[]{:S(2)}) collective-permute-start(bf16[128,512]{1,0:T(8,128)(2,1)S(1)} %constant_dynamic-slice_fusion.4), channel_id=1, source_target_pairs={{0,8},{4,12},{8,0},{12,4},{16,24},{20,28},{24,16},{28,20},{1,9},{5... | collective-permute-start | bytes 393224 | tf_op jit(solution)/shard_map/ppermute | solution.py:307
  100.8 11.6 %collective-permute-start.10 = (bf16[528,512]{1,0:T(8,128)(2,1)S(1)}, bf16[528,512]{1,0:T(8,128)(2,1)S(1)}, u32[]{:S(2)}, u32[]{:S(2)}) collective-permute-start(bf16[528,512]{1,0:T(8,128)(2,1)S(1)} %fusion), channel_id=1, source_target_pairs={{0,2},{1,3},{2,0},{3,1},{4,6},{5,7},{6,4},{7,5},{8,10},{9,11},{10,... | collective-permute-start | bytes 1622024 | tf_op jit(solution)/shard_map/ppermute | solution.py:307
  105.0 7.4 %collective-permute-start.14 = (bf16[64,512]{1,0:T(8,128)(2,1)S(1)}, bf16[64,512]{1,0:T(8,128)(2,1)S(1)}, u32[]{:S(2)}, u32[]{:S(2)}) collective-permute-start(bf16[64,512]{1,0:T(8,128)(2,1)S(1)} %constant_dynamic-slice_fusion.3), channel_id=1, source_target_pairs={{0,16},{4,20},{8,24},{12,28},{16,0},{20,4},{24,8},{28,12},{1,17},{... | collective-permute-start | bytes 196616 | tf_op jit(solution)/shard_map/ppermute | solution.py:307
  105.4 9.2 %collective-permute-start.23 = (bf16[512,512]{1,0:T(8,128)(2,1)S(1)}, bf16[512,512]{1,0:T(8,128)(2,1)S(1)}, u32[]{:S(2)}, u32[]{:S(2)}) collective-permute-start(bf16[512,512]{1,0:T(8,128)(2,1)S(1)} %maximum_select_fusion.2), channel_id=1, source_target_pairs={{0,4},{4,0},{8,12},{12,8},{16,20},{20,16},{24,28},{28,24},{1,5},{5... | collective-permute-start | bytes 1572872 | tf_op jit(solution)/shard_map/ppermute | solution.py:307
  112.6 5.9 %collective-permute-start.15 = (bf16[96,512]{1,0:T(8,128)(2,1)S(1)}, bf16[96,512]{1,0:T(8,128)(2,1)S(1)}, u32[]{:S(2)}, u32[]{:S(2)}) collective-permute-start(bf16[96,512]{1,0:T(8,128)(2,1)S(1)} %pad_maximum_fusion.6), channel_id=1, source_target_pairs={{0,16},{4,20},{8,24},{12,28},{16,0},{20,4},{24,8},{28,12},{1,17},{... | collective-permute-start | bytes 294920 | tf_op jit(solution)/shard_map/ppermute | solution.py:307
  118.5 5.4 %collective-permute-start.16 = (bf16[160,512]{1,0:T(8,128)(2,1)S(1)}, bf16[160,512]{1,0:T(8,128)(2,1)S(1)}, u32[]{:S(2)}, u32[]{:S(2)}) collective-permute-start(bf16[160,512]{1,0:T(8,128)(2,1)S(1)} %pad_maximum_fusion.5), channel_id=1, source_target_pairs={{0,8},{4,12},{8,0},{12,4},{16,24},{20,28},{24,16},{28,20},{1,9},{5... | collective-permute-start | bytes 491528 | tf_op jit(solution)/shard_map/ppermute | solution.py:307
  120.2 4.5 %collective-permute-start.11 = (bf16[528,512]{1,0:T(8,128)(2,1)S(1)}, bf16[528,512]{1,0:T(8,128)(2,1)S(1)}, u32[]{:S(2)}, u32[]{:S(2)}) collective-permute-start(bf16[528,512]{1,0:T(8,128)(2,1)S(1)} %add_convert_fusion), channel_id=1, source_target_pairs={{0,1},{1,0},{2,3},{3,2},{4,5},{5,4},{6,7},{7,6},{8,9},{9,8},{10,11... | collective-permute-start | bytes 1622024 | tf_op jit(solution)/shard_map/ppermute | solution.py:307
  124.1 1.2 copy-start.4
  124.1 1.2 copy-start.35
  124.1 1.2 copy-start.41
  124.1 6.8 %collective-permute-start.17 = (bf16[288,512]{1,0:T(8,128)(2,1)S(1)}, bf16[288,512]{1,0:T(8,128)(2,1)S(1)}, u32[]{:S(2)}, u32[]{:S(2)}) collective-permute-start(bf16[288,512]{1,0:T(8,128)(2,1)S(1)} %pad_maximum_fusion.1), channel_id=1, source_target_pairs={{0,4},{4,0},{8,12},{12,8},{16,20},{20,16},{24,28},{28,24},{1,5},{5... | collective-permute-start | bytes 884744 | tf_op jit(solution)/shard_map/ppermute | solution.py:307
  (31 other events, 23.9 us)

commit v2 on v1

--- a/solution.py
+++ b/solution.py
@@ -15,6 +15,7 @@
 F32 = jnp.float32
 EXACT = lax.Precision.HIGHEST
 VMEM_BYTES = 24 * 1024 * 1024
+ROWS = 16
 
 
 def dot(left, right):
@@ -63,8 +64,102 @@
     return iota((BLOCK, BLOCK), 1) // HD == head
 
 
+class Loaded:
+    def __init__(self, source, buffer, sem):
+        self.buffer, self.shape, self.dtype = buffer, source.shape, source.dtype
+        self.copy = pltpu.make_async_copy(source, buffer, sem)
+        self.copy.start()
+
+    def wait(self):
+        if self.copy is not None:
+            self.copy.wait()
+            self.copy = None
+
+    def __getitem__(self, at):
+        self.wait()
+        return self.buffer[at]
+
+
+class Stored:
+    def __init__(self, buffer, target, sem):
+        self.buffer, self.shape, self.dtype = buffer, target.shape, target.dtype
+        self.copy, self.sent = pltpu.make_async_copy(buffer, target, sem), False
+
+    def __getitem__(self, at):
+        return self.buffer[at]
+
+    def __setitem__(self, at, value):
+        self.buffer[at] = value
+
+    def send(self):
+        if not self.sent:
+            self.copy.start()
+            self.sent = True
+
+
+def send_off(ref):
+    if isinstance(ref, Stored):
+        ref.send()
+
+
+def call(kernel, outs, args, scratch=(), flops=0, exports=()):
+    spaces = {"smem": pltpu.SMEM, "vmem": pltpu.VMEM, "hbm": pltpu.HBM, "hsmem": pltpu.HBM}
+    plain = len(outs)
+    outs = list(outs) + [(args[i][0].shape, args[i][0].dtype, "vmem") for i in exports]
+    loads = [i for i, (_, where) in enumerate(args) if where[0] == "h"]
+    stores = [i for i, (_, _, where) in enumerate(outs) if where == "hbm"]
+    shapes = [jax.ShapeDtypeStruct(shape, dtype) for shape, dtype, _ in outs]
+    pinned = [spaces[where](shape, dtype) for shape, dtype, where in outs]
+    operands = [
+        pltpu.with_memory_space_constraint(a, pltpu.HBM) if where[0] == "h" else a
+        for a, where in args
+    ]
+    buffers = []
+    for i in loads:
+        if i in exports:
+            continue
+        array, where = args[i]
+        space = pltpu.SMEM if where == "hsmem" else pltpu.VMEM
+        buffers.append(space(array.shape, array.dtype))
+    buffers += [pltpu.VMEM(outs[i][0], outs[i][1]) for i in stores]
+    sems = [pltpu.SemaphoreType.DMA] * (len(loads) + len(stores))
+
+    def body(*refs):
+        refs = list(refs)
+        ins, rest = refs[:len(args)], refs[len(args):]
+        results, rest = rest[:len(outs)], rest[len(outs):]
+        own, rest = rest[:len(scratch)], rest[len(scratch):]
+        holds, marks = list(rest[:len(buffers)]), list(rest[len(buffers):])
+        given = dict(zip(exports, results[plain:]))
+        for i in loads:
+            hold = given[i] if i in given else holds.pop(0)
+            ins[i] = Loaded(ins[i], hold, marks.pop(0))
+        for i in stores:
+            results[i] = Stored(holds.pop(0), results[i], marks.pop(0))
+        kernel(*ins, *results[:plain], *own)
+        for i in loads:
+            ins[i].wait()
+        for i in stores:
+            results[i].send()
+        for i in stores:
+            results[i].copy.wait()
+
+    moved = sum(a.size * a.dtype.itemsize for a in [a for a, _ in args] + shapes)
+    return pl.pallas_call(
+        body,
+        name=kernel.__name__,
+        out_shape=pinned,
+        in_specs=[pl.BlockSpec(memory_space=spaces[where]) for _, where in args],
+        out_specs=[pl.BlockSpec(memory_space=spaces[where]) for _, _, where in outs],
+        scratch_shapes=[pltpu.VMEM(shape, dtype) for shape, dtype in scratch] + buffers + sems,
+        compiler_params=pltpu.CompilerParams(vmem_limit_bytes=VMEM_BYTES),
+        cost_estimate=pl.CostEstimate(flops=flops, bytes_accessed=moved, transcendentals=0),
+    )(*operands)
+
+
 def attend_kernel(
-    rel, seg, valid, pidx, x, wq, wk, wv, bq, bv, g1, s1, att, first, q, k, v, probs
+    spot, x, g1, s1, rel, pidx, wq, wk, wv, bq, bv, seg, valid, wo, bo, g2, s2, w1, b1, cot, w2, b2,
+    att, first, q, k, v, probs
 ):
     tokens = x.shape[0]
     heads = wq.shape[1] // HD
@@ -73,15 +168,19 @@
         rows = pl.ds(b * BLOCK, BLOCK)
         normed, _ = normalize(x[rows, :].astype(F32))
         first[rows, :] = (normed * row(g1) + row(s1)).astype(BF)
+    send_off(first)
     q[...] = (dot(first[...], wq[...]) + row(bq)).astype(BF)
+    send_off(q)
     k[...] = dot(first[...], wk[...]).astype(BF)
+    send_off(k)
     v[...] = (dot(first[...], wv[...]) + row(bv)).astype(BF)
+    send_off(v)
     spread = (place(iota((BLOCK, WIN), 0)) == iota((BLOCK, WIN), 1)).astype(F32)
     index = pidx[...]
     biases = [jnp.zeros((WIN, WIN), F32) for _ in range(heads)]
-    for o in range(rel.shape[0]):
+    for o in range(rel.shape[1]):
         hit = index == o
-        biases = [jnp.where(hit, rel[o, h], biases[h]) for h in range(heads)]
+        biases = [jnp.where(hit, rel[h, o], biases[h]) for h in range(heads)]
     biases = [
         lax.dot_general(
             jnp.dot(spread, bias, precision=EXACT, preferred_element_type=F32),
@@ -114,10 +213,11 @@
             probs[b * heads + h] = prob
             total = total + dot(prob.astype(BF), vh)
         att[rows, :] = total.astype(BF)
+    send_off(probs)
 
 
 def mlp_kernel(
-    spot, x, cot, a0, a1, a2, a3, p0, p1, p2, p3, bo, g2, s2, w1, b1, w2,
+    spot, a0, a1, a2, a3, p0, p1, p2, p3, x, bo, g2, s2, w1, b1, cot, w2,
     mid, second, hidden, gpre, keep, send, att_all, wo_all,
 ):
     me = spot[0]
@@ -142,6 +242,7 @@
         hidden[rows, :] = (pre * upper).astype(BF)
         slope = upper + 0.5 * pre * (1.0 - bend * bend) * (curve * (1.0 + 0.134145 * square))
         gpre[rows, :] = (dot_nt(cot[rows, :], w2[...]) * slope).astype(BF)
+    send_off(mid)
     core = me % 2
     mine = pl.ds(pl.multiple_of(core * half, half), half)
     other = pl.ds(pl.multiple_of((1 - core) * half, half), half)
@@ -150,26 +251,31 @@
 
 
 def mlp_grad_kernel(
-    spot, cot, second, hidden, gpre, w2, w1_grad, w2_grad, keep, send, small
+    spot, second, hidden, gpre, cot, w2, own, away, keep, send, small, grads
 ):
-    core = spot[0] % 2
+    core, side = spot[0] % 2, spot[1] % 2
     half = cot.shape[0] // 2
     mine = pl.ds(pl.multiple_of(core * half, half), half)
     other = pl.ds(pl.multiple_of((1 - core) * half, half), half)
-    w2_grad[...] = dot_tn(hidden[...], cot[...]).astype(BF)
-    w1_grad[...] = dot_tn(second[...], gpre[...]).astype(BF)
+    grads[0] = dot_tn(second[...], gpre[...]).astype(BF)
+    grads[1] = dot_tn(hidden[...], cot[...]).astype(BF)
+    own[...] = grads[side]
+    away[...] = grads[1 - side]
     send[...] = dot(hidden[other, :], w2[...]).astype(BF)
-    keep[...] = dot(hidden[mine, :], w2[...])
-    small[...] = jnp.zeros_like(small)
-    small[0:1, :] = jnp.sum(gpre[...].astype(F32), axis=0, keepdims=True)
-    small[1:2, :] = jnp.sum(cot[...].astype(F32), axis=0, keepdims=True)
+    send_off(send)
+    keep[...] = dot(hidden[mine, :], w2[...]).astype(BF)
+    send_off(keep)
+    which = iota(small.shape, 0)
+    first = jnp.sum(gpre[...].astype(F32), axis=0, keepdims=True)
+    later = jnp.sum(cot[...].astype(F32), axis=0, keepdims=True)
+    small[...] = jnp.where(which == 0, first, jnp.where(which == 1, later, 0.0)).astype(BF)
 
 
 def attend_back_kernel(
-    spot, pidx, s2a, s2b, cot, mid, x, g2, att, wo, q, k, v, probs, first, wq, wk, wv,
-    gmid, pay, keep, send, small, gsec, gproj, gatt, gq, gk, gv,
+    spot, s2a, s2b, keep2, send2, mid, cot, g2, wo, v, probs, k, q, first, att, wq, wk, wv, x, pidx,
+    gmid, own, away, keep, send, small, gsec, gproj, gatt, gq, gk, gv, pay, sums,
 ):
-    core = spot[0] % 2
+    core, side = spot[0] % 2, spot[1] % 2
     tokens = x.shape[0]
     half = tokens // 2
     heads = wq.shape[1] // HD
@@ -192,6 +298,7 @@
         gmid[rows, :] = value
         proj_sum += jnp.sum(value, axis=0, keepdims=True)
         gproj[rows, :] = value.astype(BF)
+    send_off(gmid)
     gatt[...] = dot_nt(gproj[...], wo[...]).astype(BF)
     factor = HD ** (-0.5)
     score_sums = [jnp.zeros((BLOCK, BLOCK), F32) for _ in range(heads)]
@@ -202,15 +309,15 @@
         sum_k = jnp.zeros((BLOCK, BLOCK), F32)
         sum_v = jnp.zeros((BLOCK, BLOCK), F32)
         for h in range(heads):
-            own = head_mask(h)
+            lane = head_mask(h)
             zero = jnp.zeros_like(qb)
             prob = probs[b * heads + h]
-            grad = dot_nt(gb, jnp.where(own, vb, zero))
-            sum_v += dot_tn(prob.astype(BF), jnp.where(own, gb, zero))
+            grad = dot_nt(gb, jnp.where(lane, vb, zero))
+            sum_v += dot_tn(prob.astype(BF), jnp.where(lane, gb, zero))
             inner = jnp.sum(prob * grad, axis=-1, keepdims=True)
             gscore = (prob * (grad - inner)).astype(BF)
-            sum_q += dot(gscore, jnp.where(own, kb, zero))
-            sum_k += dot_tn(gscore, jnp.where(own, qb, zero))
+            sum_q += dot(gscore, jnp.where(lane, kb, zero))
+            sum_k += dot_tn(gscore, jnp.where(lane, qb, zero))
             score_sums[h] += gscore.astype(F32)
         gq[rows, :] = (factor * sum_q).astype(BF)
         gk[rows, :] = (factor * sum_k).astype(BF)
@@ -221,6 +328,9 @@
         for i in range(width // span):
             pay[j * span:(j + 1) * span, i * span:(i + 1) * span] = grads[i * span:(i + 1) * span]
     pay[3 * span:4 * span, :] = dot_tn(att[...], gproj[...]).astype(BF)
+    part = 2 * span
+    own[...] = pay[pl.ds(pl.multiple_of(side * part, part), part), :]
+    away[...] = pay[pl.ds(pl.multiple_of((1 - side) * part, part), part), :]
     norm1_gain = jnp.zeros((1, width), F32)
     norm1_shift = jnp.zeros((1, width), F32)
     for part, where in ((0, mine), (1, other)):
@@ -233,14 +343,15 @@
         norm1_gain += jnp.sum(grads * normed, axis=0, keepdims=True)
         norm1_shift += jnp.sum(grads, axis=0, keepdims=True)
         if part == 0:
-            keep[0:half, :] = grads
+            keep[0:half, :] = grads.astype(BF)
         else:
             send[0:half, :] = grads.astype(BF)
-    tail = keep.shape[0] - half
-    which = iota((tail, width), 0)
-    sums = jnp.where(which == 0, norm1_gain, jnp.where(which == 1, norm1_shift, 0.0))
-    keep[half:, :] = sums
-    send[half:, :] = sums.astype(BF)
+    which = iota((ROWS, width), 0)
+    pair = jnp.where(which == 0, norm1_gain, jnp.where(which == 1, norm1_shift, 0.0)).astype(BF)
+    keep[half:half + ROWS, :] = pair
+    send[half:half + ROWS, :] = pair
+    keep[half + ROWS:, :] = keep2[...]
+    send[half + ROWS:, :] = send2[...]
     at = place(iota((BLOCK, WIN), 0)) == iota((BLOCK, WIN), 1)
     fold = at.astype(F32)
     lanes = heads * WIN
@@ -264,43 +375,63 @@
     offsets = lax.dot_general(
         pick, by_offset, (((1,), (1,)), ((), ())), precision=EXACT, preferred_element_type=F32
     )
-    small[...] = jnp.zeros_like(small)
-    small[0:1, :] = gain_sum
-    small[1:2, :] = shift_sum
-    small[2:3, :] = proj_sum
-    small[3:4, 0:span] = jnp.sum(gq[...].astype(F32), axis=0, keepdims=True)
-    small[3:4, span:2 * span] = jnp.sum(gv[...].astype(F32), axis=0, keepdims=True)
-    small[8:16, 0:slots] = offsets
-
-
-def finish_kernel(spot, s4a, s4b, m4a, m4b, gmid, x, g1, mid, b2, layer_out, input_grad):
+    sums[...] = jnp.zeros_like(sums)
+    sums[0:1, :] = gain_sum
+    sums[1:2, :] = shift_sum
+    sums[2:3, :] = proj_sum
+    sums[3:4, 0:span] = jnp.sum(gq[...].astype(F32), axis=0, keepdims=True)
+    sums[3:4, span:2 * span] = jnp.sum(gv[...].astype(F32), axis=0, keepdims=True)
+    sums[8:16, 0:slots] = offsets
+    small[...] = sums[...].astype(BF)
+
+
+def finish_kernel(spot, s4, r4, gmid, x, g1, mid, b2, layer_out, input_grad):
     core = spot[0] % 2
     half = x.shape[0] // 2
-    for part, (gref, mref) in enumerate(((s4a, m4a), (s4b, m4b))):
+    for part, ref in enumerate((s4, r4)):
         start = core if part == 0 else 1 - core
         where = pl.ds(pl.multiple_of(start * half, half), half)
         normed, inverse = normalize(x[where, :].astype(F32))
-        grad = gref[0:half, :].astype(F32)
+        grad = ref[0:half, :].astype(F32)
         input_grad[where, :] = gmid[where, :] + norm_back(grad, normed, inverse, row(g1))
-        layer_out[where, :] = mid[where, :] + mref[...].astype(F32) + row(b2)
-
-
-def call(kernel, outs, args, scalars, scratch=(), flops=0):
-    in_specs = [
-        pl.BlockSpec(memory_space=pltpu.SMEM if i in scalars else pltpu.VMEM)
-        for i in range(len(args))
-    ]
-    shapes = [jax.ShapeDtypeStruct(shape, dtype) for shape, dtype in outs]
-    moved = sum(a.size * a.dtype.itemsize for a in list(args) + shapes)
-    return pl.pallas_call(
-        kernel,
-        out_shape=shapes,
-        in_specs=in_specs,
-        out_specs=[pl.BlockSpec(memory_space=pltpu.VMEM)] * len(shapes),
-        scratch_shapes=[pltpu.VMEM(shape, dtype) for shape, dtype in scratch],
-        compiler_params=pltpu.CompilerParams(vmem_limit_bytes=VMEM_BYTES),
-        cost_estimate=pl.CostEstimate(flops=flops, bytes_accessed=moved, transcendentals=0),
-    )(*args)
+        mlp = ref[half + ROWS:, :].astype(F32)
+        layer_out[where, :] = mid[where, :] + mlp + row(b2)
+
+
+def widen_kernel(spot, near, far, first, second):
+    side = spot[1] % 2
+    @pl.when(side == 0)
+    def _():
+        first[...] = near[...].astype(F32)
+        second[...] = far[...].astype(F32)
+    @pl.when(side == 1)
+    def _():
+        first[...] = far[...].astype(F32)
+        second[...] = near[...].astype(F32)
+
+
+def unpack_kernel(
+    spot, near, far, small, wq, wk, wv, wo, b1, b2, g2, s2, bo, bq, bv, rel, g1, s1, both
+):
+    side = spot[1] % 2
+    part = near.shape[0]
+    span = part // 2
+    width = near.shape[1]
+    both[pl.ds(pl.multiple_of(side * part, part), part), :] = near[...]
+    both[pl.ds(pl.multiple_of((1 - side) * part, part), part), :] = far[0:part, :]
+    for j, ref in enumerate((wq, wk, wv)):
+        for i in range(width // span):
+            block = both[j * span:(j + 1) * span, i * span:(i + 1) * span]
+            ref[i * span:(i + 1) * span, :] = block.astype(F32)
+        send_off(ref)
+    wo[...] = both[3 * span:, :].astype(F32)
+    send_off(wo)
+    sums = small[...].astype(F32) + far[part:, :].astype(F32)
+    for at, ref in ((0, b1), (1, b2), (8, g2), (9, s2), (10, bo), (24, g1), (25, s1)):
+        ref[...] = sums[at].astype(BF).astype(F32)
+    bq[...] = sums[11, :span].astype(BF).astype(F32)
+    bv[...] = sums[11, span:2 * span].astype(BF).astype(F32)
+    rel[...] = sums[16:16 + rel.shape[0], :rel.shape[1]].astype(BF).astype(F32)
 
 
 def swap(value, axis, bit, size):
@@ -339,28 +470,54 @@
     heads = span // HD
     blocks = tokens // BLOCK
     me = lax.axis_index("tensor")
-    spot = me.astype(jnp.int32).reshape(1)
     mate = lax.axis_index("dp")
+    bits = [1 << i for i in range(dp.bit_length() - 1)]
+    flags = [(mate >> i) & 1 for i in range(len(bits))]
+    lower = [flag == 0 for flag in flags]
+    sizes = [(width >> (i + 1)) * n for i in range(len(bits)) for n in (1, 2)]
+    starts = {
+        (i, size): (flags[i] * size).astype(jnp.uint32) for i in range(len(bits)) for size in sizes
+    }
+    stops = {
+        at: ((1 - flags[at[0]]) * at[1]).astype(jnp.uint32) for at in starts
+    }
+    spot = jnp.stack(
+        [me, mate]
+        + flags
+        + [flag.astype(jnp.int32) for flag in lower]
+        + [at.astype(jnp.int32) for at in list(starts.values()) + list(stops.values())]
+    )
     seg = segment_ids.reshape(1, tokens)
     valid = valid_mask.reshape(1, tokens)
+    wide = (tokens, width)
+    narrow = (tokens, span)
 
     wo_x = swap(proj_weight, "tensor", 2, tensor)
     wo_c = swap(proj_weight, "tensor", 1, tensor)
     wo_d = swap(wo_x, "tensor", 1, tensor)
 
-    att, first, q, k, v, probs = call(
+    (
+        att, first, q, k, v, probs, x, norm1_gain, norm1_shift, position_index, query_weight,
+        key_weight, value_weight, proj_weight, proj_bias, norm2_gain, norm2_shift, up_weight,
+        up_bias, out_cotangent, down_weight, down_bias,
+    ) = call(
         attend_kernel,
         [
-            ((tokens, span), BF), ((tokens, width), BF), ((tokens, span), BF),
-            ((tokens, span), BF), ((tokens, span), BF), ((blocks * heads, BLOCK, BLOCK), F32),
-        ],
-        [
-            position_bias, seg, valid, position_index, inputs, query_weight, key_weight,
-            value_weight, query_bias, value_bias, norm1_gain, norm1_shift,
-        ],
-        (0,),
-        flops=2 * tokens * width * 3 * span,
-    )
+            (narrow, BF, "vmem"), (wide, BF, "vmem"), (narrow, BF, "vmem"), (narrow, BF, "vmem"),
+            (narrow, BF, "vmem"), ((blocks * heads, BLOCK, BLOCK), F32, "vmem"),
+        ],
+        [
+            (spot, "smem"), (inputs, "hbm"), (norm1_gain, "hbm"), (norm1_shift, "hbm"),
+            (position_bias.T, "hsmem"), (position_index, "hbm"), (query_weight, "hbm"),
+            (key_weight, "hbm"), (value_weight, "hbm"), (query_bias, "hbm"), (value_bias, "hbm"),
+            (seg, "hbm"), (valid, "hbm"), (proj_weight, "hbm"), (proj_bias, "hbm"),
+            (norm2_gain, "hbm"), (norm2_shift, "hbm"), (up_weight, "hbm"), (up_bias, "hbm"),
+            (out_cotangent, "hbm"), (down_weight, "hbm"), (down_bias, "hbm"),
+        ],
+        exports=(1, 2, 3, 5, 6, 7, 8, 13, 14, 15, 16, 17, 18, 19, 20, 21),
+        flops=5 * 10 ** 9,
+    )
+    inputs = x
     att_x = swap(att, "tensor", 2, tensor)
     att_c = swap(att, "tensor", 1, tensor)
     att_d = swap(att_x, "tensor", 1, tensor)
@@ -368,14 +525,15 @@
     mid, second, hidden, gpre, keep3, send3 = call(
         mlp_kernel,
         [
-            ((tokens, width), F32), ((tokens, width), BF), ((tokens, units), BF),
-            ((tokens, units), BF), ((half, width), F32), ((half, width), BF),
-        ],
-        [
-            spot, inputs, out_cotangent, att, att_c, att_x, att_d, proj_weight, wo_c, wo_x, wo_d,
-            proj_bias, norm2_gain, norm2_shift, up_weight, up_bias, down_weight,
-        ],
-        (0,),
+            (wide, F32, "vmem"), (wide, BF, "vmem"), ((tokens, units), BF, "vmem"),
+            ((tokens, units), BF, "vmem"), ((half, width), F32, "vmem"), ((half, width), BF, "vmem"),
+        ],
+        [
+            (spot, "smem"), (att, "vmem"), (att_c, "vmem"), (att_x, "vmem"), (att_d, "vmem"),
+            (proj_weight, "vmem"), (wo_c, "vmem"), (wo_x, "vmem"), (wo_d, "vmem"),
+            (inputs, "vmem"), (proj_bias, "vmem"), (norm2_gain, "vmem"), (norm2_shift, "vmem"),
+            (up_weight, "vmem"), (up_bias, "vmem"), (out_cotangent, "vmem"), (down_weight, "vmem"),
+        ],
         scratch=[((tokens, tensor * span), BF), ((tensor * span, width), BF)],
         flops=2 * tokens * width * 4 * units,
     )
@@ -387,99 +545,106 @@
     sum3 = fold(pair3, swap(pair3, "tensor", 2, tensor))
     rest3 = swap(sum3, "tensor", 1, tensor)
 
-    w1_pay, w2_pay, keep2, send2, small_a = call(
+    mlp_own, mlp_away, keep2, send2, small_a = call(
         mlp_grad_kernel,
         [
-            ((width, units), BF), ((units, width), BF), ((half, width), F32),
-            ((half, width), BF), ((8, width), F32),
-        ],
-        [spot, out_cotangent, second, hidden, gpre, down_weight],
-        (0,),
+            ((width, units), BF, "vmem"), ((units, width), BF, "vmem"), ((half, width), BF, "vmem"),
+            ((half, width), BF, "vmem"), ((8, width), BF, "vmem"),
+        ],
+        [
+            (spot, "smem"), (second, "vmem"), (hidden, "vmem"), (gpre, "vmem"),
+            (out_cotangent, "vmem"), (down_weight, "vmem"),
+        ],
+        scratch=[((2, width, units), BF)],
         flops=2 * tokens * width * 3 * units,
     )
 
-    gmid, pay, keep4, send4, small_b = call(
+    merged = half + ROWS + half
+    gmid, att_own, att_away, keep4, send4, small_b = call(
         attend_back_kernel,
         [
-            ((tokens, width), F32), ((4 * span, width), BF), ((half + 16, width), F32),
-            ((half + 16, width), BF), ((16, width), F32),
-        ],
-        [
-            spot, position_index, sum3, rest3, out_cotangent, mid, inputs, norm2_gain, att,
-            proj_weight, q, k, v, probs, first, query_weight, key_weight, value_weight,
-        ],
-        (0,),
+            (wide, F32, "vmem"), ((2 * span, width), BF, "vmem"), ((2 * span, width), BF, "vmem"),
+            ((merged, width), BF, "vmem"), ((merged, width), BF, "vmem"), ((16, width), BF, "vmem"),
+        ],
+        [
+            (spot, "smem"), (sum3, "vmem"), (rest3, "vmem"), (keep2, "vmem"), (send2, "vmem"),
+            (mid, "vmem"), (out_cotangent, "vmem"), (norm2_gain, "vmem"), (proj_weight, "vmem"),
+            (v, "vmem"), (probs, "vmem"), (k, "vmem"), (q, "vmem"), (first, "vmem"), (att, "vmem"),
+            (query_weight, "vmem"), (key_weight, "vmem"), (value_weight, "vmem"), (inputs, "vmem"),
+            (position_index, "vmem"),
+        ],
         scratch=[
-            ((tokens, width), F32), ((tokens, width), BF), ((tokens, span), BF),
-            ((tokens, span), BF), ((tokens, span), BF), ((tokens, span), BF),
+            (wide, F32), (wide, BF), (narrow, BF), (narrow, BF), (narrow, BF), (narrow, BF),
+            ((4 * span, width), BF), ((16, width), F32),
         ],
         flops=2 * tokens * width * 8 * span,
     )
 
-    keep4 = jnp.concatenate([keep4, keep2])
-    send4 = jnp.concatenate([send4, send2])
     pair4 = fold(keep4, swap(send4, "tensor", 1, tensor))
     sum4 = fold(pair4, swap(pair4, "tensor", 2, tensor))
     rest4 = swap(sum4, "tensor", 1, tensor)
 
-    bits = [1 << i for i in range(dp.bit_length() - 1)]
-
-    def scatter(value):
-        for bit in bits:
+    left = jnp.uint32(0)
+
+    def scatter(own, away):
+        value = fold(own, swap(away, "dp", bits[0], dp))
+        for i, bit in enumerate(bits[1:], 1):
             part = value.shape[0] // 2
-            flag = (mate // bit) % 2
-            own = lax.dynamic_slice_in_dim(value, flag * part, part)
-            away = lax.dynamic_slice_in_dim(value, (1 - flag) * part, part)
+            own = lax.dynamic_slice(value, (starts[i, part], left), (part, width))
+            away = lax.dynamic_slice(value, (stops[i, part], left), (part, width))
             value = fold(own, swap(away, "dp", bit, dp))
         return value
 
-    def join(bit, own, other):
-        flag = (mate // bit) % 2
+    def join(i, own, other):
         return jnp.where(
-            flag == 0, jnp.concatenate([own, other]), jnp.concatenate([other, own])
+            lower[i], jnp.concatenate([own, other]), jnp.concatenate([other, own])
         )
 
-    def gather(value, extra=None):
-        for bit in reversed(bits):
-            if extra is None:
-                value = join(bit, value, swap(value, "dp", bit, dp))
-            else:
-                rows = value.shape[0]
-                come = swap(jnp.concatenate([value, extra]), "dp", bit, dp)
-                value = join(bit, value, come[:rows])
-                extra = fold(extra, come[rows:])
-        return value if extra is None else (value, extra)
-
-    mlp_total = gather(scatter(jnp.concatenate([w1_pay, w2_pay])))
-    w1_total = mlp_total[:width].astype(F32)
-    w2_total = mlp_total[width:].astype(F32)
-
-    small = jnp.concatenate([small_a.astype(BF), small_b.astype(BF), sum4[half:half + 8]])
-    att_total, small = gather(scatter(pay), small)
-    att_total = att_total.astype(F32)
-    small = small.astype(F32)
-
-    def unfold(block):
-        return jnp.concatenate([block[:, i * span:(i + 1) * span] for i in range(width // span)])
-
-    wq_total = unfold(att_total[:span])
-    wk_total = unfold(att_total[span:2 * span])
-    wv_total = unfold(att_total[2 * span:3 * span])
-    wo_total = att_total[3 * span:]
-    b1_total, b2_total = small[0], small[1]
-    g2_total, s2_total, bo_total = small[8], small[9], small[10]
-    bq_total, bv_total = small[11, :span], small[11, span:2 * span]
-    rel_total = small[16:16 + heads, :position_bias.shape[0]].T
-    g1_total, s1_total = small[24], small[25]
+    def gather(value):
+        for i in reversed(range(1, len(bits))):
+            value = join(i, value, swap(value, "dp", bits[i], dp))
+        return value, swap(value, "dp", bits[0], dp)
+
+    def gather_with(value, extra):
+        for i in reversed(range(1, len(bits))):
+            rows = value.shape[0]
+            come = swap(jnp.concatenate([value, extra]), "dp", bits[i], dp)
+            value = join(i, value, come[:rows])
+            extra = fold(extra, come[rows:])
+        return value, extra, swap(jnp.concatenate([value, extra]), "dp", bits[0], dp)
+
+    near, far = gather(scatter(mlp_own, mlp_away))
+    w1_total, w2_total = call(
+        widen_kernel,
+        [((width, units), F32, "hbm"), ((units, width), F32, "hbm")],
+        [(spot, "smem"), (near, "vmem"), (far, "vmem")],
+    )
+
+    small = jnp.concatenate([small_a, small_b, sum4[half:half + 8]])
+    near, small, far = gather_with(scatter(att_own, att_away), small)
+    vector, short = ((width,), F32, "hbm"), ((span,), F32, "hbm")
+    (
+        wq_total, wk_total, wv_total, wo_total, b1_total, b2_total, g2_total, s2_total, bo_total,
+        bq_total, bv_total, rel_total, g1_total, s1_total,
+    ) = call(
+        unpack_kernel,
+        [
+            ((width, span), F32, "hbm"), ((width, span), F32, "hbm"), ((width, span), F32, "hbm"),
+            ((span, width), F32, "hbm"), vector, vector, vector, vector, vector, short, short,
+            ((heads, position_bias.shape[0]), F32, "hbm"), vector, vector,
+        ],
+        [(spot, "smem"), (near, "vmem"), (far, "vmem"), (small, "vmem")],
+        scratch=[((4 * span, width), BF)],
+    )
+    rel_total = rel_total.T
 
     layer_out, input_grad = call(
         finish_kernel,
-        [((tokens, width), F32), ((tokens, width), F32)],
-        [
-            spot, sum4[:half], rest4[:half], sum4[half + 16:], rest4[half + 16:], gmid, inputs,
-            norm1_gain, mid, down_bias,
-        ],
-        (0,),
+        [(wide, F32, "hbm"), (wide, F32, "hbm")],
+        [
+            (spot, "smem"), (sum4, "vmem"), (rest4, "vmem"), (gmid, "vmem"), (inputs, "vmem"),
+            (norm1_gain, "vmem"), (mid, "vmem"), (down_bias, "vmem"),
+        ],
         flops=tokens * width,
     )
     return (

time: 136 us -> 96.7 us (0.71)
  local copies, waits for them, and re-layouts: 38.6 us -> 0.49 us
  other arithmetic: 12.8 us -> 1.29 us
  Pallas kernels: 16.2 us -> 25.5 us
  starting transfers between devices: 16.2 us -> 24 us
  waiting for transfers between devices: 50.3 us -> 44.2 us
    unnamed x112 -> x2, local copies, waits for them, and re-layouts: 33.6 us -> 0.01 us
    pallas_call x5 -> x7, Pallas kernels: 16.2 us -> 25.5 us  [call(): pl.pallas_call(body, name=kernel.__name__, out_shape=pinned, in_specs=[pl...]
    ppermute x24, starting transfers between devices: 16.2 us -> 24 us  [swap(): return lax.ppermute(value, axis, [(i, i ^ bit) for i in range(size)])]
    ppermute x24, waiting for transfers between devices: 50.3 us -> 44.2 us  [swap(): return lax.ppermute(value, axis, [(i, i ^ bit) for i in range(size)])]
    convert_element_type x12, other arithmetic: 6.73 us -> 0.89 us  [fold(): return (value.astype(F32) + other.astype(F32)).astype(BF)]
    concatenate x6 -> x3, other arithmetic: 2.42 us -> 0.04 us  [the longest x2 0.02 us: gather_with(): come = swap(jnp.concatenate([value, extra]), 'dp', bits[i], dp)]
    dynamic_slice x6 -> x4, local copies, waits for them, and re-layouts: 2.39 us -> 0.36 us  [scatter(): away = lax.dynamic_slice(value, (stops[i, part], left), (part, width))]
    convert_element_type x5 -> x0, other arithmetic: 1.83 us -> none  [the longest x1 1.61 us: shards(): w2_total = mlp_total[width:].astype(F32)]
  transfers between devices with their start and end apart: 24 -> 24, of which waited for: 12 -> 15; matrix products, arithmetic and copies ran while one was open for 10% -> 2% of each run, Pallas kernels for 9% -> 22%
where the time goes in v2:
time: 96.7 us; the launch traced here: 96.5 us
  waiting for transfers between devices  44.2 us (46%)
  Pallas kernels  25.5 us (26%)
  starting transfers between devices  24 us (25%)
  other arithmetic  1.29 us (1%)
  between operations  1.09 us (1%)
    ppermute x24, waiting for transfers between devices, swap(): return lax.ppermute(value, axis, [(i, i ^ bit) for i in range(size)])  44.2 us
    pallas_call x7, Pallas kernels, call(): pl.pallas_call(body, name=kernel.__name__, out_shape=pinned, in_specs=[pl...  25.5 us
    ppermute x24, starting transfers between devices, swap(): return lax.ppermute(value, axis, [(i, i ^ bit) for i in range(size)])  24 us
  transfers between devices with their start and end apart: 24, of which 15 were waited for; matrix products, arithmetic and copies ran while one was open for 2% of the time, Pallas kernels for 22%

profile of v2, /device:TPU:0, one launch (start us, length us, event | category | flops | bytes accessed | tf_op | source)
XLA Modules:
  0.0 96.5 jit_solution(13454969409202296302)
XLA Ops:
  0.7 3.0 %collective-permute-start.4 = (bf16[128,512]{1,0:T(8,128)(2,1)}, bf16[128,512]{1,0:T(8,128)(2,1)S(1)}, u32[]{:S(2)}, u32[]{:S(2)}) collective-permute-start(bf16[128,512]{1,0:T(8,128)(2,1)} %refs_13_.1), channel_id=1, source_target_pairs={{0,2},{1,3},{2,0},{3,1},{4,6},{5,7},{6,4},{7,5},{8,10},{9,11},{10,... | collective-permute-start | bytes 393224 | tf_op jit(solution)/shard_map/ppermute | solution.py:438
  3.7 0.1 stack.143.refs_0_
  3.8 7.7 %attend_kernel.1 = (bf16[512,128]{1,0:T(8,128)(2,1)S(1)}, bf16[512,512]{1,0:T(8,128)(2,1)S(1)}, bf16[512,128]{1,0:T(8,128)(2,1)S(1)}, bf16[512,128]{1,0:T(8,128)...) custom-call(s32[32]{0:T(128)S(1)} %stack.143.refs_0_, ...), custom_call_target="tpu_custom_call" | custom-call | flops 5000000000 | bytes 7376784 | tf_op jit(solution)/shard_map/attend_kernel/pallas_call | solution.py:148
  11.5 0.1 collective-permute-start.1
  11.7 0.5 collective-permute-start
  12.2 0.1 collective-permute-start.5
  12.3 4.3 %collective-permute-done.1.refs_3_ = bf16[512,128]{1,0:T(8,128)(2,1)S(1)} collective-permute-done((bf16[512,128]{1,0:T(8,128)(2,1)S(1)}, bf16[512,128]{1,0:T(8,128)(2,1)S(1)}, u32[]{:S(2)}, u32[]{:S(2)}) %collective-permute-start.1) | collective-permute-done | bytes 131104 | tf_op jit(solution)/shard_map/ppermute | solution.py:438
  16.6 1.3 %collective-permute-done.2.refs_4_ = bf16[512,128]{1,0:T(8,128)(2,1)S(1)} collective-permute-done((bf16[512,128]{1,0:T(8,128)(2,1)S(1)}, bf16[512,128]{1,0:T(8,128)(2,1)S(1)}, u32[]{:S(2)}, u32[]{:S(2)}) %collective-permute-start.2) | collective-permute-done | bytes 131104 | tf_op jit(solution)/shard_map/ppermute | solution.py:438
  17.9 2.9 %mlp_kernel.1 = (f32[512,512]{1,0:T(8,128)S(1)}, bf16[512,512]{1,0:T(8,128)(2,1)S(1)}, bf16[512,512]{1,0:T(8,128)(2,1)S(1)}, bf16[512,512]{1,0:T(8,128)(2,1)S(1)...) custom-call(s32[32]{0:T(128)S(1)} %stack.143.refs_0_, bf16[512,128]{1,0:T(8,128)(2,1)S(1)} %get-tuple-element.74.refs_1_.refs_14_, ...), custom_call_target="tpu_custom_call" | custom-call | flops 1073741824 | bytes 6561920 | tf_op jit(solution)/shard_map/mlp_kernel/pallas_call | solution.py:148
  20.8 0.2 collective-permute-start.6
  21.0 1.4 %collective-permute-done.6 = bf16[256,512]{1,0:T(8,128)(2,1)S(1)} collective-permute-done((bf16[256,512]{1,0:T(8,128)(2,1)S(1)}, bf16[256,512]{1,0:T(8,128)(2,1)S(1)}, u32[]{:S(2)}, u32[]{:S(2)}) %collective-permute-start.6) | collective-permute-done | bytes 262176 | tf_op jit(solution)/shard_map/ppermute | solution.py:438
  22.4 0.1 add_convert_fusion.6
  22.5 0.4 collective-permute-start.7
  22.9 1.7 %mlp_grad_kernel.1 = (bf16[512,512]{1,0:T(8,128)(2,1)S(1)}, bf16[512,512]{1,0:T(8,128)(2,1)S(1)}, bf16[256,512]{1,0:T(8,128)(2,1)S(1)}, bf16[256,512]{1,0:T(8,128)(2,1)S(1)}, bf16[8,512]{1,0:T(8,128)(2,1)S(1)}) custom-call(s32[32]{0:T(128)S(1)} %stack.143.refs_0_, bf16[512,512]{1,0:T(8,128)(2,1)S(1)} %get-tuple-element.86.refs_1_, ...), custom_call_target="tpu_custom_call" | custom-call | flops 805306368 | bytes 4202624 | tf_op jit(solution)/shard_map/mlp_grad_kernel/pallas_call | solution.py:148
  24.6 1.8 %collective-permute-start.18 = (bf16[512,512]{1,0:T(8,128)(2,1)S(1)}, bf16[512,512]{1,0:T(8,128)(2,1)S(1)}, u32[]{:S(2)}, u32[]{:S(2)}) collective-permute-start(bf16[512,512]{1,0:T(8,128)(2,1)S(1)} %get-tuple-element.125), channel_id=1, source_target_pairs={{0,4},{4,0},{8,12},{12,8},{16,20},{20,16},{24,28},{28,24},{1,5},{5... | collective-permute-start | bytes 1572872 | tf_op jit(solution)/shard_map/ppermute | solution.py:438
  26.4 4.5 %collective-permute-done.7 = bf16[256,512]{1,0:T(8,128)(2,1)S(1)} collective-permute-done((bf16[256,512]{1,0:T(8,128)(2,1)S(1)}, bf16[256,512]{1,0:T(8,128)(2,1)S(1)}, u32[]{:S(2)}, u32[]{:S(2)}) %collective-permute-start.7) | collective-permute-done | bytes 262176 | tf_op jit(solution)/shard_map/ppermute | solution.py:438
  31.0 0.1 collective-permute-start.8
  31.1 1.5 %collective-permute-done.8.refs_2_ = bf16[256,512]{1,0:T(8,128)(2,1)S(1)} collective-permute-done((bf16[256,512]{1,0:T(8,128)(2,1)S(1)}, bf16[256,512]{1,0:T(8,128)(2,1)S(1)}, u32[]{:S(2)}, u32[]{:S(2)}) %collective-permute-start.8) | collective-permute-done | bytes 262176 | tf_op jit(solution)/shard_map/ppermute | solution.py:438
  32.6 6.8 %attend_back_kernel.1 = (f32[512,512]{1,0:T(8,128)S(1)}, bf16[256,512]{1,0:T(8,128)(2,1)S(1)}, bf16[256,512]{1,0:T(8,128)(2,1)S(1)}, bf16[528,512]{1,0:T(8,128)(...) custom-call(s32[32]{0:T(128)S(1)} %stack.143.refs_0_, ...), custom_call_target="tpu_custom_call" | custom-call | flops 536870912 | bytes 8440960 | tf_op jit(solution)/shard_map/attend_back_kernel/pallas_call | solution.py:148
  39.4 1.5 %collective-permute-start.12 = (bf16[256,512]{1,0:T(8,128)(2,1)S(1)}, bf16[256,512]{1,0:T(8,128)(2,1)S(1)}, u32[]{:S(2)}, u32[]{:S(2)}) collective-permute-start(bf16[256,512]{1,0:T(8,128)(2,1)S(1)} %get-tuple-element.109), channel_id=1, source_target_pairs={{0,4},{4,0},{8,12},{12,8},{16,20},{20,16},{24,28},{28,24},{1,5},{5... | collective-permute-start | bytes 786440 | tf_op jit(solution)/shard_map/ppermute | solution.py:438
  40.9 0.1 add_convert_fusion.2
  41.1 0.3 constant_dynamic-slice_fusion.1
  41.3 1.6 %collective-permute-start.19 = (bf16[256,512]{1,0:T(8,128)(2,1)S(1)}, bf16[256,512]{1,0:T(8,128)(2,1)S(1)}, u32[]{:S(2)}, u32[]{:S(2)}) collective-permute-start(bf16[256,512]{1,0:T(8,128)(2,1)S(1)} %constant_dynamic-slice_fusion.1), channel_id=1, source_target_pairs={{0,8},{4,12},{8,0},{12,4},{16,24},{20,28},{24,16},{28,20},{1,9},{5... | collective-permute-start | bytes 786440 | tf_op jit(solution)/shard_map/ppermute | solution.py:438
  43.0 4.8 %collective-permute-done.12 = bf16[256,512]{1,0:T(8,128)(2,1)S(1)} collective-permute-done((bf16[256,512]{1,0:T(8,128)(2,1)S(1)}, bf16[256,512]{1,0:T(8,128)(2,1)S(1)}, u32[]{:S(2)}, u32[]{:S(2)}) %collective-permute-start.12) | collective-permute-done | bytes 262176 | tf_op jit(solution)/shard_map/ppermute | solution.py:438
  47.9 1.6 %collective-permute-start.13 = (bf16[128,512]{1,0:T(8,128)(2,1)S(1)}, bf16[128,512]{1,0:T(8,128)(2,1)S(1)}, u32[]{:S(2)}, u32[]{:S(2)}) collective-permute-start(bf16[128,512]{1,0:T(8,128)(2,1)S(1)} %constant_dynamic-slice_fusion.3), channel_id=1, source_target_pairs={{0,8},{4,12},{8,0},{12,4},{16,24},{20,28},{24,16},{28,20},{1,9},{5... | collective-permute-start | bytes 393224 | tf_op jit(solution)/shard_map/ppermute | solution.py:438
  49.5 0.1 add_convert_fusion.3
  49.7 2.7 %collective-permute-start.20 = (bf16[128,512]{1,0:T(8,128)(2,1)S(1)}, bf16[128,512]{1,0:T(8,128)(2,1)S(1)}, u32[]{:S(2)}, u32[]{:S(2)}) collective-permute-start(bf16[128,512]{1,0:T(8,128)(2,1)S(1)} %constant_dynamic-slice_fusion), channel_id=1, source_target_pairs={{0,16},{4,20},{8,24},{12,28},{16,0},{20,4},{24,8},{28,12},{1,17},{... | collective-permute-start | bytes 393224 | tf_op jit(solution)/shard_map/ppermute | solution.py:438
  52.3 1.8 %collective-permute-done.13 = bf16[128,512]{1,0:T(8,128)(2,1)S(1)} collective-permute-done((bf16[128,512]{1,0:T(8,128)(2,1)S(1)}, bf16[128,512]{1,0:T(8,128)(2,1)S(1)}, u32[]{:S(2)}, u32[]{:S(2)}) %collective-permute-start.13) | collective-permute-done | bytes 131104 | tf_op jit(solution)/shard_map/ppermute | solution.py:438
  54.2 0.1 add_convert_fusion.1
  54.4 0.2 collective-permute-start.10
  54.6 3.0 %collective-permute-start.14 = (bf16[64,512]{1,0:T(8,128)(2,1)S(1)}, bf16[64,512]{1,0:T(8,128)(2,1)S(1)}, u32[]{:S(2)}, u32[]{:S(2)}) collective-permute-start(bf16[64,512]{1,0:T(8,128)(2,1)S(1)} %constant_dynamic-slice_fusion.2), channel_id=1, source_target_pairs={{0,16},{4,20},{8,24},{12,28},{16,0},{20,4},{24,8},{28,12},{1,17},{... | collective-permute-start | bytes 196616 | tf_op jit(solution)/shard_map/ppermute | solution.py:438
  57.6 2.1 %collective-permute-done.20 = bf16[128,512]{1,0:T(8,128)(2,1)S(1)} collective-permute-done((bf16[128,512]{1,0:T(8,128)(2,1)S(1)}, bf16[128,512]{1,0:T(8,128)(2,1)S(1)}, u32[]{:S(2)}, u32[]{:S(2)}) %collective-permute-start.20) | collective-permute-done | bytes 131104 | tf_op jit(solution)/shard_map/ppermute | solution.py:438
  59.8 2.0 %collective-permute-done.14 = bf16[64,512]{1,0:T(8,128)(2,1)S(1)} collective-permute-done((bf16[64,512]{1,0:T(8,128)(2,1)S(1)}, bf16[64,512]{1,0:T(8,128)(2,1)S(1)}, u32[]{:S(2)}, u32[]{:S(2)}) %collective-permute-start.14) | collective-permute-done | bytes 65568 | tf_op jit(solution)/shard_map/ppermute | solution.py:438
  61.8 3.7 %collective-permute-done.10 = bf16[528,512]{1,0:T(8,128)(2,1)S(1)} collective-permute-done((bf16[528,512]{1,0:T(8,128)(2,1)S(1)}, bf16[528,512]{1,0:T(8,128)(2,1)S(1)}, u32[]{:S(2)}, u32[]{:S(2)}) %collective-permute-start.10) | collective-permute-done | bytes 540704 | tf_op jit(solution)/shard_map/ppermute | solution.py:438
  65.6 0.1 add_convert_fusion.refs_1_
  65.7 2.6 %collective-permute-start.15 = (bf16[96,512]{1,0:T(8,128)(2,1)S(1)}, bf16[96,512]{1,0:T(8,128)(2,1)S(1)}, u32[]{:S(2)}, u32[]{:S(2)}) collective-permute-start(bf16[96,512]{1,0:T(8,128)(2,1)S(1)} %pad_maximum_fusion.2), channel_id=1, source_target_pairs={{0,16},{4,20},{8,24},{12,28},{16,0},{20,4},{24,8},{28,12},{1,17},{... | collective-permute-start | bytes 294920 | tf_op jit(solution)/shard_map/ppermute | solution.py:438
  68.4 2.0 %collective-permute-done.21 = bf16[128,512]{1,0:T(8,128)(2,1)S(1)} collective-permute-done((bf16[128,512]{1,0:T(8,128)(2,1)S(1)}, bf16[128,512]{1,0:T(8,128)(2,1)S(1)}, u32[]{:S(2)}, u32[]{:S(2)}) %collective-permute-start.21) | collective-permute-done | bytes 131104 | tf_op jit(solution)/shard_map/ppermute | solution.py:438
  70.5 0.9 collective-permute-done.15
  71.5 2.3 %collective-permute-start.16 = (bf16[160,512]{1,0:T(8,128)(2,1)S(1)}, bf16[160,512]{1,0:T(8,128)(2,1)S(1)}, u32[]{:S(2)}, u32[]{:S(2)}) collective-permute-start(bf16[160,512]{1,0:T(8,128)(2,1)S(1)} %pad_maximum_fusion.1), channel_id=1, source_target_pairs={{0,8},{4,12},{8,0},{12,4},{16,24},{20,28},{24,16},{28,20},{1,9},{5... | collective-permute-start | bytes 491528 | tf_op jit(solution)/shard_map/ppermute | solution.py:438
  73.8 3.6 %collective-permute-done.22 = bf16[256,512]{1,0:T(8,128)(2,1)S(1)} collective-permute-done((bf16[256,512]{1,0:T(8,128)(2,1)S(1)}, bf16[256,512]{1,0:T(8,128)(2,1)S(1)}, u32[]{:S(2)}, u32[]{:S(2)}) %collective-permute-start.22) | collective-permute-done | bytes 262176 | tf_op jit(solution)/shard_map/ppermute | solution.py:438
  77.4 0.2 maximum_select_fusion.refs_1_
  77.6 1.0 %collective-permute-start.23 = (bf16[512,512]{1,0:T(8,128)(2,1)S(1)}, bf16[512,512]{1,0:T(8,128)(2,1)S(1)}, u32[]{:S(2)}, u32[]{:S(2)}) collective-permute-start(bf16[512,512]{1,0:T(8,128)(2,1)S(1)} %maximum_select_fusion.refs_1_), channel_id=1, source_target_pairs={{0,4},{4,0},{8,12},{12,8},{16,20},{20,16},{24,28},{28,24},{1,5},{5... | collective-permute-start | bytes 1572872 | tf_op jit(solution)/shard_map/ppermute | solution.py:438
  78.6 0.5 collective-permute-done.16
  79.3 1.0 %collective-permute-start.17 = (bf16[288,512]{1,0:T(8,128)(2,1)S(1)}, bf16[288,512]{1,0:T(8,128)(2,1)S(1)}, u32[]{:S(2)}, u32[]{:S(2)}) collective-permute-start(bf16[288,512]{1,0:T(8,128)(2,1)S(1)} %pad_maximum_fusion), channel_id=1, source_target_pairs={{0,4},{4,0},{8,12},{12,8},{16,20},{20,16},{24,28},{28,24},{1,5},{5... | collective-permute-start | bytes 884744 | tf_op jit(solution)/shard_map/ppermute | solution.py:438
  80.3 9.7 %collective-permute-done.23.refs_2_ = bf16[512,512]{1,0:T(8,128)(2,1)S(1)} collective-permute-done((bf16[512,512]{1,0:T(8,128)(2,1)S(1)}, bf16[512,512]{1,0:T(8,128)(2,1)S(1)}, u32[]{:S(2)}, u32[]{:S(2)}) %collective-permute-start.23) | collective-permute-done | bytes 524320 | tf_op jit(solution)/shard_map/ppermute | solution.py:438
  90.0 2.0 %widen_kernel.1 = (f32[512,512]{1,0:T(8,128)}, f32[512,512]{1,0:T(8,128)}) custom-call(s32[32]{0:T(128)S(1)} %stack.143.refs_0_, bf16[512,512]{1,0:T(8,128)(2,1)S(1)} %maximum_select_fusion.refs_1_, bf16[512,512]{1,0:T(8,128)(2,1)S(1)} %collective-permute-done.23.refs_2_), custom_call_target="tpu_custom_call" | custom-call | bytes 3145856 | tf_op jit(solution)/shard_map/widen_kernel/pallas_call | solution.py:148
  92.1 2.6 %finish_kernel.1 = (f32[512,512]{1,0:T(8,128)}, f32[512,512]{1,0:T(8,128)}) custom-call(s32[32]{0:T(128)S(1)} %stack.143.refs_0_, bf16[528,512]{1,0:T(8,128)(2,1)S(1)} %add_convert_fusion.refs_1_, bf16[528,512]{1,0:T(8,128)(2,1)S(1)} %collective-permute-done.11.refs_2_, f32[512,512]{1,0:T(8,128)S(1)} %get-tuple-element.103.refs_3_, ...), custom_call_target="tpu_custom_call" | custom-call | flops 262144 | bytes 5804160 | tf_op jit(solution)/shard_map/finish_kernel/pallas_call | solution.py:148
  94.7 1.7 %unpack_kernel.1 = (f32[512,128]{1,0:T(8,128)}, f32[512,128]{1,0:T(8,128)}, f32[512,128]{1,0:T(8,128)}, f32[128,512]{1,0:T(8,128)}, f32[512]{0:T(512)}, /*index=...) custom-call(s32[32]{0:T(128)S(1)} %stack.143.refs_0_, ...), custom_call_target="tpu_custom_call" | custom-call | bytes 1654672 | tf_op jit(solution)/shard_map/unpack_kernel/pallas_call | solution.py:148
  (36 shorter events, 0.8 us)
Async XLA Ops:
  0.7 11.5 %collective-permute-start.4 = (bf16[128,512]{1,0:T(8,128)(2,1)}, bf16[128,512]{1,0:T(8,128)(2,1)S(1)}, u32[]{:S(2)}, u32[]{:S(2)}) collective-permute-start(bf16[128,512]{1,0:T(8,128)(2,1)} %refs_13_.1), channel_id=1, source_target_pairs={{0,2},{1,3},{2,0},{3,1},{4,6},{5,7},{6,4},{7,5},{8,10},{9,11},{10,... | collective-permute-start | bytes 393224 | tf_op jit(solution)/shard_map/ppermute | solution.py:438
  3.8 7.9 %copy-start = (bf16[128,512]{1,0:T(8,128)(2,1)S(1)}, bf16[128,512]{1,0:T(8,128)(2,1)}, u32[]{:S(2)}) copy-start(bf16[128,512]{1,0:T(8,128)(2,1)} %refs_13_.1) | copy-start | bytes 393220
  11.5 5.0 %collective-permute-start.1 = (bf16[512,128]{1,0:T(8,128)(2,1)S(1)}, bf16[512,128]{1,0:T(8,128)(2,1)S(1)}, u32[]{:S(2)}, u32[]{:S(2)}) collective-permute-start(bf16[512,128]{1,0:T(8,128)(2,1)S(1)} %get-tuple-element.74.refs_1_.refs_14_), channel_id=1, source_target_pairs={{0,2},{1,3},{2,0},{3,1},{4,6},{5,7},{6,4},{7,5},{8,10},{9,11},{10,... | collective-permute-start | bytes 393224 | tf_op jit(solution)/shard_map/ppermute | solution.py:438
  11.6 4.9 %collective-permute-start.3 = (bf16[128,512]{1,0:T(8,128)(2,1)S(1)}, bf16[128,512]{1,0:T(8,128)(2,1)S(1)}, u32[]{:S(2)}, u32[]{:S(2)}) collective-permute-start(bf16[128,512]{1,0:T(8,128)(2,1)S(1)} %copy-done), channel_id=1, source_target_pairs={{0,1},{1,0},{2,3},{3,2},{4,5},{5,4},{6,7},{7,6},{8,9},{9,8},{10,11... | collective-permute-start | bytes 393224 | tf_op jit(solution)/shard_map/ppermute | solution.py:438
  11.7 4.9 %collective-permute-start = (bf16[512,128]{1,0:T(8,128)(2,1)S(1)}, bf16[512,128]{1,0:T(8,128)(2,1)S(1)}, u32[]{:S(2)}, u32[]{:S(2)}) collective-permute-start(bf16[512,128]{1,0:T(8,128)(2,1)S(1)} %get-tuple-element.74.refs_1_.refs_14_), channel_id=1, source_target_pairs={{0,1},{1,0},{2,3},{3,2},{4,5},{5,4},{6,7},{7,6},{8,9},{9,8},{10,11... | collective-permute-start | bytes 393224 | tf_op jit(solution)/shard_map/ppermute | solution.py:438
  12.2 4.4 %collective-permute-start.5 = (bf16[128,512]{1,0:T(8,128)(2,1)S(1)}, bf16[128,512]{1,0:T(8,128)(2,1)S(1)}, u32[]{:S(2)}, u32[]{:S(2)}) collective-permute-start(bf16[128,512]{1,0:T(8,128)(2,1)S(1)} %collective-permute-done.4.refs_7_), channel_id=1, source_target_pairs={{0,1},{1,0},{2,3},{3,2},{4,5},{5,4},{6,7},{7,6},{8,9},{9,8},{10,11... | collective-permute-start | bytes 393224 | tf_op jit(solution)/shard_map/ppermute | solution.py:438
  16.6 1.3 %collective-permute-start.2 = (bf16[512,128]{1,0:T(8,128)(2,1)S(1)}, bf16[512,128]{1,0:T(8,128)(2,1)S(1)}, u32[]{:S(2)}, u32[]{:S(2)}) collective-permute-start(bf16[512,128]{1,0:T(8,128)(2,1)S(1)} %collective-permute-done.1.refs_3_), channel_id=1, source_target_pairs={{0,1},{1,0},{2,3},{3,2},{4,5},{5,4},{6,7},{7,6},{8,9},{9,8},{10,11... | collective-permute-start | bytes 393224 | tf_op jit(solution)/shard_map/ppermute | solution.py:438
  20.8 1.6 %collective-permute-start.6 = (bf16[256,512]{1,0:T(8,128)(2,1)S(1)}, bf16[256,512]{1,0:T(8,128)(2,1)S(1)}, u32[]{:S(2)}, u32[]{:S(2)}) collective-permute-start(bf16[256,512]{1,0:T(8,128)(2,1)S(1)} %get-tuple-element.85), channel_id=1, source_target_pairs={{0,1},{1,0},{2,3},{3,2},{4,5},{5,4},{6,7},{7,6},{8,9},{9,8},{10,11... | collective-permute-start | bytes 786440 | tf_op jit(solution)/shard_map/ppermute | solution.py:438
  22.5 8.4 %collective-permute-start.7 = (bf16[256,512]{1,0:T(8,128)(2,1)S(1)}, bf16[256,512]{1,0:T(8,128)(2,1)S(1)}, u32[]{:S(2)}, u32[]{:S(2)}) collective-permute-start(bf16[256,512]{1,0:T(8,128)(2,1)S(1)} %add_convert_fusion.6), channel_id=1, source_target_pairs={{0,2},{1,3},{2,0},{3,1},{4,6},{5,7},{6,4},{7,5},{8,10},{9,11},{10,... | collective-permute-start | bytes 786440 | tf_op jit(solution)/shard_map/ppermute | solution.py:438
  24.6 16.3 %collective-permute-start.18 = (bf16[512,512]{1,0:T(8,128)(2,1)S(1)}, bf16[512,512]{1,0:T(8,128)(2,1)S(1)}, u32[]{:S(2)}, u32[]{:S(2)}) collective-permute-start(bf16[512,512]{1,0:T(8,128)(2,1)S(1)} %get-tuple-element.125), channel_id=1, source_target_pairs={{0,4},{4,0},{8,12},{12,8},{16,20},{20,16},{24,28},{28,24},{1,5},{5... | collective-permute-start | bytes 1572872 | tf_op jit(solution)/shard_map/ppermute | solution.py:438
  31.0 1.6 %collective-permute-start.8 = (bf16[256,512]{1,0:T(8,128)(2,1)S(1)}, bf16[256,512]{1,0:T(8,128)(2,1)S(1)}, u32[]{:S(2)}, u32[]{:S(2)}) collective-permute-start(bf16[256,512]{1,0:T(8,128)(2,1)S(1)} %add_convert_fusion.5.refs_1_), channel_id=1, source_target_pairs={{0,1},{1,0},{2,3},{3,2},{4,5},{5,4},{6,7},{7,6},{8,9},{9,8},{10,11... | collective-permute-start | bytes 786440 | tf_op jit(solution)/shard_map/ppermute | solution.py:438
  39.4 8.4 %collective-permute-start.12 = (bf16[256,512]{1,0:T(8,128)(2,1)S(1)}, bf16[256,512]{1,0:T(8,128)(2,1)S(1)}, u32[]{:S(2)}, u32[]{:S(2)}) collective-permute-start(bf16[256,512]{1,0:T(8,128)(2,1)S(1)} %get-tuple-element.109), channel_id=1, source_target_pairs={{0,4},{4,0},{8,12},{12,8},{16,20},{20,16},{24,28},{28,24},{1,5},{5... | collective-permute-start | bytes 786440 | tf_op jit(solution)/shard_map/ppermute | solution.py:438
  41.3 8.2 %collective-permute-start.19 = (bf16[256,512]{1,0:T(8,128)(2,1)S(1)}, bf16[256,512]{1,0:T(8,128)(2,1)S(1)}, u32[]{:S(2)}, u32[]{:S(2)}) collective-permute-start(bf16[256,512]{1,0:T(8,128)(2,1)S(1)} %constant_dynamic-slice_fusion.1), channel_id=1, source_target_pairs={{0,8},{4,12},{8,0},{12,4},{16,24},{20,28},{24,16},{28,20},{1,9},{5... | collective-permute-start | bytes 786440 | tf_op jit(solution)/shard_map/ppermute | solution.py:438
  43.0 11.2 %collective-permute-start.9 = (bf16[528,512]{1,0:T(8,128)(2,1)S(1)}, bf16[528,512]{1,0:T(8,128)(2,1)S(1)}, u32[]{:S(2)}, u32[]{:S(2)}) collective-permute-start(bf16[528,512]{1,0:T(8,128)(2,1)S(1)} %get-tuple-element.102), channel_id=1, source_target_pairs={{0,1},{1,0},{2,3},{3,2},{4,5},{5,4},{6,7},{7,6},{8,9},{9,8},{10,11... | collective-permute-start | bytes 1622024 | tf_op jit(solution)/shard_map/ppermute | solution.py:438
  47.9 6.3 %collective-permute-start.13 = (bf16[128,512]{1,0:T(8,128)(2,1)S(1)}, bf16[128,512]{1,0:T(8,128)(2,1)S(1)}, u32[]{:S(2)}, u32[]{:S(2)}) collective-permute-start(bf16[128,512]{1,0:T(8,128)(2,1)S(1)} %constant_dynamic-slice_fusion.3), channel_id=1, source_target_pairs={{0,8},{4,12},{8,0},{12,4},{16,24},{20,28},{24,16},{28,20},{1,9},{5... | collective-permute-start | bytes 393224 | tf_op jit(solution)/shard_map/ppermute | solution.py:438
  49.7 10.0 %collective-permute-start.20 = (bf16[128,512]{1,0:T(8,128)(2,1)S(1)}, bf16[128,512]{1,0:T(8,128)(2,1)S(1)}, u32[]{:S(2)}, u32[]{:S(2)}) collective-permute-start(bf16[128,512]{1,0:T(8,128)(2,1)S(1)} %constant_dynamic-slice_fusion), channel_id=1, source_target_pairs={{0,16},{4,20},{8,24},{12,28},{16,0},{20,4},{24,8},{28,12},{1,17},{... | collective-permute-start | bytes 393224 | tf_op jit(solution)/shard_map/ppermute | solution.py:438
  54.4 11.2 %collective-permute-start.10 = (bf16[528,512]{1,0:T(8,128)(2,1)S(1)}, bf16[528,512]{1,0:T(8,128)(2,1)S(1)}, u32[]{:S(2)}, u32[]{:S(2)}) collective-permute-start(bf16[528,512]{1,0:T(8,128)(2,1)S(1)} %add_convert_fusion.1), channel_id=1, source_target_pairs={{0,2},{1,3},{2,0},{3,1},{4,6},{5,7},{6,4},{7,5},{8,10},{9,11},{10,... | collective-permute-start | bytes 1622024 | tf_op jit(solution)/shard_map/ppermute | solution.py:438
  54.6 7.2 %collective-permute-start.14 = (bf16[64,512]{1,0:T(8,128)(2,1)S(1)}, bf16[64,512]{1,0:T(8,128)(2,1)S(1)}, u32[]{:S(2)}, u32[]{:S(2)}) collective-permute-start(bf16[64,512]{1,0:T(8,128)(2,1)S(1)} %constant_dynamic-slice_fusion.2), channel_id=1, source_target_pairs={{0,16},{4,20},{8,24},{12,28},{16,0},{20,4},{24,8},{28,12},{1,17},{... | collective-permute-start | bytes 196616 | tf_op jit(solution)/shard_map/ppermute | solution.py:438
  59.7 10.6 %collective-permute-start.21 = (bf16[128,512]{1,0:T(8,128)(2,1)S(1)}, bf16[128,512]{1,0:T(8,128)(2,1)S(1)}, u32[]{:S(2)}, u32[]{:S(2)}) collective-permute-start(bf16[128,512]{1,0:T(8,128)(2,1)S(1)} %add_convert_fusion.7), channel_id=1, source_target_pairs={{0,16},{4,20},{8,24},{12,28},{16,0},{20,4},{24,8},{28,12},{1,17},{... | collective-permute-start | bytes 393224 | tf_op jit(solution)/shard_map/ppermute | solution.py:438
  65.7 5.7 %collective-permute-start.15 = (bf16[96,512]{1,0:T(8,128)(2,1)S(1)}, bf16[96,512]{1,0:T(8,128)(2,1)S(1)}, u32[]{:S(2)}, u32[]{:S(2)}) collective-permute-start(bf16[96,512]{1,0:T(8,128)(2,1)S(1)} %pad_maximum_fusion.2), channel_id=1, source_target_pairs={{0,16},{4,20},{8,24},{12,28},{16,0},{20,4},{24,8},{28,12},{1,17},{... | collective-permute-start | bytes 294920 | tf_op jit(solution)/shard_map/ppermute | solution.py:438
  70.4 7.0 %collective-permute-start.22 = (bf16[256,512]{1,0:T(8,128)(2,1)S(1)}, bf16[256,512]{1,0:T(8,128)(2,1)S(1)}, u32[]{:S(2)}, u32[]{:S(2)}) collective-permute-start(bf16[256,512]{1,0:T(8,128)(2,1)S(1)} %maximum_select_fusion.2), channel_id=1, source_target_pairs={{0,8},{4,12},{8,0},{12,4},{16,24},{20,28},{24,16},{28,20},{1,9},{5... | collective-permute-start | bytes 786440 | tf_op jit(solution)/shard_map/ppermute | solution.py:438
  71.5 7.7 %collective-permute-start.16 = (bf16[160,512]{1,0:T(8,128)(2,1)S(1)}, bf16[160,512]{1,0:T(8,128)(2,1)S(1)}, u32[]{:S(2)}, u32[]{:S(2)}) collective-permute-start(bf16[160,512]{1,0:T(8,128)(2,1)S(1)} %pad_maximum_fusion.1), channel_id=1, source_target_pairs={{0,8},{4,12},{8,0},{12,4},{16,24},{20,28},{24,16},{28,20},{1,9},{5... | collective-permute-start | bytes 491528 | tf_op jit(solution)/shard_map/ppermute | solution.py:438
  77.6 12.4 %collective-permute-start.23 = (bf16[512,512]{1,0:T(8,128)(2,1)S(1)}, bf16[512,512]{1,0:T(8,128)(2,1)S(1)}, u32[]{:S(2)}, u32[]{:S(2)}) collective-permute-start(bf16[512,512]{1,0:T(8,128)(2,1)S(1)} %maximum_select_fusion.refs_1_), channel_id=1, source_target_pairs={{0,4},{4,0},{8,12},{12,8},{16,20},{20,16},{24,28},{28,24},{1,5},{5... | collective-permute-start | bytes 1572872 | tf_op jit(solution)/shard_map/ppermute | solution.py:438
  78.6 13.4 %collective-permute-start.11 = (bf16[528,512]{1,0:T(8,128)(2,1)S(1)}, bf16[528,512]{1,0:T(8,128)(2,1)S(1)}, u32[]{:S(2)}, u32[]{:S(2)}) collective-permute-start(bf16[528,512]{1,0:T(8,128)(2,1)S(1)} %add_convert_fusion.refs_1_), channel_id=1, source_target_pairs={{0,1},{1,0},{2,3},{3,2},{4,5},{5,4},{6,7},{7,6},{8,9},{9,8},{10,11... | collective-permute-start | bytes 1622024 | tf_op jit(solution)/shard_map/ppermute | solution.py:438
  79.3 15.4 %collective-permute-start.17 = (bf16[288,512]{1,0:T(8,128)(2,1)S(1)}, bf16[288,512]{1,0:T(8,128)(2,1)S(1)}, u32[]{:S(2)}, u32[]{:S(2)}) collective-permute-start(bf16[288,512]{1,0:T(8,128)(2,1)S(1)} %pad_maximum_fusion), channel_id=1, source_target_pairs={{0,4},{4,0},{8,12},{12,8},{16,20},{20,16},{24,28},{28,24},{1,5},{5... | collective-permute-start | bytes 884744 | tf_op jit(solution)/shard_map/ppermute | solution.py:438

commit v3 on v2

v3 whole, which is shorter than its diff:
```python
import jax
import jax.numpy as jnp
from jax import lax
from jax.experimental import pallas as pl
from jax.experimental.pallas import tpu as pltpu
from jax.sharding import PartitionSpec as P

HD = 32
GW = 8
WS = 4
WIN = WS * WS
BLOCK = 128
NEG_FILL = -1e30
BF = jnp.bfloat16
F32 = jnp.float32
EXACT = lax.Precision.HIGHEST
VMEM_BYTES = 24 * 1024 * 1024
ROWS = 16


def dot(left, right):
    return jnp.dot(left, right, preferred_element_type=F32)


def dot_nt(left, right):
    return lax.dot_general(left, right, (((1,), (1,)), ((), ())), preferred_element_type=F32)


def dot_tn(left, right):
    return lax.dot_general(left, right, (((0,), (0,)), ((), ())), preferred_element_type=F32)


def exact_nt(left, right):
    return lax.dot_general(
        left, right, (((1,), (1,)), ((), ())), precision=EXACT, preferred_element_type=F32
    )


def normalize(value):
    centre = value - jnp.mean(value, axis=-1, keepdims=True)
    spread = jnp.mean(centre * centre, axis=-1, keepdims=True)
    inverse = lax.rsqrt(spread + 1e-06)
    return centre * inverse, inverse


def norm_back(grad_out, normed, inverse, gain):
    scaled = grad_out * gain
    first_mean = jnp.mean(scaled, axis=-1, keepdims=True)
    second_mean = jnp.mean(scaled * normed, axis=-1, keepdims=True)
    return inverse * (scaled - first_mean - normed * second_mean)


def row(ref):
    return ref[...].reshape(1, -1)


def iota(shape, axis):
    return lax.broadcasted_iota(jnp.int32, shape, axis)


def place(token):
    return (token // GW) % WS * WS + token % WS


def window(token):
    return token // (GW * WS) * (GW // WS) + token % GW // WS


def by_head(value, heads):
    head = iota(value.shape, 1) // HD
    return jnp.concatenate(
        [jnp.where(head == h, value, jnp.zeros_like(value)) for h in range(heads)]
    )


def own_lanes(value, heads):
    rows = value.shape[0] // heads
    head = iota((rows, value.shape[1]), 1) // HD
    total = value[:rows]
    for h in range(1, heads):
        total = jnp.where(head == h, value[h * rows:(h + 1) * rows], total)
    return total


class Loaded:
    def __init__(self, source, buffer, sem):
        self.buffer, self.shape, self.dtype = buffer, source.shape, source.dtype
        self.copy, self.started = pltpu.make_async_copy(source, buffer, sem), False

    def start(self):
        if not self.started:
            self.copy.start()
            self.started = True

    def wait(self):
        if self.copy is not None:
            self.start()
            self.copy.wait()
            self.copy = None

    def __getitem__(self, at):
        self.wait()
        return self.buffer[at]


class Stored:
    def __init__(self, buffer, target, sem):
        self.buffer, self.shape, self.dtype = buffer, target.shape, target.dtype
        self.copy, self.sent = pltpu.make_async_copy(buffer, target, sem), False

    def __getitem__(self, at):
        return self.buffer[at]

    def __setitem__(self, at, value):
        self.buffer[at] = value

    def send(self):
        if not self.sent:
            self.copy.start()
            self.sent = True


def send_off(ref):
    if isinstance(ref, Stored):
        ref.send()


def call(kernel, outs, args, scratch=(), cost=0, exports=(), later=()):
    spaces = {"smem": pltpu.SMEM, "vmem": pltpu.VMEM, "hbm": pltpu.HBM, "hsmem": pltpu.HBM}
    spaces["keep"] = pltpu.HBM
    plain = len(outs)
    outs = list(outs) + [(args[i][0].shape, args[i][0].dtype, "vmem") for i in exports]
    loads = [i for i, (_, where) in enumerate(args) if where[0] == "h"]
    stores = [i for i, (_, _, where) in enumerate(outs) if where == "hbm"]
    shapes = [jax.ShapeDtypeStruct(shape, dtype) for shape, dtype, _ in outs]
    pinned = [spaces[where](shape, dtype) for shape, dtype, where in outs]
    operands = [
        pltpu.with_memory_space_constraint(a, pltpu.HBM) if spaces[where] == pltpu.HBM else a
        for a, where in args
    ]
    buffers = []
    for i in loads:
        if i in exports:
            continue
        array, where = args[i]
        space = pltpu.SMEM if where == "hsmem" else pltpu.VMEM
        buffers.append(space(array.shape, array.dtype))
    buffers += [pltpu.VMEM(outs[i][0], outs[i][1]) for i in stores]
    sems = [pltpu.SemaphoreType.DMA] * (len(loads) + len(stores))

    def body(*refs):
        refs = list(refs)
        ins, rest = refs[:len(args)], refs[len(args):]
        results, rest = rest[:len(outs)], rest[len(outs):]
        own, rest = rest[:len(scratch)], rest[len(scratch):]
        holds, marks = list(rest[:len(buffers)]), list(rest[len(buffers):])
        given = dict(zip(exports, results[plain:]))
        for i in loads:
            hold = given[i] if i in given else holds.pop(0)
            ins[i] = Loaded(ins[i], hold, marks.pop(0))
            if i not in later:
                ins[i].start()
        for i in stores:
            results[i] = Stored(holds.pop(0), results[i], marks.pop(0))
        kernel(*ins, *results[:plain], *own)
        for i in loads:
            ins[i].wait()
        for i in stores:
            results[i].send()
        for i in stores:
            results[i].copy.wait()

    return pl.pallas_call(
        body,
        name=kernel.__name__,
        out_shape=pinned,
        in_specs=[pl.BlockSpec(memory_space=spaces[where]) for _, where in args],
        out_specs=[pl.BlockSpec(memory_space=spaces[where]) for _, _, where in outs],
        scratch_shapes=[pltpu.VMEM(shape, dtype) for shape, dtype in scratch] + buffers + sems,
        compiler_params=pltpu.CompilerParams(vmem_limit_bytes=VMEM_BYTES),
        cost_estimate=pl.CostEstimate(flops=cost * 10 ** 9, bytes_accessed=0, transcendentals=0),
    )(*operands)


def attend_kernel(
    spot, x, g1, s1, wq, wk, wv, bq, bv, rel, pidx, seg, valid, att, first, q, k, v, probs,
):
    tokens, span = x.shape[0], wq.shape[1]
    heads = span // HD
    blocks = tokens // BLOCK
    for b in range(blocks):
        rows = pl.ds(b * BLOCK, BLOCK)
        normed, _ = normalize(x[rows, :].astype(F32))
        first[rows, :] = (normed * row(g1) + row(s1)).astype(BF)
    weights = jnp.concatenate([wq[...], wk[...], wv[...]], axis=1)
    for i in range(2):
        rows = pl.ds(i * (tokens // 2), tokens // 2)
        mixed = dot(first[rows, :], weights)
        q[rows, :] = (mixed[:, :span] + row(bq)).astype(BF)
        k[rows, :] = mixed[:, span:2 * span].astype(BF)
        v[rows, :] = (mixed[:, 2 * span:] + row(bv)).astype(BF)
    lanes = 2 * heads * WIN
    group = heads * WIN
    table = rel[...]
    coarse = table.astype(BF)
    fine = (table - coarse.astype(F32)).astype(BF)
    lane = iota((heads, lanes), 1)
    mine = lane % group // WIN == iota((heads, lanes), 0)
    rows_by_offset = dot_tn(coarse, (mine & (lane < group)).astype(BF)) + dot_tn(
        fine, (mine & (lane >= group)).astype(BF)
    )
    index = jnp.concatenate([pidx[...]] * (2 * heads), axis=1)
    terms = jnp.zeros((WIN, lanes), F32)
    for o in range(rel.shape[1]):
        terms = jnp.where(index == o, rows_by_offset[o:o + 1, :], terms)
    spread = (place(iota((BLOCK, WIN), 0)) == iota((BLOCK, WIN), 1)).astype(BF)
    terms = dot(spread, terms.astype(BF)).astype(BF)
    lane = iota((lanes, BLOCK), 0)
    here = lane % WIN == place(iota((lanes, BLOCK), 1))
    bias = jnp.concatenate(
        [dot(terms, (here & (lane % group // WIN == h)).astype(BF)) for h in range(heads)]
    )
    query_at, key_at = iota((BLOCK, BLOCK), 0), iota((BLOCK, BLOCK), 1)
    near = window(query_at) == window(key_at)
    selfs = query_at == key_at
    factor = HD ** (-0.5)
    for b in range(blocks):
        rows = pl.ds(b * BLOCK, BLOCK)
        seg_keys = jnp.broadcast_to(seg[:, rows].astype(F32), (BLOCK, BLOCK))
        valid_keys = jnp.broadcast_to(valid[:, rows], (BLOCK, BLOCK)) > 0
        allowed = near & (seg_keys == seg_keys.T) & (valid_keys | selfs)
        wall = jnp.where(allowed, 0.0, NEG_FILL)
        scores = dot_nt(by_head(q[rows, :], heads), k[rows, :]) * factor + bias
        scores = jnp.where(jnp.concatenate([wall] * heads) < 0.0, NEG_FILL, scores)
        expo = jnp.exp(scores - jnp.max(scores, axis=-1, keepdims=True))
        prob = expo * (1.0 / jnp.sum(expo, axis=-1, keepdims=True))
        probs[b] = prob
        att[rows, :] = own_lanes(dot(prob.astype(BF), v[rows, :]), heads).astype(BF)


def fetch_kernel(after, also, *operands):
    for ref in operands[:-1]:
        ref.wait()
    operands[-1][...] = jnp.zeros_like(operands[-1])


def mlp_kernel(
    spot, a0, a1, a2, a3, p0, p1, p2, p3, x, bo, g2, s2, w1, b1, cot, w2,
    mid, second, hidden, gpre, keep, send, att_all, wo_all,
):
    me = spot[0]
    width = a0.shape[1]
    for j, (a, p) in enumerate(((a0, p0), (a1, p1), (a2, p2), (a3, p3))):
        here = pl.ds(pl.multiple_of((me ^ j) * width, width), width)
        att_all[:, here] = a[...]
        wo_all[here, :] = p[...]
    tokens = x.shape[0]
    half = tokens // 2
    curve = (2.0 / jnp.pi) ** 0.5
    for i in range(2):
        rows = pl.ds(i * half, half)
        value = x[rows, :].astype(F32) + dot(att_all[rows, :], wo_all[...]) + row(bo)
        mid[rows, :] = value
        normed, _ = normalize(value)
        second[rows, :] = (normed * row(g2) + row(s2)).astype(BF)
        pre = dot(second[rows, :], w1[...]) + row(b1)
        square = pre * pre
        bend = jnp.tanh(curve * (pre + 0.044715 * (pre * square)))
        upper = 0.5 * (1.0 + bend)
        hidden[rows, :] = (pre * upper).astype(BF)
        slope = upper + 0.5 * pre * (1.0 - bend * bend) * (curve * (1.0 + 0.134145 * square))
        gpre[rows, :] = (dot_nt(cot[rows, :], w2[...]) * slope).astype(BF)
    send_off(mid)
    core = me % 2
    mine = pl.ds(pl.multiple_of(core * half, half), half)
    other = pl.ds(pl.multiple_of((1 - core) * half, half), half)
    send[...] = dot_nt(gpre[other, :], w1[...]).astype(BF)
    keep[...] = dot_nt(gpre[mine, :], w1[...])


def halves(flag, rows):
    near = pl.ds(pl.multiple_of(flag * rows, rows), rows)
    return near, pl.ds(pl.multiple_of((1 - flag) * rows, rows), rows)


def mlp_grad_kernel(spot, second, hidden, gpre, cot, own1, away1, own2, away2, small, grads):
    part = own1.shape[0]
    mine, other = halves(spot[2], part)
    grads[...] = dot_tn(second[...], gpre[...]).astype(BF)
    own1[...] = grads[mine, :]
    away1[...] = grads[other, :]
    mine, other = halves(spot[3], part)
    grads[...] = dot_tn(hidden[...], cot[...]).astype(BF)
    own2[...] = grads[mine, :]
    away2[...] = grads[other, :]
    which = iota(small.shape, 0)
    first = jnp.sum(gpre[...].astype(F32), axis=0, keepdims=True)
    later = jnp.sum(cot[...].astype(F32), axis=0, keepdims=True)
    small[...] = jnp.where(which == 0, first, jnp.where(which == 1, later, 0.0)).astype(BF)


def attend_back_kernel(
    spot, s2a, s2b, mid, cot, g2, wo, v, probs, k, q, first, att, wq, wk, wv, g1, s1,
    gmid, own, to_y, to_z, to_yz, gq, gk, gv, scores, sums, norm1, gsec, gproj, gatt, pay,
):
    core, place_yz = spot[0] % 2, 2 * spot[2] + spot[3]
    tokens, width = cot.shape
    half = tokens // 2
    span = wq.shape[1]
    heads = span // HD
    blocks = tokens // BLOCK
    mine, other = halves(core, half)
    gsec[mine, :] = s2a[...].astype(F32)
    gsec[other, :] = s2b[...].astype(F32)
    gain_sum = jnp.zeros((1, width), F32)
    shift_sum = jnp.zeros((1, width), F32)
    proj_sum = jnp.zeros((1, width), F32)
    for b in range(blocks):
        rows = pl.ds(b * BLOCK, BLOCK)
        grad = gsec[rows, :]
        normed, inverse = normalize(mid[rows, :])
        gain_sum += jnp.sum(grad * normed, axis=0, keepdims=True)
        shift_sum += jnp.sum(grad, axis=0, keepdims=True)
        value = cot[rows, :].astype(F32) + norm_back(grad, normed, inverse, row(g2))
        gmid[rows, :] = value
        proj_sum += jnp.sum(value, axis=0, keepdims=True)
        gproj[rows, :] = value.astype(BF)
    gatt[...] = dot_nt(gproj[...], wo[...]).astype(BF)
    factor = HD ** (-0.5)
    score_sum = jnp.zeros((heads * BLOCK, BLOCK), F32)
    for b in range(blocks):
        rows = pl.ds(b * BLOCK, BLOCK)
        grads = by_head(gatt[rows, :], heads)
        prob = probs[b]
        grad = dot_nt(grads, v[rows, :])
        gv[rows, :] = dot_tn(prob.astype(BF), grads).astype(BF)
        inner = jnp.sum(prob * grad, axis=-1, keepdims=True)
        gscore = (prob * (grad - inner)).astype(BF)
        score_sum += gscore.astype(F32)
        gq[rows, :] = (factor * own_lanes(dot(gscore, k[rows, :]), heads)).astype(BF)
        gk[rows, :] = (factor * dot_tn(gscore, by_head(q[rows, :], heads))).astype(BF)
    scores[...] = score_sum
    shift = jnp.zeros((8, width), F32)
    gain = jnp.zeros((8, width), F32)
    ones = jnp.ones((8, span), BF)
    eight = iota((8, span), 0)
    mixed = dot_tn(first[...], jnp.concatenate([gq[...], gk[...], gv[...]], axis=1))
    for j, (part, weight) in enumerate(((gq, wq), (gk, wk), (gv, wv))):
        grads = mixed[:, j * span:(j + 1) * span]
        total = jnp.sum(part[...].astype(F32), axis=0, keepdims=True)
        if j != 1:
            at = 0 if j == 0 else span
            sums[3:4, at:at + span] = total
        coarse = total.astype(BF)
        fine = (total - coarse.astype(F32)).astype(BF)
        pair = jnp.where(eight == 0, coarse, jnp.where(eight == 1, fine, jnp.zeros_like(coarse)))
        shift += dot_nt(pair, weight[...])
        product = weight[...].astype(F32) * grads
        coarse = product.astype(BF)
        gain += dot_nt(ones, coarse) + dot_nt(ones, (product - coarse.astype(F32)).astype(BF))
        grads = grads.astype(BF)
        for i in range(width // span):
            pay[j * span:(j + 1) * span, i * span:(i + 1) * span] = grads[i * span:(i + 1) * span]
    pay[3 * span:4 * span, :] = dot_tn(att[...], gproj[...]).astype(BF)
    for ref, flip in ((own, 0), (to_y, 2), (to_z, 1), (to_yz, 3)):
        ref[...] = pay[pl.ds(pl.multiple_of((place_yz ^ flip) * span, span), span), :]
    sums[3:4, 2 * span:] = jnp.zeros((1, width - 2 * span), F32)
    which = iota((ROWS, width), 0)
    shift = shift[0:1, :] + shift[1:2, :]
    gain = (gain[0:1, :] - row(s1) * shift) / row(g1)
    norm1[...] = jnp.where(which == 0, gain, jnp.where(which == 1, shift, 0.0)).astype(BF)
    sums[0:1, :] = gain_sum
    sums[1:2, :] = shift_sum
    sums[2:3, :] = proj_sum


def attend_out_kernel(spot, after, gq, gk, gv, wq, wk, wv, hidden, w2, keep, send):
    half = hidden.shape[0] // 2
    for where, ref in zip(halves(spot[0] % 2, half), (keep, send)):
        ref[0:half, :] = (
            dot_nt(gq[where, :], wq[...])
            + dot_nt(gk[where, :], wk[...])
            + dot_nt(gv[where, :], wv[...])
        ).astype(BF)
        ref[half:, :] = dot(hidden[where, :], w2[...]).astype(BF)


def sums_kernel(after, scores, sums, pidx, small, all_sums):
    heads = scores.shape[0] // BLOCK
    at = place(iota((BLOCK, WIN), 0)) == iota((BLOCK, WIN), 1)
    fold = at.astype(F32)
    lanes = heads * WIN
    folded = jnp.zeros((WIN, lanes), F32)
    for h in range(heads):
        lane = iota((BLOCK, lanes), 1)
        lay = ((place(iota((BLOCK, lanes), 0)) == lane % WIN) & (lane // WIN == h)).astype(F32)
        once = lax.dot_general(
            fold, scores[h * BLOCK:(h + 1) * BLOCK, :], (((0,), (0,)), ((), ())),
            precision=EXACT, preferred_element_type=F32,
        )
        folded += jnp.dot(once, lay, precision=EXACT, preferred_element_type=F32)
    index = jnp.concatenate([pidx[...]] * heads, axis=1)
    slots = 64
    slot = iota((slots, lanes), 0)
    by_offset = jnp.zeros((slots, lanes), F32)
    for o in range(49):
        total = jnp.sum(jnp.where(index == o, folded, 0.0), axis=0, keepdims=True)
        by_offset = jnp.where(slot == o, total, by_offset)
    pick = (iota((8, lanes), 1) // WIN == iota((8, lanes), 0)).astype(F32)
    offsets = lax.dot_general(
        pick, by_offset, (((1,), (1,)), ((), ())), precision=EXACT, preferred_element_type=F32
    )
    all_sums[...] = jnp.zeros_like(all_sums)
    all_sums[0:3, :] = sums[0:3, :]
    all_sums[3:4, :] = sums[3:4, :]
    all_sums[8:16, 0:slots] = offsets
    small[...] = all_sums[...].astype(BF)


def finish_kernel(spot, s4, r4, gmid, x, g1, mid, b2, layer_out, input_grad):
    core = spot[0] % 2
    half = x.shape[0] // 2
    for part, ref in enumerate((s4, r4)):
        start = core if part == 0 else 1 - core
        where = pl.ds(pl.multiple_of(start * half, half), half)
        normed, inverse = normalize(x[where, :].astype(F32))
        grad = ref[0:half, :].astype(F32)
        input_grad[where, :] = gmid[where, :] + norm_back(grad, normed, inverse, row(g1))
        mlp = ref[half:, :].astype(F32)
        layer_out[where, :] = mid[where, :] + mlp + row(b2)


def widen_kernel(spot, after, near1, far1, near2, far2, w1, w2):
    part = near1.shape[0]
    for flag, near, far, ref in ((spot[2], near1, far1, w1), (spot[3], near2, far2, w2)):
        mine, other = halves(flag, part)
        ref[mine, :] = near[...].astype(F32)
        ref[other, :] = far[...].astype(F32)
        send_off(ref)


def unpack_kernel(
    spot, after, near, from_y, from_z, from_yz,
    wq, wk, wv, wo, b1, b2, g2, s2, bo, bq, bv, rel, g1, s1, both,
):
    place_yz = 2 * spot[2] + spot[3]
    width = near.shape[1]
    span = wo.shape[0]
    for ref, flip in ((near, 0), (from_y, 2), (from_z, 1), (from_yz, 3)):
        both[place_yz ^ flip] = ref[0:span, :]
    for j, ref in enumerate((wq, wk, wv)):
        for i in range(width // span):
            block = both[j, :, i * span:(i + 1) * span]
            ref[i * span:(i + 1) * span, :] = block.astype(F32)
        send_off(ref)
    wo[...] = both[3].astype(F32)
    send_off(wo)
    sums = (near[span:, :].astype(F32) + from_y[span:, :].astype(F32)) + (
        from_z[span:, :].astype(F32) + from_yz[span:, :].astype(F32)
    )
    for at, ref in ((0, b1), (1, b2), (8, g2), (9, s2), (10, bo), (24, g1), (25, s1)):
        ref[...] = sums[at]
    bq[...] = sums[11, :span]
    bv[...] = sums[11, span:2 * span]
    rel[...] = sums[16:16 + rel.shape[0], :rel.shape[1]]


def swap(value, axis, bit, size):
    return lax.ppermute(value, axis, [(i, i ^ bit) for i in range(size)])


def shards(
    inputs,
    query_weight,
    key_weight,
    value_weight,
    query_bias,
    value_bias,
    position_bias,
    proj_weight,
    proj_bias,
    norm1_gain,
    norm1_shift,
    norm2_gain,
    norm2_shift,
    up_weight,
    up_bias,
    down_weight,
    down_bias,
    segment_ids,
    valid_mask,
    position_index,
    out_cotangent,
    dp,
    tensor,
):
    tokens, width = inputs.shape
    half = tokens // 2
    span = query_weight.shape[1]
    units = up_weight.shape[1]
    heads = span // HD
    blocks = tokens // BLOCK
    me = lax.axis_index("tensor")
    mate = lax.axis_index("dp")
    bits = [1 << i for i in range(dp.bit_length() - 1)]
    flags = [(mate >> i) & 1 for i in range(len(bits))]
    lower = [flag == 0 for flag in flags]
    sizes = [(width >> (i + 1)) * n for i in range(len(bits)) for n in (1, 2)]
    starts = {
        (i, size): (flags[i] * size).astype(jnp.uint32) for i in range(len(bits)) for size in sizes
    }
    stops = {
        at: ((1 - flags[at[0]]) * at[1]).astype(jnp.uint32) for at in starts
    }
    spot = jnp.stack(
        [me, mate]
        + flags
        + [flag.astype(jnp.int32) for flag in lower]
        + [at.astype(jnp.int32) for at in list(starts.values()) + list(stops.values())]
    )
    seg = segment_ids.reshape(1, tokens)
    valid = valid_mask.reshape(1, tokens)
    wide = (tokens, width)
    narrow = (tokens, span)

    wo_x = swap(proj_weight, "tensor", 2, tensor)
    wo_c = swap(proj_weight, "tensor", 1, tensor)
    wo_d = swap(wo_x, "tensor", 1, tensor)

    att, first, q, k, v, probs = call(
        attend_kernel,
        [
            (narrow, BF, "vmem"), (wide, BF, "vmem"), (narrow, BF, "vmem"), (narrow, BF, "vmem"),
            (narrow, BF, "vmem"), ((blocks, heads * BLOCK, BLOCK), F32, "vmem"),
        ],
        [
            (spot, "smem"), (inputs, "hbm"), (norm1_gain, "hbm"), (norm1_shift, "hbm"),
            (query_weight, "hbm"), (key_weight, "hbm"), (value_weight, "hbm"), (query_bias, "hbm"),
            (value_bias, "hbm"), (position_bias.T, "hbm"), (position_index, "hbm"), (seg, "hbm"),
            (valid, "hbm"),
        ],
        cost=20,
    )
    (
        _, inputs, norm1_gain, norm1_shift, position_index, query_weight, key_weight, value_weight,
        proj_weight, proj_bias, norm2_gain, norm2_shift, up_weight, up_bias, out_cotangent,
        down_weight, down_bias,
    ) = call(
        fetch_kernel,
        [((8, BLOCK), F32, "vmem")],
        [(att, "vmem"), (wo_x, "vmem")]
        + [
            (value, "hbm")
            for value in (
                inputs, norm1_gain, norm1_shift, position_index, query_weight, key_weight,
                value_weight, proj_weight, proj_bias, norm2_gain, norm2_shift, up_weight, up_bias,
                out_cotangent, down_weight, down_bias,
            )
        ],
        exports=tuple(range(2, 18)),
        cost=0,
    )
    att_x, down_bias = lax.optimization_barrier((swap(att, "tensor", 2, tensor), down_bias))
    att_c = swap(att, "tensor", 1, tensor)
    att_d = swap(att_x, "tensor", 1, tensor)

    mid, second, hidden, gpre, keep3, send3 = call(
        mlp_kernel,
        [
            (wide, F32, "vmem"), (wide, BF, "vmem"), ((tokens, units), BF, "vmem"),
            ((tokens, units), BF, "vmem"), ((half, width), F32, "vmem"), ((half, width), BF, "vmem"),
        ],
        [
            (spot, "smem"), (att, "vmem"), (att_c, "vmem"), (att_x, "vmem"), (att_d, "vmem"),
            (proj_weight, "vmem"), (wo_c, "vmem"), (wo_x, "vmem"), (wo_d, "vmem"),
            (inputs, "vmem"), (proj_bias, "vmem"), (norm2_gain, "vmem"), (norm2_shift, "vmem"),
            (up_weight, "vmem"), (up_bias, "vmem"), (out_cotangent, "vmem"), (down_weight, "vmem"),
        ],
        scratch=[((tokens, tensor * span), BF), ((tensor * span, width), BF)],
        cost=2,
    )

    def fold(value, other):
        return (value.astype(F32) + other.astype(F32)).astype(BF)

    own1, away1, own2, away2, small_a = call(
        mlp_grad_kernel,
        [((half, width), BF, "vmem")] * 4 + [((8, width), BF, "vmem")],
        [
            (spot, "smem"), (second, "vmem"), (hidden, "vmem"), (gpre, "vmem"),
            (out_cotangent, "vmem"),
        ],
        scratch=[((width, units), BF)],
        cost=2,
    )
    come3 = swap(send3, "tensor", 1, tensor)
    come3, small_a, away1, away2 = lax.optimization_barrier((come3, small_a, away1, away2))
    pair3 = fold(keep3, come3)
    come3, come_a, come_b = lax.optimization_barrier(
        (
            swap(pair3, "tensor", 2, tensor),
            swap(away1, "dp", bits[0], dp),
            swap(away2, "dp", bits[1], dp),
        )
    )
    sum3 = fold(pair3, come3)
    rest3 = swap(sum3, "tensor", 1, tensor)

    def meet(own, along_y, along_z, along_yz):
        return (
            own,
            swap(along_y, "dp", bits[0], dp),
            swap(along_z, "dp", bits[1], dp),
            swap(along_yz, "dp", bits[0] | bits[1], dp),
        )

    def combine(parts):
        own, y, z, yz = [part.astype(F32) for part in parts]
        return ((own + y) + (z + yz)).astype(BF)

    piece = ((span, width), BF, "vmem")
    gmid, att_own, att_y, att_z, att_yz, gq, gk, gv, scores, sums, norm1 = call(
        attend_back_kernel,
        [
            (wide, F32, "vmem"), piece, piece, piece, piece, (narrow, BF, "vmem"),
            (narrow, BF, "vmem"), (narrow, BF, "vmem"), ((heads * BLOCK, BLOCK), F32, "vmem"),
            ((8, width), F32, "vmem"), ((ROWS, width), BF, "vmem"),
        ],
        [
            (spot, "smem"), (sum3, "vmem"), (rest3, "vmem"), (mid, "vmem"),
            (out_cotangent, "vmem"), (norm2_gain, "vmem"), (proj_weight, "vmem"), (v, "vmem"),
            (probs, "vmem"), (k, "vmem"), (q, "vmem"), (first, "vmem"), (att, "vmem"),
            (query_weight, "vmem"), (key_weight, "vmem"), (value_weight, "vmem"),
            (norm1_gain, "vmem"), (norm1_shift, "vmem"),
        ],
        scratch=[(wide, F32), (wide, BF), (narrow, BF), ((4 * span, width), BF)],
        cost=1,
    )
    att_parts = meet(att_own, att_y, att_z, att_yz)
    chunk = combine(att_parts)
    across = [swap(norm1, "tensor", flip, tensor).astype(F32) for flip in (1, 2, 3)]
    norm1 = ((norm1.astype(F32) + across[0]) + (across[1] + across[2])).astype(BF)
    (small_b,) = call(
        sums_kernel,
        [((16, width), BF, "vmem")],
        [(norm1, "vmem"), (scores, "vmem"), (sums, "vmem"), (position_index, "vmem")],
        scratch=[((16, width), F32)],
        cost=1,
    )
    keep4, send4 = call(
        attend_out_kernel,
        [((tokens, width), BF, "vmem"), ((tokens, width), BF, "vmem")],
        [
            (spot, "smem"), (chunk, "vmem"), (gq, "vmem"), (gk, "vmem"), (gv, "vmem"),
            (query_weight, "vmem"), (key_weight, "vmem"), (value_weight, "vmem"),
            (hidden, "vmem"), (down_weight, "vmem"),
        ],
        cost=1,
    )

    pair4 = fold(keep4, swap(send4, "tensor", 1, tensor))
    sum4 = fold(pair4, swap(pair4, "tensor", 2, tensor))
    rest4 = swap(sum4, "tensor", 1, tensor)

    left = jnp.uint32(0)

    def pick(value, i):
        part = value.shape[0] // 2
        return (
            lax.dynamic_slice(value, (starts[i, part], left), (part, width)),
            lax.dynamic_slice(value, (stops[i, part], left), (part, width)),
        )

    def scatter(value, i):
        own, away = pick(value, i)
        return fold(own, swap(away, "dp", bits[i], dp))

    def gather(own, i):
        other = swap(own, "dp", bits[i], dp)
        return jnp.where(
            lower[i], jnp.concatenate([own, other]), jnp.concatenate([other, own])
        )

    more = range(2, len(bits))

    keep_a, away_a = pick(fold(own1, come_a), 1)
    keep_b, away_b = pick(fold(own2, come_b), 0)
    come_a, come_b, gq = lax.optimization_barrier(
        (swap(away_a, "dp", bits[1], dp), swap(away_b, "dp", bits[0], dp), gq)
    )
    mlp_chunk = jnp.concatenate([fold(keep_a, come_a), fold(keep_b, come_b)])
    for i in more:
        mlp_chunk = fold(mlp_chunk, swap(mlp_chunk, "dp", bits[i], dp))
    chunk = jnp.concatenate([chunk, small_a, small_b, norm1[:8]])
    for i in more:
        chunk = fold(chunk, swap(chunk, "dp", bits[i], dp))
    chunks = meet(chunk, chunk, chunk, chunk)
    near1 = gather(mlp_chunk[:mlp_chunk.shape[0] // 2], 1)
    near2 = gather(mlp_chunk[mlp_chunk.shape[0] // 2:], 0)
    far1 = swap(near1, "dp", bits[0], dp)
    far2 = swap(near2, "dp", bits[1], dp)
    layer_out, input_grad = call(
        finish_kernel,
        [(wide, F32, "hbm"), (wide, F32, "hbm")],
        [
            (spot, "smem"), (sum4, "vmem"), (rest4, "vmem"), (gmid, "vmem"), (inputs, "vmem"),
            (norm1_gain, "vmem"), (mid, "vmem"), (down_bias, "vmem"),
        ],
        cost=2,
    )
    vector, short = ((width,), F32, "hbm"), ((span,), F32, "hbm")
    (
        wq_total, wk_total, wv_total, wo_total, b1_total, b2_total, g2_total, s2_total, bo_total,
        bq_total, bv_total, rel_total, g1_total, s1_total,
    ) = call(
        unpack_kernel,
        [
            ((width, span), F32, "hbm"), ((width, span), F32, "hbm"), ((width, span), F32, "hbm"),
            ((span, width), F32, "hbm"), vector, vector, vector, vector, vector, short, short,
            ((heads, position_bias.shape[0]), F32, "hbm"), vector, vector,
        ],
        [(spot, "smem"), (layer_out, "keep")] + [(value, "vmem") for value in chunks],
        scratch=[((4, span, width), BF)],
    )
    rel_total = rel_total.T
    w1_total, w2_total = call(
        widen_kernel,
        [((width, units), F32, "hbm"), ((units, width), F32, "hbm")],
        [(spot, "smem"), (wq_total, "keep")]
        + [(value, "vmem") for value in (near1, far1, near2, far2)],
    )

    return (
        layer_out,
        input_grad,
        wq_total,
        wk_total,
        wv_total,
        bq_total,
        bv_total,
        rel_total,
        wo_total,
        bo_total,
        g1_total,
        s1_total,
        g2_total,
        s2_total,
        w1_total,
        b1_total,
        w2_total,
        b2_total,
    )


def solution(mesh):
    dp, tensor = mesh.shape["dp"], mesh.shape["tensor"]

    def body(*args):
        return shards(*args, dp=dp, tensor=tensor)

    column, line, whole = P(None, "tensor"), P("tensor"), P()
    return jax.shard_map(
        body,
        mesh=mesh,
        in_specs=(
            P("dp", None),
            column,
            column,
            column,
            line,
            line,
            column,
            P("tensor", None),
            whole,
            whole,
            whole,
            whole,
            whole,
            column,
            line,
            P("tensor", None),
            whole,
            P("dp", None),
            P("dp", None),
            whole,
            P("dp", None),
        ),
        out_specs=(
            P("dp", None),
            P("dp", None),
            column,
            column,
            column,
            line,
            line,
            column,
            P("tensor", None),
            whole,
            whole,
            whole,
            whole,
            whole,
            column,
            line,
            P("tensor", None),
            whole,
        ),
        check_vma=False,
    )
```

time: 96.7 us -> 91.5 us (0.946)
  waiting for transfers between devices: 44.2 us -> 35.3 us
  starting transfers between devices: 24 us -> 30.1 us
  Pallas kernels: 25.5 us -> 23.8 us
    ppermute x24 -> x31, waiting for transfers between devices: 44.2 us -> 35.3 us  [swap(): return lax.ppermute(value, axis, [(i, i ^ bit) for i in range(size)])]
    ppermute x24 -> x31, starting transfers between devices: 24 us -> 30.1 us  [swap(): return lax.ppermute(value, axis, [(i, i ^ bit) for i in range(size)])]
    pallas_call x7 -> x10, Pallas kernels: 25.5 us -> 23.8 us  [call(): pl.pallas_call(body, name=kernel.__name__, out_shape=pinned, in_specs=[pl...]
  transfers between devices with their start and end apart: 24 -> 31, of which waited for: 15 -> 15; matrix products, arithmetic and copies ran while one was open for 2% -> 1% of each run, Pallas kernels for 22% -> 21%
where the time goes in v3:
time: 91.5 us; the launch traced here: 91.3 us
  waiting for transfers between devices  35.3 us (39%)
  starting transfers between devices  30.1 us (33%)
  Pallas kernels  23.8 us (26%)
  other arithmetic  1.01 us (1%)
  between operations  0.92 us (1%)
    ppermute x31, waiting for transfers between devices, swap(): return lax.ppermute(value, axis, [(i, i ^ bit) for i in range(size)])  35.3 us
    ppermute x31, starting transfers between devices, swap(): return lax.ppermute(value, axis, [(i, i ^ bit) for i in range(size)])  30.1 us
    pallas_call x10, Pallas kernels, call(): pl.pallas_call(body, name=kernel.__name__, out_shape=pinned, in_specs=[pl...  23.8 us
  transfers between devices with their start and end apart: 31, of which 15 were waited for; matrix products, arithmetic and copies ran while one was open for 1% of the time, Pallas kernels for 21%

profile of v3, /device:TPU:0, one launch (start us, length us, event | category | flops | bytes accessed | tf_op | source)
XLA Modules:
  0.0 91.3 jit_solution(3348681646192471313)
XLA Ops:
  0.7 3.0 %collective-permute-start.2 = (bf16[128,512]{1,0:T(8,128)(2,1)}, bf16[128,512]{1,0:T(8,128)(2,1)S(1)}, u32[]{:S(2)}, u32[]{:S(2)}) collective-permute-start(bf16[128,512]{1,0:T(8,128)(2,1)} %refs_9_.1), channel_id=1, source_target_pairs={{0,2},{1,3},{2,0},{3,1},{4,6},{5,7},{6,4},{7,5},{8,10},{9,11},{10,... | collective-permute-start | bytes 393224 | tf_op jit(solution)/shard_map/ppermute | solution.py:469
  3.8 4.8 %attend_kernel.1 = (bf16[512,128]{1,0:T(8,128)(2,1)S(1)}, bf16[512,512]{1,0:T(8,128)(2,1)S(1)}, bf16[512,128]{1,0:T(8,128)(2,1)S(1)}, bf16[512,128]{1,0:T(8,128)...) custom-call(s32[32]{0:T(128)S(1)} %stack.143.refs_0_, bf16[512,512]{1,0:T(8,128)(2,1)} %refs_2_.3, ...), custom_call_target="tpu_custom_call" | custom-call | flops 20000000000 | tf_op jit(solution)/shard_map/attend_kernel/pallas_call | solution.py:173
  8.8 0.5 collective-permute-start
  9.3 2.5 %fetch_kernel.1 = (f32[8,128]{1,0:T(8,128)}, bf16[512,512]{1,0:T(8,128)(2,1)S(1)}, f32[512]{0:T(512)S(1)}, f32[512]{0:T(512)S(1)}, s32[16,16]{1,0:T(8,128)S(1)},...) custom-call(bf16[512,128]{1,0:T(8,128)(2,1)S(1)} %get-tuple-element., ...), custom_call_target="tpu_custom_call" | custom-call | tf_op jit(solution)/shard_map/fetch_kernel/pallas_call | solution.py:173
  11.7 1.9 %collective-permute-done.1.refs_3_ = bf16[512,128]{1,0:T(8,128)(2,1)S(1)} collective-permute-done((bf16[512,128]{1,0:T(8,128)(2,1)S(1)}, bf16[512,128]{1,0:T(8,128)(2,1)S(1)}, u32[]{:S(2)}, u32[]{:S(2)}) %collective-permute-start.1) | collective-permute-done | bytes 131104 | tf_op jit(solution)/shard_map/ppermute | solution.py:469
  13.6 0.5 collective-permute-start.3
  14.1 0.8 collective-permute-done.5.refs_8_
  15.0 0.2 collective-permute-done.3.refs_4_
  15.2 2.9 %mlp_kernel.1 = (f32[512,512]{1,0:T(8,128)S(1)}, bf16[512,512]{1,0:T(8,128)(2,1)S(1)}, bf16[512,512]{1,0:T(8,128)(2,1)S(1)}, bf16[512,512]{1,0:T(8,128)(2,1)S(1)...) custom-call(s32[32]{0:T(128)S(1)} %stack.143.refs_0_, ...), custom_call_target="tpu_custom_call" | custom-call | flops 2000000000 | tf_op jit(solution)/shard_map/mlp_kernel/pallas_call | solution.py:173
  18.1 0.4 collective-permute-start.6
  18.5 1.4 %mlp_grad_kernel.1 = (bf16[256,512]{1,0:T(8,128)(2,1)S(1)}, bf16[256,512]{1,0:T(8,128)(2,1)S(1)}, bf16[256,512]{1,0:T(8,128)(2,1)S(1)}, bf16[256,512]{1,0:T(8,128)(2,1)S(1)}, bf16[8,512]{1,0:T(8,128)(2,1)S(1)}) custom-call(s32[32]{0:T(128)S(1)} %stack.143.refs_0_, bf16[512,512]{1,0:T(8,128)(2,1)S(1)} %get-tuple-element.107.refs_1_, ...), custom_call_target="tpu_custom_call" | custom-call | flops 2000000000 | tf_op jit(solution)/shard_map/mlp_grad_kernel/pallas_call | solution.py:173
  20.0 0.4 collective-permute-start.7
  20.4 1.7 %collective-permute-start.8 = (bf16[256,512]{1,0:T(8,128)(2,1)S(1)}, bf16[256,512]{1,0:T(8,128)(2,1)S(1)}, u32[]{:S(2)}, u32[]{:S(2)}) collective-permute-start(bf16[256,512]{1,0:T(8,128)(2,1)S(1)} %get-tuple-element.114), channel_id=1, source_target_pairs={{0,4},{4,0},{8,12},{12,8},{16,20},{20,16},{24,28},{28,24},{1,5},{5... | collective-permute-start | bytes 786440 | tf_op jit(solution)/shard_map/ppermute | solution.py:469
  22.1 1.6 %collective-permute-start.9 = (bf16[256,512]{1,0:T(8,128)(2,1)S(1)}, bf16[256,512]{1,0:T(8,128)(2,1)S(1)}, u32[]{:S(2)}, u32[]{:S(2)}) collective-permute-start(bf16[256,512]{1,0:T(8,128)(2,1)S(1)} %get-tuple-element.115), channel_id=1, source_target_pairs={{0,8},{4,12},{8,0},{12,4},{16,24},{20,28},{24,16},{28,20},{1,9},{5... | collective-permute-start | bytes 786440 | tf_op jit(solution)/shard_map/ppermute | solution.py:469
  23.7 4.8 %collective-permute-done.7 = bf16[256,512]{1,0:T(8,128)(2,1)S(1)} collective-permute-done((bf16[256,512]{1,0:T(8,128)(2,1)S(1)}, bf16[256,512]{1,0:T(8,128)(2,1)S(1)}, u32[]{:S(2)}, u32[]{:S(2)}) %collective-permute-start.7) | collective-permute-done | bytes 262176 | tf_op jit(solution)/shard_map/ppermute | solution.py:469
  28.5 1.4 %collective-permute-done.9 = bf16[256,512]{1,0:T(8,128)(2,1)S(1)} collective-permute-done((bf16[256,512]{1,0:T(8,128)(2,1)S(1)}, bf16[256,512]{1,0:T(8,128)(2,1)S(1)}, u32[]{:S(2)}, u32[]{:S(2)}) %collective-permute-start.9) | collective-permute-done | bytes 262176 | tf_op jit(solution)/shard_map/ppermute | solution.py:469
  30.1 0.4 collective-permute-start.25
  30.7 1.8 %collective-permute-start.24 = (bf16[128,512]{1,0:T(8,128)(2,1)S(1)}, bf16[128,512]{1,0:T(8,128)(2,1)S(1)}, u32[]{:S(2)}, u32[]{:S(2)}) collective-permute-start(bf16[128,512]{1,0:T(8,128)(2,1)S(1)} %constant_dynamic-slice_fusion.1), channel_id=1, source_target_pairs={{0,8},{4,12},{8,0},{12,4},{16,24},{20,28},{24,16},{28,20},{1,9},{5... | collective-permute-start | bytes 393224 | tf_op jit(solution)/shard_map/ppermute | solution.py:469
  32.5 3.4 %attend_back_kernel.1 = (f32[512,512]{1,0:T(8,128)S(1)}, bf16[128,512]{1,0:T(8,128)(2,1)S(1)}, bf16[128,512]{1,0:T(8,128)(2,1)S(1)}, bf16[128,512]{1,0:T(8,128)(...) custom-call(s32[32]{0:T(128)S(1)} %stack.143.refs_0_, ...), custom_call_target="tpu_custom_call" | custom-call | flops 1000000000 | tf_op jit(solution)/shard_map/attend_back_kernel/pallas_call | solution.py:173
  35.9 1.6 %collective-permute-start.11 = (bf16[128,512]{1,0:T(8,128)(2,1)S(1)}, bf16[128,512]{1,0:T(8,128)(2,1)S(1)}, u32[]{:S(2)}, u32[]{:S(2)}) collective-permute-start(bf16[128,512]{1,0:T(8,128)(2,1)S(1)} %get-tuple-element.129), channel_id=1, source_target_pairs={{0,4},{4,0},{8,12},{12,8},{16,20},{20,16},{24,28},{28,24},{1,5},{5... | collective-permute-start | bytes 393224 | tf_op jit(solution)/shard_map/ppermute | solution.py:469
  37.5 1.3 %collective-permute-start.12 = (bf16[128,512]{1,0:T(8,128)(2,1)S(1)}, bf16[128,512]{1,0:T(8,128)(2,1)S(1)}, u32[]{:S(2)}, u32[]{:S(2)}) collective-permute-start(bf16[128,512]{1,0:T(8,128)(2,1)S(1)} %get-tuple-element.130), channel_id=1, source_target_pairs={{0,8},{4,12},{8,0},{12,4},{16,24},{20,28},{24,16},{28,20},{1,9},{5... | collective-permute-start | bytes 393224 | tf_op jit(solution)/shard_map/ppermute | solution.py:469
  38.8 0.6 collective-permute-start.13
  39.5 0.5 collective-permute-start.19
  40.0 1.1 %collective-permute-start.18 = (bf16[16,512]{1,0:T(8,128)(2,1)S(1)}, bf16[16,512]{1,0:T(8,128)(2,1)S(1)}, u32[]{:S(2)}, u32[]{:S(2)}) collective-permute-start(bf16[16,512]{1,0:T(8,128)(2,1)S(1)} %get-tuple-element.142), channel_id=1, source_target_pairs={{0,2},{1,3},{2,0},{3,1},{4,6},{5,7},{6,4},{7,5},{8,10},{9,11},{10,... | collective-permute-start | bytes 49160 | tf_op jit(solution)/shard_map/ppermute | solution.py:469
  41.0 0.6 collective-permute-done.11
  41.6 2.2 %collective-permute-done.12 = bf16[128,512]{1,0:T(8,128)(2,1)S(1)} collective-permute-done((bf16[128,512]{1,0:T(8,128)(2,1)S(1)}, bf16[128,512]{1,0:T(8,128)(2,1)S(1)}, u32[]{:S(2)}, u32[]{:S(2)}) %collective-permute-start.12) | collective-permute-done | bytes 131104 | tf_op jit(solution)/shard_map/ppermute | solution.py:469
  43.9 1.7 %collective-permute-done.13 = bf16[128,512]{1,0:T(8,128)(2,1)S(1)} collective-permute-done((bf16[128,512]{1,0:T(8,128)(2,1)S(1)}, bf16[128,512]{1,0:T(8,128)(2,1)S(1)}, u32[]{:S(2)}, u32[]{:S(2)}) %collective-permute-start.13) | collective-permute-done | bytes 131104 | tf_op jit(solution)/shard_map/ppermute | solution.py:469
  45.7 1.4 %attend_out_kernel.1 = (bf16[512,512]{1,0:T(8,128)(2,1)S(1)}, bf16[512,512]{1,0:T(8,128)(2,1)S(1)}) custom-call(s32[32]{0:T(128)S(1)} %stack.143.refs_0_, bf16[128,512]{1,0:T(8,128)(2,1)S(1)} %add_convert_fusion.10.refs_1_, bf16[512,128]{1,0:T(8,128)(2,1)S(1)} %get-tuple-element.132.refs_2_, bf16[512,128]{1,0:T(8,128)(2,1)S(1)} %get-tuple-element.133.refs_3_, ...), custom_call_target="tpu_custom_call" | custom-call | flops 1000000000 | tf_op jit(solution)/shard_map/attend_out_kernel/pallas_call | solution.py:173
  47.3 2.6 %collective-permute-start.26 = (bf16[256,512]{1,0:T(8,128)(2,1)S(1)}, bf16[256,512]{1,0:T(8,128)(2,1)S(1)}, u32[]{:S(2)}, u32[]{:S(2)}) collective-permute-start(bf16[256,512]{1,0:T(8,128)(2,1)S(1)} %pad_maximum_fusion), channel_id=1, source_target_pairs={{0,16},{4,20},{8,24},{12,28},{16,0},{20,4},{24,8},{28,12},{1,17},{... | collective-permute-start | bytes 786440 | tf_op jit(solution)/shard_map/ppermute | solution.py:469
  50.0 0.1 add_convert_fusion.1
  50.2 1.6 %collective-permute-start.15 = (bf16[512,512]{1,0:T(8,128)(2,1)S(1)}, bf16[512,512]{1,0:T(8,128)(2,1)S(1)}, u32[]{:S(2)}, u32[]{:S(2)}) collective-permute-start(bf16[512,512]{1,0:T(8,128)(2,1)S(1)} %add_convert_fusion.1), channel_id=1, source_target_pairs={{0,2},{1,3},{2,0},{3,1},{4,6},{5,7},{6,4},{7,5},{8,10},{9,11},{10,... | collective-permute-start | bytes 1572872 | tf_op jit(solution)/shard_map/ppermute | solution.py:469
  51.7 1.1 %sums_kernel.1 = bf16[16,512]{1,0:T(8,128)(2,1)S(1)} custom-call(bf16[16,512]{1,0:T(8,128)(2,1)S(1)} %add_convert_fusion.11.refs_0_, f32[512,128]{1,0:T(8,128)S(1)} %get-tuple-element.143.refs_1_, f32[8,512]{1,0:T(8,128)S(1)} %get-tuple-element.144.refs_2_, s32[16,16]{1,0:T(8,128)S(1)} %get-tuple-element.145.refs_3_), custom_call_target="tpu_custom_call" | custom-call | flops 1000000000 | tf_op jit(solution)/shard_map/sums_kernel/pallas_call | solution.py:173
  52.8 9.7 %collective-permute-done.26 = bf16[256,512]{1,0:T(8,128)(2,1)S(1)} collective-permute-done((bf16[256,512]{1,0:T(8,128)(2,1)S(1)}, bf16[256,512]{1,0:T(8,128)(2,1)S(1)}, u32[]{:S(2)}, u32[]{:S(2)}) %collective-permute-start.26) | collective-permute-done | bytes 262176 | tf_op jit(solution)/shard_map/ppermute | solution.py:469
  62.7 1.6 %collective-permute-start.29 = (bf16[128,512]{1,0:T(8,128)(2,1)S(1)}, bf16[128,512]{1,0:T(8,128)(2,1)S(1)}, u32[]{:S(2)}, u32[]{:S(2)}) collective-permute-start(bf16[128,512]{1,0:T(8,128)(2,1)S(1)} %get-tuple-element.168), channel_id=1, source_target_pairs={{0,4},{4,0},{8,12},{12,8},{16,20},{20,16},{24,28},{28,24},{1,5},{5... | collective-permute-start | bytes 393224 | tf_op jit(solution)/shard_map/ppermute | solution.py:469
  64.3 0.5 collective-permute-start.27
  65.0 3.4 %collective-permute-start.20 = (bf16[160,512]{1,0:T(8,128)(2,1)S(1)}, bf16[160,512]{1,0:T(8,128)(2,1)S(1)}, u32[]{:S(2)}, u32[]{:S(2)}) collective-permute-start(bf16[160,512]{1,0:T(8,128)(2,1)S(1)} %pad_maximum_fusion.1), channel_id=1, source_target_pairs={{0,16},{4,20},{8,24},{12,28},{16,0},{20,4},{24,8},{28,12},{1,17},{... | collective-permute-start | bytes 491528 | tf_op jit(solution)/shard_map/ppermute | solution.py:469
  68.4 0.8 collective-permute-done.27
  69.3 0.6 collective-permute-start.28
  69.9 0.5 collective-permute-start.30
  70.5 6.4 %collective-permute-done.20 = bf16[160,512]{1,0:T(8,128)(2,1)S(1)} collective-permute-done((bf16[160,512]{1,0:T(8,128)(2,1)S(1)}, bf16[160,512]{1,0:T(8,128)(2,1)S(1)}, u32[]{:S(2)}, u32[]{:S(2)}) %collective-permute-start.20) | collective-permute-done | bytes 163872 | tf_op jit(solution)/shard_map/ppermute | solution.py:469
  77.0 2.0 %collective-permute-start.22 = (bf16[160,512]{1,0:T(8,128)(2,1)S(1)}, bf16[160,512]{1,0:T(8,128)(2,1)S(1)}, u32[]{:S(2)}, u32[]{:S(2)}) collective-permute-start(bf16[160,512]{1,0:T(8,128)(2,1)S(1)} %add_convert_fusion.7.refs_2_), channel_id=1, source_target_pairs={{0,8},{4,12},{8,0},{12,4},{16,24},{20,28},{24,16},{28,20},{1,9},{5... | collective-permute-start | bytes 491528 | tf_op jit(solution)/shard_map/ppermute | solution.py:469
  79.0 1.5 %collective-permute-start.21 = (bf16[160,512]{1,0:T(8,128)(2,1)S(1)}, bf16[160,512]{1,0:T(8,128)(2,1)S(1)}, u32[]{:S(2)}, u32[]{:S(2)}) collective-permute-start(bf16[160,512]{1,0:T(8,128)(2,1)S(1)} %add_convert_fusion.7.refs_2_), channel_id=1, source_target_pairs={{0,4},{4,0},{8,12},{12,8},{16,20},{20,16},{24,28},{28,24},{1,5},{5... | collective-permute-start | bytes 491528 | tf_op jit(solution)/shard_map/ppermute | solution.py:469
  80.5 2.6 %finish_kernel.1 = (f32[512,512]{1,0:T(8,128)}, f32[512,512]{1,0:T(8,128)}) custom-call(s32[32]{0:T(128)S(1)} %stack.143.refs_0_, bf16[512,512]{1,0:T(8,128)(2,1)S(1)} %add_convert_fusion.refs_1_, bf16[512,512]{1,0:T(8,128)(2,1)S(1)} %collective-permute-done.16.refs_2_, f32[512,512]{1,0:T(8,128)S(1)} %get-tuple-element.137.refs_3_, ...), custom_call_target="tpu_custom_call" | custom-call | flops 2000000000 | tf_op jit(solution)/shard_map/finish_kernel/pallas_call | solution.py:173
  83.1 1.9 %collective-permute-done.23.refs_5_ = bf16[160,512]{1,0:T(8,128)(2,1)S(1)} collective-permute-done((bf16[160,512]{1,0:T(8,128)(2,1)S(1)}, bf16[160,512]{1,0:T(8,128)(2,1)S(1)}, u32[]{:S(2)}, u32[]{:S(2)}) %collective-permute-start.23) | collective-permute-done | bytes 163872 | tf_op jit(solution)/shard_map/ppermute | solution.py:469
  85.0 1.9 %collective-permute-done.22.refs_4_ = bf16[160,512]{1,0:T(8,128)(2,1)S(1)} collective-permute-done((bf16[160,512]{1,0:T(8,128)(2,1)S(1)}, bf16[160,512]{1,0:T(8,128)(2,1)S(1)}, u32[]{:S(2)}, u32[]{:S(2)}) %collective-permute-start.22) | collective-permute-done | bytes 163872 | tf_op jit(solution)/shard_map/ppermute | solution.py:469
  86.9 0.7 collective-permute-done.21.refs_3_
  87.6 1.7 %unpack_kernel.1 = (f32[512,128]{1,0:T(8,128)}, f32[512,128]{1,0:T(8,128)}, f32[512,128]{1,0:T(8,128)}, f32[128,512]{1,0:T(8,128)}, f32[512]{0:T(512)}, /*index=...) custom-call(s32[32]{0:T(128)S(1)} %stack.143.refs_0_, ...), custom_call_target="tpu_custom_call" | custom-call | tf_op jit(solution)/shard_map/unpack_kernel/pallas_call | solution.py:173
  89.4 2.0 %widen_kernel.1 = (f32[512,512]{1,0:T(8,128)}, f32[512,512]{1,0:T(8,128)}) custom-call(s32[32]{0:T(128)S(1)} %stack.143.refs_0_, f32[512,128]{1,0:T(8,128)} %get-tuple-element.77.refs_1_, bf16[256,512]{1,0:T(8,128)(2,1)S(1)} %maximum_select_fusion.refs_2_, bf16[256,512]{1,0:T(8,128)(2,1)S(1)} %collective-permute-done.28.refs_3_, ...), custom_call_target="tpu_custom_call" | custom-call | tf_op jit(solution)/shard_map/widen_kernel/pallas_call | solution.py:173
  (46 shorter events, 1.6 us)
Async XLA Ops:
  0.7 8.6 %collective-permute-start.2 = (bf16[128,512]{1,0:T(8,128)(2,1)}, bf16[128,512]{1,0:T(8,128)(2,1)S(1)}, u32[]{:S(2)}, u32[]{:S(2)}) collective-permute-start(bf16[128,512]{1,0:T(8,128)(2,1)} %refs_9_.1), channel_id=1, source_target_pairs={{0,2},{1,3},{2,0},{3,1},{4,6},{5,7},{6,4},{7,5},{8,10},{9,11},{10,... | collective-permute-start | bytes 393224 | tf_op jit(solution)/shard_map/ppermute | solution.py:469
  3.8 4.9 %copy-start = (bf16[128,512]{1,0:T(8,128)(2,1)S(1)}, bf16[128,512]{1,0:T(8,128)(2,1)}, u32[]{:S(2)}) copy-start(bf16[128,512]{1,0:T(8,128)(2,1)} %refs_9_.1) | copy-start | bytes 393220
  8.6 5.0 %collective-permute-start.1 = (bf16[512,128]{1,0:T(8,128)(2,1)S(1)}, bf16[512,128]{1,0:T(8,128)(2,1)S(1)}, u32[]{:S(2)}, u32[]{:S(2)}) collective-permute-start(bf16[512,128]{1,0:T(8,128)(2,1)S(1)} %get-tuple-element.93.refs_0_.refs_1_.refs_12_), channel_id=1, source_target_pairs={{0,2},{1,3},{2,0},{3,1},{4,6},{5,7},{6,4},{7,5},{8,10},{9,11},{10,... | collective-permute-start | bytes 393224 | tf_op jit(solution)/shard_map/ppermute | solution.py:469
  8.7 5.4 %collective-permute-start.4 = (bf16[128,512]{1,0:T(8,128)(2,1)S(1)}, bf16[128,512]{1,0:T(8,128)(2,1)S(1)}, u32[]{:S(2)}, u32[]{:S(2)}) collective-permute-start(bf16[128,512]{1,0:T(8,128)(2,1)S(1)} %copy-done), channel_id=1, source_target_pairs={{0,1},{1,0},{2,3},{3,2},{4,5},{5,4},{6,7},{7,6},{8,9},{9,8},{10,11... | collective-permute-start | bytes 393224 | tf_op jit(solution)/shard_map/ppermute | solution.py:469
  8.8 5.4 %collective-permute-start = (bf16[512,128]{1,0:T(8,128)(2,1)S(1)}, bf16[512,128]{1,0:T(8,128)(2,1)S(1)}, u32[]{:S(2)}, u32[]{:S(2)}) collective-permute-start(bf16[512,128]{1,0:T(8,128)(2,1)S(1)} %get-tuple-element.93.refs_0_.refs_1_.refs_12_), channel_id=1, source_target_pairs={{0,1},{1,0},{2,3},{3,2},{4,5},{5,4},{6,7},{7,6},{8,9},{9,8},{10,11... | collective-permute-start | bytes 393224 | tf_op jit(solution)/shard_map/ppermute | solution.py:469
  13.6 1.3 %collective-permute-start.5 = (bf16[128,512]{1,0:T(8,128)(2,1)S(1)}, bf16[128,512]{1,0:T(8,128)(2,1)S(1)}, u32[]{:S(2)}, u32[]{:S(2)}) collective-permute-start(bf16[128,512]{1,0:T(8,128)(2,1)S(1)} %collective-permute-done.2.refs_1_.refs_7_), channel_id=1, source_target_pairs={{0,1},{1,0},{2,3},{3,2},{4,5},{5,4},{6,7},{7,6},{8,9},{9,8},{10,11... | collective-permute-start | bytes 393224 | tf_op jit(solution)/shard_map/ppermute | solution.py:469
  13.6 1.5 %collective-permute-start.3 = (bf16[512,128]{1,0:T(8,128)(2,1)S(1)}, bf16[512,128]{1,0:T(8,128)(2,1)S(1)}, u32[]{:S(2)}, u32[]{:S(2)}) collective-permute-start(bf16[512,128]{1,0:T(8,128)(2,1)S(1)} %collective-permute-done.1.refs_3_), channel_id=1, source_target_pairs={{0,1},{1,0},{2,3},{3,2},{4,5},{5,4},{6,7},{7,6},{8,9},{9,8},{10,11... | collective-permute-start | bytes 393224 | tf_op jit(solution)/shard_map/ppermute | solution.py:469
  18.1 1.8 %collective-permute-start.6 = (bf16[256,512]{1,0:T(8,128)(2,1)S(1)}, bf16[256,512]{1,0:T(8,128)(2,1)S(1)}, u32[]{:S(2)}, u32[]{:S(2)}) collective-permute-start(bf16[256,512]{1,0:T(8,128)(2,1)S(1)} %get-tuple-element.106), channel_id=1, source_target_pairs={{0,1},{1,0},{2,3},{3,2},{4,5},{5,4},{6,7},{7,6},{8,9},{9,8},{10,11... | collective-permute-start | bytes 786440 | tf_op jit(solution)/shard_map/ppermute | solution.py:469
  20.0 8.5 %collective-permute-start.7 = (bf16[256,512]{1,0:T(8,128)(2,1)S(1)}, bf16[256,512]{1,0:T(8,128)(2,1)S(1)}, u32[]{:S(2)}, u32[]{:S(2)}) collective-permute-start(bf16[256,512]{1,0:T(8,128)(2,1)S(1)} %add_convert_fusion.6), channel_id=1, source_target_pairs={{0,2},{1,3},{2,0},{3,1},{4,6},{5,7},{6,4},{7,5},{8,10},{9,11},{10,... | collective-permute-start | bytes 786440 | tf_op jit(solution)/shard_map/ppermute | solution.py:469
  20.4 8.2 %collective-permute-start.8 = (bf16[256,512]{1,0:T(8,128)(2,1)S(1)}, bf16[256,512]{1,0:T(8,128)(2,1)S(1)}, u32[]{:S(2)}, u32[]{:S(2)}) collective-permute-start(bf16[256,512]{1,0:T(8,128)(2,1)S(1)} %get-tuple-element.114), channel_id=1, source_target_pairs={{0,4},{4,0},{8,12},{12,8},{16,20},{20,16},{24,28},{28,24},{1,5},{5... | collective-permute-start | bytes 786440 | tf_op jit(solution)/shard_map/ppermute | solution.py:469
  22.1 7.8 %collective-permute-start.9 = (bf16[256,512]{1,0:T(8,128)(2,1)S(1)}, bf16[256,512]{1,0:T(8,128)(2,1)S(1)}, u32[]{:S(2)}, u32[]{:S(2)}) collective-permute-start(bf16[256,512]{1,0:T(8,128)(2,1)S(1)} %get-tuple-element.115), channel_id=1, source_target_pairs={{0,8},{4,12},{8,0},{12,4},{16,24},{20,28},{24,16},{28,20},{1,9},{5... | collective-permute-start | bytes 786440 | tf_op jit(solution)/shard_map/ppermute | solution.py:469
  30.1 9.4 %collective-permute-start.25 = (bf16[128,512]{1,0:T(8,128)(2,1)S(1)}, bf16[128,512]{1,0:T(8,128)(2,1)S(1)}, u32[]{:S(2)}, u32[]{:S(2)}) collective-permute-start(bf16[128,512]{1,0:T(8,128)(2,1)S(1)} %constant_dynamic-slice_fusion), channel_id=1, source_target_pairs={{0,4},{4,0},{8,12},{12,8},{16,20},{20,16},{24,28},{28,24},{1,5},{5... | collective-permute-start | bytes 393224 | tf_op jit(solution)/shard_map/ppermute | solution.py:469
  30.5 1.9 %collective-permute-start.10 = (bf16[256,512]{1,0:T(8,128)(2,1)S(1)}, bf16[256,512]{1,0:T(8,128)(2,1)S(1)}, u32[]{:S(2)}, u32[]{:S(2)}) collective-permute-start(bf16[256,512]{1,0:T(8,128)(2,1)S(1)} %add_convert_fusion.5.refs_1_), channel_id=1, source_target_pairs={{0,1},{1,0},{2,3},{3,2},{4,5},{5,4},{6,7},{7,6},{8,9},{9,8},{10,11... | collective-permute-start | bytes 786440 | tf_op jit(solution)/shard_map/ppermute | solution.py:469
  30.7 9.3 %collective-permute-start.24 = (bf16[128,512]{1,0:T(8,128)(2,1)S(1)}, bf16[128,512]{1,0:T(8,128)(2,1)S(1)}, u32[]{:S(2)}, u32[]{:S(2)}) collective-permute-start(bf16[128,512]{1,0:T(8,128)(2,1)S(1)} %constant_dynamic-slice_fusion.1), channel_id=1, source_target_pairs={{0,8},{4,12},{8,0},{12,4},{16,24},{20,28},{24,16},{28,20},{1,9},{5... | collective-permute-start | bytes 393224 | tf_op jit(solution)/shard_map/ppermute | solution.py:469
  35.9 5.7 %collective-permute-start.11 = (bf16[128,512]{1,0:T(8,128)(2,1)S(1)}, bf16[128,512]{1,0:T(8,128)(2,1)S(1)}, u32[]{:S(2)}, u32[]{:S(2)}) collective-permute-start(bf16[128,512]{1,0:T(8,128)(2,1)S(1)} %get-tuple-element.129), channel_id=1, source_target_pairs={{0,4},{4,0},{8,12},{12,8},{16,20},{20,16},{24,28},{28,24},{1,5},{5... | collective-permute-start | bytes 393224 | tf_op jit(solution)/shard_map/ppermute | solution.py:469
  37.5 6.4 %collective-permute-start.12 = (bf16[128,512]{1,0:T(8,128)(2,1)S(1)}, bf16[128,512]{1,0:T(8,128)(2,1)S(1)}, u32[]{:S(2)}, u32[]{:S(2)}) collective-permute-start(bf16[128,512]{1,0:T(8,128)(2,1)S(1)} %get-tuple-element.130), channel_id=1, source_target_pairs={{0,8},{4,12},{8,0},{12,4},{16,24},{20,28},{24,16},{28,20},{1,9},{5... | collective-permute-start | bytes 393224 | tf_op jit(solution)/shard_map/ppermute | solution.py:469
  38.8 6.8 %collective-permute-start.13 = (bf16[128,512]{1,0:T(8,128)(2,1)S(1)}, bf16[128,512]{1,0:T(8,128)(2,1)S(1)}, u32[]{:S(2)}, u32[]{:S(2)}) collective-permute-start(bf16[128,512]{1,0:T(8,128)(2,1)S(1)} %get-tuple-element.131), channel_id=1, source_target_pairs={{0,12},{4,8},{8,4},{12,0},{16,28},{20,24},{24,20},{28,16},{1,13},{... | collective-permute-start | bytes 393224 | tf_op jit(solution)/shard_map/ppermute | solution.py:469
  39.5 10.5 %collective-permute-start.19 = (bf16[16,512]{1,0:T(8,128)(2,1)S(1)}, bf16[16,512]{1,0:T(8,128)(2,1)S(1)}, u32[]{:S(2)}, u32[]{:S(2)}) collective-permute-start(bf16[16,512]{1,0:T(8,128)(2,1)S(1)} %get-tuple-element.142), channel_id=1, source_target_pairs={{0,3},{1,2},{2,1},{3,0},{4,7},{5,6},{6,5},{7,4},{8,11},{9,10},{10,... | collective-permute-start | bytes 49160 | tf_op jit(solution)/shard_map/ppermute | solution.py:469
  40.0 10.0 %collective-permute-start.18 = (bf16[16,512]{1,0:T(8,128)(2,1)S(1)}, bf16[16,512]{1,0:T(8,128)(2,1)S(1)}, u32[]{:S(2)}, u32[]{:S(2)}) collective-permute-start(bf16[16,512]{1,0:T(8,128)(2,1)S(1)} %get-tuple-element.142), channel_id=1, source_target_pairs={{0,2},{1,3},{2,0},{3,1},{4,6},{5,7},{6,4},{7,5},{8,10},{9,11},{10,... | collective-permute-start | bytes 49160 | tf_op jit(solution)/shard_map/ppermute | solution.py:469
  41.6 8.3 %collective-permute-start.17 = (bf16[16,512]{1,0:T(8,128)(2,1)S(1)}, bf16[16,512]{1,0:T(8,128)(2,1)S(1)}, u32[]{:S(2)}, u32[]{:S(2)}) collective-permute-start(bf16[16,512]{1,0:T(8,128)(2,1)S(1)} %get-tuple-element.142), channel_id=1, source_target_pairs={{0,1},{1,0},{2,3},{3,2},{4,5},{5,4},{6,7},{7,6},{8,9},{9,8},{10,11... | collective-permute-start | bytes 49160 | tf_op jit(solution)/shard_map/ppermute | solution.py:469
  47.1 2.9 %collective-permute-start.14 = (bf16[512,512]{1,0:T(8,128)(2,1)S(1)}, bf16[512,512]{1,0:T(8,128)(2,1)S(1)}, u32[]{:S(2)}, u32[]{:S(2)}) collective-permute-start(bf16[512,512]{1,0:T(8,128)(2,1)S(1)} %get-tuple-element.136), channel_id=1, source_target_pairs={{0,1},{1,0},{2,3},{3,2},{4,5},{5,4},{6,7},{7,6},{8,9},{9,8},{10,11... | collective-permute-start | bytes 1572872 | tf_op jit(solution)/shard_map/ppermute | solution.py:469
  47.3 15.3 %collective-permute-start.26 = (bf16[256,512]{1,0:T(8,128)(2,1)S(1)}, bf16[256,512]{1,0:T(8,128)(2,1)S(1)}, u32[]{:S(2)}, u32[]{:S(2)}) collective-permute-start(bf16[256,512]{1,0:T(8,128)(2,1)S(1)} %pad_maximum_fusion), channel_id=1, source_target_pairs={{0,16},{4,20},{8,24},{12,28},{16,0},{20,4},{24,8},{28,12},{1,17},{... | collective-permute-start | bytes 786440 | tf_op jit(solution)/shard_map/ppermute | solution.py:469
  50.2 14.6 %collective-permute-start.15 = (bf16[512,512]{1,0:T(8,128)(2,1)S(1)}, bf16[512,512]{1,0:T(8,128)(2,1)S(1)}, u32[]{:S(2)}, u32[]{:S(2)}) collective-permute-start(bf16[512,512]{1,0:T(8,128)(2,1)S(1)} %add_convert_fusion.1), channel_id=1, source_target_pairs={{0,2},{1,3},{2,0},{3,1},{4,6},{5,7},{6,4},{7,5},{8,10},{9,11},{10,... | collective-permute-start | bytes 1572872 | tf_op jit(solution)/shard_map/ppermute | solution.py:469
  62.7 7.2 %collective-permute-start.29 = (bf16[128,512]{1,0:T(8,128)(2,1)S(1)}, bf16[128,512]{1,0:T(8,128)(2,1)S(1)}, u32[]{:S(2)}, u32[]{:S(2)}) collective-permute-start(bf16[128,512]{1,0:T(8,128)(2,1)S(1)} %get-tuple-element.168), channel_id=1, source_target_pairs={{0,4},{4,0},{8,12},{12,8},{16,20},{20,16},{24,28},{28,24},{1,5},{5... | collective-permute-start | bytes 393224 | tf_op jit(solution)/shard_map/ppermute | solution.py:469
  64.3 5.0 %collective-permute-start.27 = (bf16[128,512]{1,0:T(8,128)(2,1)S(1)}, bf16[128,512]{1,0:T(8,128)(2,1)S(1)}, u32[]{:S(2)}, u32[]{:S(2)}) collective-permute-start(bf16[128,512]{1,0:T(8,128)(2,1)S(1)} %get-tuple-element.169), channel_id=1, source_target_pairs={{0,8},{4,12},{8,0},{12,4},{16,24},{20,28},{24,16},{28,20},{1,9},{5... | collective-permute-start | bytes 393224 | tf_op jit(solution)/shard_map/ppermute | solution.py:469
  64.9 14.1 %collective-permute-start.16 = (bf16[512,512]{1,0:T(8,128)(2,1)S(1)}, bf16[512,512]{1,0:T(8,128)(2,1)S(1)}, u32[]{:S(2)}, u32[]{:S(2)}) collective-permute-start(bf16[512,512]{1,0:T(8,128)(2,1)S(1)} %add_convert_fusion.refs_1_), channel_id=1, source_target_pairs={{0,1},{1,0},{2,3},{3,2},{4,5},{5,4},{6,7},{7,6},{8,9},{9,8},{10,11... | collective-permute-start | bytes 1572872 | tf_op jit(solution)/shard_map/ppermute | solution.py:469
  65.0 11.9 %collective-permute-start.20 = (bf16[160,512]{1,0:T(8,128)(2,1)S(1)}, bf16[160,512]{1,0:T(8,128)(2,1)S(1)}, u32[]{:S(2)}, u32[]{:S(2)}) collective-permute-start(bf16[160,512]{1,0:T(8,128)(2,1)S(1)} %pad_maximum_fusion.1), channel_id=1, source_target_pairs={{0,16},{4,20},{8,24},{12,28},{16,0},{20,4},{24,8},{28,12},{1,17},{... | collective-permute-start | bytes 491528 | tf_op jit(solution)/shard_map/ppermute | solution.py:469
  69.3 20.0 %collective-permute-start.28 = (bf16[256,512]{1,0:T(8,128)(2,1)S(1)}, bf16[256,512]{1,0:T(8,128)(2,1)S(1)}, u32[]{:S(2)}, u32[]{:S(2)}) collective-permute-start(bf16[256,512]{1,0:T(8,128)(2,1)S(1)} %maximum_select_fusion.refs_2_), channel_id=1, source_target_pairs={{0,4},{4,0},{8,12},{12,8},{16,20},{20,16},{24,28},{28,24},{1,5},{5... | collective-permute-start | bytes 786440 | tf_op jit(solution)/shard_map/ppermute | solution.py:469
  69.9 19.4 %collective-permute-start.30 = (bf16[256,512]{1,0:T(8,128)(2,1)S(1)}, bf16[256,512]{1,0:T(8,128)(2,1)S(1)}, u32[]{:S(2)}, u32[]{:S(2)}) collective-permute-start(bf16[256,512]{1,0:T(8,128)(2,1)S(1)} %maximum_select_fusion.1.refs_4_), channel_id=1, source_target_pairs={{0,8},{4,12},{8,0},{12,4},{16,24},{20,28},{24,16},{28,20},{1,9},{5... | collective-permute-start | bytes 786440 | tf_op jit(solution)/shard_map/ppermute | solution.py:469
  76.9 8.1 %collective-permute-start.23 = (bf16[160,512]{1,0:T(8,128)(2,1)S(1)}, bf16[160,512]{1,0:T(8,128)(2,1)S(1)}, u32[]{:S(2)}, u32[]{:S(2)}) collective-permute-start(bf16[160,512]{1,0:T(8,128)(2,1)S(1)} %add_convert_fusion.7.refs_2_), channel_id=1, source_target_pairs={{0,12},{4,8},{8,4},{12,0},{16,28},{20,24},{24,20},{28,16},{1,13},{... | collective-permute-start | bytes 491528 | tf_op jit(solution)/shard_map/ppermute | solution.py:469
  77.0 9.9 %collective-permute-start.22 = (bf16[160,512]{1,0:T(8,128)(2,1)S(1)}, bf16[160,512]{1,0:T(8,128)(2,1)S(1)}, u32[]{:S(2)}, u32[]{:S(2)}) collective-permute-start(bf16[160,512]{1,0:T(8,128)(2,1)S(1)} %add_convert_fusion.7.refs_2_), channel_id=1, source_target_pairs={{0,8},{4,12},{8,0},{12,4},{16,24},{20,28},{24,16},{28,20},{1,9},{5... | collective-permute-start | bytes 491528 | tf_op jit(solution)/shard_map/ppermute | solution.py:469
  79.0 8.6 %collective-permute-start.21 = (bf16[160,512]{1,0:T(8,128)(2,1)S(1)}, bf16[160,512]{1,0:T(8,128)(2,1)S(1)}, u32[]{:S(2)}, u32[]{:S(2)}) collective-permute-start(bf16[160,512]{1,0:T(8,128)(2,1)S(1)} %add_convert_fusion.7.refs_2_), channel_id=1, source_target_pairs={{0,4},{4,0},{8,12},{12,8},{16,20},{20,16},{24,28},{28,24},{1,5},{5... | collective-permute-start | bytes 491528 | tf_op jit(solution)/shard_map/ppermute | solution.py:469

commit v4 on v3

--- a/solution.py
+++ b/solution.py
@@ -374,15 +374,19 @@
     sums[2:3, :] = proj_sum
 
 
-def attend_out_kernel(spot, after, gq, gk, gv, wq, wk, wv, hidden, w2, keep, send):
-    half = hidden.shape[0] // 2
+def attend_out_kernel(spot, after, also, gq, gk, gv, wq, wk, wv, keep, send):
+    half = gq.shape[0] // 2
     for where, ref in zip(halves(spot[0] % 2, half), (keep, send)):
-        ref[0:half, :] = (
+        ref[...] = (
             dot_nt(gq[where, :], wq[...])
             + dot_nt(gk[where, :], wk[...])
             + dot_nt(gv[where, :], wv[...])
         ).astype(BF)
-        ref[half:, :] = dot(hidden[where, :], w2[...]).astype(BF)
+
+
+def mlp_out_kernel(spot, hidden, w2, keep, send):
+    for where, ref in zip(halves(spot[0] % 2, hidden.shape[0] // 2), (keep, send)):
+        ref[...] = dot(hidden[where, :], w2[...]).astype(BF)
 
 
 def sums_kernel(after, scores, sums, pidx, small, all_sums):
@@ -417,20 +421,21 @@
     small[...] = all_sums[...].astype(BF)
 
 
-def finish_kernel(spot, s4, r4, gmid, x, g1, mid, b2, layer_out, input_grad):
+def finish_kernel(spot, s4, r4, s2, r2, gmid, x, g1, mid, b2, layer_out, input_grad):
     core = spot[0] % 2
     half = x.shape[0] // 2
-    for part, ref in enumerate((s4, r4)):
+    for part, (ref, out) in enumerate(((s4, s2), (r4, r2))):
         start = core if part == 0 else 1 - core
         where = pl.ds(pl.multiple_of(start * half, half), half)
         normed, inverse = normalize(x[where, :].astype(F32))
-        grad = ref[0:half, :].astype(F32)
+        grad = ref[...].astype(F32)
         input_grad[where, :] = gmid[where, :] + norm_back(grad, normed, inverse, row(g1))
-        mlp = ref[half:, :].astype(F32)
+        mlp = out[...].astype(F32)
         layer_out[where, :] = mid[where, :] + mlp + row(b2)
 
 
-def widen_kernel(spot, after, near1, far1, near2, far2, w1, w2):
+def widen_kernel(spot, after, near1, far1, near2, far2, *others):
+    w1, w2 = others[-2:]
     part = near1.shape[0]
     for flag, near, far, ref in ((spot[2], near1, far1, w1), (spot[3], near2, far2, w2)):
         mine, other = halves(flag, part)
@@ -596,11 +601,19 @@
     come3 = swap(send3, "tensor", 1, tensor)
     come3, small_a, away1, away2 = lax.optimization_barrier((come3, small_a, away1, away2))
     pair3 = fold(keep3, come3)
-    come3, come_a, come_b = lax.optimization_barrier(
+    keep2, send2 = call(
+        mlp_out_kernel,
+        [((half, width), BF, "vmem"), ((half, width), BF, "vmem")],
+        [(spot, "smem"), (hidden, "vmem"), (down_weight, "vmem")],
+        cost=1,
+    )
+    come3, come_a, come_b, keep2, send2 = lax.optimization_barrier(
         (
             swap(pair3, "tensor", 2, tensor),
             swap(away1, "dp", bits[0], dp),
             swap(away2, "dp", bits[1], dp),
+            keep2,
+            send2,
         )
     )
     sum3 = fold(pair3, come3)
@@ -636,6 +649,50 @@
         scratch=[(wide, F32), (wide, BF), (narrow, BF), ((4 * span, width), BF)],
         cost=1,
     )
+    left = jnp.uint32(0)
+
+    def pick(value, i):
+        part = value.shape[0] // 2
+        return (
+            lax.dynamic_slice(value, (starts[i, part], left), (part, width)),
+            lax.dynamic_slice(value, (stops[i, part], left), (part, width)),
+        )
+
+    def settle(value, times):
+        for _ in range(times):
+            mark = swap(value, "tensor", 1, tensor)
+            value, mark = lax.optimization_barrier((value, mark))
+            marks.append(mark)
+        return value
+
+    marks = []
+
+    def scatter(value, i):
+        own, away = pick(value, i)
+        return fold(own, swap(away, "dp", bits[i], dp))
+
+    def gather(own, i):
+        other = swap(own, "dp", bits[i], dp)
+        return jnp.where(
+            lower[i], jnp.concatenate([own, other]), jnp.concatenate([other, own])
+        )
+
+    more = range(2, len(bits))
+
+    keep_a, away_a = pick(fold(own1, come_a), 1)
+    keep_b, away_b = pick(fold(own2, come_b), 0)
+    (
+        come_a, come_b, att_own, att_y, att_z, att_yz, gq, gk, gv, scores, sums, norm1,
+    ) = lax.optimization_barrier(
+        (
+            swap(away_a, "dp", bits[1], dp), swap(away_b, "dp", bits[0], dp), att_own, att_y,
+            att_z, att_yz, gq, gk, gv, scores, sums, norm1,
+        )
+    )
+    mlp_chunk = jnp.concatenate([fold(keep_a, come_a), fold(keep_b, come_b)])
+    pair2 = fold(keep2, swap(send2, "tensor", 1, tensor))
+    sum2 = fold(pair2, swap(pair2, "tensor", 2, tensor))
+    rest2 = swap(sum2, "tensor", 1, tensor)
     att_parts = meet(att_own, att_y, att_z, att_yz)
     chunk = combine(att_parts)
     across = [swap(norm1, "tensor", flip, tensor).astype(F32) for flip in (1, 2, 3)]
@@ -643,17 +700,16 @@
     (small_b,) = call(
         sums_kernel,
         [((16, width), BF, "vmem")],
-        [(norm1, "vmem"), (scores, "vmem"), (sums, "vmem"), (position_index, "vmem")],
+        [(att_own, "vmem"), (scores, "vmem"), (sums, "vmem"), (position_index, "vmem")],
         scratch=[((16, width), F32)],
         cost=1,
     )
     keep4, send4 = call(
         attend_out_kernel,
-        [((tokens, width), BF, "vmem"), ((tokens, width), BF, "vmem")],
-        [
-            (spot, "smem"), (chunk, "vmem"), (gq, "vmem"), (gk, "vmem"), (gv, "vmem"),
+        [((half, width), BF, "vmem"), ((half, width), BF, "vmem")],
+        [
+            (spot, "smem"), (chunk, "vmem"), (sum2, "vmem"), (gq, "vmem"), (gk, "vmem"), (gv, "vmem"),
             (query_weight, "vmem"), (key_weight, "vmem"), (value_weight, "vmem"),
-            (hidden, "vmem"), (down_weight, "vmem"),
         ],
         cost=1,
     )
@@ -662,38 +718,13 @@
     sum4 = fold(pair4, swap(pair4, "tensor", 2, tensor))
     rest4 = swap(sum4, "tensor", 1, tensor)
 
-    left = jnp.uint32(0)
-
-    def pick(value, i):
-        part = value.shape[0] // 2
-        return (
-            lax.dynamic_slice(value, (starts[i, part], left), (part, width)),
-            lax.dynamic_slice(value, (stops[i, part], left), (part, width)),
-        )
-
-    def scatter(value, i):
-        own, away = pick(value, i)
-        return fold(own, swap(away, "dp", bits[i], dp))
-
-    def gather(own, i):
-        other = swap(own, "dp", bits[i], dp)
-        return jnp.where(
-            lower[i], jnp.concatenate([own, other]), jnp.concatenate([other, own])
-        )
-
-    more = range(2, len(bits))
-
-    keep_a, away_a = pick(fold(own1, come_a), 1)
-    keep_b, away_b = pick(fold(own2, come_b), 0)
-    come_a, come_b, gq = lax.optimization_barrier(
-        (swap(away_a, "dp", bits[1], dp), swap(away_b, "dp", bits[0], dp), gq)
-    )
-    mlp_chunk = jnp.concatenate([fold(keep_a, come_a), fold(keep_b, come_b)])
     for i in more:
         mlp_chunk = fold(mlp_chunk, swap(mlp_chunk, "dp", bits[i], dp))
+    mlp_chunk = settle(mlp_chunk, 0)
     chunk = jnp.concatenate([chunk, small_a, small_b, norm1[:8]])
     for i in more:
         chunk = fold(chunk, swap(chunk, "dp", bits[i], dp))
+    chunk = settle(chunk, 1)
     chunks = meet(chunk, chunk, chunk, chunk)
     near1 = gather(mlp_chunk[:mlp_chunk.shape[0] // 2], 1)
     near2 = gather(mlp_chunk[mlp_chunk.shape[0] // 2:], 0)
@@ -703,10 +734,16 @@
         finish_kernel,
         [(wide, F32, "hbm"), (wide, F32, "hbm")],
         [
-            (spot, "smem"), (sum4, "vmem"), (rest4, "vmem"), (gmid, "vmem"), (inputs, "vmem"),
+            (spot, "smem"), (sum4, "vmem"), (rest4, "vmem"), (sum2, "vmem"), (rest2, "vmem"), (gmid, "vmem"), (inputs, "vmem"),
             (norm1_gain, "vmem"), (mid, "vmem"), (down_bias, "vmem"),
         ],
         cost=2,
+    )
+    w1_total, w2_total = call(
+        widen_kernel,
+        [((width, units), F32, "hbm"), ((units, width), F32, "hbm")],
+        [(spot, "smem"), (layer_out, "keep")]
+        + [(value, "vmem") for value in [near1, far1, near2, far2] + marks],
     )
     vector, short = ((width,), F32, "hbm"), ((span,), F32, "hbm")
     (
@@ -719,16 +756,10 @@
             ((span, width), F32, "hbm"), vector, vector, vector, vector, vector, short, short,
             ((heads, position_bias.shape[0]), F32, "hbm"), vector, vector,
         ],
-        [(spot, "smem"), (layer_out, "keep")] + [(value, "vmem") for value in chunks],
+        [(spot, "smem"), (w1_total, "keep")] + [(value, "vmem") for value in chunks],
         scratch=[((4, span, width), BF)],
     )
     rel_total = rel_total.T
-    w1_total, w2_total = call(
-        widen_kernel,
-        [((width, units), F32, "hbm"), ((units, width), F32, "hbm")],
-        [(spot, "smem"), (wq_total, "keep")]
-        + [(value, "vmem") for value in (near1, far1, near2, far2)],
-    )
 
     return (
         layer_out,

time: 91.5 us -> 85.9 us (0.939)
  waiting for transfers between devices: 35.3 us -> 24.5 us
  starting transfers between devices: 30.1 us -> 34.6 us
    ppermute x31 -> x35, waiting for transfers between devices: 35.3 us -> 24.5 us  [swap(): return lax.ppermute(value, axis, [(i, i ^ bit) for i in range(size)])]
    ppermute x31 -> x35, starting transfers between devices: 30.1 us -> 34.6 us  [swap(): return lax.ppermute(value, axis, [(i, i ^ bit) for i in range(size)])]
    pallas_call x10 -> x11, Pallas kernels: 23.8 us -> 24.5 us  [call(): pl.pallas_call(body, name=kernel.__name__, out_shape=pinned, in_specs=[pl...]
  transfers between devices with their start and end apart: 31 -> 35, of which waited for: 15 -> 16; matrix products, arithmetic and copies ran while one was open for 1% -> 1% of each run, Pallas kernels for 21% -> 23%
where the time goes in v4:
time: 85.9 us; the launch traced here: 85.7 us
  starting transfers between devices  34.6 us (40%)
  Pallas kernels  24.5 us (29%)
  waiting for transfers between devices  24.5 us (29%)
  other arithmetic  0.99 us (1%)
  between operations  0.93 us (1%)
    ppermute x35, starting transfers between devices, swap(): return lax.ppermute(value, axis, [(i, i ^ bit) for i in range(size)])  34.6 us
    pallas_call x11, Pallas kernels, call(): pl.pallas_call(body, name=kernel.__name__, out_shape=pinned, in_specs=[pl...  24.5 us
    ppermute x35, waiting for transfers between devices, swap(): return lax.ppermute(value, axis, [(i, i ^ bit) for i in range(size)])  24.5 us
  transfers between devices with their start and end apart: 35, of which 16 were waited for; matrix products, arithmetic and copies ran while one was open for 1% of the time, Pallas kernels for 23%

profile of v4, /device:TPU:0, one launch (start us, length us, event | category | flops | bytes accessed | tf_op | source)
XLA Modules:
  0.0 85.7 jit_solution(11249083717310107100)
XLA Ops:
  0.7 3.0 %collective-permute-start.2 = (bf16[128,512]{1,0:T(8,128)(2,1)}, bf16[128,512]{1,0:T(8,128)(2,1)S(1)}, u32[]{:S(2)}, u32[]{:S(2)}) collective-permute-start(bf16[128,512]{1,0:T(8,128)(2,1)} %refs_9_.1), channel_id=1, source_target_pairs={{0,2},{1,3},{2,0},{3,1},{4,6},{5,7},{6,4},{7,5},{8,10},{9,11},{10,... | collective-permute-start | bytes 393224 | tf_op jit(solution)/shard_map/ppermute | solution.py:474
  3.8 4.8 %attend_kernel.1 = (bf16[512,128]{1,0:T(8,128)(2,1)S(1)}, bf16[512,512]{1,0:T(8,128)(2,1)S(1)}, bf16[512,128]{1,0:T(8,128)(2,1)S(1)}, bf16[512,128]{1,0:T(8,128)...) custom-call(s32[32]{0:T(128)S(1)} %stack.143.refs_0_, bf16[512,512]{1,0:T(8,128)(2,1)} %refs_2_.3, ...), custom_call_target="tpu_custom_call" | custom-call | flops 20000000000 | tf_op jit(solution)/shard_map/attend_kernel/pallas_call | solution.py:173
  8.8 0.5 collective-permute-start
  9.3 2.5 %fetch_kernel.1 = (f32[8,128]{1,0:T(8,128)}, bf16[512,512]{1,0:T(8,128)(2,1)S(1)}, f32[512]{0:T(512)S(1)}, f32[512]{0:T(512)S(1)}, s32[16,16]{1,0:T(8,128)S(1)},...) custom-call(bf16[512,128]{1,0:T(8,128)(2,1)S(1)} %get-tuple-element., ...), custom_call_target="tpu_custom_call" | custom-call | tf_op jit(solution)/shard_map/fetch_kernel/pallas_call | solution.py:173
  11.7 1.9 %collective-permute-done.1.refs_3_ = bf16[512,128]{1,0:T(8,128)(2,1)S(1)} collective-permute-done((bf16[512,128]{1,0:T(8,128)(2,1)S(1)}, bf16[512,128]{1,0:T(8,128)(2,1)S(1)}, u32[]{:S(2)}, u32[]{:S(2)}) %collective-permute-start.1) | collective-permute-done | bytes 131104 | tf_op jit(solution)/shard_map/ppermute | solution.py:474
  13.6 0.5 collective-permute-start.3
  14.1 0.8 collective-permute-done.5.refs_8_
  15.2 2.9 %mlp_kernel.1 = (f32[512,512]{1,0:T(8,128)S(1)}, bf16[512,512]{1,0:T(8,128)(2,1)S(1)}, bf16[512,512]{1,0:T(8,128)(2,1)S(1)}, bf16[512,512]{1,0:T(8,128)(2,1)S(1)...) custom-call(s32[32]{0:T(128)S(1)} %stack.143.refs_0_, ...), custom_call_target="tpu_custom_call" | custom-call | flops 2000000000 | tf_op jit(solution)/shard_map/mlp_kernel/pallas_call | solution.py:173
  18.5 1.4 %mlp_grad_kernel.1 = (bf16[256,512]{1,0:T(8,128)(2,1)S(1)}, bf16[256,512]{1,0:T(8,128)(2,1)S(1)}, bf16[256,512]{1,0:T(8,128)(2,1)S(1)}, bf16[256,512]{1,0:T(8,128)(2,1)S(1)}, bf16[8,512]{1,0:T(8,128)(2,1)S(1)}) custom-call(s32[32]{0:T(128)S(1)} %stack.143.refs_0_, bf16[512,512]{1,0:T(8,128)(2,1)S(1)} %get-tuple-element.121.refs_1_, ...), custom_call_target="tpu_custom_call" | custom-call | flops 2000000000 | tf_op jit(solution)/shard_map/mlp_grad_kernel/pallas_call | solution.py:173
  20.0 0.4 collective-permute-start.7
  20.4 1.7 %collective-permute-start.8 = (bf16[256,512]{1,0:T(8,128)(2,1)S(1)}, bf16[256,512]{1,0:T(8,128)(2,1)S(1)}, u32[]{:S(2)}, u32[]{:S(2)}) collective-permute-start(bf16[256,512]{1,0:T(8,128)(2,1)S(1)} %get-tuple-element.131), channel_id=1, source_target_pairs={{0,4},{4,0},{8,12},{12,8},{16,20},{20,16},{24,28},{28,24},{1,5},{5... | collective-permute-start | bytes 786440 | tf_op jit(solution)/shard_map/ppermute | solution.py:474
  22.1 1.6 %collective-permute-start.9 = (bf16[256,512]{1,0:T(8,128)(2,1)S(1)}, bf16[256,512]{1,0:T(8,128)(2,1)S(1)}, u32[]{:S(2)}, u32[]{:S(2)}) collective-permute-start(bf16[256,512]{1,0:T(8,128)(2,1)S(1)} %get-tuple-element.132), channel_id=1, source_target_pairs={{0,8},{4,12},{8,0},{12,4},{16,24},{20,28},{24,16},{28,20},{1,9},{5... | collective-permute-start | bytes 786440 | tf_op jit(solution)/shard_map/ppermute | solution.py:474
  23.7 1.0 %mlp_out_kernel.1 = (bf16[256,512]{1,0:T(8,128)(2,1)S(1)}, bf16[256,512]{1,0:T(8,128)(2,1)S(1)}) custom-call(s32[32]{0:T(128)S(1)} %stack.143.refs_0_, bf16[512,512]{1,0:T(8,128)(2,1)S(1)} %get-tuple-element.122.refs_2_.refs_1_, bf16[512,512]{1,0:T(8,128)(2,1)S(1)} %get-tuple-element.120.refs_16_.refs_2_), custom_call_target="tpu_custom_call" | custom-call | flops 1000000000 | tf_op jit(solution)/shard_map/mlp_out_kernel/pallas_call | solution.py:173
  24.6 3.8 %collective-permute-done.7 = bf16[256,512]{1,0:T(8,128)(2,1)S(1)} collective-permute-done((bf16[256,512]{1,0:T(8,128)(2,1)S(1)}, bf16[256,512]{1,0:T(8,128)(2,1)S(1)}, u32[]{:S(2)}, u32[]{:S(2)}) %collective-permute-start.7) | collective-permute-done | bytes 262176 | tf_op jit(solution)/shard_map/ppermute | solution.py:474
  28.5 1.4 %collective-permute-done.9 = bf16[256,512]{1,0:T(8,128)(2,1)S(1)} collective-permute-done((bf16[256,512]{1,0:T(8,128)(2,1)S(1)}, bf16[256,512]{1,0:T(8,128)(2,1)S(1)}, u32[]{:S(2)}, u32[]{:S(2)}) %collective-permute-start.9) | collective-permute-done | bytes 262176 | tf_op jit(solution)/shard_map/ppermute | solution.py:474
  30.3 1.7 %collective-permute-start.10 = (bf16[128,512]{1,0:T(8,128)(2,1)S(1)}, bf16[128,512]{1,0:T(8,128)(2,1)S(1)}, u32[]{:S(2)}, u32[]{:S(2)}) collective-permute-start(bf16[128,512]{1,0:T(8,128)(2,1)S(1)} %constant_dynamic-slice_fusion.1), channel_id=1, source_target_pairs={{0,8},{4,12},{8,0},{12,4},{16,24},{20,28},{24,16},{28,20},{1,9},{5... | collective-permute-start | bytes 393224 | tf_op jit(solution)/shard_map/ppermute | solution.py:474
  32.0 0.5 collective-permute-start.11
  32.5 3.5 %attend_back_kernel.1 = (f32[512,512]{1,0:T(8,128)S(1)}, bf16[128,512]{1,0:T(8,128)(2,1)S(1)}, bf16[128,512]{1,0:T(8,128)(2,1)S(1)}, bf16[128,512]{1,0:T(8,128)(...) custom-call(s32[32]{0:T(128)S(1)} %stack.143.refs_0_, ...), custom_call_target="tpu_custom_call" | custom-call | flops 1000000000 | tf_op jit(solution)/shard_map/attend_back_kernel/pallas_call | solution.py:173
  36.3 1.3 %collective-permute-done.11 = bf16[128,512]{1,0:T(8,128)(2,1)S(1)} collective-permute-done((bf16[128,512]{1,0:T(8,128)(2,1)S(1)}, bf16[128,512]{1,0:T(8,128)(2,1)S(1)}, u32[]{:S(2)}, u32[]{:S(2)}) %collective-permute-start.11) | collective-permute-done | bytes 131104 | tf_op jit(solution)/shard_map/ppermute | solution.py:474
  37.6 0.5 collective-permute-start.29
  38.1 1.0 %collective-permute-start.28 = (bf16[16,512]{1,0:T(8,128)(2,1)S(1)}, bf16[16,512]{1,0:T(8,128)(2,1)S(1)}, u32[]{:S(2)}, u32[]{:S(2)}) collective-permute-start(bf16[16,512]{1,0:T(8,128)(2,1)S(1)} %get-tuple-element.181), channel_id=1, source_target_pairs={{0,2},{1,3},{2,0},{3,1},{4,6},{5,7},{6,4},{7,5},{8,10},{9,11},{10,... | collective-permute-start | bytes 49160 | tf_op jit(solution)/shard_map/ppermute | solution.py:474
  39.4 0.5 collective-permute-start.13
  40.1 0.4 collective-permute-start.14
  40.6 1.1 %sums_kernel.1 = bf16[16,512]{1,0:T(8,128)(2,1)S(1)} custom-call(bf16[128,512]{1,0:T(8,128)(2,1)S(1)} %get-tuple-element.160.refs_0_, f32[512,128]{1,0:T(8,128)S(1)} %get-tuple-element.178.refs_1_, f32[8,512]{1,0:T(8,128)S(1)} %get-tuple-element.179.refs_2_, s32[16,16]{1,0:T(8,128)S(1)} %get-tuple-element.180.refs_3_), custom_call_target="tpu_custom_call" | custom-call | flops 1000000000 | tf_op jit(solution)/shard_map/sums_kernel/pallas_call | solution.py:173
  41.7 2.7 %collective-permute-start.15 = (bf16[128,512]{1,0:T(8,128)(2,1)S(1)}, bf16[128,512]{1,0:T(8,128)(2,1)S(1)}, u32[]{:S(2)}, u32[]{:S(2)}) collective-permute-start(bf16[128,512]{1,0:T(8,128)(2,1)S(1)} %get-tuple-element.163), channel_id=1, source_target_pairs={{0,12},{4,8},{8,4},{12,0},{16,28},{20,24},{24,20},{28,16},{1,13},{... | collective-permute-start | bytes 393224 | tf_op jit(solution)/shard_map/ppermute | solution.py:474
  44.4 2.6 %collective-permute-start.22 = (bf16[256,512]{1,0:T(8,128)(2,1)S(1)}, bf16[256,512]{1,0:T(8,128)(2,1)S(1)}, u32[]{:S(2)}, u32[]{:S(2)}) collective-permute-start(bf16[256,512]{1,0:T(8,128)(2,1)S(1)} %pad_maximum_fusion), channel_id=1, source_target_pairs={{0,16},{4,20},{8,24},{12,28},{16,0},{20,4},{24,8},{28,12},{1,17},{... | collective-permute-start | bytes 786440 | tf_op jit(solution)/shard_map/ppermute | solution.py:474
  47.0 1.5 %collective-permute-start.17 = (bf16[256,512]{1,0:T(8,128)(2,1)S(1)}, bf16[256,512]{1,0:T(8,128)(2,1)S(1)}, u32[]{:S(2)}, u32[]{:S(2)}) collective-permute-start(bf16[256,512]{1,0:T(8,128)(2,1)S(1)} %add_convert_fusion.4), channel_id=1, source_target_pairs={{0,2},{1,3},{2,0},{3,1},{4,6},{5,7},{6,4},{7,5},{8,10},{9,11},{10,... | collective-permute-start | bytes 786440 | tf_op jit(solution)/shard_map/ppermute | solution.py:474
  48.5 4.8 %collective-permute-done.15 = bf16[128,512]{1,0:T(8,128)(2,1)S(1)} collective-permute-done((bf16[128,512]{1,0:T(8,128)(2,1)S(1)}, bf16[128,512]{1,0:T(8,128)(2,1)S(1)}, u32[]{:S(2)}, u32[]{:S(2)}) %collective-permute-start.15) | collective-permute-done | bytes 131104 | tf_op jit(solution)/shard_map/ppermute | solution.py:474
  53.4 0.9 %collective-permute-done.17 = bf16[256,512]{1,0:T(8,128)(2,1)S(1)} collective-permute-done((bf16[256,512]{1,0:T(8,128)(2,1)S(1)}, bf16[256,512]{1,0:T(8,128)(2,1)S(1)}, u32[]{:S(2)}, u32[]{:S(2)}) %collective-permute-start.17) | collective-permute-done | bytes 262176 | tf_op jit(solution)/shard_map/ppermute | solution.py:474
  54.3 1.1 %attend_out_kernel.1 = (bf16[256,512]{1,0:T(8,128)(2,1)S(1)}, bf16[256,512]{1,0:T(8,128)(2,1)S(1)}) custom-call(s32[32]{0:T(128)S(1)} %stack.143.refs_0_, bf16[128,512]{1,0:T(8,128)(2,1)S(1)} %add_convert_fusion.12.refs_1_, bf16[256,512]{1,0:T(8,128)(2,1)S(1)} %add_convert_fusion.3.refs_2_.refs_3_, bf16[512,128]{1,0:T(8,128)(2,1)S(1)} %get-tuple-element.166.refs_3_, ...), custom_call_target="tpu_custom_call" | custom-call | flops 1000000000 | tf_op jit(solution)/shard_map/attend_out_kernel/pallas_call | solution.py:173
  55.5 0.4 collective-permute-start.30
  56.2 2.3 %collective-permute-done.22 = bf16[256,512]{1,0:T(8,128)(2,1)S(1)} collective-permute-done((bf16[256,512]{1,0:T(8,128)(2,1)S(1)}, bf16[256,512]{1,0:T(8,128)(2,1)S(1)}, u32[]{:S(2)}, u32[]{:S(2)}) %collective-permute-start.22) | collective-permute-done | bytes 262176 | tf_op jit(solution)/shard_map/ppermute | solution.py:474
  58.6 1.4 %collective-permute-start.19 = (bf16[256,512]{1,0:T(8,128)(2,1)S(1)}, bf16[256,512]{1,0:T(8,128)(2,1)S(1)}, u32[]{:S(2)}, u32[]{:S(2)}) collective-permute-start(bf16[256,512]{1,0:T(8,128)(2,1)S(1)} %add_convert_fusion.2), channel_id=1, source_target_pairs={{0,2},{1,3},{2,0},{3,1},{4,6},{5,7},{6,4},{7,5},{8,10},{9,11},{10,... | collective-permute-start | bytes 786440 | tf_op jit(solution)/shard_map/ppermute | solution.py:474
  60.0 0.8 collective-permute-start.25
  60.9 4.1 %collective-permute-start.23 = (bf16[128,512]{1,0:T(8,128)(2,1)S(1)}, bf16[128,512]{1,0:T(8,128)(2,1)S(1)}, u32[]{:S(2)}, u32[]{:S(2)}) collective-permute-start(bf16[128,512]{1,0:T(8,128)(2,1)S(1)} %get-tuple-element.201), channel_id=1, source_target_pairs={{0,8},{4,12},{8,0},{12,4},{16,24},{20,28},{24,16},{28,20},{1,9},{5... | collective-permute-start | bytes 393224 | tf_op jit(solution)/shard_map/ppermute | solution.py:474
  65.0 1.5 %collective-permute-done.30 = bf16[160,512]{1,0:T(8,128)(2,1)S(1)} collective-permute-done((bf16[160,512]{1,0:T(8,128)(2,1)S(1)}, bf16[160,512]{1,0:T(8,128)(2,1)S(1)}, u32[]{:S(2)}, u32[]{:S(2)}) %collective-permute-start.30) | collective-permute-done | bytes 163872 | tf_op jit(solution)/shard_map/ppermute | solution.py:474
  66.7 0.5 collective-permute-start.20
  67.2 0.7 collective-permute-done.23
  68.0 1.3 %collective-permute-start.24 = (bf16[256,512]{1,0:T(8,128)(2,1)S(1)}, bf16[256,512]{1,0:T(8,128)(2,1)S(1)}, u32[]{:S(2)}, u32[]{:S(2)}) collective-permute-start(bf16[256,512]{1,0:T(8,128)(2,1)S(1)} %maximum_select_fusion.refs_2_), channel_id=1, source_target_pairs={{0,4},{4,0},{8,12},{12,8},{16,20},{20,16},{24,28},{28,24},{1,5},{5... | collective-permute-start | bytes 786440 | tf_op jit(solution)/shard_map/ppermute | solution.py:474
  69.4 2.1 %collective-permute-start.26 = (bf16[256,512]{1,0:T(8,128)(2,1)S(1)}, bf16[256,512]{1,0:T(8,128)(2,1)S(1)}, u32[]{:S(2)}, u32[]{:S(2)}) collective-permute-start(bf16[256,512]{1,0:T(8,128)(2,1)S(1)} %maximum_select_fusion.1.refs_4_), channel_id=1, source_target_pairs={{0,8},{4,12},{8,0},{12,4},{16,24},{20,28},{24,16},{28,20},{1,9},{5... | collective-permute-start | bytes 786440 | tf_op jit(solution)/shard_map/ppermute | solution.py:474
  71.8 1.9 %collective-permute-start.33 = (bf16[160,512]{1,0:T(8,128)(2,1)S(1)}, bf16[160,512]{1,0:T(8,128)(2,1)S(1)}, u32[]{:S(2)}, u32[]{:S(2)}) collective-permute-start(bf16[160,512]{1,0:T(8,128)(2,1)S(1)} %add_convert_fusion.9.refs_2_), channel_id=1, source_target_pairs={{0,8},{4,12},{8,0},{12,4},{16,24},{20,28},{24,16},{28,20},{1,9},{5... | collective-permute-start | bytes 491528 | tf_op jit(solution)/shard_map/ppermute | solution.py:474
  73.7 1.3 %collective-permute-start.32 = (bf16[160,512]{1,0:T(8,128)(2,1)S(1)}, bf16[160,512]{1,0:T(8,128)(2,1)S(1)}, u32[]{:S(2)}, u32[]{:S(2)}) collective-permute-start(bf16[160,512]{1,0:T(8,128)(2,1)S(1)} %add_convert_fusion.9.refs_2_), channel_id=1, source_target_pairs={{0,4},{4,0},{8,12},{12,8},{16,20},{20,16},{24,28},{28,24},{1,5},{5... | collective-permute-start | bytes 491528 | tf_op jit(solution)/shard_map/ppermute | solution.py:474
  75.0 2.6 %finish_kernel.1 = (f32[512,512]{1,0:T(8,128)}, f32[512,512]{1,0:T(8,128)}) custom-call(s32[32]{0:T(128)S(1)} %stack.143.refs_0_, bf16[256,512]{1,0:T(8,128)(2,1)S(1)} %add_convert_fusion.1.refs_1_, bf16[256,512]{1,0:T(8,128)(2,1)S(1)} %collective-permute-done.20.refs_2_, bf16[256,512]{1,0:T(8,128)(2,1)S(1)} %add_convert_fusion.3.refs_2_.refs_3_, ...), custom_call_target="tpu_custom_call" | custom-call | flops 2000000000 | tf_op jit(solution)/shard_map/finish_kernel/pallas_call | solution.py:173
  77.6 1.1 %collective-permute-done.26.refs_5_ = bf16[256,512]{1,0:T(8,128)(2,1)S(1)} collective-permute-done((bf16[256,512]{1,0:T(8,128)(2,1)S(1)}, bf16[256,512]{1,0:T(8,128)(2,1)S(1)}, u32[]{:S(2)}, u32[]{:S(2)}) %collective-permute-start.26) | collective-permute-done | bytes 262176 | tf_op jit(solution)/shard_map/ppermute | solution.py:474
  78.7 2.0 %widen_kernel.1 = (f32[512,512]{1,0:T(8,128)}, f32[512,512]{1,0:T(8,128)}) custom-call(s32[32]{0:T(128)S(1)} %stack.143.refs_0_, f32[512,512]{1,0:T(8,128)} %get-tuple-element.91.refs_1_, bf16[256,512]{1,0:T(8,128)(2,1)S(1)} %maximum_select_fusion.refs_2_, bf16[256,512]{1,0:T(8,128)(2,1)S(1)} %collective-permute-done.24.refs_3_, ...), custom_call_target="tpu_custom_call" | custom-call | tf_op jit(solution)/shard_map/widen_kernel/pallas_call | solution.py:173
  80.7 1.7 %collective-permute-done.34.refs_5_ = bf16[160,512]{1,0:T(8,128)(2,1)S(1)} collective-permute-done((bf16[160,512]{1,0:T(8,128)(2,1)S(1)}, bf16[160,512]{1,0:T(8,128)(2,1)S(1)}, u32[]{:S(2)}, u32[]{:S(2)}) %collective-permute-start.34) | collective-permute-done | bytes 163872 | tf_op jit(solution)/shard_map/ppermute | solution.py:474
  82.4 1.6 %collective-permute-done.33.refs_4_ = bf16[160,512]{1,0:T(8,128)(2,1)S(1)} collective-permute-done((bf16[160,512]{1,0:T(8,128)(2,1)S(1)}, bf16[160,512]{1,0:T(8,128)(2,1)S(1)}, u32[]{:S(2)}, u32[]{:S(2)}) %collective-permute-start.33) | collective-permute-done | bytes 163872 | tf_op jit(solution)/shard_map/ppermute | solution.py:474
  84.0 1.7 %unpack_kernel.1 = (f32[512,128]{1,0:T(8,128)}, f32[512,128]{1,0:T(8,128)}, f32[512,128]{1,0:T(8,128)}, f32[128,512]{1,0:T(8,128)}, f32[512]{0:T(512)}, /*index=...) custom-call(s32[32]{0:T(128)S(1)} %stack.143.refs_0_, ...), custom_call_target="tpu_custom_call" | custom-call | tf_op jit(solution)/shard_map/unpack_kernel/pallas_call | solution.py:173
  (56 shorter events, 3.5 us)
Async XLA Ops:
  0.7 8.6 %collective-permute-start.2 = (bf16[128,512]{1,0:T(8,128)(2,1)}, bf16[128,512]{1,0:T(8,128)(2,1)S(1)}, u32[]{:S(2)}, u32[]{:S(2)}) collective-permute-start(bf16[128,512]{1,0:T(8,128)(2,1)} %refs_9_.1), channel_id=1, source_target_pairs={{0,2},{1,3},{2,0},{3,1},{4,6},{5,7},{6,4},{7,5},{8,10},{9,11},{10,... | collective-permute-start | bytes 393224 | tf_op jit(solution)/shard_map/ppermute | solution.py:474
  3.8 4.9 %copy-start = (bf16[128,512]{1,0:T(8,128)(2,1)S(1)}, bf16[128,512]{1,0:T(8,128)(2,1)}, u32[]{:S(2)}) copy-start(bf16[128,512]{1,0:T(8,128)(2,1)} %refs_9_.1) | copy-start | bytes 393220
  8.6 5.0 %collective-permute-start.1 = (bf16[512,128]{1,0:T(8,128)(2,1)S(1)}, bf16[512,128]{1,0:T(8,128)(2,1)S(1)}, u32[]{:S(2)}, u32[]{:S(2)}) collective-permute-start(bf16[512,128]{1,0:T(8,128)(2,1)S(1)} %get-tuple-element.109.refs_0_.refs_1_.refs_12_), channel_id=1, source_target_pairs={{0,2},{1,3},{2,0},{3,1},{4,6},{5,7},{6,4},{7,5},{8,10},{9,11},{10,... | collective-permute-start | bytes 393224 | tf_op jit(solution)/shard_map/ppermute | solution.py:474
  8.7 5.4 %collective-permute-start.4 = (bf16[128,512]{1,0:T(8,128)(2,1)S(1)}, bf16[128,512]{1,0:T(8,128)(2,1)S(1)}, u32[]{:S(2)}, u32[]{:S(2)}) collective-permute-start(bf16[128,512]{1,0:T(8,128)(2,1)S(1)} %copy-done), channel_id=1, source_target_pairs={{0,1},{1,0},{2,3},{3,2},{4,5},{5,4},{6,7},{7,6},{8,9},{9,8},{10,11... | collective-permute-start | bytes 393224 | tf_op jit(solution)/shard_map/ppermute | solution.py:474
  8.8 5.4 %collective-permute-start = (bf16[512,128]{1,0:T(8,128)(2,1)S(1)}, bf16[512,128]{1,0:T(8,128)(2,1)S(1)}, u32[]{:S(2)}, u32[]{:S(2)}) collective-permute-start(bf16[512,128]{1,0:T(8,128)(2,1)S(1)} %get-tuple-element.109.refs_0_.refs_1_.refs_12_), channel_id=1, source_target_pairs={{0,1},{1,0},{2,3},{3,2},{4,5},{5,4},{6,7},{7,6},{8,9},{9,8},{10,11... | collective-permute-start | bytes 393224 | tf_op jit(solution)/shard_map/ppermute | solution.py:474
  13.6 1.3 %collective-permute-start.5 = (bf16[128,512]{1,0:T(8,128)(2,1)S(1)}, bf16[128,512]{1,0:T(8,128)(2,1)S(1)}, u32[]{:S(2)}, u32[]{:S(2)}) collective-permute-start(bf16[128,512]{1,0:T(8,128)(2,1)S(1)} %collective-permute-done.2.refs_1_.refs_7_), channel_id=1, source_target_pairs={{0,1},{1,0},{2,3},{3,2},{4,5},{5,4},{6,7},{7,6},{8,9},{9,8},{10,11... | collective-permute-start | bytes 393224 | tf_op jit(solution)/shard_map/ppermute | solution.py:474
  13.6 1.5 %collective-permute-start.3 = (bf16[512,128]{1,0:T(8,128)(2,1)S(1)}, bf16[512,128]{1,0:T(8,128)(2,1)S(1)}, u32[]{:S(2)}, u32[]{:S(2)}) collective-permute-start(bf16[512,128]{1,0:T(8,128)(2,1)S(1)} %collective-permute-done.1.refs_3_), channel_id=1, source_target_pairs={{0,1},{1,0},{2,3},{3,2},{4,5},{5,4},{6,7},{7,6},{8,9},{9,8},{10,11... | collective-permute-start | bytes 393224 | tf_op jit(solution)/shard_map/ppermute | solution.py:474
  18.1 1.8 %collective-permute-start.6 = (bf16[256,512]{1,0:T(8,128)(2,1)S(1)}, bf16[256,512]{1,0:T(8,128)(2,1)S(1)}, u32[]{:S(2)}, u32[]{:S(2)}) collective-permute-start(bf16[256,512]{1,0:T(8,128)(2,1)S(1)} %get-tuple-element.126), channel_id=1, source_target_pairs={{0,1},{1,0},{2,3},{3,2},{4,5},{5,4},{6,7},{7,6},{8,9},{9,8},{10,11... | collective-permute-start | bytes 786440 | tf_op jit(solution)/shard_map/ppermute | solution.py:474
  20.0 8.5 %collective-permute-start.7 = (bf16[256,512]{1,0:T(8,128)(2,1)S(1)}, bf16[256,512]{1,0:T(8,128)(2,1)S(1)}, u32[]{:S(2)}, u32[]{:S(2)}) collective-permute-start(bf16[256,512]{1,0:T(8,128)(2,1)S(1)} %add_convert_fusion.8), channel_id=1, source_target_pairs={{0,2},{1,3},{2,0},{3,1},{4,6},{5,7},{6,4},{7,5},{8,10},{9,11},{10,... | collective-permute-start | bytes 786440 | tf_op jit(solution)/shard_map/ppermute | solution.py:474
  20.4 8.1 %collective-permute-start.8 = (bf16[256,512]{1,0:T(8,128)(2,1)S(1)}, bf16[256,512]{1,0:T(8,128)(2,1)S(1)}, u32[]{:S(2)}, u32[]{:S(2)}) collective-permute-start(bf16[256,512]{1,0:T(8,128)(2,1)S(1)} %get-tuple-element.131), channel_id=1, source_target_pairs={{0,4},{4,0},{8,12},{12,8},{16,20},{20,16},{24,28},{28,24},{1,5},{5... | collective-permute-start | bytes 786440 | tf_op jit(solution)/shard_map/ppermute | solution.py:474
  22.1 7.8 %collective-permute-start.9 = (bf16[256,512]{1,0:T(8,128)(2,1)S(1)}, bf16[256,512]{1,0:T(8,128)(2,1)S(1)}, u32[]{:S(2)}, u32[]{:S(2)}) collective-permute-start(bf16[256,512]{1,0:T(8,128)(2,1)S(1)} %get-tuple-element.132), channel_id=1, source_target_pairs={{0,8},{4,12},{8,0},{12,4},{16,24},{20,28},{24,16},{28,20},{1,9},{5... | collective-permute-start | bytes 786440 | tf_op jit(solution)/shard_map/ppermute | solution.py:474
  30.0 2.5 %collective-permute-start.12 = (bf16[256,512]{1,0:T(8,128)(2,1)S(1)}, bf16[256,512]{1,0:T(8,128)(2,1)S(1)}, u32[]{:S(2)}, u32[]{:S(2)}) collective-permute-start(bf16[256,512]{1,0:T(8,128)(2,1)S(1)} %add_convert_fusion.5.refs_1_), channel_id=1, source_target_pairs={{0,1},{1,0},{2,3},{3,2},{4,5},{5,4},{6,7},{7,6},{8,9},{9,8},{10,11... | collective-permute-start | bytes 786440 | tf_op jit(solution)/shard_map/ppermute | solution.py:474
  30.3 6.0 %collective-permute-start.10 = (bf16[128,512]{1,0:T(8,128)(2,1)S(1)}, bf16[128,512]{1,0:T(8,128)(2,1)S(1)}, u32[]{:S(2)}, u32[]{:S(2)}) collective-permute-start(bf16[128,512]{1,0:T(8,128)(2,1)S(1)} %constant_dynamic-slice_fusion.1), channel_id=1, source_target_pairs={{0,8},{4,12},{8,0},{12,4},{16,24},{20,28},{24,16},{28,20},{1,9},{5... | collective-permute-start | bytes 393224 | tf_op jit(solution)/shard_map/ppermute | solution.py:474
  32.0 5.6 %collective-permute-start.11 = (bf16[128,512]{1,0:T(8,128)(2,1)S(1)}, bf16[128,512]{1,0:T(8,128)(2,1)S(1)}, u32[]{:S(2)}, u32[]{:S(2)}) collective-permute-start(bf16[128,512]{1,0:T(8,128)(2,1)S(1)} %constant_dynamic-slice_fusion), channel_id=1, source_target_pairs={{0,4},{4,0},{8,12},{12,8},{16,20},{20,16},{24,28},{28,24},{1,5},{5... | collective-permute-start | bytes 393224 | tf_op jit(solution)/shard_map/ppermute | solution.py:474
  32.5 7.6 %collective-permute-start.16 = (bf16[256,512]{1,0:T(8,128)(2,1)S(1)}, bf16[256,512]{1,0:T(8,128)(2,1)S(1)}, u32[]{:S(2)}, u32[]{:S(2)}) collective-permute-start(bf16[256,512]{1,0:T(8,128)(2,1)S(1)} %get-tuple-element.165), channel_id=1, source_target_pairs={{0,1},{1,0},{2,3},{3,2},{4,5},{5,4},{6,7},{7,6},{8,9},{9,8},{10,11... | collective-permute-start | bytes 786440 | tf_op jit(solution)/shard_map/ppermute | solution.py:474
  37.6 4.1 %collective-permute-start.29 = (bf16[16,512]{1,0:T(8,128)(2,1)S(1)}, bf16[16,512]{1,0:T(8,128)(2,1)S(1)}, u32[]{:S(2)}, u32[]{:S(2)}) collective-permute-start(bf16[16,512]{1,0:T(8,128)(2,1)S(1)} %get-tuple-element.181), channel_id=1, source_target_pairs={{0,3},{1,2},{2,1},{3,0},{4,7},{5,6},{6,5},{7,4},{8,11},{9,10},{10,... | collective-permute-start | bytes 49160 | tf_op jit(solution)/shard_map/ppermute | solution.py:474
  38.1 6.3 %collective-permute-start.28 = (bf16[16,512]{1,0:T(8,128)(2,1)S(1)}, bf16[16,512]{1,0:T(8,128)(2,1)S(1)}, u32[]{:S(2)}, u32[]{:S(2)}) collective-permute-start(bf16[16,512]{1,0:T(8,128)(2,1)S(1)} %get-tuple-element.181), channel_id=1, source_target_pairs={{0,2},{1,3},{2,0},{3,1},{4,6},{5,7},{6,4},{7,5},{8,10},{9,11},{10,... | collective-permute-start | bytes 49160 | tf_op jit(solution)/shard_map/ppermute | solution.py:474
  39.1 7.9 %collective-permute-start.27 = (bf16[16,512]{1,0:T(8,128)(2,1)S(1)}, bf16[16,512]{1,0:T(8,128)(2,1)S(1)}, u32[]{:S(2)}, u32[]{:S(2)}) collective-permute-start(bf16[16,512]{1,0:T(8,128)(2,1)S(1)} %get-tuple-element.181), channel_id=1, source_target_pairs={{0,1},{1,0},{2,3},{3,2},{4,5},{5,4},{6,7},{7,6},{8,9},{9,8},{10,11... | collective-permute-start | bytes 49160 | tf_op jit(solution)/shard_map/ppermute | solution.py:474
  39.4 9.0 %collective-permute-start.13 = (bf16[128,512]{1,0:T(8,128)(2,1)S(1)}, bf16[128,512]{1,0:T(8,128)(2,1)S(1)}, u32[]{:S(2)}, u32[]{:S(2)}) collective-permute-start(bf16[128,512]{1,0:T(8,128)(2,1)S(1)} %get-tuple-element.161), channel_id=1, source_target_pairs={{0,4},{4,0},{8,12},{12,8},{16,20},{20,16},{24,28},{28,24},{1,5},{5... | collective-permute-start | bytes 393224 | tf_op jit(solution)/shard_map/ppermute | solution.py:474
  40.1 8.4 %collective-permute-start.14 = (bf16[128,512]{1,0:T(8,128)(2,1)S(1)}, bf16[128,512]{1,0:T(8,128)(2,1)S(1)}, u32[]{:S(2)}, u32[]{:S(2)}) collective-permute-start(bf16[128,512]{1,0:T(8,128)(2,1)S(1)} %get-tuple-element.162), channel_id=1, source_target_pairs={{0,8},{4,12},{8,0},{12,4},{16,24},{20,28},{24,16},{28,20},{1,9},{5... | collective-permute-start | bytes 393224 | tf_op jit(solution)/shard_map/ppermute | solution.py:474
  41.7 11.6 %collective-permute-start.15 = (bf16[128,512]{1,0:T(8,128)(2,1)S(1)}, bf16[128,512]{1,0:T(8,128)(2,1)S(1)}, u32[]{:S(2)}, u32[]{:S(2)}) collective-permute-start(bf16[128,512]{1,0:T(8,128)(2,1)S(1)} %get-tuple-element.163), channel_id=1, source_target_pairs={{0,12},{4,8},{8,4},{12,0},{16,28},{20,24},{24,20},{28,16},{1,13},{... | collective-permute-start | bytes 393224 | tf_op jit(solution)/shard_map/ppermute | solution.py:474
  44.4 14.1 %collective-permute-start.22 = (bf16[256,512]{1,0:T(8,128)(2,1)S(1)}, bf16[256,512]{1,0:T(8,128)(2,1)S(1)}, u32[]{:S(2)}, u32[]{:S(2)}) collective-permute-start(bf16[256,512]{1,0:T(8,128)(2,1)S(1)} %pad_maximum_fusion), channel_id=1, source_target_pairs={{0,16},{4,20},{8,24},{12,28},{16,0},{20,4},{24,8},{28,12},{1,17},{... | collective-permute-start | bytes 786440 | tf_op jit(solution)/shard_map/ppermute | solution.py:474
  47.0 7.3 %collective-permute-start.17 = (bf16[256,512]{1,0:T(8,128)(2,1)S(1)}, bf16[256,512]{1,0:T(8,128)(2,1)S(1)}, u32[]{:S(2)}, u32[]{:S(2)}) collective-permute-start(bf16[256,512]{1,0:T(8,128)(2,1)S(1)} %add_convert_fusion.4), channel_id=1, source_target_pairs={{0,2},{1,3},{2,0},{3,1},{4,6},{5,7},{6,4},{7,5},{8,10},{9,11},{10,... | collective-permute-start | bytes 786440 | tf_op jit(solution)/shard_map/ppermute | solution.py:474
  55.4 3.1 %collective-permute-start.18 = (bf16[256,512]{1,0:T(8,128)(2,1)S(1)}, bf16[256,512]{1,0:T(8,128)(2,1)S(1)}, u32[]{:S(2)}, u32[]{:S(2)}) collective-permute-start(bf16[256,512]{1,0:T(8,128)(2,1)S(1)} %get-tuple-element.170), channel_id=1, source_target_pairs={{0,1},{1,0},{2,3},{3,2},{4,5},{5,4},{6,7},{7,6},{8,9},{9,8},{10,11... | collective-permute-start | bytes 786440 | tf_op jit(solution)/shard_map/ppermute | solution.py:474
  55.5 11.0 %collective-permute-start.30 = (bf16[160,512]{1,0:T(8,128)(2,1)S(1)}, bf16[160,512]{1,0:T(8,128)(2,1)S(1)}, u32[]{:S(2)}, u32[]{:S(2)}) collective-permute-start(bf16[160,512]{1,0:T(8,128)(2,1)S(1)} %pad_maximum_fusion.1), channel_id=1, source_target_pairs={{0,16},{4,20},{8,24},{12,28},{16,0},{20,4},{24,8},{28,12},{1,17},{... | collective-permute-start | bytes 491528 | tf_op jit(solution)/shard_map/ppermute | solution.py:474
  55.9 15.8 %collective-permute-start.21 = (bf16[256,512]{1,0:T(8,128)(2,1)S(1)}, bf16[256,512]{1,0:T(8,128)(2,1)S(1)}, u32[]{:S(2)}, u32[]{:S(2)}) collective-permute-start(bf16[256,512]{1,0:T(8,128)(2,1)S(1)} %add_convert_fusion.3.refs_2_.refs_3_), channel_id=1, source_target_pairs={{0,1},{1,0},{2,3},{3,2},{4,5},{5,4},{6,7},{7,6},{8,9},{9,8},{10,11... | collective-permute-start | bytes 786440 | tf_op jit(solution)/shard_map/ppermute | solution.py:474
  58.6 8.0 %collective-permute-start.19 = (bf16[256,512]{1,0:T(8,128)(2,1)S(1)}, bf16[256,512]{1,0:T(8,128)(2,1)S(1)}, u32[]{:S(2)}, u32[]{:S(2)}) collective-permute-start(bf16[256,512]{1,0:T(8,128)(2,1)S(1)} %add_convert_fusion.2), channel_id=1, source_target_pairs={{0,2},{1,3},{2,0},{3,1},{4,6},{5,7},{6,4},{7,5},{8,10},{9,11},{10,... | collective-permute-start | bytes 786440 | tf_op jit(solution)/shard_map/ppermute | solution.py:474
  60.0 9.3 %collective-permute-start.25 = (bf16[128,512]{1,0:T(8,128)(2,1)S(1)}, bf16[128,512]{1,0:T(8,128)(2,1)S(1)}, u32[]{:S(2)}, u32[]{:S(2)}) collective-permute-start(bf16[128,512]{1,0:T(8,128)(2,1)S(1)} %get-tuple-element.200), channel_id=1, source_target_pairs={{0,4},{4,0},{8,12},{12,8},{16,20},{20,16},{24,28},{28,24},{1,5},{5... | collective-permute-start | bytes 393224 | tf_op jit(solution)/shard_map/ppermute | solution.py:474
  60.9 7.1 %collective-permute-start.23 = (bf16[128,512]{1,0:T(8,128)(2,1)S(1)}, bf16[128,512]{1,0:T(8,128)(2,1)S(1)}, u32[]{:S(2)}, u32[]{:S(2)}) collective-permute-start(bf16[128,512]{1,0:T(8,128)(2,1)S(1)} %get-tuple-element.201), channel_id=1, source_target_pairs={{0,8},{4,12},{8,0},{12,4},{16,24},{20,28},{24,16},{28,20},{1,9},{5... | collective-permute-start | bytes 393224 | tf_op jit(solution)/shard_map/ppermute | solution.py:474
  66.5 5.0 %collective-permute-start.31 = (bf16[160,512]{1,0:T(8,128)(2,1)S(1)}, bf16[160,512]{1,0:T(8,128)(2,1)S(1)}, u32[]{:S(2)}, u32[]{:S(2)}) collective-permute-start(bf16[160,512]{1,0:T(8,128)(2,1)S(1)} %add_convert_fusion.9.refs_2_), channel_id=1, source_target_pairs={{0,1},{1,0},{2,3},{3,2},{4,5},{5,4},{6,7},{7,6},{8,9},{9,8},{10,11... | collective-permute-start | bytes 491528 | tf_op jit(solution)/shard_map/ppermute | solution.py:474
  66.7 7.0 %collective-permute-start.20 = (bf16[256,512]{1,0:T(8,128)(2,1)S(1)}, bf16[256,512]{1,0:T(8,128)(2,1)S(1)}, u32[]{:S(2)}, u32[]{:S(2)}) collective-permute-start(bf16[256,512]{1,0:T(8,128)(2,1)S(1)} %add_convert_fusion.1.refs_1_), channel_id=1, source_target_pairs={{0,1},{1,0},{2,3},{3,2},{4,5},{5,4},{6,7},{7,6},{8,9},{9,8},{10,11... | collective-permute-start | bytes 786440 | tf_op jit(solution)/shard_map/ppermute | solution.py:474
  68.0 9.6 %collective-permute-start.24 = (bf16[256,512]{1,0:T(8,128)(2,1)S(1)}, bf16[256,512]{1,0:T(8,128)(2,1)S(1)}, u32[]{:S(2)}, u32[]{:S(2)}) collective-permute-start(bf16[256,512]{1,0:T(8,128)(2,1)S(1)} %maximum_select_fusion.refs_2_), channel_id=1, source_target_pairs={{0,4},{4,0},{8,12},{12,8},{16,20},{20,16},{24,28},{28,24},{1,5},{5... | collective-permute-start | bytes 786440 | tf_op jit(solution)/shard_map/ppermute | solution.py:474
  69.4 9.3 %collective-permute-start.26 = (bf16[256,512]{1,0:T(8,128)(2,1)S(1)}, bf16[256,512]{1,0:T(8,128)(2,1)S(1)}, u32[]{:S(2)}, u32[]{:S(2)}) collective-permute-start(bf16[256,512]{1,0:T(8,128)(2,1)S(1)} %maximum_select_fusion.1.refs_4_), channel_id=1, source_target_pairs={{0,8},{4,12},{8,0},{12,4},{16,24},{20,28},{24,16},{28,20},{1,9},{5... | collective-permute-start | bytes 786440 | tf_op jit(solution)/shard_map/ppermute | solution.py:474
  71.5 10.9 %collective-permute-start.34 = (bf16[160,512]{1,0:T(8,128)(2,1)S(1)}, bf16[160,512]{1,0:T(8,128)(2,1)S(1)}, u32[]{:S(2)}, u32[]{:S(2)}) collective-permute-start(bf16[160,512]{1,0:T(8,128)(2,1)S(1)} %add_convert_fusion.9.refs_2_), channel_id=1, source_target_pairs={{0,12},{4,8},{8,4},{12,0},{16,28},{20,24},{24,20},{28,16},{1,13},{... | collective-permute-start | bytes 491528 | tf_op jit(solution)/shard_map/ppermute | solution.py:474
  71.8 12.3 %collective-permute-start.33 = (bf16[160,512]{1,0:T(8,128)(2,1)S(1)}, bf16[160,512]{1,0:T(8,128)(2,1)S(1)}, u32[]{:S(2)}, u32[]{:S(2)}) collective-permute-start(bf16[160,512]{1,0:T(8,128)(2,1)S(1)} %add_convert_fusion.9.refs_2_), channel_id=1, source_target_pairs={{0,8},{4,12},{8,0},{12,4},{16,24},{20,28},{24,16},{28,20},{1,9},{5... | collective-permute-start | bytes 491528 | tf_op jit(solution)/shard_map/ppermute | solution.py:474
  73.7 10.3 %collective-permute-start.32 = (bf16[160,512]{1,0:T(8,128)(2,1)S(1)}, bf16[160,512]{1,0:T(8,128)(2,1)S(1)}, u32[]{:S(2)}, u32[]{:S(2)}) collective-permute-start(bf16[160,512]{1,0:T(8,128)(2,1)S(1)} %add_convert_fusion.9.refs_2_), channel_id=1, source_target_pairs={{0,4},{4,0},{8,12},{12,8},{16,20},{20,16},{24,28},{28,24},{1,5},{5... | collective-permute-start | bytes 491528 | tf_op jit(solution)/shard_map/ppermute | solution.py:474

commit v5 on v4

--- a/solution.py
+++ b/solution.py
@@ -695,20 +695,21 @@
     rest2 = swap(sum2, "tensor", 1, tensor)
     att_parts = meet(att_own, att_y, att_z, att_yz)
     chunk = combine(att_parts)
-    across = [swap(norm1, "tensor", flip, tensor).astype(F32) for flip in (1, 2, 3)]
-    norm1 = ((norm1.astype(F32) + across[0]) + (across[1] + across[2])).astype(BF)
     (small_b,) = call(
         sums_kernel,
         [((16, width), BF, "vmem")],
-        [(att_own, "vmem"), (scores, "vmem"), (sums, "vmem"), (position_index, "vmem")],
+        [(att_parts[1], "vmem"), (scores, "vmem"), (sums, "vmem"), (position_index, "vmem")],
         scratch=[((16, width), F32)],
         cost=1,
     )
+    norm1, small_b = lax.optimization_barrier((norm1, small_b))
+    across = [swap(norm1, "tensor", flip, tensor).astype(F32) for flip in (1, 2, 3)]
+    norm1 = ((norm1.astype(F32) + across[0]) + (across[1] + across[2])).astype(BF)
     keep4, send4 = call(
         attend_out_kernel,
         [((half, width), BF, "vmem"), ((half, width), BF, "vmem")],
         [
-            (spot, "smem"), (chunk, "vmem"), (sum2, "vmem"), (gq, "vmem"), (gk, "vmem"), (gv, "vmem"),
+            (spot, "smem"), (chunk, "vmem"), (small_b, "vmem"), (gq, "vmem"), (gk, "vmem"), (gv, "vmem"),
             (query_weight, "vmem"), (key_weight, "vmem"), (value_weight, "vmem"),
         ],
         cost=1,

time: 85.9 us -> 82 us (0.955)
  starting transfers between devices: 34.6 us -> 28.8 us
  waiting for transfers between devices: 24.5 us -> 26.3 us
    ppermute x35, starting transfers between devices: 34.6 us -> 28.8 us  [swap(): return lax.ppermute(value, axis, [(i, i ^ bit) for i in range(size)])]
    ppermute x35, waiting for transfers between devices: 24.5 us -> 26.3 us  [swap(): return lax.ppermute(value, axis, [(i, i ^ bit) for i in range(size)])]
  transfers between devices with their start and end apart: 35 -> 35, of which waited for: 16 -> 17; matrix products, arithmetic and copies ran while one was open for 1% -> 1% of each run, Pallas kernels for 23% -> 24%
where the time goes in v5:
time: 82 us; the launch traced here: 81.8 us
  starting transfers between devices  28.8 us (35%)
  waiting for transfers between devices  26.3 us (32%)
  Pallas kernels  24.5 us (30%)
  other arithmetic  0.98 us (1%)
  between operations  0.93 us (1%)
    ppermute x35, starting transfers between devices, swap(): return lax.ppermute(value, axis, [(i, i ^ bit) for i in range(size)])  28.8 us
    ppermute x35, waiting for transfers between devices, swap(): return lax.ppermute(value, axis, [(i, i ^ bit) for i in range(size)])  26.3 us
    pallas_call x11, Pallas kernels, call(): pl.pallas_call(body, name=kernel.__name__, out_shape=pinned, in_specs=[pl...  24.5 us
  transfers between devices with their start and end apart: 35, of which 17 were waited for; matrix products, arithmetic and copies ran while one was open for 1% of the time, Pallas kernels for 24%

profile of v5, /device:TPU:0, one launch (start us, length us, event | category | flops | bytes accessed | tf_op | source)
XLA Modules:
  0.0 81.8 jit_solution(13914334784415207639)
XLA Ops:
  0.7 3.0 %collective-permute-start.2 = (bf16[128,512]{1,0:T(8,128)(2,1)}, bf16[128,512]{1,0:T(8,128)(2,1)S(1)}, u32[]{:S(2)}, u32[]{:S(2)}) collective-permute-start(bf16[128,512]{1,0:T(8,128)(2,1)} %refs_9_.1), channel_id=1, source_target_pairs={{0,2},{1,3},{2,0},{3,1},{4,6},{5,7},{6,4},{7,5},{8,10},{9,11},{10,... | collective-permute-start | bytes 393224 | tf_op jit(solution)/shard_map/ppermute | solution.py:474
  3.8 4.8 %attend_kernel.1 = (bf16[512,128]{1,0:T(8,128)(2,1)S(1)}, bf16[512,512]{1,0:T(8,128)(2,1)S(1)}, bf16[512,128]{1,0:T(8,128)(2,1)S(1)}, bf16[512,128]{1,0:T(8,128)...) custom-call(s32[32]{0:T(128)S(1)} %stack.143.refs_0_, bf16[512,512]{1,0:T(8,128)(2,1)} %refs_2_.3, ...), custom_call_target="tpu_custom_call" | custom-call | flops 20000000000 | tf_op jit(solution)/shard_map/attend_kernel/pallas_call | solution.py:173
  8.8 0.5 collective-permute-start
  9.3 2.5 %fetch_kernel.1 = (f32[8,128]{1,0:T(8,128)}, bf16[512,512]{1,0:T(8,128)(2,1)S(1)}, f32[512]{0:T(512)S(1)}, f32[512]{0:T(512)S(1)}, s32[16,16]{1,0:T(8,128)S(1)},...) custom-call(bf16[512,128]{1,0:T(8,128)(2,1)S(1)} %get-tuple-element., ...), custom_call_target="tpu_custom_call" | custom-call | tf_op jit(solution)/shard_map/fetch_kernel/pallas_call | solution.py:173
  11.7 1.9 %collective-permute-done.1.refs_3_ = bf16[512,128]{1,0:T(8,128)(2,1)S(1)} collective-permute-done((bf16[512,128]{1,0:T(8,128)(2,1)S(1)}, bf16[512,128]{1,0:T(8,128)(2,1)S(1)}, u32[]{:S(2)}, u32[]{:S(2)}) %collective-permute-start.1) | collective-permute-done | bytes 131104 | tf_op jit(solution)/shard_map/ppermute | solution.py:474
  13.6 0.5 collective-permute-start.3
  14.1 0.8 %collective-permute-done.5.refs_8_ = bf16[128,512]{1,0:T(8,128)(2,1)S(1)} collective-permute-done((bf16[128,512]{1,0:T(8,128)(2,1)S(1)}, bf16[128,512]{1,0:T(8,128)(2,1)S(1)}, u32[]{:S(2)}, u32[]{:S(2)}) %collective-permute-start.5) | collective-permute-done | bytes 131104 | tf_op jit(solution)/shard_map/ppermute | solution.py:474
  15.2 2.9 %mlp_kernel.1 = (f32[512,512]{1,0:T(8,128)S(1)}, bf16[512,512]{1,0:T(8,128)(2,1)S(1)}, bf16[512,512]{1,0:T(8,128)(2,1)S(1)}, bf16[512,512]{1,0:T(8,128)(2,1)S(1)...) custom-call(s32[32]{0:T(128)S(1)} %stack.143.refs_0_, ...), custom_call_target="tpu_custom_call" | custom-call | flops 2000000000 | tf_op jit(solution)/shard_map/mlp_kernel/pallas_call | solution.py:173
  18.1 0.4 collective-permute-start.6
  18.5 1.4 %mlp_grad_kernel.1 = (bf16[256,512]{1,0:T(8,128)(2,1)S(1)}, bf16[256,512]{1,0:T(8,128)(2,1)S(1)}, bf16[256,512]{1,0:T(8,128)(2,1)S(1)}, bf16[256,512]{1,0:T(8,128)(2,1)S(1)}, bf16[8,512]{1,0:T(8,128)(2,1)S(1)}) custom-call(s32[32]{0:T(128)S(1)} %stack.143.refs_0_, bf16[512,512]{1,0:T(8,128)(2,1)S(1)} %get-tuple-element.123.refs_1_, ...), custom_call_target="tpu_custom_call" | custom-call | flops 2000000000 | tf_op jit(solution)/shard_map/mlp_grad_kernel/pallas_call | solution.py:173
  20.0 0.4 collective-permute-start.7
  20.4 1.7 %collective-permute-start.8 = (bf16[256,512]{1,0:T(8,128)(2,1)S(1)}, bf16[256,512]{1,0:T(8,128)(2,1)S(1)}, u32[]{:S(2)}, u32[]{:S(2)}) collective-permute-start(bf16[256,512]{1,0:T(8,128)(2,1)S(1)} %get-tuple-element.133), channel_id=1, source_target_pairs={{0,4},{4,0},{8,12},{12,8},{16,20},{20,16},{24,28},{28,24},{1,5},{5... | collective-permute-start | bytes 786440 | tf_op jit(solution)/shard_map/ppermute | solution.py:474
  22.1 1.6 %collective-permute-start.9 = (bf16[256,512]{1,0:T(8,128)(2,1)S(1)}, bf16[256,512]{1,0:T(8,128)(2,1)S(1)}, u32[]{:S(2)}, u32[]{:S(2)}) collective-permute-start(bf16[256,512]{1,0:T(8,128)(2,1)S(1)} %get-tuple-element.134), channel_id=1, source_target_pairs={{0,8},{4,12},{8,0},{12,4},{16,24},{20,28},{24,16},{28,20},{1,9},{5... | collective-permute-start | bytes 786440 | tf_op jit(solution)/shard_map/ppermute | solution.py:474
  23.7 1.0 %mlp_out_kernel.1 = (bf16[256,512]{1,0:T(8,128)(2,1)S(1)}, bf16[256,512]{1,0:T(8,128)(2,1)S(1)}) custom-call(s32[32]{0:T(128)S(1)} %stack.143.refs_0_, bf16[512,512]{1,0:T(8,128)(2,1)S(1)} %get-tuple-element.124.refs_2_.refs_1_, bf16[512,512]{1,0:T(8,128)(2,1)S(1)} %get-tuple-element.122.refs_16_.refs_2_), custom_call_target="tpu_custom_call" | custom-call | flops 1000000000 | tf_op jit(solution)/shard_map/mlp_out_kernel/pallas_call | solution.py:173
  24.6 3.8 %collective-permute-done.7 = bf16[256,512]{1,0:T(8,128)(2,1)S(1)} collective-permute-done((bf16[256,512]{1,0:T(8,128)(2,1)S(1)}, bf16[256,512]{1,0:T(8,128)(2,1)S(1)}, u32[]{:S(2)}, u32[]{:S(2)}) %collective-permute-start.7) | collective-permute-done | bytes 262176 | tf_op jit(solution)/shard_map/ppermute | solution.py:474
  28.5 1.4 %collective-permute-done.9 = bf16[256,512]{1,0:T(8,128)(2,1)S(1)} collective-permute-done((bf16[256,512]{1,0:T(8,128)(2,1)S(1)}, bf16[256,512]{1,0:T(8,128)(2,1)S(1)}, u32[]{:S(2)}, u32[]{:S(2)}) %collective-permute-start.9) | collective-permute-done | bytes 262176 | tf_op jit(solution)/shard_map/ppermute | solution.py:474
  30.3 1.6 %collective-permute-start.10 = (bf16[128,512]{1,0:T(8,128)(2,1)S(1)}, bf16[128,512]{1,0:T(8,128)(2,1)S(1)}, u32[]{:S(2)}, u32[]{:S(2)}) collective-permute-start(bf16[128,512]{1,0:T(8,128)(2,1)S(1)} %constant_dynamic-slice_fusion.1), channel_id=1, source_target_pairs={{0,8},{4,12},{8,0},{12,4},{16,24},{20,28},{24,16},{28,20},{1,9},{5... | collective-permute-start | bytes 393224 | tf_op jit(solution)/shard_map/ppermute | solution.py:474
  32.0 0.5 collective-permute-start.11
  32.5 3.5 %attend_back_kernel.1 = (f32[512,512]{1,0:T(8,128)S(1)}, bf16[128,512]{1,0:T(8,128)(2,1)S(1)}, bf16[128,512]{1,0:T(8,128)(2,1)S(1)}, bf16[128,512]{1,0:T(8,128)(...) custom-call(s32[32]{0:T(128)S(1)} %stack.143.refs_0_, ...), custom_call_target="tpu_custom_call" | custom-call | flops 1000000000 | tf_op jit(solution)/shard_map/attend_back_kernel/pallas_call | solution.py:173
  36.3 1.3 %collective-permute-done.11 = bf16[128,512]{1,0:T(8,128)(2,1)S(1)} collective-permute-done((bf16[128,512]{1,0:T(8,128)(2,1)S(1)}, bf16[128,512]{1,0:T(8,128)(2,1)S(1)}, u32[]{:S(2)}, u32[]{:S(2)}) %collective-permute-start.11) | collective-permute-done | bytes 131104 | tf_op jit(solution)/shard_map/ppermute | solution.py:474
  37.6 0.5 collective-permute-start.13
  38.1 0.4 collective-permute-start.14
  38.4 2.6 %collective-permute-start.15 = (bf16[128,512]{1,0:T(8,128)(2,1)S(1)}, bf16[128,512]{1,0:T(8,128)(2,1)S(1)}, u32[]{:S(2)}, u32[]{:S(2)}) collective-permute-start(bf16[128,512]{1,0:T(8,128)(2,1)S(1)} %get-tuple-element.165), channel_id=1, source_target_pairs={{0,12},{4,8},{8,4},{12,0},{16,28},{20,24},{24,20},{28,16},{1,13},{... | collective-permute-start | bytes 393224 | tf_op jit(solution)/shard_map/ppermute | solution.py:474
  41.2 2.7 %collective-permute-start.22 = (bf16[256,512]{1,0:T(8,128)(2,1)S(1)}, bf16[256,512]{1,0:T(8,128)(2,1)S(1)}, u32[]{:S(2)}, u32[]{:S(2)}) collective-permute-start(bf16[256,512]{1,0:T(8,128)(2,1)S(1)} %pad_maximum_fusion), channel_id=1, source_target_pairs={{0,16},{4,20},{8,24},{12,28},{16,0},{20,4},{24,8},{28,12},{1,17},{... | collective-permute-start | bytes 786440 | tf_op jit(solution)/shard_map/ppermute | solution.py:474
  43.9 1.6 %collective-permute-start.20 = (bf16[256,512]{1,0:T(8,128)(2,1)S(1)}, bf16[256,512]{1,0:T(8,128)(2,1)S(1)}, u32[]{:S(2)}, u32[]{:S(2)}) collective-permute-start(bf16[256,512]{1,0:T(8,128)(2,1)S(1)} %add_convert_fusion.2), channel_id=1, source_target_pairs={{0,2},{1,3},{2,0},{3,1},{4,6},{5,7},{6,4},{7,5},{8,10},{9,11},{10,... | collective-permute-start | bytes 786440 | tf_op jit(solution)/shard_map/ppermute | solution.py:474
  45.5 1.1 %sums_kernel.1.refs_2_ = bf16[16,512]{1,0:T(8,128)(2,1)S(1)} custom-call(bf16[128,512]{1,0:T(8,128)(2,1)S(1)} %collective-permute-done.13.refs_0_, f32[512,128]{1,0:T(8,128)S(1)} %get-tuple-element.167.refs_1_, f32[8,512]{1,0:T(8,128)S(1)} %get-tuple-element.168.refs_2_, s32[16,16]{1,0:T(8,128)S(1)} %get-tuple-element.169.refs_3_), custom_call_target="tpu_custom_call" | custom-call | flops 1000000000 | tf_op jit(solution)/shard_map/sums_kernel/pallas_call | solution.py:173
  46.6 2.3 %collective-permute-done.14 = bf16[128,512]{1,0:T(8,128)(2,1)S(1)} collective-permute-done((bf16[128,512]{1,0:T(8,128)(2,1)S(1)}, bf16[128,512]{1,0:T(8,128)(2,1)S(1)}, u32[]{:S(2)}, u32[]{:S(2)}) %collective-permute-start.14) | collective-permute-done | bytes 131104 | tf_op jit(solution)/shard_map/ppermute | solution.py:474
  49.0 1.5 %collective-permute-start.28 = (bf16[16,512]{1,0:T(8,128)(2,1)S(1)}, bf16[16,512]{1,0:T(8,128)(2,1)S(1)}, u32[]{:S(2)}, u32[]{:S(2)}) collective-permute-start(bf16[16,512]{1,0:T(8,128)(2,1)S(1)} %get-tuple-element.185), channel_id=1, source_target_pairs={{0,2},{1,3},{2,0},{3,1},{4,6},{5,7},{6,4},{7,5},{8,10},{9,11},{10,... | collective-permute-start | bytes 49160 | tf_op jit(solution)/shard_map/ppermute | solution.py:474
  50.4 0.5 collective-permute-done.15
  51.1 1.1 %attend_out_kernel.1 = (bf16[256,512]{1,0:T(8,128)(2,1)S(1)}, bf16[256,512]{1,0:T(8,128)(2,1)S(1)}) custom-call(s32[32]{0:T(128)S(1)} %stack.143.refs_0_, bf16[128,512]{1,0:T(8,128)(2,1)S(1)} %add_convert_fusion.12.refs_1_, bf16[16,512]{1,0:T(8,128)(2,1)S(1)} %sums_kernel.1.refs_2_, bf16[512,128]{1,0:T(8,128)(2,1)S(1)} %get-tuple-element.171.refs_3_, ...), custom_call_target="tpu_custom_call" | custom-call | flops 1000000000 | tf_op jit(solution)/shard_map/attend_out_kernel/pallas_call | solution.py:173
  52.2 0.6 collective-permute-start.16
  52.9 1.7 %collective-permute-done.22 = bf16[256,512]{1,0:T(8,128)(2,1)S(1)} collective-permute-done((bf16[256,512]{1,0:T(8,128)(2,1)S(1)}, bf16[256,512]{1,0:T(8,128)(2,1)S(1)}, u32[]{:S(2)}, u32[]{:S(2)}) %collective-permute-start.22) | collective-permute-done | bytes 262176 | tf_op jit(solution)/shard_map/ppermute | solution.py:474
  54.7 1.2 %collective-permute-start.25 = (bf16[128,512]{1,0:T(8,128)(2,1)S(1)}, bf16[128,512]{1,0:T(8,128)(2,1)S(1)}, u32[]{:S(2)}, u32[]{:S(2)}) collective-permute-start(bf16[128,512]{1,0:T(8,128)(2,1)S(1)} %get-tuple-element.204), channel_id=1, source_target_pairs={{0,4},{4,0},{8,12},{12,8},{16,20},{20,16},{24,28},{28,24},{1,5},{5... | collective-permute-start | bytes 393224 | tf_op jit(solution)/shard_map/ppermute | solution.py:474
  55.9 1.6 %collective-permute-start.17 = (bf16[256,512]{1,0:T(8,128)(2,1)S(1)}, bf16[256,512]{1,0:T(8,128)(2,1)S(1)}, u32[]{:S(2)}, u32[]{:S(2)}) collective-permute-start(bf16[256,512]{1,0:T(8,128)(2,1)S(1)} %add_convert_fusion.4), channel_id=1, source_target_pairs={{0,2},{1,3},{2,0},{3,1},{4,6},{5,7},{6,4},{7,5},{8,10},{9,11},{10,... | collective-permute-start | bytes 786440 | tf_op jit(solution)/shard_map/ppermute | solution.py:474
  57.7 4.6 %collective-permute-done.30 = bf16[160,512]{1,0:T(8,128)(2,1)S(1)} collective-permute-done((bf16[160,512]{1,0:T(8,128)(2,1)S(1)}, bf16[160,512]{1,0:T(8,128)(2,1)S(1)}, u32[]{:S(2)}, u32[]{:S(2)}) %collective-permute-start.30) | collective-permute-done | bytes 163872 | tf_op jit(solution)/shard_map/ppermute | solution.py:474
  62.4 0.4 collective-permute-done.17
  63.0 0.5 collective-permute-done.23
  63.6 0.9 %collective-permute-start.24 = (bf16[256,512]{1,0:T(8,128)(2,1)S(1)}, bf16[256,512]{1,0:T(8,128)(2,1)S(1)}, u32[]{:S(2)}, u32[]{:S(2)}) collective-permute-start(bf16[256,512]{1,0:T(8,128)(2,1)S(1)} %maximum_select_fusion.refs_2_), channel_id=1, source_target_pairs={{0,4},{4,0},{8,12},{12,8},{16,20},{20,16},{24,28},{28,24},{1,5},{5... | collective-permute-start | bytes 786440 | tf_op jit(solution)/shard_map/ppermute | solution.py:474
  64.6 1.2 %collective-permute-start.26 = (bf16[256,512]{1,0:T(8,128)(2,1)S(1)}, bf16[256,512]{1,0:T(8,128)(2,1)S(1)}, u32[]{:S(2)}, u32[]{:S(2)}) collective-permute-start(bf16[256,512]{1,0:T(8,128)(2,1)S(1)} %maximum_select_fusion.1.refs_4_), channel_id=1, source_target_pairs={{0,8},{4,12},{8,0},{12,4},{16,24},{20,28},{24,16},{28,20},{1,9},{5... | collective-permute-start | bytes 786440 | tf_op jit(solution)/shard_map/ppermute | solution.py:474
  65.7 1.6 %collective-permute-start.34 = (bf16[160,512]{1,0:T(8,128)(2,1)S(1)}, bf16[160,512]{1,0:T(8,128)(2,1)S(1)}, u32[]{:S(2)}, u32[]{:S(2)}) collective-permute-start(bf16[160,512]{1,0:T(8,128)(2,1)S(1)} %add_convert_fusion.9.refs_2_), channel_id=1, source_target_pairs={{0,12},{4,8},{8,4},{12,0},{16,28},{20,24},{24,20},{28,16},{1,13},{... | collective-permute-start | bytes 491528 | tf_op jit(solution)/shard_map/ppermute | solution.py:474
  67.3 1.0 %collective-permute-start.33 = (bf16[160,512]{1,0:T(8,128)(2,1)S(1)}, bf16[160,512]{1,0:T(8,128)(2,1)S(1)}, u32[]{:S(2)}, u32[]{:S(2)}) collective-permute-start(bf16[160,512]{1,0:T(8,128)(2,1)S(1)} %add_convert_fusion.9.refs_2_), channel_id=1, source_target_pairs={{0,8},{4,12},{8,0},{12,4},{16,24},{20,28},{24,16},{28,20},{1,9},{5... | collective-permute-start | bytes 491528 | tf_op jit(solution)/shard_map/ppermute | solution.py:474
  68.3 0.9 %collective-permute-start.32 = (bf16[160,512]{1,0:T(8,128)(2,1)S(1)}, bf16[160,512]{1,0:T(8,128)(2,1)S(1)}, u32[]{:S(2)}, u32[]{:S(2)}) collective-permute-start(bf16[160,512]{1,0:T(8,128)(2,1)S(1)} %add_convert_fusion.9.refs_2_), channel_id=1, source_target_pairs={{0,4},{4,0},{8,12},{12,8},{16,20},{20,16},{24,28},{28,24},{1,5},{5... | collective-permute-start | bytes 491528 | tf_op jit(solution)/shard_map/ppermute | solution.py:474
  69.2 2.6 %finish_kernel.1 = (f32[512,512]{1,0:T(8,128)}, f32[512,512]{1,0:T(8,128)}) custom-call(s32[32]{0:T(128)S(1)} %stack.143.refs_0_, bf16[256,512]{1,0:T(8,128)(2,1)S(1)} %add_convert_fusion.3.refs_1_, bf16[256,512]{1,0:T(8,128)(2,1)S(1)} %collective-permute-done.18.refs_2_, bf16[256,512]{1,0:T(8,128)(2,1)S(1)} %add_convert_fusion.1.refs_3_, ...), custom_call_target="tpu_custom_call" | custom-call | flops 2000000000 | tf_op jit(solution)/shard_map/finish_kernel/pallas_call | solution.py:173
  71.9 2.1 %collective-permute-done.24.refs_3_ = bf16[256,512]{1,0:T(8,128)(2,1)S(1)} collective-permute-done((bf16[256,512]{1,0:T(8,128)(2,1)S(1)}, bf16[256,512]{1,0:T(8,128)(2,1)S(1)}, u32[]{:S(2)}, u32[]{:S(2)}) %collective-permute-start.24) | collective-permute-done | bytes 262176 | tf_op jit(solution)/shard_map/ppermute | solution.py:474
  74.0 2.0 %widen_kernel.1 = (f32[512,512]{1,0:T(8,128)}, f32[512,512]{1,0:T(8,128)}) custom-call(s32[32]{0:T(128)S(1)} %stack.143.refs_0_, f32[512,512]{1,0:T(8,128)} %get-tuple-element.93.refs_1_, bf16[256,512]{1,0:T(8,128)(2,1)S(1)} %maximum_select_fusion.refs_2_, bf16[256,512]{1,0:T(8,128)(2,1)S(1)} %collective-permute-done.24.refs_3_, ...), custom_call_target="tpu_custom_call" | custom-call | tf_op jit(solution)/shard_map/widen_kernel/pallas_call | solution.py:173
  76.0 2.0 %collective-permute-done.34.refs_5_ = bf16[160,512]{1,0:T(8,128)(2,1)S(1)} collective-permute-done((bf16[160,512]{1,0:T(8,128)(2,1)S(1)}, bf16[160,512]{1,0:T(8,128)(2,1)S(1)}, u32[]{:S(2)}, u32[]{:S(2)}) %collective-permute-start.34) | collective-permute-done | bytes 163872 | tf_op jit(solution)/shard_map/ppermute | solution.py:474
  78.0 2.1 %collective-permute-done.33.refs_4_ = bf16[160,512]{1,0:T(8,128)(2,1)S(1)} collective-permute-done((bf16[160,512]{1,0:T(8,128)(2,1)S(1)}, bf16[160,512]{1,0:T(8,128)(2,1)S(1)}, u32[]{:S(2)}, u32[]{:S(2)}) %collective-permute-start.33) | collective-permute-done | bytes 163872 | tf_op jit(solution)/shard_map/ppermute | solution.py:474
  80.1 1.7 %unpack_kernel.1 = (f32[512,128]{1,0:T(8,128)}, f32[512,128]{1,0:T(8,128)}, f32[512,128]{1,0:T(8,128)}, f32[128,512]{1,0:T(8,128)}, f32[512]{0:T(512)}, /*index=...) custom-call(s32[32]{0:T(128)S(1)} %stack.143.refs_0_, ...), custom_call_target="tpu_custom_call" | custom-call | tf_op jit(solution)/shard_map/unpack_kernel/pallas_call | solution.py:173
  (56 shorter events, 2.4 us)
Async XLA Ops:
  0.7 8.6 %collective-permute-start.2 = (bf16[128,512]{1,0:T(8,128)(2,1)}, bf16[128,512]{1,0:T(8,128)(2,1)S(1)}, u32[]{:S(2)}, u32[]{:S(2)}) collective-permute-start(bf16[128,512]{1,0:T(8,128)(2,1)} %refs_9_.1), channel_id=1, source_target_pairs={{0,2},{1,3},{2,0},{3,1},{4,6},{5,7},{6,4},{7,5},{8,10},{9,11},{10,... | collective-permute-start | bytes 393224 | tf_op jit(solution)/shard_map/ppermute | solution.py:474
  3.8 4.9 %copy-start = (bf16[128,512]{1,0:T(8,128)(2,1)S(1)}, bf16[128,512]{1,0:T(8,128)(2,1)}, u32[]{:S(2)}) copy-start(bf16[128,512]{1,0:T(8,128)(2,1)} %refs_9_.1) | copy-start | bytes 393220
  8.6 5.0 %collective-permute-start.1 = (bf16[512,128]{1,0:T(8,128)(2,1)S(1)}, bf16[512,128]{1,0:T(8,128)(2,1)S(1)}, u32[]{:S(2)}, u32[]{:S(2)}) collective-permute-start(bf16[512,128]{1,0:T(8,128)(2,1)S(1)} %get-tuple-element.111.refs_0_.refs_1_.refs_12_), channel_id=1, source_target_pairs={{0,2},{1,3},{2,0},{3,1},{4,6},{5,7},{6,4},{7,5},{8,10},{9,11},{10,... | collective-permute-start | bytes 393224 | tf_op jit(solution)/shard_map/ppermute | solution.py:474
  8.7 5.4 %collective-permute-start.4 = (bf16[128,512]{1,0:T(8,128)(2,1)S(1)}, bf16[128,512]{1,0:T(8,128)(2,1)S(1)}, u32[]{:S(2)}, u32[]{:S(2)}) collective-permute-start(bf16[128,512]{1,0:T(8,128)(2,1)S(1)} %copy-done), channel_id=1, source_target_pairs={{0,1},{1,0},{2,3},{3,2},{4,5},{5,4},{6,7},{7,6},{8,9},{9,8},{10,11... | collective-permute-start | bytes 393224 | tf_op jit(solution)/shard_map/ppermute | solution.py:474
  8.8 5.4 %collective-permute-start = (bf16[512,128]{1,0:T(8,128)(2,1)S(1)}, bf16[512,128]{1,0:T(8,128)(2,1)S(1)}, u32[]{:S(2)}, u32[]{:S(2)}) collective-permute-start(bf16[512,128]{1,0:T(8,128)(2,1)S(1)} %get-tuple-element.111.refs_0_.refs_1_.refs_12_), channel_id=1, source_target_pairs={{0,1},{1,0},{2,3},{3,2},{4,5},{5,4},{6,7},{7,6},{8,9},{9,8},{10,11... | collective-permute-start | bytes 393224 | tf_op jit(solution)/shard_map/ppermute | solution.py:474
  13.6 1.3 %collective-permute-start.5 = (bf16[128,512]{1,0:T(8,128)(2,1)S(1)}, bf16[128,512]{1,0:T(8,128)(2,1)S(1)}, u32[]{:S(2)}, u32[]{:S(2)}) collective-permute-start(bf16[128,512]{1,0:T(8,128)(2,1)S(1)} %collective-permute-done.2.refs_1_.refs_7_), channel_id=1, source_target_pairs={{0,1},{1,0},{2,3},{3,2},{4,5},{5,4},{6,7},{7,6},{8,9},{9,8},{10,11... | collective-permute-start | bytes 393224 | tf_op jit(solution)/shard_map/ppermute | solution.py:474
  13.6 1.5 %collective-permute-start.3 = (bf16[512,128]{1,0:T(8,128)(2,1)S(1)}, bf16[512,128]{1,0:T(8,128)(2,1)S(1)}, u32[]{:S(2)}, u32[]{:S(2)}) collective-permute-start(bf16[512,128]{1,0:T(8,128)(2,1)S(1)} %collective-permute-done.1.refs_3_), channel_id=1, source_target_pairs={{0,1},{1,0},{2,3},{3,2},{4,5},{5,4},{6,7},{7,6},{8,9},{9,8},{10,11... | collective-permute-start | bytes 393224 | tf_op jit(solution)/shard_map/ppermute | solution.py:474
  18.1 1.8 %collective-permute-start.6 = (bf16[256,512]{1,0:T(8,128)(2,1)S(1)}, bf16[256,512]{1,0:T(8,128)(2,1)S(1)}, u32[]{:S(2)}, u32[]{:S(2)}) collective-permute-start(bf16[256,512]{1,0:T(8,128)(2,1)S(1)} %get-tuple-element.128), channel_id=1, source_target_pairs={{0,1},{1,0},{2,3},{3,2},{4,5},{5,4},{6,7},{7,6},{8,9},{9,8},{10,11... | collective-permute-start | bytes 786440 | tf_op jit(solution)/shard_map/ppermute | solution.py:474
  20.0 8.5 %collective-permute-start.7 = (bf16[256,512]{1,0:T(8,128)(2,1)S(1)}, bf16[256,512]{1,0:T(8,128)(2,1)S(1)}, u32[]{:S(2)}, u32[]{:S(2)}) collective-permute-start(bf16[256,512]{1,0:T(8,128)(2,1)S(1)} %add_convert_fusion.8), channel_id=1, source_target_pairs={{0,2},{1,3},{2,0},{3,1},{4,6},{5,7},{6,4},{7,5},{8,10},{9,11},{10,... | collective-permute-start | bytes 786440 | tf_op jit(solution)/shard_map/ppermute | solution.py:474
  20.4 8.2 %collective-permute-start.8 = (bf16[256,512]{1,0:T(8,128)(2,1)S(1)}, bf16[256,512]{1,0:T(8,128)(2,1)S(1)}, u32[]{:S(2)}, u32[]{:S(2)}) collective-permute-start(bf16[256,512]{1,0:T(8,128)(2,1)S(1)} %get-tuple-element.133), channel_id=1, source_target_pairs={{0,4},{4,0},{8,12},{12,8},{16,20},{20,16},{24,28},{28,24},{1,5},{5... | collective-permute-start | bytes 786440 | tf_op jit(solution)/shard_map/ppermute | solution.py:474
  22.1 7.8 %collective-permute-start.9 = (bf16[256,512]{1,0:T(8,128)(2,1)S(1)}, bf16[256,512]{1,0:T(8,128)(2,1)S(1)}, u32[]{:S(2)}, u32[]{:S(2)}) collective-permute-start(bf16[256,512]{1,0:T(8,128)(2,1)S(1)} %get-tuple-element.134), channel_id=1, source_target_pairs={{0,8},{4,12},{8,0},{12,4},{16,24},{20,28},{24,16},{28,20},{1,9},{5... | collective-permute-start | bytes 786440 | tf_op jit(solution)/shard_map/ppermute | solution.py:474
  30.0 2.5 %collective-permute-start.12 = (bf16[256,512]{1,0:T(8,128)(2,1)S(1)}, bf16[256,512]{1,0:T(8,128)(2,1)S(1)}, u32[]{:S(2)}, u32[]{:S(2)}) collective-permute-start(bf16[256,512]{1,0:T(8,128)(2,1)S(1)} %add_convert_fusion.5.refs_1_), channel_id=1, source_target_pairs={{0,1},{1,0},{2,3},{3,2},{4,5},{5,4},{6,7},{7,6},{8,9},{9,8},{10,11... | collective-permute-start | bytes 786440 | tf_op jit(solution)/shard_map/ppermute | solution.py:474
  30.3 6.0 %collective-permute-start.10 = (bf16[128,512]{1,0:T(8,128)(2,1)S(1)}, bf16[128,512]{1,0:T(8,128)(2,1)S(1)}, u32[]{:S(2)}, u32[]{:S(2)}) collective-permute-start(bf16[128,512]{1,0:T(8,128)(2,1)S(1)} %constant_dynamic-slice_fusion.1), channel_id=1, source_target_pairs={{0,8},{4,12},{8,0},{12,4},{16,24},{20,28},{24,16},{28,20},{1,9},{5... | collective-permute-start | bytes 393224 | tf_op jit(solution)/shard_map/ppermute | solution.py:474
  32.0 5.6 %collective-permute-start.11 = (bf16[128,512]{1,0:T(8,128)(2,1)S(1)}, bf16[128,512]{1,0:T(8,128)(2,1)S(1)}, u32[]{:S(2)}, u32[]{:S(2)}) collective-permute-start(bf16[128,512]{1,0:T(8,128)(2,1)S(1)} %constant_dynamic-slice_fusion), channel_id=1, source_target_pairs={{0,4},{4,0},{8,12},{12,8},{16,20},{20,16},{24,28},{28,24},{1,5},{5... | collective-permute-start | bytes 393224 | tf_op jit(solution)/shard_map/ppermute | solution.py:474
  32.5 11.4 %collective-permute-start.19 = (bf16[256,512]{1,0:T(8,128)(2,1)S(1)}, bf16[256,512]{1,0:T(8,128)(2,1)S(1)}, u32[]{:S(2)}, u32[]{:S(2)}) collective-permute-start(bf16[256,512]{1,0:T(8,128)(2,1)S(1)} %get-tuple-element.177), channel_id=1, source_target_pairs={{0,1},{1,0},{2,3},{3,2},{4,5},{5,4},{6,7},{7,6},{8,9},{9,8},{10,11... | collective-permute-start | bytes 786440 | tf_op jit(solution)/shard_map/ppermute | solution.py:474
  37.6 7.9 %collective-permute-start.13 = (bf16[128,512]{1,0:T(8,128)(2,1)S(1)}, bf16[128,512]{1,0:T(8,128)(2,1)S(1)}, u32[]{:S(2)}, u32[]{:S(2)}) collective-permute-start(bf16[128,512]{1,0:T(8,128)(2,1)S(1)} %get-tuple-element.163), channel_id=1, source_target_pairs={{0,4},{4,0},{8,12},{12,8},{16,20},{20,16},{24,28},{28,24},{1,5},{5... | collective-permute-start | bytes 393224 | tf_op jit(solution)/shard_map/ppermute | solution.py:474
  38.1 10.9 %collective-permute-start.14 = (bf16[128,512]{1,0:T(8,128)(2,1)S(1)}, bf16[128,512]{1,0:T(8,128)(2,1)S(1)}, u32[]{:S(2)}, u32[]{:S(2)}) collective-permute-start(bf16[128,512]{1,0:T(8,128)(2,1)S(1)} %get-tuple-element.164), channel_id=1, source_target_pairs={{0,8},{4,12},{8,0},{12,4},{16,24},{20,28},{24,16},{28,20},{1,9},{5... | collective-permute-start | bytes 393224 | tf_op jit(solution)/shard_map/ppermute | solution.py:474
  38.4 12.5 %collective-permute-start.15 = (bf16[128,512]{1,0:T(8,128)(2,1)S(1)}, bf16[128,512]{1,0:T(8,128)(2,1)S(1)}, u32[]{:S(2)}, u32[]{:S(2)}) collective-permute-start(bf16[128,512]{1,0:T(8,128)(2,1)S(1)} %get-tuple-element.165), channel_id=1, source_target_pairs={{0,12},{4,8},{8,4},{12,0},{16,28},{20,24},{24,20},{28,16},{1,13},{... | collective-permute-start | bytes 393224 | tf_op jit(solution)/shard_map/ppermute | solution.py:474
  41.2 13.4 %collective-permute-start.22 = (bf16[256,512]{1,0:T(8,128)(2,1)S(1)}, bf16[256,512]{1,0:T(8,128)(2,1)S(1)}, u32[]{:S(2)}, u32[]{:S(2)}) collective-permute-start(bf16[256,512]{1,0:T(8,128)(2,1)S(1)} %pad_maximum_fusion), channel_id=1, source_target_pairs={{0,16},{4,20},{8,24},{12,28},{16,0},{20,4},{24,8},{28,12},{1,17},{... | collective-permute-start | bytes 786440 | tf_op jit(solution)/shard_map/ppermute | solution.py:474
  43.9 13.6 %collective-permute-start.20 = (bf16[256,512]{1,0:T(8,128)(2,1)S(1)}, bf16[256,512]{1,0:T(8,128)(2,1)S(1)}, u32[]{:S(2)}, u32[]{:S(2)}) collective-permute-start(bf16[256,512]{1,0:T(8,128)(2,1)S(1)} %add_convert_fusion.2), channel_id=1, source_target_pairs={{0,2},{1,3},{2,0},{3,1},{4,6},{5,7},{6,4},{7,5},{8,10},{9,11},{10,... | collective-permute-start | bytes 786440 | tf_op jit(solution)/shard_map/ppermute | solution.py:474
  46.6 5.6 %collective-permute-start.29 = (bf16[16,512]{1,0:T(8,128)(2,1)S(1)}, bf16[16,512]{1,0:T(8,128)(2,1)S(1)}, u32[]{:S(2)}, u32[]{:S(2)}) collective-permute-start(bf16[16,512]{1,0:T(8,128)(2,1)S(1)} %get-tuple-element.185), channel_id=1, source_target_pairs={{0,3},{1,2},{2,1},{3,0},{4,7},{5,6},{6,5},{7,4},{8,11},{9,10},{10,... | collective-permute-start | bytes 49160 | tf_op jit(solution)/shard_map/ppermute | solution.py:474
  49.0 3.8 %collective-permute-start.28 = (bf16[16,512]{1,0:T(8,128)(2,1)S(1)}, bf16[16,512]{1,0:T(8,128)(2,1)S(1)}, u32[]{:S(2)}, u32[]{:S(2)}) collective-permute-start(bf16[16,512]{1,0:T(8,128)(2,1)S(1)} %get-tuple-element.185), channel_id=1, source_target_pairs={{0,2},{1,3},{2,0},{3,1},{4,6},{5,7},{6,4},{7,5},{8,10},{9,11},{10,... | collective-permute-start | bytes 49160 | tf_op jit(solution)/shard_map/ppermute | solution.py:474
  51.0 1.8 %collective-permute-start.27 = (bf16[16,512]{1,0:T(8,128)(2,1)S(1)}, bf16[16,512]{1,0:T(8,128)(2,1)S(1)}, u32[]{:S(2)}, u32[]{:S(2)}) collective-permute-start(bf16[16,512]{1,0:T(8,128)(2,1)S(1)} %get-tuple-element.185), channel_id=1, source_target_pairs={{0,1},{1,0},{2,3},{3,2},{4,5},{5,4},{6,7},{7,6},{8,9},{9,8},{10,11... | collective-permute-start | bytes 49160 | tf_op jit(solution)/shard_map/ppermute | solution.py:474
  52.2 3.7 %collective-permute-start.16 = (bf16[256,512]{1,0:T(8,128)(2,1)S(1)}, bf16[256,512]{1,0:T(8,128)(2,1)S(1)}, u32[]{:S(2)}, u32[]{:S(2)}) collective-permute-start(bf16[256,512]{1,0:T(8,128)(2,1)S(1)} %get-tuple-element.175), channel_id=1, source_target_pairs={{0,1},{1,0},{2,3},{3,2},{4,5},{5,4},{6,7},{7,6},{8,9},{9,8},{10,11... | collective-permute-start | bytes 786440 | tf_op jit(solution)/shard_map/ppermute | solution.py:474
  52.8 9.5 %collective-permute-start.30 = (bf16[160,512]{1,0:T(8,128)(2,1)S(1)}, bf16[160,512]{1,0:T(8,128)(2,1)S(1)}, u32[]{:S(2)}, u32[]{:S(2)}) collective-permute-start(bf16[160,512]{1,0:T(8,128)(2,1)S(1)} %pad_maximum_fusion.1), channel_id=1, source_target_pairs={{0,16},{4,20},{8,24},{12,28},{16,0},{20,4},{24,8},{28,12},{1,17},{... | collective-permute-start | bytes 491528 | tf_op jit(solution)/shard_map/ppermute | solution.py:474
  54.7 9.8 %collective-permute-start.25 = (bf16[128,512]{1,0:T(8,128)(2,1)S(1)}, bf16[128,512]{1,0:T(8,128)(2,1)S(1)}, u32[]{:S(2)}, u32[]{:S(2)}) collective-permute-start(bf16[128,512]{1,0:T(8,128)(2,1)S(1)} %get-tuple-element.204), channel_id=1, source_target_pairs={{0,4},{4,0},{8,12},{12,8},{16,20},{20,16},{24,28},{28,24},{1,5},{5... | collective-permute-start | bytes 393224 | tf_op jit(solution)/shard_map/ppermute | solution.py:474
  55.8 7.7 %collective-permute-start.23 = (bf16[128,512]{1,0:T(8,128)(2,1)S(1)}, bf16[128,512]{1,0:T(8,128)(2,1)S(1)}, u32[]{:S(2)}, u32[]{:S(2)}) collective-permute-start(bf16[128,512]{1,0:T(8,128)(2,1)S(1)} %get-tuple-element.205), channel_id=1, source_target_pairs={{0,8},{4,12},{8,0},{12,4},{16,24},{20,28},{24,16},{28,20},{1,9},{5... | collective-permute-start | bytes 393224 | tf_op jit(solution)/shard_map/ppermute | solution.py:474
  55.9 6.9 %collective-permute-start.17 = (bf16[256,512]{1,0:T(8,128)(2,1)S(1)}, bf16[256,512]{1,0:T(8,128)(2,1)S(1)}, u32[]{:S(2)}, u32[]{:S(2)}) collective-permute-start(bf16[256,512]{1,0:T(8,128)(2,1)S(1)} %add_convert_fusion.4), channel_id=1, source_target_pairs={{0,2},{1,3},{2,0},{3,1},{4,6},{5,7},{6,4},{7,5},{8,10},{9,11},{10,... | collective-permute-start | bytes 786440 | tf_op jit(solution)/shard_map/ppermute | solution.py:474
  57.6 9.7 %collective-permute-start.21 = (bf16[256,512]{1,0:T(8,128)(2,1)S(1)}, bf16[256,512]{1,0:T(8,128)(2,1)S(1)}, u32[]{:S(2)}, u32[]{:S(2)}) collective-permute-start(bf16[256,512]{1,0:T(8,128)(2,1)S(1)} %add_convert_fusion.1.refs_3_), channel_id=1, source_target_pairs={{0,1},{1,0},{2,3},{3,2},{4,5},{5,4},{6,7},{7,6},{8,9},{9,8},{10,11... | collective-permute-start | bytes 786440 | tf_op jit(solution)/shard_map/ppermute | solution.py:474
  62.3 3.4 %collective-permute-start.31 = (bf16[160,512]{1,0:T(8,128)(2,1)S(1)}, bf16[160,512]{1,0:T(8,128)(2,1)S(1)}, u32[]{:S(2)}, u32[]{:S(2)}) collective-permute-start(bf16[160,512]{1,0:T(8,128)(2,1)S(1)} %add_convert_fusion.9.refs_2_), channel_id=1, source_target_pairs={{0,1},{1,0},{2,3},{3,2},{4,5},{5,4},{6,7},{7,6},{8,9},{9,8},{10,11... | collective-permute-start | bytes 491528 | tf_op jit(solution)/shard_map/ppermute | solution.py:474
  62.9 5.4 %collective-permute-start.18 = (bf16[256,512]{1,0:T(8,128)(2,1)S(1)}, bf16[256,512]{1,0:T(8,128)(2,1)S(1)}, u32[]{:S(2)}, u32[]{:S(2)}) collective-permute-start(bf16[256,512]{1,0:T(8,128)(2,1)S(1)} %add_convert_fusion.3.refs_1_), channel_id=1, source_target_pairs={{0,1},{1,0},{2,3},{3,2},{4,5},{5,4},{6,7},{7,6},{8,9},{9,8},{10,11... | collective-permute-start | bytes 786440 | tf_op jit(solution)/shard_map/ppermute | solution.py:474
  63.6 10.4 %collective-permute-start.24 = (bf16[256,512]{1,0:T(8,128)(2,1)S(1)}, bf16[256,512]{1,0:T(8,128)(2,1)S(1)}, u32[]{:S(2)}, u32[]{:S(2)}) collective-permute-start(bf16[256,512]{1,0:T(8,128)(2,1)S(1)} %maximum_select_fusion.refs_2_), channel_id=1, source_target_pairs={{0,4},{4,0},{8,12},{12,8},{16,20},{20,16},{24,28},{28,24},{1,5},{5... | collective-permute-start | bytes 786440 | tf_op jit(solution)/shard_map/ppermute | solution.py:474
  64.6 9.4 %collective-permute-start.26 = (bf16[256,512]{1,0:T(8,128)(2,1)S(1)}, bf16[256,512]{1,0:T(8,128)(2,1)S(1)}, u32[]{:S(2)}, u32[]{:S(2)}) collective-permute-start(bf16[256,512]{1,0:T(8,128)(2,1)S(1)} %maximum_select_fusion.1.refs_4_), channel_id=1, source_target_pairs={{0,8},{4,12},{8,0},{12,4},{16,24},{20,28},{24,16},{28,20},{1,9},{5... | collective-permute-start | bytes 786440 | tf_op jit(solution)/shard_map/ppermute | solution.py:474
  65.7 12.3 %collective-permute-start.34 = (bf16[160,512]{1,0:T(8,128)(2,1)S(1)}, bf16[160,512]{1,0:T(8,128)(2,1)S(1)}, u32[]{:S(2)}, u32[]{:S(2)}) collective-permute-start(bf16[160,512]{1,0:T(8,128)(2,1)S(1)} %add_convert_fusion.9.refs_2_), channel_id=1, source_target_pairs={{0,12},{4,8},{8,4},{12,0},{16,28},{20,24},{24,20},{28,16},{1,13},{... | collective-permute-start | bytes 491528 | tf_op jit(solution)/shard_map/ppermute | solution.py:474
  67.3 12.8 %collective-permute-start.33 = (bf16[160,512]{1,0:T(8,128)(2,1)S(1)}, bf16[160,512]{1,0:T(8,128)(2,1)S(1)}, u32[]{:S(2)}, u32[]{:S(2)}) collective-permute-start(bf16[160,512]{1,0:T(8,128)(2,1)S(1)} %add_convert_fusion.9.refs_2_), channel_id=1, source_target_pairs={{0,8},{4,12},{8,0},{12,4},{16,24},{20,28},{24,16},{28,20},{1,9},{5... | collective-permute-start | bytes 491528 | tf_op jit(solution)/shard_map/ppermute | solution.py:474
  68.3 11.8 %collective-permute-start.32 = (bf16[160,512]{1,0:T(8,128)(2,1)S(1)}, bf16[160,512]{1,0:T(8,128)(2,1)S(1)}, u32[]{:S(2)}, u32[]{:S(2)}) collective-permute-start(bf16[160,512]{1,0:T(8,128)(2,1)S(1)} %add_convert_fusion.9.refs_2_), channel_id=1, source_target_pairs={{0,4},{4,0},{8,12},{12,8},{16,20},{20,16},{24,28},{28,24},{1,5},{5... | collective-permute-start | bytes 491528 | tf_op jit(solution)/shard_map/ppermute | solution.py:474

commit v6 on v5

--- a/solution.py
+++ b/solution.py
@@ -238,14 +238,15 @@
         att[rows, :] = own_lanes(dot(prob.astype(BF), v[rows, :]), heads).astype(BF)
 
 
-def fetch_kernel(after, also, *operands):
+def fetch_kernel(after, also, cot, w2, *operands):
+    grad_hidden = operands[-1]
+    grad_hidden[...] = dot_nt(cot[...], w2[...])
     for ref in operands[:-1]:
         ref.wait()
-    operands[-1][...] = jnp.zeros_like(operands[-1])
 
 
 def mlp_kernel(
-    spot, a0, a1, a2, a3, p0, p1, p2, p3, x, bo, g2, s2, w1, b1, cot, w2,
+    spot, a0, a1, a2, a3, p0, p1, p2, p3, x, bo, g2, s2, w1, b1, gh,
     mid, second, hidden, gpre, keep, send, att_all, wo_all,
 ):
     me = spot[0]
@@ -269,7 +270,7 @@
         upper = 0.5 * (1.0 + bend)
         hidden[rows, :] = (pre * upper).astype(BF)
         slope = upper + 0.5 * pre * (1.0 - bend * bend) * (curve * (1.0 + 0.134145 * square))
-        gpre[rows, :] = (dot_nt(cot[rows, :], w2[...]) * slope).astype(BF)
+        gpre[rows, :] = (gh[rows, :] * slope).astype(BF)
     send_off(mid)
     core = me % 2
     mine = pl.ds(pl.multiple_of(core * half, half), half)
@@ -368,7 +369,7 @@
     which = iota((ROWS, width), 0)
     shift = shift[0:1, :] + shift[1:2, :]
     gain = (gain[0:1, :] - row(s1) * shift) / row(g1)
-    norm1[...] = jnp.where(which == 0, gain, jnp.where(which == 1, shift, 0.0)).astype(BF)
+    norm1[...] = jnp.where(which == 6, gain, jnp.where(which == 7, shift, 0.0)).astype(BF)
     sums[0:1, :] = gain_sum
     sums[1:2, :] = shift_sum
     sums[2:3, :] = proj_sum
@@ -389,7 +390,7 @@
         ref[...] = dot(hidden[where, :], w2[...]).astype(BF)
 
 
-def sums_kernel(after, scores, sums, pidx, small, all_sums):
+def sums_kernel(after, scores, sums, pidx, small_a, small, all_sums):
     heads = scores.shape[0] // BLOCK
     at = place(iota((BLOCK, WIN), 0)) == iota((BLOCK, WIN), 1)
     fold = at.astype(F32)
@@ -415,8 +416,8 @@
         pick, by_offset, (((1,), (1,)), ((), ())), precision=EXACT, preferred_element_type=F32
     )
     all_sums[...] = jnp.zeros_like(all_sums)
-    all_sums[0:3, :] = sums[0:3, :]
-    all_sums[3:4, :] = sums[3:4, :]
+    all_sums[0:2, :] = small_a[0:2, :].astype(F32)
+    all_sums[2:6, :] = sums[0:4, :]
     all_sums[8:16, 0:slots] = offsets
     small[...] = all_sums[...].astype(BF)
 
@@ -463,11 +464,11 @@
     sums = (near[span:, :].astype(F32) + from_y[span:, :].astype(F32)) + (
         from_z[span:, :].astype(F32) + from_yz[span:, :].astype(F32)
     )
-    for at, ref in ((0, b1), (1, b2), (8, g2), (9, s2), (10, bo), (24, g1), (25, s1)):
+    for at, ref in ((0, b1), (1, b2), (2, g2), (3, s2), (4, bo), (6, g1), (7, s1)):
         ref[...] = sums[at]
-    bq[...] = sums[11, :span]
-    bv[...] = sums[11, span:2 * span]
-    rel[...] = sums[16:16 + rel.shape[0], :rel.shape[1]]
+    bq[...] = sums[5, :span]
+    bv[...] = sums[5, span:2 * span]
+    rel[...] = sums[8:8 + rel.shape[0], :rel.shape[1]]
 
 
 def swap(value, axis, bit, size):
@@ -547,19 +548,19 @@
         cost=20,
     )
     (
-        _, inputs, norm1_gain, norm1_shift, position_index, query_weight, key_weight, value_weight,
-        proj_weight, proj_bias, norm2_gain, norm2_shift, up_weight, up_bias, out_cotangent,
-        down_weight, down_bias,
+        grad_hidden, out_cotangent, down_weight, inputs, norm1_gain, norm1_shift, position_index,
+        query_weight, key_weight, value_weight, proj_weight, proj_bias, norm2_gain, norm2_shift,
+        up_weight, up_bias, down_bias,
     ) = call(
         fetch_kernel,
-        [((8, BLOCK), F32, "vmem")],
+        [((tokens, units), F32, "vmem")],
         [(att, "vmem"), (wo_x, "vmem")]
         + [
             (value, "hbm")
             for value in (
-                inputs, norm1_gain, norm1_shift, position_index, query_weight, key_weight,
-                value_weight, proj_weight, proj_bias, norm2_gain, norm2_shift, up_weight, up_bias,
-                out_cotangent, down_weight, down_bias,
+                out_cotangent, down_weight, inputs, norm1_gain, norm1_shift, position_index,
+                query_weight, key_weight, value_weight, proj_weight, proj_bias, norm2_gain,
+                norm2_shift, up_weight, up_bias, down_bias,
             )
         ],
         exports=tuple(range(2, 18)),
@@ -579,7 +580,7 @@
             (spot, "smem"), (att, "vmem"), (att_c, "vmem"), (att_x, "vmem"), (att_d, "vmem"),
             (proj_weight, "vmem"), (wo_c, "vmem"), (wo_x, "vmem"), (wo_d, "vmem"),
             (inputs, "vmem"), (proj_bias, "vmem"), (norm2_gain, "vmem"), (norm2_shift, "vmem"),
-            (up_weight, "vmem"), (up_bias, "vmem"), (out_cotangent, "vmem"), (down_weight, "vmem"),
+            (up_weight, "vmem"), (up_bias, "vmem"), (grad_hidden, "vmem"),
         ],
         scratch=[((tokens, tensor * span), BF), ((tensor * span, width), BF)],
         cost=2,
@@ -698,7 +699,9 @@
     (small_b,) = call(
         sums_kernel,
         [((16, width), BF, "vmem")],
-        [(att_parts[1], "vmem"), (scores, "vmem"), (sums, "vmem"), (position_index, "vmem")],
+        [(att_parts[1], "vmem"), (scores, "vmem"), (sums, "vmem"), (position_index, "vmem"),
+            (small_a, "vmem"),
+        ],
         scratch=[((16, width), F32)],
         cost=1,
     )
@@ -722,7 +725,7 @@
     for i in more:
         mlp_chunk = fold(mlp_chunk, swap(mlp_chunk, "dp", bits[i], dp))
     mlp_chunk = settle(mlp_chunk, 0)
-    chunk = jnp.concatenate([chunk, small_a, small_b, norm1[:8]])
+    chunk = jnp.concatenate([chunk, small_b + norm1])
     for i in more:
         chunk = fold(chunk, swap(chunk, "dp", bits[i], dp))
     chunk = settle(chunk, 1)

time: 82 us -> 81.2 us (level)
  no operation moved by 1% of the time
where the time goes in v6:
time: 81.2 us; the launch traced here: 81 us
  starting transfers between devices  29.4 us (36%)
  waiting for transfers between devices  25.7 us (32%)
  Pallas kernels  23.8 us (29%)
  other arithmetic  0.98 us (1%)
  between operations  0.94 us (1%)
    ppermute x35, starting transfers between devices, swap(): return lax.ppermute(value, axis, [(i, i ^ bit) for i in range(size)])  29.4 us
    ppermute x35, waiting for transfers between devices, swap(): return lax.ppermute(value, axis, [(i, i ^ bit) for i in range(size)])  25.7 us
    pallas_call x11, Pallas kernels, call(): pl.pallas_call(body, name=kernel.__name__, out_shape=pinned, in_specs=[pl...  23.8 us
  transfers between devices with their start and end apart: 35, of which 17 were waited for; matrix products, arithmetic and copies ran while one was open for 1% of the time, Pallas kernels for 24%

profile of v6, /device:TPU:0, one launch (start us, length us, event | category | flops | bytes accessed | tf_op | source)
XLA Modules:
  0.0 81.0 jit_solution(13127413354399475146)
XLA Ops:
  0.7 3.0 %collective-permute-start.2 = (bf16[128,512]{1,0:T(8,128)(2,1)}, bf16[128,512]{1,0:T(8,128)(2,1)S(1)}, u32[]{:S(2)}, u32[]{:S(2)}) collective-permute-start(bf16[128,512]{1,0:T(8,128)(2,1)} %refs_11_.3), channel_id=1, source_target_pairs={{0,2},{1,3},{2,0},{3,1},{4,6},{5,7},{6,4},{7,5},{8,10},{9,11},{10,... | collective-permute-start | bytes 393224 | tf_op jit(solution)/shard_map/ppermute | solution.py:475
  3.8 4.8 %attend_kernel.1 = (bf16[512,128]{1,0:T(8,128)(2,1)S(1)}, bf16[512,512]{1,0:T(8,128)(2,1)S(1)}, bf16[512,128]{1,0:T(8,128)(2,1)S(1)}, bf16[512,128]{1,0:T(8,128)...) custom-call(s32[32]{0:T(128)S(1)} %stack.143.refs_0_, bf16[512,512]{1,0:T(8,128)(2,1)} %refs_4_.3, ...), custom_call_target="tpu_custom_call" | custom-call | flops 20000000000 | tf_op jit(solution)/shard_map/attend_kernel/pallas_call | solution.py:173
  8.8 0.5 collective-permute-start
  9.3 1.9 %fetch_kernel.1 = (f32[512,512]{1,0:T(8,128)S(1)}, bf16[512,512]{1,0:T(8,128)(2,1)S(1)}, bf16[512,512]{1,0:T(8,128)(2,1)S(1)}, bf16[512,512]{1,0:T(8,128)(2,1)S(...) custom-call(bf16[512,128]{1,0:T(8,128)(2,1)S(1)} %get-tuple-element., ...), custom_call_target="tpu_custom_call" | custom-call | tf_op jit(solution)/shard_map/fetch_kernel/pallas_call | solution.py:173
  11.2 2.5 %collective-permute-done.1.refs_3_ = bf16[512,128]{1,0:T(8,128)(2,1)S(1)} collective-permute-done((bf16[512,128]{1,0:T(8,128)(2,1)S(1)}, bf16[512,128]{1,0:T(8,128)(2,1)S(1)}, u32[]{:S(2)}, u32[]{:S(2)}) %collective-permute-start.1) | collective-permute-done | bytes 131104 | tf_op jit(solution)/shard_map/ppermute | solution.py:475
  13.6 0.5 collective-permute-start.3
  14.2 0.8 %collective-permute-done.5.refs_8_ = bf16[128,512]{1,0:T(8,128)(2,1)S(1)} collective-permute-done((bf16[128,512]{1,0:T(8,128)(2,1)S(1)}, bf16[128,512]{1,0:T(8,128)(2,1)S(1)}, u32[]{:S(2)}, u32[]{:S(2)}) %collective-permute-start.5) | collective-permute-done | bytes 131104 | tf_op jit(solution)/shard_map/ppermute | solution.py:475
  15.2 2.8 %mlp_kernel.1 = (f32[512,512]{1,0:T(8,128)S(1)}, bf16[512,512]{1,0:T(8,128)(2,1)S(1)}, bf16[512,512]{1,0:T(8,128)(2,1)S(1)}, bf16[512,512]{1,0:T(8,128)(2,1)S(1)...) custom-call(s32[32]{0:T(128)S(1)} %stack.143.refs_0_, ...), custom_call_target="tpu_custom_call" | custom-call | flops 2000000000 | tf_op jit(solution)/shard_map/mlp_kernel/pallas_call | solution.py:173
  18.0 0.4 collective-permute-start.6
  18.4 1.4 %mlp_grad_kernel.1 = (bf16[256,512]{1,0:T(8,128)(2,1)S(1)}, bf16[256,512]{1,0:T(8,128)(2,1)S(1)}, bf16[256,512]{1,0:T(8,128)(2,1)S(1)}, bf16[256,512]{1,0:T(8,128)(2,1)S(1)}, bf16[8,512]{1,0:T(8,128)(2,1)S(1)}) custom-call(s32[32]{0:T(128)S(1)} %stack.143.refs_0_, bf16[512,512]{1,0:T(8,128)(2,1)S(1)} %get-tuple-element.123.refs_1_, ...), custom_call_target="tpu_custom_call" | custom-call | flops 2000000000 | tf_op jit(solution)/shard_map/mlp_grad_kernel/pallas_call | solution.py:173
  19.9 0.4 collective-permute-start.7
  20.3 1.7 %collective-permute-start.8 = (bf16[256,512]{1,0:T(8,128)(2,1)S(1)}, bf16[256,512]{1,0:T(8,128)(2,1)S(1)}, u32[]{:S(2)}, u32[]{:S(2)}) collective-permute-start(bf16[256,512]{1,0:T(8,128)(2,1)S(1)} %get-tuple-element.134), channel_id=1, source_target_pairs={{0,4},{4,0},{8,12},{12,8},{16,20},{20,16},{24,28},{28,24},{1,5},{5... | collective-permute-start | bytes 786440 | tf_op jit(solution)/shard_map/ppermute | solution.py:475
  22.0 1.6 %collective-permute-start.9 = (bf16[256,512]{1,0:T(8,128)(2,1)S(1)}, bf16[256,512]{1,0:T(8,128)(2,1)S(1)}, u32[]{:S(2)}, u32[]{:S(2)}) collective-permute-start(bf16[256,512]{1,0:T(8,128)(2,1)S(1)} %get-tuple-element.135), channel_id=1, source_target_pairs={{0,8},{4,12},{8,0},{12,4},{16,24},{20,28},{24,16},{28,20},{1,9},{5... | collective-permute-start | bytes 786440 | tf_op jit(solution)/shard_map/ppermute | solution.py:475
  23.6 1.0 %mlp_out_kernel.1 = (bf16[256,512]{1,0:T(8,128)(2,1)S(1)}, bf16[256,512]{1,0:T(8,128)(2,1)S(1)}) custom-call(s32[32]{0:T(128)S(1)} %stack.143.refs_0_, bf16[512,512]{1,0:T(8,128)(2,1)S(1)} %get-tuple-element.124.refs_2_.refs_1_, bf16[512,512]{1,0:T(8,128)(2,1)S(1)} %get-tuple-element.136.refs_2_), custom_call_target="tpu_custom_call" | custom-call | flops 1000000000 | tf_op jit(solution)/shard_map/mlp_out_kernel/pallas_call | solution.py:173
  24.6 3.8 %collective-permute-done.7 = bf16[256,512]{1,0:T(8,128)(2,1)S(1)} collective-permute-done((bf16[256,512]{1,0:T(8,128)(2,1)S(1)}, bf16[256,512]{1,0:T(8,128)(2,1)S(1)}, u32[]{:S(2)}, u32[]{:S(2)}) %collective-permute-start.7) | collective-permute-done | bytes 262176 | tf_op jit(solution)/shard_map/ppermute | solution.py:475
  28.4 1.4 %collective-permute-done.9 = bf16[256,512]{1,0:T(8,128)(2,1)S(1)} collective-permute-done((bf16[256,512]{1,0:T(8,128)(2,1)S(1)}, bf16[256,512]{1,0:T(8,128)(2,1)S(1)}, u32[]{:S(2)}, u32[]{:S(2)}) %collective-permute-start.9) | collective-permute-done | bytes 262176 | tf_op jit(solution)/shard_map/ppermute | solution.py:475
  30.2 1.7 %collective-permute-start.10 = (bf16[128,512]{1,0:T(8,128)(2,1)S(1)}, bf16[128,512]{1,0:T(8,128)(2,1)S(1)}, u32[]{:S(2)}, u32[]{:S(2)}) collective-permute-start(bf16[128,512]{1,0:T(8,128)(2,1)S(1)} %constant_dynamic-slice_fusion.1), channel_id=1, source_target_pairs={{0,8},{4,12},{8,0},{12,4},{16,24},{20,28},{24,16},{28,20},{1,9},{5... | collective-permute-start | bytes 393224 | tf_op jit(solution)/shard_map/ppermute | solution.py:475
  31.9 0.5 collective-permute-start.11
  32.4 3.4 %attend_back_kernel.1 = (f32[512,512]{1,0:T(8,128)S(1)}, bf16[128,512]{1,0:T(8,128)(2,1)S(1)}, bf16[128,512]{1,0:T(8,128)(2,1)S(1)}, bf16[128,512]{1,0:T(8,128)(...) custom-call(s32[32]{0:T(128)S(1)} %stack.143.refs_0_, ...), custom_call_target="tpu_custom_call" | custom-call | flops 1000000000 | tf_op jit(solution)/shard_map/attend_back_kernel/pallas_call | solution.py:173
  36.2 1.3 %collective-permute-done.11 = bf16[128,512]{1,0:T(8,128)(2,1)S(1)} collective-permute-done((bf16[128,512]{1,0:T(8,128)(2,1)S(1)}, bf16[128,512]{1,0:T(8,128)(2,1)S(1)}, u32[]{:S(2)}, u32[]{:S(2)}) %collective-permute-start.11) | collective-permute-done | bytes 131104 | tf_op jit(solution)/shard_map/ppermute | solution.py:475
  37.5 0.5 collective-permute-start.13
  38.0 0.4 collective-permute-start.14
  38.4 2.6 %collective-permute-start.15 = (bf16[128,512]{1,0:T(8,128)(2,1)S(1)}, bf16[128,512]{1,0:T(8,128)(2,1)S(1)}, u32[]{:S(2)}, u32[]{:S(2)}) collective-permute-start(bf16[128,512]{1,0:T(8,128)(2,1)S(1)} %get-tuple-element.167), channel_id=1, source_target_pairs={{0,12},{4,8},{8,4},{12,0},{16,28},{20,24},{24,20},{28,16},{1,13},{... | collective-permute-start | bytes 393224 | tf_op jit(solution)/shard_map/ppermute | solution.py:475
  41.1 2.6 %collective-permute-start.22 = (bf16[256,512]{1,0:T(8,128)(2,1)S(1)}, bf16[256,512]{1,0:T(8,128)(2,1)S(1)}, u32[]{:S(2)}, u32[]{:S(2)}) collective-permute-start(bf16[256,512]{1,0:T(8,128)(2,1)S(1)} %pad_maximum_fusion), channel_id=1, source_target_pairs={{0,16},{4,20},{8,24},{12,28},{16,0},{20,4},{24,8},{28,12},{1,17},{... | collective-permute-start | bytes 786440 | tf_op jit(solution)/shard_map/ppermute | solution.py:475
  43.8 1.6 %collective-permute-start.20 = (bf16[256,512]{1,0:T(8,128)(2,1)S(1)}, bf16[256,512]{1,0:T(8,128)(2,1)S(1)}, u32[]{:S(2)}, u32[]{:S(2)}) collective-permute-start(bf16[256,512]{1,0:T(8,128)(2,1)S(1)} %add_convert_fusion.2), channel_id=1, source_target_pairs={{0,2},{1,3},{2,0},{3,1},{4,6},{5,7},{6,4},{7,5},{8,10},{9,11},{10,... | collective-permute-start | bytes 786440 | tf_op jit(solution)/shard_map/ppermute | solution.py:475
  45.4 1.1 %sums_kernel.1.refs_2_ = bf16[16,512]{1,0:T(8,128)(2,1)S(1)} custom-call(bf16[128,512]{1,0:T(8,128)(2,1)S(1)} %collective-permute-done.13.refs_0_, f32[512,128]{1,0:T(8,128)S(1)} %get-tuple-element.169.refs_1_, f32[8,512]{1,0:T(8,128)S(1)} %get-tuple-element.170.refs_2_, s32[16,16]{1,0:T(8,128)S(1)} %get-tuple-element.171.refs_3_, ...), custom_call_target="tpu_custom_call" | custom-call | flops 1000000000 | tf_op jit(solution)/shard_map/sums_kernel/pallas_call | solution.py:173
  46.6 2.3 %collective-permute-done.14 = bf16[128,512]{1,0:T(8,128)(2,1)S(1)} collective-permute-done((bf16[128,512]{1,0:T(8,128)(2,1)S(1)}, bf16[128,512]{1,0:T(8,128)(2,1)S(1)}, u32[]{:S(2)}, u32[]{:S(2)}) %collective-permute-start.14) | collective-permute-done | bytes 131104 | tf_op jit(solution)/shard_map/ppermute | solution.py:475
  48.8 1.5 %collective-permute-start.28 = (bf16[16,512]{1,0:T(8,128)(2,1)S(1)}, bf16[16,512]{1,0:T(8,128)(2,1)S(1)}, u32[]{:S(2)}, u32[]{:S(2)}) collective-permute-start(bf16[16,512]{1,0:T(8,128)(2,1)S(1)} %get-tuple-element.187), channel_id=1, source_target_pairs={{0,2},{1,3},{2,0},{3,1},{4,6},{5,7},{6,4},{7,5},{8,10},{9,11},{10,... | collective-permute-start | bytes 49160 | tf_op jit(solution)/shard_map/ppermute | solution.py:475
  50.3 0.6 collective-permute-done.15
  51.0 1.1 %attend_out_kernel.1 = (bf16[256,512]{1,0:T(8,128)(2,1)S(1)}, bf16[256,512]{1,0:T(8,128)(2,1)S(1)}) custom-call(s32[32]{0:T(128)S(1)} %stack.143.refs_0_, bf16[128,512]{1,0:T(8,128)(2,1)S(1)} %add_convert_fusion.12.refs_1_, bf16[16,512]{1,0:T(8,128)(2,1)S(1)} %sums_kernel.1.refs_2_, bf16[512,128]{1,0:T(8,128)(2,1)S(1)} %get-tuple-element.174.refs_3_, ...), custom_call_target="tpu_custom_call" | custom-call | flops 1000000000 | tf_op jit(solution)/shard_map/attend_out_kernel/pallas_call | solution.py:173
  52.1 0.6 collective-permute-start.16
  52.8 1.7 %collective-permute-done.22 = bf16[256,512]{1,0:T(8,128)(2,1)S(1)} collective-permute-done((bf16[256,512]{1,0:T(8,128)(2,1)S(1)}, bf16[256,512]{1,0:T(8,128)(2,1)S(1)}, u32[]{:S(2)}, u32[]{:S(2)}) %collective-permute-start.22) | collective-permute-done | bytes 262176 | tf_op jit(solution)/shard_map/ppermute | solution.py:475
  54.6 1.1 %collective-permute-start.25 = (bf16[128,512]{1,0:T(8,128)(2,1)S(1)}, bf16[128,512]{1,0:T(8,128)(2,1)S(1)}, u32[]{:S(2)}, u32[]{:S(2)}) collective-permute-start(bf16[128,512]{1,0:T(8,128)(2,1)S(1)} %get-tuple-element.206), channel_id=1, source_target_pairs={{0,4},{4,0},{8,12},{12,8},{16,20},{20,16},{24,28},{28,24},{1,5},{5... | collective-permute-start | bytes 393224 | tf_op jit(solution)/shard_map/ppermute | solution.py:475
  55.8 1.6 %collective-permute-start.17 = (bf16[256,512]{1,0:T(8,128)(2,1)S(1)}, bf16[256,512]{1,0:T(8,128)(2,1)S(1)}, u32[]{:S(2)}, u32[]{:S(2)}) collective-permute-start(bf16[256,512]{1,0:T(8,128)(2,1)S(1)} %add_convert_fusion.4), channel_id=1, source_target_pairs={{0,2},{1,3},{2,0},{3,1},{4,6},{5,7},{6,4},{7,5},{8,10},{9,11},{10,... | collective-permute-start | bytes 786440 | tf_op jit(solution)/shard_map/ppermute | solution.py:475
  57.6 3.8 %collective-permute-done.30 = bf16[144,512]{1,0:T(8,128)(2,1)S(1)} collective-permute-done((bf16[144,512]{1,0:T(8,128)(2,1)S(1)}, bf16[144,512]{1,0:T(8,128)(2,1)S(1)}, u32[]{:S(2)}, u32[]{:S(2)}) %collective-permute-start.30) | collective-permute-done | bytes 147488 | tf_op jit(solution)/shard_map/ppermute | solution.py:475
  61.6 1.2 %collective-permute-done.17 = bf16[256,512]{1,0:T(8,128)(2,1)S(1)} collective-permute-done((bf16[256,512]{1,0:T(8,128)(2,1)S(1)}, bf16[256,512]{1,0:T(8,128)(2,1)S(1)}, u32[]{:S(2)}, u32[]{:S(2)}) %collective-permute-start.17) | collective-permute-done | bytes 262176 | tf_op jit(solution)/shard_map/ppermute | solution.py:475
  63.0 1.4 %collective-permute-start.24 = (bf16[256,512]{1,0:T(8,128)(2,1)S(1)}, bf16[256,512]{1,0:T(8,128)(2,1)S(1)}, u32[]{:S(2)}, u32[]{:S(2)}) collective-permute-start(bf16[256,512]{1,0:T(8,128)(2,1)S(1)} %maximum_select_fusion.refs_2_), channel_id=1, source_target_pairs={{0,4},{4,0},{8,12},{12,8},{16,20},{20,16},{24,28},{28,24},{1,5},{5... | collective-permute-start | bytes 786440 | tf_op jit(solution)/shard_map/ppermute | solution.py:475
  64.5 1.2 %collective-permute-start.26 = (bf16[256,512]{1,0:T(8,128)(2,1)S(1)}, bf16[256,512]{1,0:T(8,128)(2,1)S(1)}, u32[]{:S(2)}, u32[]{:S(2)}) collective-permute-start(bf16[256,512]{1,0:T(8,128)(2,1)S(1)} %maximum_select_fusion.1.refs_4_), channel_id=1, source_target_pairs={{0,8},{4,12},{8,0},{12,4},{16,24},{20,28},{24,16},{28,20},{1,9},{5... | collective-permute-start | bytes 786440 | tf_op jit(solution)/shard_map/ppermute | solution.py:475
  65.7 1.0 %collective-permute-start.34 = (bf16[144,512]{1,0:T(8,128)(2,1)S(1)}, bf16[144,512]{1,0:T(8,128)(2,1)S(1)}, u32[]{:S(2)}, u32[]{:S(2)}) collective-permute-start(bf16[144,512]{1,0:T(8,128)(2,1)S(1)} %add_convert_fusion.9.refs_2_), channel_id=1, source_target_pairs={{0,12},{4,8},{8,4},{12,0},{16,28},{20,24},{24,20},{28,16},{1,13},{... | collective-permute-start | bytes 442376 | tf_op jit(solution)/shard_map/ppermute | solution.py:475
  66.7 1.5 %collective-permute-start.33 = (bf16[144,512]{1,0:T(8,128)(2,1)S(1)}, bf16[144,512]{1,0:T(8,128)(2,1)S(1)}, u32[]{:S(2)}, u32[]{:S(2)}) collective-permute-start(bf16[144,512]{1,0:T(8,128)(2,1)S(1)} %add_convert_fusion.9.refs_2_), channel_id=1, source_target_pairs={{0,8},{4,12},{8,0},{12,4},{16,24},{20,28},{24,16},{28,20},{1,9},{5... | collective-permute-start | bytes 442376 | tf_op jit(solution)/shard_map/ppermute | solution.py:475
  68.2 1.0 %collective-permute-start.32 = (bf16[144,512]{1,0:T(8,128)(2,1)S(1)}, bf16[144,512]{1,0:T(8,128)(2,1)S(1)}, u32[]{:S(2)}, u32[]{:S(2)}) collective-permute-start(bf16[144,512]{1,0:T(8,128)(2,1)S(1)} %add_convert_fusion.9.refs_2_), channel_id=1, source_target_pairs={{0,4},{4,0},{8,12},{12,8},{16,20},{20,16},{24,28},{28,24},{1,5},{5... | collective-permute-start | bytes 442376 | tf_op jit(solution)/shard_map/ppermute | solution.py:475
  69.2 2.6 %finish_kernel.1 = (f32[512,512]{1,0:T(8,128)}, f32[512,512]{1,0:T(8,128)}) custom-call(s32[32]{0:T(128)S(1)} %stack.143.refs_0_, bf16[256,512]{1,0:T(8,128)(2,1)S(1)} %add_convert_fusion.3.refs_1_, bf16[256,512]{1,0:T(8,128)(2,1)S(1)} %collective-permute-done.18.refs_2_, bf16[256,512]{1,0:T(8,128)(2,1)S(1)} %add_convert_fusion.1.refs_3_, ...), custom_call_target="tpu_custom_call" | custom-call | flops 2000000000 | tf_op jit(solution)/shard_map/finish_kernel/pallas_call | solution.py:173
  71.8 0.4 collective-permute-done.24.refs_3_
  72.1 1.5 %collective-permute-done.26.refs_5_ = bf16[256,512]{1,0:T(8,128)(2,1)S(1)} collective-permute-done((bf16[256,512]{1,0:T(8,128)(2,1)S(1)}, bf16[256,512]{1,0:T(8,128)(2,1)S(1)}, u32[]{:S(2)}, u32[]{:S(2)}) %collective-permute-start.26) | collective-permute-done | bytes 262176 | tf_op jit(solution)/shard_map/ppermute | solution.py:475
  73.7 2.0 %widen_kernel.1 = (f32[512,512]{1,0:T(8,128)}, f32[512,512]{1,0:T(8,128)}) custom-call(s32[32]{0:T(128)S(1)} %stack.143.refs_0_, f32[512,512]{1,0:T(8,128)} %get-tuple-element.94.refs_1_, bf16[256,512]{1,0:T(8,128)(2,1)S(1)} %maximum_select_fusion.refs_2_, bf16[256,512]{1,0:T(8,128)(2,1)S(1)} %collective-permute-done.24.refs_3_, ...), custom_call_target="tpu_custom_call" | custom-call | tf_op jit(solution)/shard_map/widen_kernel/pallas_call | solution.py:173
  75.7 1.3 %collective-permute-done.34.refs_5_ = bf16[144,512]{1,0:T(8,128)(2,1)S(1)} collective-permute-done((bf16[144,512]{1,0:T(8,128)(2,1)S(1)}, bf16[144,512]{1,0:T(8,128)(2,1)S(1)}, u32[]{:S(2)}, u32[]{:S(2)}) %collective-permute-start.34) | collective-permute-done | bytes 147488 | tf_op jit(solution)/shard_map/ppermute | solution.py:475
  77.0 2.3 %collective-permute-done.33.refs_4_ = bf16[144,512]{1,0:T(8,128)(2,1)S(1)} collective-permute-done((bf16[144,512]{1,0:T(8,128)(2,1)S(1)}, bf16[144,512]{1,0:T(8,128)(2,1)S(1)}, u32[]{:S(2)}, u32[]{:S(2)}) %collective-permute-start.33) | collective-permute-done | bytes 147488 | tf_op jit(solution)/shard_map/ppermute | solution.py:475
  79.3 1.7 %unpack_kernel.1 = (f32[512,128]{1,0:T(8,128)}, f32[512,128]{1,0:T(8,128)}, f32[512,128]{1,0:T(8,128)}, f32[128,512]{1,0:T(8,128)}, f32[512]{0:T(512)}, /*index=...) custom-call(s32[32]{0:T(128)S(1)} %stack.143.refs_0_, ...), custom_call_target="tpu_custom_call" | custom-call | tf_op jit(solution)/shard_map/unpack_kernel/pallas_call | solution.py:173
  (56 shorter events, 2.4 us)
Async XLA Ops:
  0.7 8.6 %collective-permute-start.2 = (bf16[128,512]{1,0:T(8,128)(2,1)}, bf16[128,512]{1,0:T(8,128)(2,1)S(1)}, u32[]{:S(2)}, u32[]{:S(2)}) collective-permute-start(bf16[128,512]{1,0:T(8,128)(2,1)} %refs_11_.3), channel_id=1, source_target_pairs={{0,2},{1,3},{2,0},{3,1},{4,6},{5,7},{6,4},{7,5},{8,10},{9,11},{10,... | collective-permute-start | bytes 393224 | tf_op jit(solution)/shard_map/ppermute | solution.py:475
  3.8 4.9 %copy-start = (bf16[128,512]{1,0:T(8,128)(2,1)S(1)}, bf16[128,512]{1,0:T(8,128)(2,1)}, u32[]{:S(2)}) copy-start(bf16[128,512]{1,0:T(8,128)(2,1)} %refs_11_.3) | copy-start | bytes 393220
  8.6 5.0 %collective-permute-start.1 = (bf16[512,128]{1,0:T(8,128)(2,1)S(1)}, bf16[512,128]{1,0:T(8,128)(2,1)S(1)}, u32[]{:S(2)}, u32[]{:S(2)}) collective-permute-start(bf16[512,128]{1,0:T(8,128)(2,1)S(1)} %get-tuple-element.112.refs_0_.refs_1_.refs_12_), channel_id=1, source_target_pairs={{0,2},{1,3},{2,0},{3,1},{4,6},{5,7},{6,4},{7,5},{8,10},{9,11},{10,... | collective-permute-start | bytes 393224 | tf_op jit(solution)/shard_map/ppermute | solution.py:475
  8.7 5.4 %collective-permute-start.4 = (bf16[128,512]{1,0:T(8,128)(2,1)S(1)}, bf16[128,512]{1,0:T(8,128)(2,1)S(1)}, u32[]{:S(2)}, u32[]{:S(2)}) collective-permute-start(bf16[128,512]{1,0:T(8,128)(2,1)S(1)} %copy-done), channel_id=1, source_target_pairs={{0,1},{1,0},{2,3},{3,2},{4,5},{5,4},{6,7},{7,6},{8,9},{9,8},{10,11... | collective-permute-start | bytes 393224 | tf_op jit(solution)/shard_map/ppermute | solution.py:475
  8.8 5.4 %collective-permute-start = (bf16[512,128]{1,0:T(8,128)(2,1)S(1)}, bf16[512,128]{1,0:T(8,128)(2,1)S(1)}, u32[]{:S(2)}, u32[]{:S(2)}) collective-permute-start(bf16[512,128]{1,0:T(8,128)(2,1)S(1)} %get-tuple-element.112.refs_0_.refs_1_.refs_12_), channel_id=1, source_target_pairs={{0,1},{1,0},{2,3},{3,2},{4,5},{5,4},{6,7},{7,6},{8,9},{9,8},{10,11... | collective-permute-start | bytes 393224 | tf_op jit(solution)/shard_map/ppermute | solution.py:475
  13.6 1.3 %collective-permute-start.5 = (bf16[128,512]{1,0:T(8,128)(2,1)S(1)}, bf16[128,512]{1,0:T(8,128)(2,1)S(1)}, u32[]{:S(2)}, u32[]{:S(2)}) collective-permute-start(bf16[128,512]{1,0:T(8,128)(2,1)S(1)} %collective-permute-done.2.refs_1_.refs_7_), channel_id=1, source_target_pairs={{0,1},{1,0},{2,3},{3,2},{4,5},{5,4},{6,7},{7,6},{8,9},{9,8},{10,11... | collective-permute-start | bytes 393224 | tf_op jit(solution)/shard_map/ppermute | solution.py:475
  13.6 1.5 %collective-permute-start.3 = (bf16[512,128]{1,0:T(8,128)(2,1)S(1)}, bf16[512,128]{1,0:T(8,128)(2,1)S(1)}, u32[]{:S(2)}, u32[]{:S(2)}) collective-permute-start(bf16[512,128]{1,0:T(8,128)(2,1)S(1)} %collective-permute-done.1.refs_3_), channel_id=1, source_target_pairs={{0,1},{1,0},{2,3},{3,2},{4,5},{5,4},{6,7},{7,6},{8,9},{9,8},{10,11... | collective-permute-start | bytes 393224 | tf_op jit(solution)/shard_map/ppermute | solution.py:475
  18.0 1.8 %collective-permute-start.6 = (bf16[256,512]{1,0:T(8,128)(2,1)S(1)}, bf16[256,512]{1,0:T(8,128)(2,1)S(1)}, u32[]{:S(2)}, u32[]{:S(2)}) collective-permute-start(bf16[256,512]{1,0:T(8,128)(2,1)S(1)} %get-tuple-element.129), channel_id=1, source_target_pairs={{0,1},{1,0},{2,3},{3,2},{4,5},{5,4},{6,7},{7,6},{8,9},{9,8},{10,11... | collective-permute-start | bytes 786440 | tf_op jit(solution)/shard_map/ppermute | solution.py:475
  19.9 8.5 %collective-permute-start.7 = (bf16[256,512]{1,0:T(8,128)(2,1)S(1)}, bf16[256,512]{1,0:T(8,128)(2,1)S(1)}, u32[]{:S(2)}, u32[]{:S(2)}) collective-permute-start(bf16[256,512]{1,0:T(8,128)(2,1)S(1)} %add_convert_fusion.8), channel_id=1, source_target_pairs={{0,2},{1,3},{2,0},{3,1},{4,6},{5,7},{6,4},{7,5},{8,10},{9,11},{10,... | collective-permute-start | bytes 786440 | tf_op jit(solution)/shard_map/ppermute | solution.py:475
  20.3 8.2 %collective-permute-start.8 = (bf16[256,512]{1,0:T(8,128)(2,1)S(1)}, bf16[256,512]{1,0:T(8,128)(2,1)S(1)}, u32[]{:S(2)}, u32[]{:S(2)}) collective-permute-start(bf16[256,512]{1,0:T(8,128)(2,1)S(1)} %get-tuple-element.134), channel_id=1, source_target_pairs={{0,4},{4,0},{8,12},{12,8},{16,20},{20,16},{24,28},{28,24},{1,5},{5... | collective-permute-start | bytes 786440 | tf_op jit(solution)/shard_map/ppermute | solution.py:475
  22.0 7.8 %collective-permute-start.9 = (bf16[256,512]{1,0:T(8,128)(2,1)S(1)}, bf16[256,512]{1,0:T(8,128)(2,1)S(1)}, u32[]{:S(2)}, u32[]{:S(2)}) collective-permute-start(bf16[256,512]{1,0:T(8,128)(2,1)S(1)} %get-tuple-element.135), channel_id=1, source_target_pairs={{0,8},{4,12},{8,0},{12,4},{16,24},{20,28},{24,16},{28,20},{1,9},{5... | collective-permute-start | bytes 786440 | tf_op jit(solution)/shard_map/ppermute | solution.py:475
  29.9 2.5 %collective-permute-start.12 = (bf16[256,512]{1,0:T(8,128)(2,1)S(1)}, bf16[256,512]{1,0:T(8,128)(2,1)S(1)}, u32[]{:S(2)}, u32[]{:S(2)}) collective-permute-start(bf16[256,512]{1,0:T(8,128)(2,1)S(1)} %add_convert_fusion.5.refs_1_), channel_id=1, source_target_pairs={{0,1},{1,0},{2,3},{3,2},{4,5},{5,4},{6,7},{7,6},{8,9},{9,8},{10,11... | collective-permute-start | bytes 786440 | tf_op jit(solution)/shard_map/ppermute | solution.py:475
  30.2 6.0 %collective-permute-start.10 = (bf16[128,512]{1,0:T(8,128)(2,1)S(1)}, bf16[128,512]{1,0:T(8,128)(2,1)S(1)}, u32[]{:S(2)}, u32[]{:S(2)}) collective-permute-start(bf16[128,512]{1,0:T(8,128)(2,1)S(1)} %constant_dynamic-slice_fusion.1), channel_id=1, source_target_pairs={{0,8},{4,12},{8,0},{12,4},{16,24},{20,28},{24,16},{28,20},{1,9},{5... | collective-permute-start | bytes 393224 | tf_op jit(solution)/shard_map/ppermute | solution.py:475
  31.9 5.6 %collective-permute-start.11 = (bf16[128,512]{1,0:T(8,128)(2,1)S(1)}, bf16[128,512]{1,0:T(8,128)(2,1)S(1)}, u32[]{:S(2)}, u32[]{:S(2)}) collective-permute-start(bf16[128,512]{1,0:T(8,128)(2,1)S(1)} %constant_dynamic-slice_fusion), channel_id=1, source_target_pairs={{0,4},{4,0},{8,12},{12,8},{16,20},{20,16},{24,28},{28,24},{1,5},{5... | collective-permute-start | bytes 393224 | tf_op jit(solution)/shard_map/ppermute | solution.py:475
  32.4 11.4 %collective-permute-start.19 = (bf16[256,512]{1,0:T(8,128)(2,1)S(1)}, bf16[256,512]{1,0:T(8,128)(2,1)S(1)}, u32[]{:S(2)}, u32[]{:S(2)}) collective-permute-start(bf16[256,512]{1,0:T(8,128)(2,1)S(1)} %get-tuple-element.180), channel_id=1, source_target_pairs={{0,1},{1,0},{2,3},{3,2},{4,5},{5,4},{6,7},{7,6},{8,9},{9,8},{10,11... | collective-permute-start | bytes 786440 | tf_op jit(solution)/shard_map/ppermute | solution.py:475
  37.5 7.9 %collective-permute-start.13 = (bf16[128,512]{1,0:T(8,128)(2,1)S(1)}, bf16[128,512]{1,0:T(8,128)(2,1)S(1)}, u32[]{:S(2)}, u32[]{:S(2)}) collective-permute-start(bf16[128,512]{1,0:T(8,128)(2,1)S(1)} %get-tuple-element.165), channel_id=1, source_target_pairs={{0,4},{4,0},{8,12},{12,8},{16,20},{20,16},{24,28},{28,24},{1,5},{5... | collective-permute-start | bytes 393224 | tf_op jit(solution)/shard_map/ppermute | solution.py:475
  38.0 10.8 %collective-permute-start.14 = (bf16[128,512]{1,0:T(8,128)(2,1)S(1)}, bf16[128,512]{1,0:T(8,128)(2,1)S(1)}, u32[]{:S(2)}, u32[]{:S(2)}) collective-permute-start(bf16[128,512]{1,0:T(8,128)(2,1)S(1)} %get-tuple-element.166), channel_id=1, source_target_pairs={{0,8},{4,12},{8,0},{12,4},{16,24},{20,28},{24,16},{28,20},{1,9},{5... | collective-permute-start | bytes 393224 | tf_op jit(solution)/shard_map/ppermute | solution.py:475
  38.4 12.5 %collective-permute-start.15 = (bf16[128,512]{1,0:T(8,128)(2,1)S(1)}, bf16[128,512]{1,0:T(8,128)(2,1)S(1)}, u32[]{:S(2)}, u32[]{:S(2)}) collective-permute-start(bf16[128,512]{1,0:T(8,128)(2,1)S(1)} %get-tuple-element.167), channel_id=1, source_target_pairs={{0,12},{4,8},{8,4},{12,0},{16,28},{20,24},{24,20},{28,16},{1,13},{... | collective-permute-start | bytes 393224 | tf_op jit(solution)/shard_map/ppermute | solution.py:475
  41.1 13.4 %collective-permute-start.22 = (bf16[256,512]{1,0:T(8,128)(2,1)S(1)}, bf16[256,512]{1,0:T(8,128)(2,1)S(1)}, u32[]{:S(2)}, u32[]{:S(2)}) collective-permute-start(bf16[256,512]{1,0:T(8,128)(2,1)S(1)} %pad_maximum_fusion), channel_id=1, source_target_pairs={{0,16},{4,20},{8,24},{12,28},{16,0},{20,4},{24,8},{28,12},{1,17},{... | collective-permute-start | bytes 786440 | tf_op jit(solution)/shard_map/ppermute | solution.py:475
  43.8 13.6 %collective-permute-start.20 = (bf16[256,512]{1,0:T(8,128)(2,1)S(1)}, bf16[256,512]{1,0:T(8,128)(2,1)S(1)}, u32[]{:S(2)}, u32[]{:S(2)}) collective-permute-start(bf16[256,512]{1,0:T(8,128)(2,1)S(1)} %add_convert_fusion.2), channel_id=1, source_target_pairs={{0,2},{1,3},{2,0},{3,1},{4,6},{5,7},{6,4},{7,5},{8,10},{9,11},{10,... | collective-permute-start | bytes 786440 | tf_op jit(solution)/shard_map/ppermute | solution.py:475
  46.5 5.6 %collective-permute-start.29 = (bf16[16,512]{1,0:T(8,128)(2,1)S(1)}, bf16[16,512]{1,0:T(8,128)(2,1)S(1)}, u32[]{:S(2)}, u32[]{:S(2)}) collective-permute-start(bf16[16,512]{1,0:T(8,128)(2,1)S(1)} %get-tuple-element.187), channel_id=1, source_target_pairs={{0,3},{1,2},{2,1},{3,0},{4,7},{5,6},{6,5},{7,4},{8,11},{9,10},{10,... | collective-permute-start | bytes 49160 | tf_op jit(solution)/shard_map/ppermute | solution.py:475
  48.8 3.9 %collective-permute-start.28 = (bf16[16,512]{1,0:T(8,128)(2,1)S(1)}, bf16[16,512]{1,0:T(8,128)(2,1)S(1)}, u32[]{:S(2)}, u32[]{:S(2)}) collective-permute-start(bf16[16,512]{1,0:T(8,128)(2,1)S(1)} %get-tuple-element.187), channel_id=1, source_target_pairs={{0,2},{1,3},{2,0},{3,1},{4,6},{5,7},{6,4},{7,5},{8,10},{9,11},{10,... | collective-permute-start | bytes 49160 | tf_op jit(solution)/shard_map/ppermute | solution.py:475
  50.9 1.8 %collective-permute-start.27 = (bf16[16,512]{1,0:T(8,128)(2,1)S(1)}, bf16[16,512]{1,0:T(8,128)(2,1)S(1)}, u32[]{:S(2)}, u32[]{:S(2)}) collective-permute-start(bf16[16,512]{1,0:T(8,128)(2,1)S(1)} %get-tuple-element.187), channel_id=1, source_target_pairs={{0,1},{1,0},{2,3},{3,2},{4,5},{5,4},{6,7},{7,6},{8,9},{9,8},{10,11... | collective-permute-start | bytes 49160 | tf_op jit(solution)/shard_map/ppermute | solution.py:475
  52.1 3.6 %collective-permute-start.16 = (bf16[256,512]{1,0:T(8,128)(2,1)S(1)}, bf16[256,512]{1,0:T(8,128)(2,1)S(1)}, u32[]{:S(2)}, u32[]{:S(2)}) collective-permute-start(bf16[256,512]{1,0:T(8,128)(2,1)S(1)} %get-tuple-element.178), channel_id=1, source_target_pairs={{0,1},{1,0},{2,3},{3,2},{4,5},{5,4},{6,7},{7,6},{8,9},{9,8},{10,11... | collective-permute-start | bytes 786440 | tf_op jit(solution)/shard_map/ppermute | solution.py:475
  52.7 8.7 %collective-permute-start.30 = (bf16[144,512]{1,0:T(8,128)(2,1)S(1)}, bf16[144,512]{1,0:T(8,128)(2,1)S(1)}, u32[]{:S(2)}, u32[]{:S(2)}) collective-permute-start(bf16[144,512]{1,0:T(8,128)(2,1)S(1)} %pad_maximum_fusion.1), channel_id=1, source_target_pairs={{0,16},{4,20},{8,24},{12,28},{16,0},{20,4},{24,8},{28,12},{1,17},{... | collective-permute-start | bytes 442376 | tf_op jit(solution)/shard_map/ppermute | solution.py:475
  54.6 9.8 %collective-permute-start.25 = (bf16[128,512]{1,0:T(8,128)(2,1)S(1)}, bf16[128,512]{1,0:T(8,128)(2,1)S(1)}, u32[]{:S(2)}, u32[]{:S(2)}) collective-permute-start(bf16[128,512]{1,0:T(8,128)(2,1)S(1)} %get-tuple-element.206), channel_id=1, source_target_pairs={{0,4},{4,0},{8,12},{12,8},{16,20},{20,16},{24,28},{28,24},{1,5},{5... | collective-permute-start | bytes 393224 | tf_op jit(solution)/shard_map/ppermute | solution.py:475
  55.7 7.2 %collective-permute-start.23 = (bf16[128,512]{1,0:T(8,128)(2,1)S(1)}, bf16[128,512]{1,0:T(8,128)(2,1)S(1)}, u32[]{:S(2)}, u32[]{:S(2)}) collective-permute-start(bf16[128,512]{1,0:T(8,128)(2,1)S(1)} %get-tuple-element.207), channel_id=1, source_target_pairs={{0,8},{4,12},{8,0},{12,4},{16,24},{20,28},{24,16},{28,20},{1,9},{5... | collective-permute-start | bytes 393224 | tf_op jit(solution)/shard_map/ppermute | solution.py:475
  55.8 6.9 %collective-permute-start.17 = (bf16[256,512]{1,0:T(8,128)(2,1)S(1)}, bf16[256,512]{1,0:T(8,128)(2,1)S(1)}, u32[]{:S(2)}, u32[]{:S(2)}) collective-permute-start(bf16[256,512]{1,0:T(8,128)(2,1)S(1)} %add_convert_fusion.4), channel_id=1, source_target_pairs={{0,2},{1,3},{2,0},{3,1},{4,6},{5,7},{6,4},{7,5},{8,10},{9,11},{10,... | collective-permute-start | bytes 786440 | tf_op jit(solution)/shard_map/ppermute | solution.py:475
  57.5 9.1 %collective-permute-start.21 = (bf16[256,512]{1,0:T(8,128)(2,1)S(1)}, bf16[256,512]{1,0:T(8,128)(2,1)S(1)}, u32[]{:S(2)}, u32[]{:S(2)}) collective-permute-start(bf16[256,512]{1,0:T(8,128)(2,1)S(1)} %add_convert_fusion.1.refs_3_), channel_id=1, source_target_pairs={{0,1},{1,0},{2,3},{3,2},{4,5},{5,4},{6,7},{7,6},{8,9},{9,8},{10,11... | collective-permute-start | bytes 786440 | tf_op jit(solution)/shard_map/ppermute | solution.py:475
  61.5 4.2 %collective-permute-start.31 = (bf16[144,512]{1,0:T(8,128)(2,1)S(1)}, bf16[144,512]{1,0:T(8,128)(2,1)S(1)}, u32[]{:S(2)}, u32[]{:S(2)}) collective-permute-start(bf16[144,512]{1,0:T(8,128)(2,1)S(1)} %add_convert_fusion.9.refs_2_), channel_id=1, source_target_pairs={{0,1},{1,0},{2,3},{3,2},{4,5},{5,4},{6,7},{7,6},{8,9},{9,8},{10,11... | collective-permute-start | bytes 442376 | tf_op jit(solution)/shard_map/ppermute | solution.py:475
  62.8 5.4 %collective-permute-start.18 = (bf16[256,512]{1,0:T(8,128)(2,1)S(1)}, bf16[256,512]{1,0:T(8,128)(2,1)S(1)}, u32[]{:S(2)}, u32[]{:S(2)}) collective-permute-start(bf16[256,512]{1,0:T(8,128)(2,1)S(1)} %add_convert_fusion.3.refs_1_), channel_id=1, source_target_pairs={{0,1},{1,0},{2,3},{3,2},{4,5},{5,4},{6,7},{7,6},{8,9},{9,8},{10,11... | collective-permute-start | bytes 786440 | tf_op jit(solution)/shard_map/ppermute | solution.py:475
  63.0 9.2 %collective-permute-start.24 = (bf16[256,512]{1,0:T(8,128)(2,1)S(1)}, bf16[256,512]{1,0:T(8,128)(2,1)S(1)}, u32[]{:S(2)}, u32[]{:S(2)}) collective-permute-start(bf16[256,512]{1,0:T(8,128)(2,1)S(1)} %maximum_select_fusion.refs_2_), channel_id=1, source_target_pairs={{0,4},{4,0},{8,12},{12,8},{16,20},{20,16},{24,28},{28,24},{1,5},{5... | collective-permute-start | bytes 786440 | tf_op jit(solution)/shard_map/ppermute | solution.py:475
  64.5 9.2 %collective-permute-start.26 = (bf16[256,512]{1,0:T(8,128)(2,1)S(1)}, bf16[256,512]{1,0:T(8,128)(2,1)S(1)}, u32[]{:S(2)}, u32[]{:S(2)}) collective-permute-start(bf16[256,512]{1,0:T(8,128)(2,1)S(1)} %maximum_select_fusion.1.refs_4_), channel_id=1, source_target_pairs={{0,8},{4,12},{8,0},{12,4},{16,24},{20,28},{24,16},{28,20},{1,9},{5... | collective-permute-start | bytes 786440 | tf_op jit(solution)/shard_map/ppermute | solution.py:475
  65.7 11.3 %collective-permute-start.34 = (bf16[144,512]{1,0:T(8,128)(2,1)S(1)}, bf16[144,512]{1,0:T(8,128)(2,1)S(1)}, u32[]{:S(2)}, u32[]{:S(2)}) collective-permute-start(bf16[144,512]{1,0:T(8,128)(2,1)S(1)} %add_convert_fusion.9.refs_2_), channel_id=1, source_target_pairs={{0,12},{4,8},{8,4},{12,0},{16,28},{20,24},{24,20},{28,16},{1,13},{... | collective-permute-start | bytes 442376 | tf_op jit(solution)/shard_map/ppermute | solution.py:475
  66.7 12.7 %collective-permute-start.33 = (bf16[144,512]{1,0:T(8,128)(2,1)S(1)}, bf16[144,512]{1,0:T(8,128)(2,1)S(1)}, u32[]{:S(2)}, u32[]{:S(2)}) collective-permute-start(bf16[144,512]{1,0:T(8,128)(2,1)S(1)} %add_convert_fusion.9.refs_2_), channel_id=1, source_target_pairs={{0,8},{4,12},{8,0},{12,4},{16,24},{20,28},{24,16},{28,20},{1,9},{5... | collective-permute-start | bytes 442376 | tf_op jit(solution)/shard_map/ppermute | solution.py:475
  68.2 11.1 %collective-permute-start.32 = (bf16[144,512]{1,0:T(8,128)(2,1)S(1)}, bf16[144,512]{1,0:T(8,128)(2,1)S(1)}, u32[]{:S(2)}, u32[]{:S(2)}) collective-permute-start(bf16[144,512]{1,0:T(8,128)(2,1)S(1)} %add_convert_fusion.9.refs_2_), channel_id=1, source_target_pairs={{0,4},{4,0},{8,12},{12,8},{16,20},{20,16},{24,28},{28,24},{1,5},{5... | collective-permute-start | bytes 442376 | tf_op jit(solution)/shard_map/ppermute | solution.py:475

commit v7 on v6

--- a/solution.py
+++ b/solution.py
@@ -435,8 +435,7 @@
         layer_out[where, :] = mid[where, :] + mlp + row(b2)
 
 
-def widen_kernel(spot, after, near1, far1, near2, far2, *others):
-    w1, w2 = others[-2:]
+def widen_kernel(spot, after, near1, far1, near2, far2, w1, w2):
     part = near1.shape[0]
     for flag, near, far, ref in ((spot[2], near1, far1, w1), (spot[3], near2, far2, w2)):
         mine, other = halves(flag, part)
@@ -659,19 +658,6 @@
             lax.dynamic_slice(value, (stops[i, part], left), (part, width)),
         )
 
-    def settle(value, times):
-        for _ in range(times):
-            mark = swap(value, "tensor", 1, tensor)
-            value, mark = lax.optimization_barrier((value, mark))
-            marks.append(mark)
-        return value
-
-    marks = []
-
-    def scatter(value, i):
-        own, away = pick(value, i)
-        return fold(own, swap(away, "dp", bits[i], dp))
-
     def gather(own, i):
         other = swap(own, "dp", bits[i], dp)
         return jnp.where(
@@ -724,11 +710,9 @@
 
     for i in more:
         mlp_chunk = fold(mlp_chunk, swap(mlp_chunk, "dp", bits[i], dp))
-    mlp_chunk = settle(mlp_chunk, 0)
     chunk = jnp.concatenate([chunk, small_b + norm1])
     for i in more:
         chunk = fold(chunk, swap(chunk, "dp", bits[i], dp))
-    chunk = settle(chunk, 1)
     chunks = meet(chunk, chunk, chunk, chunk)
     near1 = gather(mlp_chunk[:mlp_chunk.shape[0] // 2], 1)
     near2 = gather(mlp_chunk[mlp_chunk.shape[0] // 2:], 0)
@@ -747,7 +731,7 @@
         widen_kernel,
         [((width, units), F32, "hbm"), ((units, width), F32, "hbm")],
         [(spot, "smem"), (layer_out, "keep")]
-        + [(value, "vmem") for value in [near1, far1, near2, far2] + marks],
+        + [(value, "vmem") for value in (near1, far1, near2, far2)],
     )
     vector, short = ((width,), F32, "hbm"), ((span,), F32, "hbm")
     (

time: 81.2 us -> 80.9 us (level)
  starting transfers between devices: 29.4 us -> 28.3 us
    ppermute x35 -> x34, starting transfers between devices: 29.4 us -> 28.3 us  [swap(): return lax.ppermute(value, axis, [(i, i ^ bit) for i in range(size)])]
    ppermute x35 -> x34, waiting for transfers between devices: 25.7 us -> 26.5 us  [swap(): return lax.ppermute(value, axis, [(i, i ^ bit) for i in range(size)])]
  transfers between devices with their start and end apart: 35 -> 34, of which waited for: 17 -> 15; matrix products, arithmetic and copies ran while one was open for 1% -> 1% of each run, Pallas kernels for 24% -> 24%
where the time goes in v7:
time: 80.9 us; the launch traced here: 80.8 us
  starting transfers between devices  28.3 us (35%)
  waiting for transfers between devices  26.5 us (33%)
  Pallas kernels  23.8 us (29%)
  other arithmetic  0.99 us (1%)
  between operations  0.94 us (1%)
    ppermute x34, starting transfers between devices, swap(): return lax.ppermute(value, axis, [(i, i ^ bit) for i in range(size)])  28.3 us
    ppermute x34, waiting for transfers between devices, swap(): return lax.ppermute(value, axis, [(i, i ^ bit) for i in range(size)])  26.5 us
    pallas_call x11, Pallas kernels, call(): pl.pallas_call(body, name=kernel.__name__, out_shape=pinned, in_specs=[pl...  23.8 us
  transfers between devices with their start and end apart: 34, of which 15 were waited for; matrix products, arithmetic and copies ran while one was open for 1% of the time, Pallas kernels for 24%

profile of v7, /device:TPU:0, one launch (start us, length us, event | category | flops | bytes accessed | tf_op | source)
XLA Modules:
  0.0 80.8 jit_solution(4406650997160041947)
XLA Ops:
  0.7 3.0 %collective-permute-start.2 = (bf16[128,512]{1,0:T(8,128)(2,1)}, bf16[128,512]{1,0:T(8,128)(2,1)S(1)}, u32[]{:S(2)}, u32[]{:S(2)}) collective-permute-start(bf16[128,512]{1,0:T(8,128)(2,1)} %refs_11_.3), channel_id=1, source_target_pairs={{0,2},{1,3},{2,0},{3,1},{4,6},{5,7},{6,4},{7,5},{8,10},{9,11},{10,... | collective-permute-start | bytes 393224 | tf_op jit(solution)/shard_map/ppermute | solution.py:474
  3.8 4.8 %attend_kernel.1 = (bf16[512,128]{1,0:T(8,128)(2,1)S(1)}, bf16[512,512]{1,0:T(8,128)(2,1)S(1)}, bf16[512,128]{1,0:T(8,128)(2,1)S(1)}, bf16[512,128]{1,0:T(8,128)...) custom-call(s32[32]{0:T(128)S(1)} %stack.143.refs_0_, bf16[512,512]{1,0:T(8,128)(2,1)} %refs_4_.3, ...), custom_call_target="tpu_custom_call" | custom-call | flops 20000000000 | tf_op jit(solution)/shard_map/attend_kernel/pallas_call | solution.py:173
  8.8 0.5 collective-permute-start
  9.3 1.9 %fetch_kernel.1 = (f32[512,512]{1,0:T(8,128)S(1)}, bf16[512,512]{1,0:T(8,128)(2,1)S(1)}, bf16[512,512]{1,0:T(8,128)(2,1)S(1)}, bf16[512,512]{1,0:T(8,128)(2,1)S(...) custom-call(bf16[512,128]{1,0:T(8,128)(2,1)S(1)} %get-tuple-element., ...), custom_call_target="tpu_custom_call" | custom-call | tf_op jit(solution)/shard_map/fetch_kernel/pallas_call | solution.py:173
  11.2 2.5 %collective-permute-done.1.refs_3_ = bf16[512,128]{1,0:T(8,128)(2,1)S(1)} collective-permute-done((bf16[512,128]{1,0:T(8,128)(2,1)S(1)}, bf16[512,128]{1,0:T(8,128)(2,1)S(1)}, u32[]{:S(2)}, u32[]{:S(2)}) %collective-permute-start.1) | collective-permute-done | bytes 131104 | tf_op jit(solution)/shard_map/ppermute | solution.py:474
  13.6 0.5 collective-permute-start.3
  14.2 0.8 %collective-permute-done.5.refs_8_ = bf16[128,512]{1,0:T(8,128)(2,1)S(1)} collective-permute-done((bf16[128,512]{1,0:T(8,128)(2,1)S(1)}, bf16[128,512]{1,0:T(8,128)(2,1)S(1)}, u32[]{:S(2)}, u32[]{:S(2)}) %collective-permute-start.5) | collective-permute-done | bytes 131104 | tf_op jit(solution)/shard_map/ppermute | solution.py:474
  15.0 0.2 collective-permute-done.3.refs_4_
  15.2 2.8 %mlp_kernel.1 = (f32[512,512]{1,0:T(8,128)S(1)}, bf16[512,512]{1,0:T(8,128)(2,1)S(1)}, bf16[512,512]{1,0:T(8,128)(2,1)S(1)}, bf16[512,512]{1,0:T(8,128)(2,1)S(1)...) custom-call(s32[32]{0:T(128)S(1)} %stack.143.refs_0_, ...), custom_call_target="tpu_custom_call" | custom-call | flops 2000000000 | tf_op jit(solution)/shard_map/mlp_kernel/pallas_call | solution.py:173
  18.0 0.4 collective-permute-start.6
  18.4 1.4 %mlp_grad_kernel.1 = (bf16[256,512]{1,0:T(8,128)(2,1)S(1)}, bf16[256,512]{1,0:T(8,128)(2,1)S(1)}, bf16[256,512]{1,0:T(8,128)(2,1)S(1)}, bf16[256,512]{1,0:T(8,128)(2,1)S(1)}, bf16[8,512]{1,0:T(8,128)(2,1)S(1)}) custom-call(s32[32]{0:T(128)S(1)} %stack.143.refs_0_, bf16[512,512]{1,0:T(8,128)(2,1)S(1)} %get-tuple-element.121.refs_1_, ...), custom_call_target="tpu_custom_call" | custom-call | flops 2000000000 | tf_op jit(solution)/shard_map/mlp_grad_kernel/pallas_call | solution.py:173
  19.9 0.4 collective-permute-start.7
  20.3 1.7 %collective-permute-start.8 = (bf16[256,512]{1,0:T(8,128)(2,1)S(1)}, bf16[256,512]{1,0:T(8,128)(2,1)S(1)}, u32[]{:S(2)}, u32[]{:S(2)}) collective-permute-start(bf16[256,512]{1,0:T(8,128)(2,1)S(1)} %get-tuple-element.132), channel_id=1, source_target_pairs={{0,4},{4,0},{8,12},{12,8},{16,20},{20,16},{24,28},{28,24},{1,5},{5... | collective-permute-start | bytes 786440 | tf_op jit(solution)/shard_map/ppermute | solution.py:474
  22.0 1.6 %collective-permute-start.9 = (bf16[256,512]{1,0:T(8,128)(2,1)S(1)}, bf16[256,512]{1,0:T(8,128)(2,1)S(1)}, u32[]{:S(2)}, u32[]{:S(2)}) collective-permute-start(bf16[256,512]{1,0:T(8,128)(2,1)S(1)} %get-tuple-element.133), channel_id=1, source_target_pairs={{0,8},{4,12},{8,0},{12,4},{16,24},{20,28},{24,16},{28,20},{1,9},{5... | collective-permute-start | bytes 786440 | tf_op jit(solution)/shard_map/ppermute | solution.py:474
  23.6 1.0 %mlp_out_kernel.1 = (bf16[256,512]{1,0:T(8,128)(2,1)S(1)}, bf16[256,512]{1,0:T(8,128)(2,1)S(1)}) custom-call(s32[32]{0:T(128)S(1)} %stack.143.refs_0_, bf16[512,512]{1,0:T(8,128)(2,1)S(1)} %get-tuple-element.122.refs_2_.refs_1_, bf16[512,512]{1,0:T(8,128)(2,1)S(1)} %get-tuple-element.134.refs_2_), custom_call_target="tpu_custom_call" | custom-call | flops 1000000000 | tf_op jit(solution)/shard_map/mlp_out_kernel/pallas_call | solution.py:173
  24.6 3.8 %collective-permute-done.7 = bf16[256,512]{1,0:T(8,128)(2,1)S(1)} collective-permute-done((bf16[256,512]{1,0:T(8,128)(2,1)S(1)}, bf16[256,512]{1,0:T(8,128)(2,1)S(1)}, u32[]{:S(2)}, u32[]{:S(2)}) %collective-permute-start.7) | collective-permute-done | bytes 262176 | tf_op jit(solution)/shard_map/ppermute | solution.py:474
  28.4 1.4 %collective-permute-done.9 = bf16[256,512]{1,0:T(8,128)(2,1)S(1)} collective-permute-done((bf16[256,512]{1,0:T(8,128)(2,1)S(1)}, bf16[256,512]{1,0:T(8,128)(2,1)S(1)}, u32[]{:S(2)}, u32[]{:S(2)}) %collective-permute-start.9) | collective-permute-done | bytes 262176 | tf_op jit(solution)/shard_map/ppermute | solution.py:474
  30.2 1.7 %collective-permute-start.10 = (bf16[128,512]{1,0:T(8,128)(2,1)S(1)}, bf16[128,512]{1,0:T(8,128)(2,1)S(1)}, u32[]{:S(2)}, u32[]{:S(2)}) collective-permute-start(bf16[128,512]{1,0:T(8,128)(2,1)S(1)} %constant_dynamic-slice_fusion.1), channel_id=1, source_target_pairs={{0,8},{4,12},{8,0},{12,4},{16,24},{20,28},{24,16},{28,20},{1,9},{5... | collective-permute-start | bytes 393224 | tf_op jit(solution)/shard_map/ppermute | solution.py:474
  31.9 0.5 collective-permute-start.11
  32.4 3.4 %attend_back_kernel.1 = (f32[512,512]{1,0:T(8,128)S(1)}, bf16[128,512]{1,0:T(8,128)(2,1)S(1)}, bf16[128,512]{1,0:T(8,128)(2,1)S(1)}, bf16[128,512]{1,0:T(8,128)(...) custom-call(s32[32]{0:T(128)S(1)} %stack.143.refs_0_, ...), custom_call_target="tpu_custom_call" | custom-call | flops 1000000000 | tf_op jit(solution)/shard_map/attend_back_kernel/pallas_call | solution.py:173
  35.8 0.3 collective-permute-done.10
  36.2 1.3 %collective-permute-done.11 = bf16[128,512]{1,0:T(8,128)(2,1)S(1)} collective-permute-done((bf16[128,512]{1,0:T(8,128)(2,1)S(1)}, bf16[128,512]{1,0:T(8,128)(2,1)S(1)}, u32[]{:S(2)}, u32[]{:S(2)}) %collective-permute-start.11) | collective-permute-done | bytes 131104 | tf_op jit(solution)/shard_map/ppermute | solution.py:474
  37.5 0.5 collective-permute-start.13
  38.0 0.4 collective-permute-start.14
  38.4 2.6 %collective-permute-start.15 = (bf16[128,512]{1,0:T(8,128)(2,1)S(1)}, bf16[128,512]{1,0:T(8,128)(2,1)S(1)}, u32[]{:S(2)}, u32[]{:S(2)}) collective-permute-start(bf16[128,512]{1,0:T(8,128)(2,1)S(1)} %get-tuple-element.165), channel_id=1, source_target_pairs={{0,12},{4,8},{8,4},{12,0},{16,28},{20,24},{24,20},{28,16},{1,13},{... | collective-permute-start | bytes 393224 | tf_op jit(solution)/shard_map/ppermute | solution.py:474
  41.1 2.6 %collective-permute-start.22 = (bf16[256,512]{1,0:T(8,128)(2,1)S(1)}, bf16[256,512]{1,0:T(8,128)(2,1)S(1)}, u32[]{:S(2)}, u32[]{:S(2)}) collective-permute-start(bf16[256,512]{1,0:T(8,128)(2,1)S(1)} %pad_maximum_fusion), channel_id=1, source_target_pairs={{0,16},{4,20},{8,24},{12,28},{16,0},{20,4},{24,8},{28,12},{1,17},{... | collective-permute-start | bytes 786440 | tf_op jit(solution)/shard_map/ppermute | solution.py:474
  43.8 1.6 %collective-permute-start.20 = (bf16[256,512]{1,0:T(8,128)(2,1)S(1)}, bf16[256,512]{1,0:T(8,128)(2,1)S(1)}, u32[]{:S(2)}, u32[]{:S(2)}) collective-permute-start(bf16[256,512]{1,0:T(8,128)(2,1)S(1)} %add_convert_fusion.2), channel_id=1, source_target_pairs={{0,2},{1,3},{2,0},{3,1},{4,6},{5,7},{6,4},{7,5},{8,10},{9,11},{10,... | collective-permute-start | bytes 786440 | tf_op jit(solution)/shard_map/ppermute | solution.py:474
  45.4 1.1 %sums_kernel.1.refs_2_ = bf16[16,512]{1,0:T(8,128)(2,1)S(1)} custom-call(bf16[128,512]{1,0:T(8,128)(2,1)S(1)} %collective-permute-done.13.refs_0_, f32[512,128]{1,0:T(8,128)S(1)} %get-tuple-element.167.refs_1_, f32[8,512]{1,0:T(8,128)S(1)} %get-tuple-element.168.refs_2_, s32[16,16]{1,0:T(8,128)S(1)} %get-tuple-element.169.refs_3_, ...), custom_call_target="tpu_custom_call" | custom-call | flops 1000000000 | tf_op jit(solution)/shard_map/sums_kernel/pallas_call | solution.py:173
  46.6 2.3 %collective-permute-done.14 = bf16[128,512]{1,0:T(8,128)(2,1)S(1)} collective-permute-done((bf16[128,512]{1,0:T(8,128)(2,1)S(1)}, bf16[128,512]{1,0:T(8,128)(2,1)S(1)}, u32[]{:S(2)}, u32[]{:S(2)}) %collective-permute-start.14) | collective-permute-done | bytes 131104 | tf_op jit(solution)/shard_map/ppermute | solution.py:474
  48.8 1.5 %collective-permute-start.28 = (bf16[16,512]{1,0:T(8,128)(2,1)S(1)}, bf16[16,512]{1,0:T(8,128)(2,1)S(1)}, u32[]{:S(2)}, u32[]{:S(2)}) collective-permute-start(bf16[16,512]{1,0:T(8,128)(2,1)S(1)} %get-tuple-element.186), channel_id=1, source_target_pairs={{0,2},{1,3},{2,0},{3,1},{4,6},{5,7},{6,4},{7,5},{8,10},{9,11},{10,... | collective-permute-start | bytes 49160 | tf_op jit(solution)/shard_map/ppermute | solution.py:474
  50.3 0.6 collective-permute-done.15
  51.0 1.1 %attend_out_kernel.1 = (bf16[256,512]{1,0:T(8,128)(2,1)S(1)}, bf16[256,512]{1,0:T(8,128)(2,1)S(1)}) custom-call(s32[32]{0:T(128)S(1)} %stack.143.refs_0_, bf16[128,512]{1,0:T(8,128)(2,1)S(1)} %add_convert_fusion.12.refs_1_, bf16[16,512]{1,0:T(8,128)(2,1)S(1)} %sums_kernel.1.refs_2_, bf16[512,128]{1,0:T(8,128)(2,1)S(1)} %get-tuple-element.172.refs_3_, ...), custom_call_target="tpu_custom_call" | custom-call | flops 1000000000 | tf_op jit(solution)/shard_map/attend_out_kernel/pallas_call | solution.py:173
  52.1 0.6 collective-permute-start.16
  52.8 1.7 %collective-permute-done.22 = bf16[256,512]{1,0:T(8,128)(2,1)S(1)} collective-permute-done((bf16[256,512]{1,0:T(8,128)(2,1)S(1)}, bf16[256,512]{1,0:T(8,128)(2,1)S(1)}, u32[]{:S(2)}, u32[]{:S(2)}) %collective-permute-start.22) | collective-permute-done | bytes 262176 | tf_op jit(solution)/shard_map/ppermute | solution.py:474
  54.6 1.1 %collective-permute-start.25 = (bf16[128,512]{1,0:T(8,128)(2,1)S(1)}, bf16[128,512]{1,0:T(8,128)(2,1)S(1)}, u32[]{:S(2)}, u32[]{:S(2)}) collective-permute-start(bf16[128,512]{1,0:T(8,128)(2,1)S(1)} %get-tuple-element.202), channel_id=1, source_target_pairs={{0,4},{4,0},{8,12},{12,8},{16,20},{20,16},{24,28},{28,24},{1,5},{5... | collective-permute-start | bytes 393224 | tf_op jit(solution)/shard_map/ppermute | solution.py:474
  55.8 1.6 %collective-permute-start.17 = (bf16[256,512]{1,0:T(8,128)(2,1)S(1)}, bf16[256,512]{1,0:T(8,128)(2,1)S(1)}, u32[]{:S(2)}, u32[]{:S(2)}) collective-permute-start(bf16[256,512]{1,0:T(8,128)(2,1)S(1)} %add_convert_fusion.4), channel_id=1, source_target_pairs={{0,2},{1,3},{2,0},{3,1},{4,6},{5,7},{6,4},{7,5},{8,10},{9,11},{10,... | collective-permute-start | bytes 786440 | tf_op jit(solution)/shard_map/ppermute | solution.py:474
  57.6 5.1 %collective-permute-done.23 = bf16[128,512]{1,0:T(8,128)(2,1)S(1)} collective-permute-done((bf16[128,512]{1,0:T(8,128)(2,1)S(1)}, bf16[128,512]{1,0:T(8,128)(2,1)S(1)}, u32[]{:S(2)}, u32[]{:S(2)}) %collective-permute-start.23) | collective-permute-done | bytes 131104 | tf_op jit(solution)/shard_map/ppermute | solution.py:474
  62.8 0.9 %collective-permute-start.24 = (bf16[256,512]{1,0:T(8,128)(2,1)S(1)}, bf16[256,512]{1,0:T(8,128)(2,1)S(1)}, u32[]{:S(2)}, u32[]{:S(2)}) collective-permute-start(bf16[256,512]{1,0:T(8,128)(2,1)S(1)} %maximum_select_fusion.refs_2_), channel_id=1, source_target_pairs={{0,4},{4,0},{8,12},{12,8},{16,20},{20,16},{24,28},{28,24},{1,5},{5... | collective-permute-start | bytes 786440 | tf_op jit(solution)/shard_map/ppermute | solution.py:474
  64.0 0.6 collective-permute-start.26
  64.6 2.1 %collective-permute-start.33 = (bf16[144,512]{1,0:T(8,128)(2,1)S(1)}, bf16[144,512]{1,0:T(8,128)(2,1)S(1)}, u32[]{:S(2)}, u32[]{:S(2)}) collective-permute-start(bf16[144,512]{1,0:T(8,128)(2,1)S(1)} %add_convert_fusion.9.refs_2_), channel_id=1, source_target_pairs={{0,12},{4,8},{8,4},{12,0},{16,28},{20,24},{24,20},{28,16},{1,13},{... | collective-permute-start | bytes 442376 | tf_op jit(solution)/shard_map/ppermute | solution.py:474
  66.8 0.3 collective-permute-start.32
  67.1 1.1 %collective-permute-start.31 = (bf16[144,512]{1,0:T(8,128)(2,1)S(1)}, bf16[144,512]{1,0:T(8,128)(2,1)S(1)}, u32[]{:S(2)}, u32[]{:S(2)}) collective-permute-start(bf16[144,512]{1,0:T(8,128)(2,1)S(1)} %add_convert_fusion.9.refs_2_), channel_id=1, source_target_pairs={{0,4},{4,0},{8,12},{12,8},{16,20},{20,16},{24,28},{28,24},{1,5},{5... | collective-permute-start | bytes 442376 | tf_op jit(solution)/shard_map/ppermute | solution.py:474
  68.2 2.6 %finish_kernel.1 = (f32[512,512]{1,0:T(8,128)}, f32[512,512]{1,0:T(8,128)}) custom-call(s32[32]{0:T(128)S(1)} %stack.143.refs_0_, bf16[256,512]{1,0:T(8,128)(2,1)S(1)} %add_convert_fusion.3.refs_1_, bf16[256,512]{1,0:T(8,128)(2,1)S(1)} %collective-permute-done.18.refs_2_, bf16[256,512]{1,0:T(8,128)(2,1)S(1)} %add_convert_fusion.1.refs_3_, ...), custom_call_target="tpu_custom_call" | custom-call | flops 2000000000 | tf_op jit(solution)/shard_map/finish_kernel/pallas_call | solution.py:173
  70.8 2.3 %collective-permute-done.26.refs_5_ = bf16[256,512]{1,0:T(8,128)(2,1)S(1)} collective-permute-done((bf16[256,512]{1,0:T(8,128)(2,1)S(1)}, bf16[256,512]{1,0:T(8,128)(2,1)S(1)}, u32[]{:S(2)}, u32[]{:S(2)}) %collective-permute-start.26) | collective-permute-done | bytes 262176 | tf_op jit(solution)/shard_map/ppermute | solution.py:474
  73.1 2.0 %widen_kernel.1 = (f32[512,512]{1,0:T(8,128)}, f32[512,512]{1,0:T(8,128)}) custom-call(s32[32]{0:T(128)S(1)} %stack.143.refs_0_, f32[512,512]{1,0:T(8,128)} %get-tuple-element.92.refs_1_, bf16[256,512]{1,0:T(8,128)(2,1)S(1)} %maximum_select_fusion.refs_2_, bf16[256,512]{1,0:T(8,128)(2,1)S(1)} %collective-permute-done.24.refs_3_, ...), custom_call_target="tpu_custom_call" | custom-call | tf_op jit(solution)/shard_map/widen_kernel/pallas_call | solution.py:173
  75.1 1.8 %collective-permute-done.33.refs_5_ = bf16[144,512]{1,0:T(8,128)(2,1)S(1)} collective-permute-done((bf16[144,512]{1,0:T(8,128)(2,1)S(1)}, bf16[144,512]{1,0:T(8,128)(2,1)S(1)}, u32[]{:S(2)}, u32[]{:S(2)}) %collective-permute-start.33) | collective-permute-done | bytes 147488 | tf_op jit(solution)/shard_map/ppermute | solution.py:474
  76.9 2.2 %collective-permute-done.32.refs_4_ = bf16[144,512]{1,0:T(8,128)(2,1)S(1)} collective-permute-done((bf16[144,512]{1,0:T(8,128)(2,1)S(1)}, bf16[144,512]{1,0:T(8,128)(2,1)S(1)}, u32[]{:S(2)}, u32[]{:S(2)}) %collective-permute-start.32) | collective-permute-done | bytes 147488 | tf_op jit(solution)/shard_map/ppermute | solution.py:474
  79.1 1.7 %unpack_kernel.1 = (f32[512,128]{1,0:T(8,128)}, f32[512,128]{1,0:T(8,128)}, f32[512,128]{1,0:T(8,128)}, f32[128,512]{1,0:T(8,128)}, f32[512]{0:T(512)}, /*index=...) custom-call(s32[32]{0:T(128)S(1)} %stack.143.refs_0_, ...), custom_call_target="tpu_custom_call" | custom-call | tf_op jit(solution)/shard_map/unpack_kernel/pallas_call | solution.py:173
  (54 shorter events, 1.8 us)
Async XLA Ops:
  0.7 8.6 %collective-permute-start.2 = (bf16[128,512]{1,0:T(8,128)(2,1)}, bf16[128,512]{1,0:T(8,128)(2,1)S(1)}, u32[]{:S(2)}, u32[]{:S(2)}) collective-permute-start(bf16[128,512]{1,0:T(8,128)(2,1)} %refs_11_.3), channel_id=1, source_target_pairs={{0,2},{1,3},{2,0},{3,1},{4,6},{5,7},{6,4},{7,5},{8,10},{9,11},{10,... | collective-permute-start | bytes 393224 | tf_op jit(solution)/shard_map/ppermute | solution.py:474
  3.8 4.9 %copy-start = (bf16[128,512]{1,0:T(8,128)(2,1)S(1)}, bf16[128,512]{1,0:T(8,128)(2,1)}, u32[]{:S(2)}) copy-start(bf16[128,512]{1,0:T(8,128)(2,1)} %refs_11_.3) | copy-start | bytes 393220
  8.6 5.0 %collective-permute-start.1 = (bf16[512,128]{1,0:T(8,128)(2,1)S(1)}, bf16[512,128]{1,0:T(8,128)(2,1)S(1)}, u32[]{:S(2)}, u32[]{:S(2)}) collective-permute-start(bf16[512,128]{1,0:T(8,128)(2,1)S(1)} %get-tuple-element.110.refs_0_.refs_1_.refs_12_), channel_id=1, source_target_pairs={{0,2},{1,3},{2,0},{3,1},{4,6},{5,7},{6,4},{7,5},{8,10},{9,11},{10,... | collective-permute-start | bytes 393224 | tf_op jit(solution)/shard_map/ppermute | solution.py:474
  8.7 5.4 %collective-permute-start.4 = (bf16[128,512]{1,0:T(8,128)(2,1)S(1)}, bf16[128,512]{1,0:T(8,128)(2,1)S(1)}, u32[]{:S(2)}, u32[]{:S(2)}) collective-permute-start(bf16[128,512]{1,0:T(8,128)(2,1)S(1)} %copy-done), channel_id=1, source_target_pairs={{0,1},{1,0},{2,3},{3,2},{4,5},{5,4},{6,7},{7,6},{8,9},{9,8},{10,11... | collective-permute-start | bytes 393224 | tf_op jit(solution)/shard_map/ppermute | solution.py:474
  8.8 5.4 %collective-permute-start = (bf16[512,128]{1,0:T(8,128)(2,1)S(1)}, bf16[512,128]{1,0:T(8,128)(2,1)S(1)}, u32[]{:S(2)}, u32[]{:S(2)}) collective-permute-start(bf16[512,128]{1,0:T(8,128)(2,1)S(1)} %get-tuple-element.110.refs_0_.refs_1_.refs_12_), channel_id=1, source_target_pairs={{0,1},{1,0},{2,3},{3,2},{4,5},{5,4},{6,7},{7,6},{8,9},{9,8},{10,11... | collective-permute-start | bytes 393224 | tf_op jit(solution)/shard_map/ppermute | solution.py:474
  13.6 1.3 %collective-permute-start.5 = (bf16[128,512]{1,0:T(8,128)(2,1)S(1)}, bf16[128,512]{1,0:T(8,128)(2,1)S(1)}, u32[]{:S(2)}, u32[]{:S(2)}) collective-permute-start(bf16[128,512]{1,0:T(8,128)(2,1)S(1)} %collective-permute-done.2.refs_1_.refs_7_), channel_id=1, source_target_pairs={{0,1},{1,0},{2,3},{3,2},{4,5},{5,4},{6,7},{7,6},{8,9},{9,8},{10,11... | collective-permute-start | bytes 393224 | tf_op jit(solution)/shard_map/ppermute | solution.py:474
  13.6 1.5 %collective-permute-start.3 = (bf16[512,128]{1,0:T(8,128)(2,1)S(1)}, bf16[512,128]{1,0:T(8,128)(2,1)S(1)}, u32[]{:S(2)}, u32[]{:S(2)}) collective-permute-start(bf16[512,128]{1,0:T(8,128)(2,1)S(1)} %collective-permute-done.1.refs_3_), channel_id=1, source_target_pairs={{0,1},{1,0},{2,3},{3,2},{4,5},{5,4},{6,7},{7,6},{8,9},{9,8},{10,11... | collective-permute-start | bytes 393224 | tf_op jit(solution)/shard_map/ppermute | solution.py:474
  18.0 1.8 %collective-permute-start.6 = (bf16[256,512]{1,0:T(8,128)(2,1)S(1)}, bf16[256,512]{1,0:T(8,128)(2,1)S(1)}, u32[]{:S(2)}, u32[]{:S(2)}) collective-permute-start(bf16[256,512]{1,0:T(8,128)(2,1)S(1)} %get-tuple-element.127), channel_id=1, source_target_pairs={{0,1},{1,0},{2,3},{3,2},{4,5},{5,4},{6,7},{7,6},{8,9},{9,8},{10,11... | collective-permute-start | bytes 786440 | tf_op jit(solution)/shard_map/ppermute | solution.py:474
  19.9 8.5 %collective-permute-start.7 = (bf16[256,512]{1,0:T(8,128)(2,1)S(1)}, bf16[256,512]{1,0:T(8,128)(2,1)S(1)}, u32[]{:S(2)}, u32[]{:S(2)}) collective-permute-start(bf16[256,512]{1,0:T(8,128)(2,1)S(1)} %add_convert_fusion.8), channel_id=1, source_target_pairs={{0,2},{1,3},{2,0},{3,1},{4,6},{5,7},{6,4},{7,5},{8,10},{9,11},{10,... | collective-permute-start | bytes 786440 | tf_op jit(solution)/shard_map/ppermute | solution.py:474
  20.3 8.2 %collective-permute-start.8 = (bf16[256,512]{1,0:T(8,128)(2,1)S(1)}, bf16[256,512]{1,0:T(8,128)(2,1)S(1)}, u32[]{:S(2)}, u32[]{:S(2)}) collective-permute-start(bf16[256,512]{1,0:T(8,128)(2,1)S(1)} %get-tuple-element.132), channel_id=1, source_target_pairs={{0,4},{4,0},{8,12},{12,8},{16,20},{20,16},{24,28},{28,24},{1,5},{5... | collective-permute-start | bytes 786440 | tf_op jit(solution)/shard_map/ppermute | solution.py:474
  22.0 7.8 %collective-permute-start.9 = (bf16[256,512]{1,0:T(8,128)(2,1)S(1)}, bf16[256,512]{1,0:T(8,128)(2,1)S(1)}, u32[]{:S(2)}, u32[]{:S(2)}) collective-permute-start(bf16[256,512]{1,0:T(8,128)(2,1)S(1)} %get-tuple-element.133), channel_id=1, source_target_pairs={{0,8},{4,12},{8,0},{12,4},{16,24},{20,28},{24,16},{28,20},{1,9},{5... | collective-permute-start | bytes 786440 | tf_op jit(solution)/shard_map/ppermute | solution.py:474
  29.9 2.5 %collective-permute-start.12 = (bf16[256,512]{1,0:T(8,128)(2,1)S(1)}, bf16[256,512]{1,0:T(8,128)(2,1)S(1)}, u32[]{:S(2)}, u32[]{:S(2)}) collective-permute-start(bf16[256,512]{1,0:T(8,128)(2,1)S(1)} %add_convert_fusion.5.refs_1_), channel_id=1, source_target_pairs={{0,1},{1,0},{2,3},{3,2},{4,5},{5,4},{6,7},{7,6},{8,9},{9,8},{10,11... | collective-permute-start | bytes 786440 | tf_op jit(solution)/shard_map/ppermute | solution.py:474
  30.2 6.0 %collective-permute-start.10 = (bf16[128,512]{1,0:T(8,128)(2,1)S(1)}, bf16[128,512]{1,0:T(8,128)(2,1)S(1)}, u32[]{:S(2)}, u32[]{:S(2)}) collective-permute-start(bf16[128,512]{1,0:T(8,128)(2,1)S(1)} %constant_dynamic-slice_fusion.1), channel_id=1, source_target_pairs={{0,8},{4,12},{8,0},{12,4},{16,24},{20,28},{24,16},{28,20},{1,9},{5... | collective-permute-start | bytes 393224 | tf_op jit(solution)/shard_map/ppermute | solution.py:474
  31.9 5.6 %collective-permute-start.11 = (bf16[128,512]{1,0:T(8,128)(2,1)S(1)}, bf16[128,512]{1,0:T(8,128)(2,1)S(1)}, u32[]{:S(2)}, u32[]{:S(2)}) collective-permute-start(bf16[128,512]{1,0:T(8,128)(2,1)S(1)} %constant_dynamic-slice_fusion), channel_id=1, source_target_pairs={{0,4},{4,0},{8,12},{12,8},{16,20},{20,16},{24,28},{28,24},{1,5},{5... | collective-permute-start | bytes 393224 | tf_op jit(solution)/shard_map/ppermute | solution.py:474
  32.4 11.4 %collective-permute-start.19 = (bf16[256,512]{1,0:T(8,128)(2,1)S(1)}, bf16[256,512]{1,0:T(8,128)(2,1)S(1)}, u32[]{:S(2)}, u32[]{:S(2)}) collective-permute-start(bf16[256,512]{1,0:T(8,128)(2,1)S(1)} %get-tuple-element.178), channel_id=1, source_target_pairs={{0,1},{1,0},{2,3},{3,2},{4,5},{5,4},{6,7},{7,6},{8,9},{9,8},{10,11... | collective-permute-start | bytes 786440 | tf_op jit(solution)/shard_map/ppermute | solution.py:474
  37.5 7.9 %collective-permute-start.13 = (bf16[128,512]{1,0:T(8,128)(2,1)S(1)}, bf16[128,512]{1,0:T(8,128)(2,1)S(1)}, u32[]{:S(2)}, u32[]{:S(2)}) collective-permute-start(bf16[128,512]{1,0:T(8,128)(2,1)S(1)} %get-tuple-element.163), channel_id=1, source_target_pairs={{0,4},{4,0},{8,12},{12,8},{16,20},{20,16},{24,28},{28,24},{1,5},{5... | collective-permute-start | bytes 393224 | tf_op jit(solution)/shard_map/ppermute | solution.py:474
  38.0 10.8 %collective-permute-start.14 = (bf16[128,512]{1,0:T(8,128)(2,1)S(1)}, bf16[128,512]{1,0:T(8,128)(2,1)S(1)}, u32[]{:S(2)}, u32[]{:S(2)}) collective-permute-start(bf16[128,512]{1,0:T(8,128)(2,1)S(1)} %get-tuple-element.164), channel_id=1, source_target_pairs={{0,8},{4,12},{8,0},{12,4},{16,24},{20,28},{24,16},{28,20},{1,9},{5... | collective-permute-start | bytes 393224 | tf_op jit(solution)/shard_map/ppermute | solution.py:474
  38.4 12.5 %collective-permute-start.15 = (bf16[128,512]{1,0:T(8,128)(2,1)S(1)}, bf16[128,512]{1,0:T(8,128)(2,1)S(1)}, u32[]{:S(2)}, u32[]{:S(2)}) collective-permute-start(bf16[128,512]{1,0:T(8,128)(2,1)S(1)} %get-tuple-element.165), channel_id=1, source_target_pairs={{0,12},{4,8},{8,4},{12,0},{16,28},{20,24},{24,20},{28,16},{1,13},{... | collective-permute-start | bytes 393224 | tf_op jit(solution)/shard_map/ppermute | solution.py:474
  41.1 13.4 %collective-permute-start.22 = (bf16[256,512]{1,0:T(8,128)(2,1)S(1)}, bf16[256,512]{1,0:T(8,128)(2,1)S(1)}, u32[]{:S(2)}, u32[]{:S(2)}) collective-permute-start(bf16[256,512]{1,0:T(8,128)(2,1)S(1)} %pad_maximum_fusion), channel_id=1, source_target_pairs={{0,16},{4,20},{8,24},{12,28},{16,0},{20,4},{24,8},{28,12},{1,17},{... | collective-permute-start | bytes 786440 | tf_op jit(solution)/shard_map/ppermute | solution.py:474
  43.8 13.6 %collective-permute-start.20 = (bf16[256,512]{1,0:T(8,128)(2,1)S(1)}, bf16[256,512]{1,0:T(8,128)(2,1)S(1)}, u32[]{:S(2)}, u32[]{:S(2)}) collective-permute-start(bf16[256,512]{1,0:T(8,128)(2,1)S(1)} %add_convert_fusion.2), channel_id=1, source_target_pairs={{0,2},{1,3},{2,0},{3,1},{4,6},{5,7},{6,4},{7,5},{8,10},{9,11},{10,... | collective-permute-start | bytes 786440 | tf_op jit(solution)/shard_map/ppermute | solution.py:474
  46.6 5.5 %collective-permute-start.29 = (bf16[16,512]{1,0:T(8,128)(2,1)S(1)}, bf16[16,512]{1,0:T(8,128)(2,1)S(1)}, u32[]{:S(2)}, u32[]{:S(2)}) collective-permute-start(bf16[16,512]{1,0:T(8,128)(2,1)S(1)} %get-tuple-element.186), channel_id=1, source_target_pairs={{0,3},{1,2},{2,1},{3,0},{4,7},{5,6},{6,5},{7,4},{8,11},{9,10},{10,... | collective-permute-start | bytes 49160 | tf_op jit(solution)/shard_map/ppermute | solution.py:474
  48.8 3.9 %collective-permute-start.28 = (bf16[16,512]{1,0:T(8,128)(2,1)S(1)}, bf16[16,512]{1,0:T(8,128)(2,1)S(1)}, u32[]{:S(2)}, u32[]{:S(2)}) collective-permute-start(bf16[16,512]{1,0:T(8,128)(2,1)S(1)} %get-tuple-element.186), channel_id=1, source_target_pairs={{0,2},{1,3},{2,0},{3,1},{4,6},{5,7},{6,4},{7,5},{8,10},{9,11},{10,... | collective-permute-start | bytes 49160 | tf_op jit(solution)/shard_map/ppermute | solution.py:474
  50.9 1.8 %collective-permute-start.27 = (bf16[16,512]{1,0:T(8,128)(2,1)S(1)}, bf16[16,512]{1,0:T(8,128)(2,1)S(1)}, u32[]{:S(2)}, u32[]{:S(2)}) collective-permute-start(bf16[16,512]{1,0:T(8,128)(2,1)S(1)} %get-tuple-element.186), channel_id=1, source_target_pairs={{0,1},{1,0},{2,3},{3,2},{4,5},{5,4},{6,7},{7,6},{8,9},{9,8},{10,11... | collective-permute-start | bytes 49160 | tf_op jit(solution)/shard_map/ppermute | solution.py:474
  52.1 3.6 %collective-permute-start.16 = (bf16[256,512]{1,0:T(8,128)(2,1)S(1)}, bf16[256,512]{1,0:T(8,128)(2,1)S(1)}, u32[]{:S(2)}, u32[]{:S(2)}) collective-permute-start(bf16[256,512]{1,0:T(8,128)(2,1)S(1)} %get-tuple-element.176), channel_id=1, source_target_pairs={{0,1},{1,0},{2,3},{3,2},{4,5},{5,4},{6,7},{7,6},{8,9},{9,8},{10,11... | collective-permute-start | bytes 786440 | tf_op jit(solution)/shard_map/ppermute | solution.py:474
  52.7 11.9 %collective-permute-start.30 = (bf16[144,512]{1,0:T(8,128)(2,1)S(1)}, bf16[144,512]{1,0:T(8,128)(2,1)S(1)}, u32[]{:S(2)}, u32[]{:S(2)}) collective-permute-start(bf16[144,512]{1,0:T(8,128)(2,1)S(1)} %pad_maximum_fusion.1), channel_id=1, source_target_pairs={{0,16},{4,20},{8,24},{12,28},{16,0},{20,4},{24,8},{28,12},{1,17},{... | collective-permute-start | bytes 442376 | tf_op jit(solution)/shard_map/ppermute | solution.py:474
  54.6 9.3 %collective-permute-start.25 = (bf16[128,512]{1,0:T(8,128)(2,1)S(1)}, bf16[128,512]{1,0:T(8,128)(2,1)S(1)}, u32[]{:S(2)}, u32[]{:S(2)}) collective-permute-start(bf16[128,512]{1,0:T(8,128)(2,1)S(1)} %get-tuple-element.202), channel_id=1, source_target_pairs={{0,4},{4,0},{8,12},{12,8},{16,20},{20,16},{24,28},{28,24},{1,5},{5... | collective-permute-start | bytes 393224 | tf_op jit(solution)/shard_map/ppermute | solution.py:474
  55.8 7.0 %collective-permute-start.23 = (bf16[128,512]{1,0:T(8,128)(2,1)S(1)}, bf16[128,512]{1,0:T(8,128)(2,1)S(1)}, u32[]{:S(2)}, u32[]{:S(2)}) collective-permute-start(bf16[128,512]{1,0:T(8,128)(2,1)S(1)} %get-tuple-element.203), channel_id=1, source_target_pairs={{0,8},{4,12},{8,0},{12,4},{16,24},{20,28},{24,16},{28,20},{1,9},{5... | collective-permute-start | bytes 393224 | tf_op jit(solution)/shard_map/ppermute | solution.py:474
  55.8 7.9 %collective-permute-start.17 = (bf16[256,512]{1,0:T(8,128)(2,1)S(1)}, bf16[256,512]{1,0:T(8,128)(2,1)S(1)}, u32[]{:S(2)}, u32[]{:S(2)}) collective-permute-start(bf16[256,512]{1,0:T(8,128)(2,1)S(1)} %add_convert_fusion.4), channel_id=1, source_target_pairs={{0,2},{1,3},{2,0},{3,1},{4,6},{5,7},{6,4},{7,5},{8,10},{9,11},{10,... | collective-permute-start | bytes 786440 | tf_op jit(solution)/shard_map/ppermute | solution.py:474
  57.5 9.2 %collective-permute-start.21 = (bf16[256,512]{1,0:T(8,128)(2,1)S(1)}, bf16[256,512]{1,0:T(8,128)(2,1)S(1)}, u32[]{:S(2)}, u32[]{:S(2)}) collective-permute-start(bf16[256,512]{1,0:T(8,128)(2,1)S(1)} %add_convert_fusion.1.refs_3_), channel_id=1, source_target_pairs={{0,1},{1,0},{2,3},{3,2},{4,5},{5,4},{6,7},{7,6},{8,9},{9,8},{10,11... | collective-permute-start | bytes 786440 | tf_op jit(solution)/shard_map/ppermute | solution.py:474
  62.8 8.0 %collective-permute-start.24 = (bf16[256,512]{1,0:T(8,128)(2,1)S(1)}, bf16[256,512]{1,0:T(8,128)(2,1)S(1)}, u32[]{:S(2)}, u32[]{:S(2)}) collective-permute-start(bf16[256,512]{1,0:T(8,128)(2,1)S(1)} %maximum_select_fusion.refs_2_), channel_id=1, source_target_pairs={{0,4},{4,0},{8,12},{12,8},{16,20},{20,16},{24,28},{28,24},{1,5},{5... | collective-permute-start | bytes 786440 | tf_op jit(solution)/shard_map/ppermute | solution.py:474
  63.8 3.3 %collective-permute-start.18 = (bf16[256,512]{1,0:T(8,128)(2,1)S(1)}, bf16[256,512]{1,0:T(8,128)(2,1)S(1)}, u32[]{:S(2)}, u32[]{:S(2)}) collective-permute-start(bf16[256,512]{1,0:T(8,128)(2,1)S(1)} %add_convert_fusion.3.refs_1_), channel_id=1, source_target_pairs={{0,1},{1,0},{2,3},{3,2},{4,5},{5,4},{6,7},{7,6},{8,9},{9,8},{10,11... | collective-permute-start | bytes 786440 | tf_op jit(solution)/shard_map/ppermute | solution.py:474
  64.0 9.2 %collective-permute-start.26 = (bf16[256,512]{1,0:T(8,128)(2,1)S(1)}, bf16[256,512]{1,0:T(8,128)(2,1)S(1)}, u32[]{:S(2)}, u32[]{:S(2)}) collective-permute-start(bf16[256,512]{1,0:T(8,128)(2,1)S(1)} %maximum_select_fusion.1.refs_4_), channel_id=1, source_target_pairs={{0,8},{4,12},{8,0},{12,4},{16,24},{20,28},{24,16},{28,20},{1,9},{5... | collective-permute-start | bytes 786440 | tf_op jit(solution)/shard_map/ppermute | solution.py:474
  64.6 12.3 %collective-permute-start.33 = (bf16[144,512]{1,0:T(8,128)(2,1)S(1)}, bf16[144,512]{1,0:T(8,128)(2,1)S(1)}, u32[]{:S(2)}, u32[]{:S(2)}) collective-permute-start(bf16[144,512]{1,0:T(8,128)(2,1)S(1)} %add_convert_fusion.9.refs_2_), channel_id=1, source_target_pairs={{0,12},{4,8},{8,4},{12,0},{16,28},{20,24},{24,20},{28,16},{1,13},{... | collective-permute-start | bytes 442376 | tf_op jit(solution)/shard_map/ppermute | solution.py:474
  66.8 12.3 %collective-permute-start.32 = (bf16[144,512]{1,0:T(8,128)(2,1)S(1)}, bf16[144,512]{1,0:T(8,128)(2,1)S(1)}, u32[]{:S(2)}, u32[]{:S(2)}) collective-permute-start(bf16[144,512]{1,0:T(8,128)(2,1)S(1)} %add_convert_fusion.9.refs_2_), channel_id=1, source_target_pairs={{0,8},{4,12},{8,0},{12,4},{16,24},{20,28},{24,16},{28,20},{1,9},{5... | collective-permute-start | bytes 442376 | tf_op jit(solution)/shard_map/ppermute | solution.py:474
  67.1 11.9 %collective-permute-start.31 = (bf16[144,512]{1,0:T(8,128)(2,1)S(1)}, bf16[144,512]{1,0:T(8,128)(2,1)S(1)}, u32[]{:S(2)}, u32[]{:S(2)}) collective-permute-start(bf16[144,512]{1,0:T(8,128)(2,1)S(1)} %add_convert_fusion.9.refs_2_), channel_id=1, source_target_pairs={{0,4},{4,0},{8,12},{12,8},{16,20},{20,16},{24,28},{28,24},{1,5},{5... | collective-permute-start | bytes 442376 | tf_op jit(solution)/shard_map/ppermute | solution.py:474

commit v8 on v7

--- a/solution.py
+++ b/solution.py
@@ -258,8 +258,8 @@
     tokens = x.shape[0]
     half = tokens // 2
     curve = (2.0 / jnp.pi) ** 0.5
-    for i in range(2):
-        rows = pl.ds(i * half, half)
+    for i in range(1):
+        rows = pl.ds(0, tokens)
         value = x[rows, :].astype(F32) + dot(att_all[rows, :], wo_all[...]) + row(bo)
         mid[rows, :] = value
         normed, _ = normalize(value)

time: 80.9 us -> 80.7 us (level)
  no operation moved by 1% of the time
where the time goes in v8:
time: 80.7 us; the launch traced here: 80.6 us
  starting transfers between devices  28.2 us (35%)
  waiting for transfers between devices  26.6 us (33%)
  Pallas kernels  23.6 us (29%)
  other arithmetic  0.99 us (1%)
  between operations  0.94 us (1%)
    ppermute x34, starting transfers between devices, swap(): return lax.ppermute(value, axis, [(i, i ^ bit) for i in range(size)])  28.2 us
    ppermute x34, waiting for transfers between devices, swap(): return lax.ppermute(value, axis, [(i, i ^ bit) for i in range(size)])  26.6 us
    pallas_call x11, Pallas kernels, call(): pl.pallas_call(body, name=kernel.__name__, out_shape=pinned, in_specs=[pl...  23.6 us
  transfers between devices with their start and end apart: 34, of which 15 were waited for; matrix products, arithmetic and copies ran while one was open for 1% of the time, Pallas kernels for 24%

profile of v8, /device:TPU:0, one launch (start us, length us, event | category | flops | bytes accessed | tf_op | source)
XLA Modules:
  0.0 80.6 jit_solution(852312892791583546)
XLA Ops:
  0.7 3.0 %collective-permute-start.2 = (bf16[128,512]{1,0:T(8,128)(2,1)}, bf16[128,512]{1,0:T(8,128)(2,1)S(1)}, u32[]{:S(2)}, u32[]{:S(2)}) collective-permute-start(bf16[128,512]{1,0:T(8,128)(2,1)} %refs_11_.3), channel_id=1, source_target_pairs={{0,2},{1,3},{2,0},{3,1},{4,6},{5,7},{6,4},{7,5},{8,10},{9,11},{10,... | collective-permute-start | bytes 393224 | tf_op jit(solution)/shard_map/ppermute | solution.py:474
  3.8 4.8 %attend_kernel.1 = (bf16[512,128]{1,0:T(8,128)(2,1)S(1)}, bf16[512,512]{1,0:T(8,128)(2,1)S(1)}, bf16[512,128]{1,0:T(8,128)(2,1)S(1)}, bf16[512,128]{1,0:T(8,128)...) custom-call(s32[32]{0:T(128)S(1)} %stack.143.refs_0_, bf16[512,512]{1,0:T(8,128)(2,1)} %refs_4_.3, ...), custom_call_target="tpu_custom_call" | custom-call | flops 20000000000 | tf_op jit(solution)/shard_map/attend_kernel/pallas_call | solution.py:173
  8.8 0.5 collective-permute-start
  9.3 1.9 %fetch_kernel.1 = (f32[512,512]{1,0:T(8,128)S(1)}, bf16[512,512]{1,0:T(8,128)(2,1)S(1)}, bf16[512,512]{1,0:T(8,128)(2,1)S(1)}, bf16[512,512]{1,0:T(8,128)(2,1)S(...) custom-call(bf16[512,128]{1,0:T(8,128)(2,1)S(1)} %get-tuple-element., ...), custom_call_target="tpu_custom_call" | custom-call | tf_op jit(solution)/shard_map/fetch_kernel/pallas_call | solution.py:173
  11.2 2.5 %collective-permute-done.1.refs_3_ = bf16[512,128]{1,0:T(8,128)(2,1)S(1)} collective-permute-done((bf16[512,128]{1,0:T(8,128)(2,1)S(1)}, bf16[512,128]{1,0:T(8,128)(2,1)S(1)}, u32[]{:S(2)}, u32[]{:S(2)}) %collective-permute-start.1) | collective-permute-done | bytes 131104 | tf_op jit(solution)/shard_map/ppermute | solution.py:474
  13.6 0.5 collective-permute-start.3
  14.2 0.8 %collective-permute-done.5.refs_8_ = bf16[128,512]{1,0:T(8,128)(2,1)S(1)} collective-permute-done((bf16[128,512]{1,0:T(8,128)(2,1)S(1)}, bf16[128,512]{1,0:T(8,128)(2,1)S(1)}, u32[]{:S(2)}, u32[]{:S(2)}) %collective-permute-start.5) | collective-permute-done | bytes 131104 | tf_op jit(solution)/shard_map/ppermute | solution.py:474
  15.0 0.2 collective-permute-done.3.refs_4_
  15.2 2.6 %mlp_kernel.1 = (f32[512,512]{1,0:T(8,128)S(1)}, bf16[512,512]{1,0:T(8,128)(2,1)S(1)}, bf16[512,512]{1,0:T(8,128)(2,1)S(1)}, bf16[512,512]{1,0:T(8,128)(2,1)S(1)...) custom-call(s32[32]{0:T(128)S(1)} %stack.143.refs_0_, ...), custom_call_target="tpu_custom_call" | custom-call | flops 2000000000 | tf_op jit(solution)/shard_map/mlp_kernel/pallas_call | solution.py:173
  17.8 0.4 collective-permute-start.6
  18.2 1.4 %mlp_grad_kernel.1 = (bf16[256,512]{1,0:T(8,128)(2,1)S(1)}, bf16[256,512]{1,0:T(8,128)(2,1)S(1)}, bf16[256,512]{1,0:T(8,128)(2,1)S(1)}, bf16[256,512]{1,0:T(8,128)(2,1)S(1)}, bf16[8,512]{1,0:T(8,128)(2,1)S(1)}) custom-call(s32[32]{0:T(128)S(1)} %stack.143.refs_0_, bf16[512,512]{1,0:T(8,128)(2,1)S(1)} %get-tuple-element.121.refs_1_, ...), custom_call_target="tpu_custom_call" | custom-call | flops 2000000000 | tf_op jit(solution)/shard_map/mlp_grad_kernel/pallas_call | solution.py:173
  19.7 0.4 collective-permute-start.7
  20.0 1.7 %collective-permute-start.8 = (bf16[256,512]{1,0:T(8,128)(2,1)S(1)}, bf16[256,512]{1,0:T(8,128)(2,1)S(1)}, u32[]{:S(2)}, u32[]{:S(2)}) collective-permute-start(bf16[256,512]{1,0:T(8,128)(2,1)S(1)} %get-tuple-element.132), channel_id=1, source_target_pairs={{0,4},{4,0},{8,12},{12,8},{16,20},{20,16},{24,28},{28,24},{1,5},{5... | collective-permute-start | bytes 786440 | tf_op jit(solution)/shard_map/ppermute | solution.py:474
  21.8 1.6 %collective-permute-start.9 = (bf16[256,512]{1,0:T(8,128)(2,1)S(1)}, bf16[256,512]{1,0:T(8,128)(2,1)S(1)}, u32[]{:S(2)}, u32[]{:S(2)}) collective-permute-start(bf16[256,512]{1,0:T(8,128)(2,1)S(1)} %get-tuple-element.133), channel_id=1, source_target_pairs={{0,8},{4,12},{8,0},{12,4},{16,24},{20,28},{24,16},{28,20},{1,9},{5... | collective-permute-start | bytes 786440 | tf_op jit(solution)/shard_map/ppermute | solution.py:474
  23.4 1.0 %mlp_out_kernel.1 = (bf16[256,512]{1,0:T(8,128)(2,1)S(1)}, bf16[256,512]{1,0:T(8,128)(2,1)S(1)}) custom-call(s32[32]{0:T(128)S(1)} %stack.143.refs_0_, bf16[512,512]{1,0:T(8,128)(2,1)S(1)} %get-tuple-element.122.refs_2_.refs_1_, bf16[512,512]{1,0:T(8,128)(2,1)S(1)} %get-tuple-element.134.refs_2_), custom_call_target="tpu_custom_call" | custom-call | flops 1000000000 | tf_op jit(solution)/shard_map/mlp_out_kernel/pallas_call | solution.py:173
  24.3 3.8 %collective-permute-done.7 = bf16[256,512]{1,0:T(8,128)(2,1)S(1)} collective-permute-done((bf16[256,512]{1,0:T(8,128)(2,1)S(1)}, bf16[256,512]{1,0:T(8,128)(2,1)S(1)}, u32[]{:S(2)}, u32[]{:S(2)}) %collective-permute-start.7) | collective-permute-done | bytes 262176 | tf_op jit(solution)/shard_map/ppermute | solution.py:474
  28.2 1.4 %collective-permute-done.9 = bf16[256,512]{1,0:T(8,128)(2,1)S(1)} collective-permute-done((bf16[256,512]{1,0:T(8,128)(2,1)S(1)}, bf16[256,512]{1,0:T(8,128)(2,1)S(1)}, u32[]{:S(2)}, u32[]{:S(2)}) %collective-permute-start.9) | collective-permute-done | bytes 262176 | tf_op jit(solution)/shard_map/ppermute | solution.py:474
  30.0 1.7 %collective-permute-start.10 = (bf16[128,512]{1,0:T(8,128)(2,1)S(1)}, bf16[128,512]{1,0:T(8,128)(2,1)S(1)}, u32[]{:S(2)}, u32[]{:S(2)}) collective-permute-start(bf16[128,512]{1,0:T(8,128)(2,1)S(1)} %constant_dynamic-slice_fusion.1), channel_id=1, source_target_pairs={{0,8},{4,12},{8,0},{12,4},{16,24},{20,28},{24,16},{28,20},{1,9},{5... | collective-permute-start | bytes 393224 | tf_op jit(solution)/shard_map/ppermute | solution.py:474
  31.7 0.5 collective-permute-start.11
  32.2 3.4 %attend_back_kernel.1 = (f32[512,512]{1,0:T(8,128)S(1)}, bf16[128,512]{1,0:T(8,128)(2,1)S(1)}, bf16[128,512]{1,0:T(8,128)(2,1)S(1)}, bf16[128,512]{1,0:T(8,128)(...) custom-call(s32[32]{0:T(128)S(1)} %stack.143.refs_0_, ...), custom_call_target="tpu_custom_call" | custom-call | flops 1000000000 | tf_op jit(solution)/shard_map/attend_back_kernel/pallas_call | solution.py:173
  35.6 0.3 collective-permute-done.10
  36.0 1.3 %collective-permute-done.11 = bf16[128,512]{1,0:T(8,128)(2,1)S(1)} collective-permute-done((bf16[128,512]{1,0:T(8,128)(2,1)S(1)}, bf16[128,512]{1,0:T(8,128)(2,1)S(1)}, u32[]{:S(2)}, u32[]{:S(2)}) %collective-permute-start.11) | collective-permute-done | bytes 131104 | tf_op jit(solution)/shard_map/ppermute | solution.py:474
  37.3 0.5 collective-permute-start.13
  37.8 0.4 collective-permute-start.14
  38.2 2.6 %collective-permute-start.15 = (bf16[128,512]{1,0:T(8,128)(2,1)S(1)}, bf16[128,512]{1,0:T(8,128)(2,1)S(1)}, u32[]{:S(2)}, u32[]{:S(2)}) collective-permute-start(bf16[128,512]{1,0:T(8,128)(2,1)S(1)} %get-tuple-element.165), channel_id=1, source_target_pairs={{0,12},{4,8},{8,4},{12,0},{16,28},{20,24},{24,20},{28,16},{1,13},{... | collective-permute-start | bytes 393224 | tf_op jit(solution)/shard_map/ppermute | solution.py:474
  40.9 2.6 %collective-permute-start.22 = (bf16[256,512]{1,0:T(8,128)(2,1)S(1)}, bf16[256,512]{1,0:T(8,128)(2,1)S(1)}, u32[]{:S(2)}, u32[]{:S(2)}) collective-permute-start(bf16[256,512]{1,0:T(8,128)(2,1)S(1)} %pad_maximum_fusion), channel_id=1, source_target_pairs={{0,16},{4,20},{8,24},{12,28},{16,0},{20,4},{24,8},{28,12},{1,17},{... | collective-permute-start | bytes 786440 | tf_op jit(solution)/shard_map/ppermute | solution.py:474
  43.6 1.5 %collective-permute-start.20 = (bf16[256,512]{1,0:T(8,128)(2,1)S(1)}, bf16[256,512]{1,0:T(8,128)(2,1)S(1)}, u32[]{:S(2)}, u32[]{:S(2)}) collective-permute-start(bf16[256,512]{1,0:T(8,128)(2,1)S(1)} %add_convert_fusion.2), channel_id=1, source_target_pairs={{0,2},{1,3},{2,0},{3,1},{4,6},{5,7},{6,4},{7,5},{8,10},{9,11},{10,... | collective-permute-start | bytes 786440 | tf_op jit(solution)/shard_map/ppermute | solution.py:474
  45.2 1.1 %sums_kernel.1.refs_2_ = bf16[16,512]{1,0:T(8,128)(2,1)S(1)} custom-call(bf16[128,512]{1,0:T(8,128)(2,1)S(1)} %collective-permute-done.13.refs_0_, f32[512,128]{1,0:T(8,128)S(1)} %get-tuple-element.167.refs_1_, f32[8,512]{1,0:T(8,128)S(1)} %get-tuple-element.168.refs_2_, s32[16,16]{1,0:T(8,128)S(1)} %get-tuple-element.169.refs_3_, ...), custom_call_target="tpu_custom_call" | custom-call | flops 1000000000 | tf_op jit(solution)/shard_map/sums_kernel/pallas_call | solution.py:173
  46.3 2.3 %collective-permute-done.14 = bf16[128,512]{1,0:T(8,128)(2,1)S(1)} collective-permute-done((bf16[128,512]{1,0:T(8,128)(2,1)S(1)}, bf16[128,512]{1,0:T(8,128)(2,1)S(1)}, u32[]{:S(2)}, u32[]{:S(2)}) %collective-permute-start.14) | collective-permute-done | bytes 131104 | tf_op jit(solution)/shard_map/ppermute | solution.py:474
  48.6 1.4 %collective-permute-start.28 = (bf16[16,512]{1,0:T(8,128)(2,1)S(1)}, bf16[16,512]{1,0:T(8,128)(2,1)S(1)}, u32[]{:S(2)}, u32[]{:S(2)}) collective-permute-start(bf16[16,512]{1,0:T(8,128)(2,1)S(1)} %get-tuple-element.186), channel_id=1, source_target_pairs={{0,2},{1,3},{2,0},{3,1},{4,6},{5,7},{6,4},{7,5},{8,10},{9,11},{10,... | collective-permute-start | bytes 49160 | tf_op jit(solution)/shard_map/ppermute | solution.py:474
  50.1 0.6 collective-permute-done.15
  50.8 1.1 %attend_out_kernel.1 = (bf16[256,512]{1,0:T(8,128)(2,1)S(1)}, bf16[256,512]{1,0:T(8,128)(2,1)S(1)}) custom-call(s32[32]{0:T(128)S(1)} %stack.143.refs_0_, bf16[128,512]{1,0:T(8,128)(2,1)S(1)} %add_convert_fusion.12.refs_1_, bf16[16,512]{1,0:T(8,128)(2,1)S(1)} %sums_kernel.1.refs_2_, bf16[512,128]{1,0:T(8,128)(2,1)S(1)} %get-tuple-element.172.refs_3_, ...), custom_call_target="tpu_custom_call" | custom-call | flops 1000000000 | tf_op jit(solution)/shard_map/attend_out_kernel/pallas_call | solution.py:173
  51.9 0.6 collective-permute-start.16
  52.6 1.7 %collective-permute-done.22 = bf16[256,512]{1,0:T(8,128)(2,1)S(1)} collective-permute-done((bf16[256,512]{1,0:T(8,128)(2,1)S(1)}, bf16[256,512]{1,0:T(8,128)(2,1)S(1)}, u32[]{:S(2)}, u32[]{:S(2)}) %collective-permute-start.22) | collective-permute-done | bytes 262176 | tf_op jit(solution)/shard_map/ppermute | solution.py:474
  54.4 1.1 %collective-permute-start.25 = (bf16[128,512]{1,0:T(8,128)(2,1)S(1)}, bf16[128,512]{1,0:T(8,128)(2,1)S(1)}, u32[]{:S(2)}, u32[]{:S(2)}) collective-permute-start(bf16[128,512]{1,0:T(8,128)(2,1)S(1)} %get-tuple-element.202), channel_id=1, source_target_pairs={{0,4},{4,0},{8,12},{12,8},{16,20},{20,16},{24,28},{28,24},{1,5},{5... | collective-permute-start | bytes 393224 | tf_op jit(solution)/shard_map/ppermute | solution.py:474
  55.6 1.6 %collective-permute-start.17 = (bf16[256,512]{1,0:T(8,128)(2,1)S(1)}, bf16[256,512]{1,0:T(8,128)(2,1)S(1)}, u32[]{:S(2)}, u32[]{:S(2)}) collective-permute-start(bf16[256,512]{1,0:T(8,128)(2,1)S(1)} %add_convert_fusion.4), channel_id=1, source_target_pairs={{0,2},{1,3},{2,0},{3,1},{4,6},{5,7},{6,4},{7,5},{8,10},{9,11},{10,... | collective-permute-start | bytes 786440 | tf_op jit(solution)/shard_map/ppermute | solution.py:474
  57.4 5.2 %collective-permute-done.23 = bf16[128,512]{1,0:T(8,128)(2,1)S(1)} collective-permute-done((bf16[128,512]{1,0:T(8,128)(2,1)S(1)}, bf16[128,512]{1,0:T(8,128)(2,1)S(1)}, u32[]{:S(2)}, u32[]{:S(2)}) %collective-permute-start.23) | collective-permute-done | bytes 131104 | tf_op jit(solution)/shard_map/ppermute | solution.py:474
  62.6 0.9 %collective-permute-start.24 = (bf16[256,512]{1,0:T(8,128)(2,1)S(1)}, bf16[256,512]{1,0:T(8,128)(2,1)S(1)}, u32[]{:S(2)}, u32[]{:S(2)}) collective-permute-start(bf16[256,512]{1,0:T(8,128)(2,1)S(1)} %maximum_select_fusion.refs_2_), channel_id=1, source_target_pairs={{0,4},{4,0},{8,12},{12,8},{16,20},{20,16},{24,28},{28,24},{1,5},{5... | collective-permute-start | bytes 786440 | tf_op jit(solution)/shard_map/ppermute | solution.py:474
  63.8 0.6 collective-permute-start.26
  64.4 2.1 %collective-permute-start.33 = (bf16[144,512]{1,0:T(8,128)(2,1)S(1)}, bf16[144,512]{1,0:T(8,128)(2,1)S(1)}, u32[]{:S(2)}, u32[]{:S(2)}) collective-permute-start(bf16[144,512]{1,0:T(8,128)(2,1)S(1)} %add_convert_fusion.9.refs_2_), channel_id=1, source_target_pairs={{0,12},{4,8},{8,4},{12,0},{16,28},{20,24},{24,20},{28,16},{1,13},{... | collective-permute-start | bytes 442376 | tf_op jit(solution)/shard_map/ppermute | solution.py:474
  66.6 0.3 collective-permute-start.32
  66.9 1.1 %collective-permute-start.31 = (bf16[144,512]{1,0:T(8,128)(2,1)S(1)}, bf16[144,512]{1,0:T(8,128)(2,1)S(1)}, u32[]{:S(2)}, u32[]{:S(2)}) collective-permute-start(bf16[144,512]{1,0:T(8,128)(2,1)S(1)} %add_convert_fusion.9.refs_2_), channel_id=1, source_target_pairs={{0,4},{4,0},{8,12},{12,8},{16,20},{20,16},{24,28},{28,24},{1,5},{5... | collective-permute-start | bytes 442376 | tf_op jit(solution)/shard_map/ppermute | solution.py:474
  68.0 2.6 %finish_kernel.1 = (f32[512,512]{1,0:T(8,128)}, f32[512,512]{1,0:T(8,128)}) custom-call(s32[32]{0:T(128)S(1)} %stack.143.refs_0_, bf16[256,512]{1,0:T(8,128)(2,1)S(1)} %add_convert_fusion.3.refs_1_, bf16[256,512]{1,0:T(8,128)(2,1)S(1)} %collective-permute-done.18.refs_2_, bf16[256,512]{1,0:T(8,128)(2,1)S(1)} %add_convert_fusion.1.refs_3_, ...), custom_call_target="tpu_custom_call" | custom-call | flops 2000000000 | tf_op jit(solution)/shard_map/finish_kernel/pallas_call | solution.py:173
  70.6 2.3 %collective-permute-done.26.refs_5_ = bf16[256,512]{1,0:T(8,128)(2,1)S(1)} collective-permute-done((bf16[256,512]{1,0:T(8,128)(2,1)S(1)}, bf16[256,512]{1,0:T(8,128)(2,1)S(1)}, u32[]{:S(2)}, u32[]{:S(2)}) %collective-permute-start.26) | collective-permute-done | bytes 262176 | tf_op jit(solution)/shard_map/ppermute | solution.py:474
  72.9 2.0 %widen_kernel.1 = (f32[512,512]{1,0:T(8,128)}, f32[512,512]{1,0:T(8,128)}) custom-call(s32[32]{0:T(128)S(1)} %stack.143.refs_0_, f32[512,512]{1,0:T(8,128)} %get-tuple-element.92.refs_1_, bf16[256,512]{1,0:T(8,128)(2,1)S(1)} %maximum_select_fusion.refs_2_, bf16[256,512]{1,0:T(8,128)(2,1)S(1)} %collective-permute-done.24.refs_3_, ...), custom_call_target="tpu_custom_call" | custom-call | tf_op jit(solution)/shard_map/widen_kernel/pallas_call | solution.py:173
  74.9 1.8 %collective-permute-done.33.refs_5_ = bf16[144,512]{1,0:T(8,128)(2,1)S(1)} collective-permute-done((bf16[144,512]{1,0:T(8,128)(2,1)S(1)}, bf16[144,512]{1,0:T(8,128)(2,1)S(1)}, u32[]{:S(2)}, u32[]{:S(2)}) %collective-permute-start.33) | collective-permute-done | bytes 147488 | tf_op jit(solution)/shard_map/ppermute | solution.py:474
  76.7 2.2 %collective-permute-done.32.refs_4_ = bf16[144,512]{1,0:T(8,128)(2,1)S(1)} collective-permute-done((bf16[144,512]{1,0:T(8,128)(2,1)S(1)}, bf16[144,512]{1,0:T(8,128)(2,1)S(1)}, u32[]{:S(2)}, u32[]{:S(2)}) %collective-permute-start.32) | collective-permute-done | bytes 147488 | tf_op jit(solution)/shard_map/ppermute | solution.py:474
  78.9 1.7 %unpack_kernel.1 = (f32[512,128]{1,0:T(8,128)}, f32[512,128]{1,0:T(8,128)}, f32[512,128]{1,0:T(8,128)}, f32[128,512]{1,0:T(8,128)}, f32[512]{0:T(512)}, /*index=...) custom-call(s32[32]{0:T(128)S(1)} %stack.143.refs_0_, ...), custom_call_target="tpu_custom_call" | custom-call | tf_op jit(solution)/shard_map/unpack_kernel/pallas_call | solution.py:173
  (54 shorter events, 1.8 us)
Async XLA Ops:
  0.7 8.6 %collective-permute-start.2 = (bf16[128,512]{1,0:T(8,128)(2,1)}, bf16[128,512]{1,0:T(8,128)(2,1)S(1)}, u32[]{:S(2)}, u32[]{:S(2)}) collective-permute-start(bf16[128,512]{1,0:T(8,128)(2,1)} %refs_11_.3), channel_id=1, source_target_pairs={{0,2},{1,3},{2,0},{3,1},{4,6},{5,7},{6,4},{7,5},{8,10},{9,11},{10,... | collective-permute-start | bytes 393224 | tf_op jit(solution)/shard_map/ppermute | solution.py:474
  3.8 4.9 %copy-start = (bf16[128,512]{1,0:T(8,128)(2,1)S(1)}, bf16[128,512]{1,0:T(8,128)(2,1)}, u32[]{:S(2)}) copy-start(bf16[128,512]{1,0:T(8,128)(2,1)} %refs_11_.3) | copy-start | bytes 393220
  8.6 5.0 %collective-permute-start.1 = (bf16[512,128]{1,0:T(8,128)(2,1)S(1)}, bf16[512,128]{1,0:T(8,128)(2,1)S(1)}, u32[]{:S(2)}, u32[]{:S(2)}) collective-permute-start(bf16[512,128]{1,0:T(8,128)(2,1)S(1)} %get-tuple-element.110.refs_0_.refs_1_.refs_12_), channel_id=1, source_target_pairs={{0,2},{1,3},{2,0},{3,1},{4,6},{5,7},{6,4},{7,5},{8,10},{9,11},{10,... | collective-permute-start | bytes 393224 | tf_op jit(solution)/shard_map/ppermute | solution.py:474
  8.7 5.4 %collective-permute-start.4 = (bf16[128,512]{1,0:T(8,128)(2,1)S(1)}, bf16[128,512]{1,0:T(8,128)(2,1)S(1)}, u32[]{:S(2)}, u32[]{:S(2)}) collective-permute-start(bf16[128,512]{1,0:T(8,128)(2,1)S(1)} %copy-done), channel_id=1, source_target_pairs={{0,1},{1,0},{2,3},{3,2},{4,5},{5,4},{6,7},{7,6},{8,9},{9,8},{10,11... | collective-permute-start | bytes 393224 | tf_op jit(solution)/shard_map/ppermute | solution.py:474
  8.8 5.4 %collective-permute-start = (bf16[512,128]{1,0:T(8,128)(2,1)S(1)}, bf16[512,128]{1,0:T(8,128)(2,1)S(1)}, u32[]{:S(2)}, u32[]{:S(2)}) collective-permute-start(bf16[512,128]{1,0:T(8,128)(2,1)S(1)} %get-tuple-element.110.refs_0_.refs_1_.refs_12_), channel_id=1, source_target_pairs={{0,1},{1,0},{2,3},{3,2},{4,5},{5,4},{6,7},{7,6},{8,9},{9,8},{10,11... | collective-permute-start | bytes 393224 | tf_op jit(solution)/shard_map/ppermute | solution.py:474
  13.6 1.3 %collective-permute-start.5 = (bf16[128,512]{1,0:T(8,128)(2,1)S(1)}, bf16[128,512]{1,0:T(8,128)(2,1)S(1)}, u32[]{:S(2)}, u32[]{:S(2)}) collective-permute-start(bf16[128,512]{1,0:T(8,128)(2,1)S(1)} %collective-permute-done.2.refs_1_.refs_7_), channel_id=1, source_target_pairs={{0,1},{1,0},{2,3},{3,2},{4,5},{5,4},{6,7},{7,6},{8,9},{9,8},{10,11... | collective-permute-start | bytes 393224 | tf_op jit(solution)/shard_map/ppermute | solution.py:474
  13.6 1.5 %collective-permute-start.3 = (bf16[512,128]{1,0:T(8,128)(2,1)S(1)}, bf16[512,128]{1,0:T(8,128)(2,1)S(1)}, u32[]{:S(2)}, u32[]{:S(2)}) collective-permute-start(bf16[512,128]{1,0:T(8,128)(2,1)S(1)} %collective-permute-done.1.refs_3_), channel_id=1, source_target_pairs={{0,1},{1,0},{2,3},{3,2},{4,5},{5,4},{6,7},{7,6},{8,9},{9,8},{10,11... | collective-permute-start | bytes 393224 | tf_op jit(solution)/shard_map/ppermute | solution.py:474
  17.8 1.8 %collective-permute-start.6 = (bf16[256,512]{1,0:T(8,128)(2,1)S(1)}, bf16[256,512]{1,0:T(8,128)(2,1)S(1)}, u32[]{:S(2)}, u32[]{:S(2)}) collective-permute-start(bf16[256,512]{1,0:T(8,128)(2,1)S(1)} %get-tuple-element.127), channel_id=1, source_target_pairs={{0,1},{1,0},{2,3},{3,2},{4,5},{5,4},{6,7},{7,6},{8,9},{9,8},{10,11... | collective-permute-start | bytes 786440 | tf_op jit(solution)/shard_map/ppermute | solution.py:474
  19.7 8.5 %collective-permute-start.7 = (bf16[256,512]{1,0:T(8,128)(2,1)S(1)}, bf16[256,512]{1,0:T(8,128)(2,1)S(1)}, u32[]{:S(2)}, u32[]{:S(2)}) collective-permute-start(bf16[256,512]{1,0:T(8,128)(2,1)S(1)} %add_convert_fusion.8), channel_id=1, source_target_pairs={{0,2},{1,3},{2,0},{3,1},{4,6},{5,7},{6,4},{7,5},{8,10},{9,11},{10,... | collective-permute-start | bytes 786440 | tf_op jit(solution)/shard_map/ppermute | solution.py:474
  20.0 8.2 %collective-permute-start.8 = (bf16[256,512]{1,0:T(8,128)(2,1)S(1)}, bf16[256,512]{1,0:T(8,128)(2,1)S(1)}, u32[]{:S(2)}, u32[]{:S(2)}) collective-permute-start(bf16[256,512]{1,0:T(8,128)(2,1)S(1)} %get-tuple-element.132), channel_id=1, source_target_pairs={{0,4},{4,0},{8,12},{12,8},{16,20},{20,16},{24,28},{28,24},{1,5},{5... | collective-permute-start | bytes 786440 | tf_op jit(solution)/shard_map/ppermute | solution.py:474
  21.8 7.8 %collective-permute-start.9 = (bf16[256,512]{1,0:T(8,128)(2,1)S(1)}, bf16[256,512]{1,0:T(8,128)(2,1)S(1)}, u32[]{:S(2)}, u32[]{:S(2)}) collective-permute-start(bf16[256,512]{1,0:T(8,128)(2,1)S(1)} %get-tuple-element.133), channel_id=1, source_target_pairs={{0,8},{4,12},{8,0},{12,4},{16,24},{20,28},{24,16},{28,20},{1,9},{5... | collective-permute-start | bytes 786440 | tf_op jit(solution)/shard_map/ppermute | solution.py:474
  29.7 2.5 %collective-permute-start.12 = (bf16[256,512]{1,0:T(8,128)(2,1)S(1)}, bf16[256,512]{1,0:T(8,128)(2,1)S(1)}, u32[]{:S(2)}, u32[]{:S(2)}) collective-permute-start(bf16[256,512]{1,0:T(8,128)(2,1)S(1)} %add_convert_fusion.5.refs_1_), channel_id=1, source_target_pairs={{0,1},{1,0},{2,3},{3,2},{4,5},{5,4},{6,7},{7,6},{8,9},{9,8},{10,11... | collective-permute-start | bytes 786440 | tf_op jit(solution)/shard_map/ppermute | solution.py:474
  30.0 6.0 %collective-permute-start.10 = (bf16[128,512]{1,0:T(8,128)(2,1)S(1)}, bf16[128,512]{1,0:T(8,128)(2,1)S(1)}, u32[]{:S(2)}, u32[]{:S(2)}) collective-permute-start(bf16[128,512]{1,0:T(8,128)(2,1)S(1)} %constant_dynamic-slice_fusion.1), channel_id=1, source_target_pairs={{0,8},{4,12},{8,0},{12,4},{16,24},{20,28},{24,16},{28,20},{1,9},{5... | collective-permute-start | bytes 393224 | tf_op jit(solution)/shard_map/ppermute | solution.py:474
  31.7 5.6 %collective-permute-start.11 = (bf16[128,512]{1,0:T(8,128)(2,1)S(1)}, bf16[128,512]{1,0:T(8,128)(2,1)S(1)}, u32[]{:S(2)}, u32[]{:S(2)}) collective-permute-start(bf16[128,512]{1,0:T(8,128)(2,1)S(1)} %constant_dynamic-slice_fusion), channel_id=1, source_target_pairs={{0,4},{4,0},{8,12},{12,8},{16,20},{20,16},{24,28},{28,24},{1,5},{5... | collective-permute-start | bytes 393224 | tf_op jit(solution)/shard_map/ppermute | solution.py:474
  32.2 11.4 %collective-permute-start.19 = (bf16[256,512]{1,0:T(8,128)(2,1)S(1)}, bf16[256,512]{1,0:T(8,128)(2,1)S(1)}, u32[]{:S(2)}, u32[]{:S(2)}) collective-permute-start(bf16[256,512]{1,0:T(8,128)(2,1)S(1)} %get-tuple-element.178), channel_id=1, source_target_pairs={{0,1},{1,0},{2,3},{3,2},{4,5},{5,4},{6,7},{7,6},{8,9},{9,8},{10,11... | collective-permute-start | bytes 786440 | tf_op jit(solution)/shard_map/ppermute | solution.py:474
  37.3 7.9 %collective-permute-start.13 = (bf16[128,512]{1,0:T(8,128)(2,1)S(1)}, bf16[128,512]{1,0:T(8,128)(2,1)S(1)}, u32[]{:S(2)}, u32[]{:S(2)}) collective-permute-start(bf16[128,512]{1,0:T(8,128)(2,1)S(1)} %get-tuple-element.163), channel_id=1, source_target_pairs={{0,4},{4,0},{8,12},{12,8},{16,20},{20,16},{24,28},{28,24},{1,5},{5... | collective-permute-start | bytes 393224 | tf_op jit(solution)/shard_map/ppermute | solution.py:474
  37.8 10.8 %collective-permute-start.14 = (bf16[128,512]{1,0:T(8,128)(2,1)S(1)}, bf16[128,512]{1,0:T(8,128)(2,1)S(1)}, u32[]{:S(2)}, u32[]{:S(2)}) collective-permute-start(bf16[128,512]{1,0:T(8,128)(2,1)S(1)} %get-tuple-element.164), channel_id=1, source_target_pairs={{0,8},{4,12},{8,0},{12,4},{16,24},{20,28},{24,16},{28,20},{1,9},{5... | collective-permute-start | bytes 393224 | tf_op jit(solution)/shard_map/ppermute | solution.py:474
  38.2 12.5 %collective-permute-start.15 = (bf16[128,512]{1,0:T(8,128)(2,1)S(1)}, bf16[128,512]{1,0:T(8,128)(2,1)S(1)}, u32[]{:S(2)}, u32[]{:S(2)}) collective-permute-start(bf16[128,512]{1,0:T(8,128)(2,1)S(1)} %get-tuple-element.165), channel_id=1, source_target_pairs={{0,12},{4,8},{8,4},{12,0},{16,28},{20,24},{24,20},{28,16},{1,13},{... | collective-permute-start | bytes 393224 | tf_op jit(solution)/shard_map/ppermute | solution.py:474
  40.9 13.4 %collective-permute-start.22 = (bf16[256,512]{1,0:T(8,128)(2,1)S(1)}, bf16[256,512]{1,0:T(8,128)(2,1)S(1)}, u32[]{:S(2)}, u32[]{:S(2)}) collective-permute-start(bf16[256,512]{1,0:T(8,128)(2,1)S(1)} %pad_maximum_fusion), channel_id=1, source_target_pairs={{0,16},{4,20},{8,24},{12,28},{16,0},{20,4},{24,8},{28,12},{1,17},{... | collective-permute-start | bytes 786440 | tf_op jit(solution)/shard_map/ppermute | solution.py:474
  43.6 13.6 %collective-permute-start.20 = (bf16[256,512]{1,0:T(8,128)(2,1)S(1)}, bf16[256,512]{1,0:T(8,128)(2,1)S(1)}, u32[]{:S(2)}, u32[]{:S(2)}) collective-permute-start(bf16[256,512]{1,0:T(8,128)(2,1)S(1)} %add_convert_fusion.2), channel_id=1, source_target_pairs={{0,2},{1,3},{2,0},{3,1},{4,6},{5,7},{6,4},{7,5},{8,10},{9,11},{10,... | collective-permute-start | bytes 786440 | tf_op jit(solution)/shard_map/ppermute | solution.py:474
  46.3 5.6 %collective-permute-start.29 = (bf16[16,512]{1,0:T(8,128)(2,1)S(1)}, bf16[16,512]{1,0:T(8,128)(2,1)S(1)}, u32[]{:S(2)}, u32[]{:S(2)}) collective-permute-start(bf16[16,512]{1,0:T(8,128)(2,1)S(1)} %get-tuple-element.186), channel_id=1, source_target_pairs={{0,3},{1,2},{2,1},{3,0},{4,7},{5,6},{6,5},{7,4},{8,11},{9,10},{10,... | collective-permute-start | bytes 49160 | tf_op jit(solution)/shard_map/ppermute | solution.py:474
  48.6 3.8 %collective-permute-start.28 = (bf16[16,512]{1,0:T(8,128)(2,1)S(1)}, bf16[16,512]{1,0:T(8,128)(2,1)S(1)}, u32[]{:S(2)}, u32[]{:S(2)}) collective-permute-start(bf16[16,512]{1,0:T(8,128)(2,1)S(1)} %get-tuple-element.186), channel_id=1, source_target_pairs={{0,2},{1,3},{2,0},{3,1},{4,6},{5,7},{6,4},{7,5},{8,10},{9,11},{10,... | collective-permute-start | bytes 49160 | tf_op jit(solution)/shard_map/ppermute | solution.py:474
  50.7 1.8 %collective-permute-start.27 = (bf16[16,512]{1,0:T(8,128)(2,1)S(1)}, bf16[16,512]{1,0:T(8,128)(2,1)S(1)}, u32[]{:S(2)}, u32[]{:S(2)}) collective-permute-start(bf16[16,512]{1,0:T(8,128)(2,1)S(1)} %get-tuple-element.186), channel_id=1, source_target_pairs={{0,1},{1,0},{2,3},{3,2},{4,5},{5,4},{6,7},{7,6},{8,9},{9,8},{10,11... | collective-permute-start | bytes 49160 | tf_op jit(solution)/shard_map/ppermute | solution.py:474
  51.9 3.6 %collective-permute-start.16 = (bf16[256,512]{1,0:T(8,128)(2,1)S(1)}, bf16[256,512]{1,0:T(8,128)(2,1)S(1)}, u32[]{:S(2)}, u32[]{:S(2)}) collective-permute-start(bf16[256,512]{1,0:T(8,128)(2,1)S(1)} %get-tuple-element.176), channel_id=1, source_target_pairs={{0,1},{1,0},{2,3},{3,2},{4,5},{5,4},{6,7},{7,6},{8,9},{9,8},{10,11... | collective-permute-start | bytes 786440 | tf_op jit(solution)/shard_map/ppermute | solution.py:474
  52.5 11.9 %collective-permute-start.30 = (bf16[144,512]{1,0:T(8,128)(2,1)S(1)}, bf16[144,512]{1,0:T(8,128)(2,1)S(1)}, u32[]{:S(2)}, u32[]{:S(2)}) collective-permute-start(bf16[144,512]{1,0:T(8,128)(2,1)S(1)} %pad_maximum_fusion.1), channel_id=1, source_target_pairs={{0,16},{4,20},{8,24},{12,28},{16,0},{20,4},{24,8},{28,12},{1,17},{... | collective-permute-start | bytes 442376 | tf_op jit(solution)/shard_map/ppermute | solution.py:474
  54.4 9.3 %collective-permute-start.25 = (bf16[128,512]{1,0:T(8,128)(2,1)S(1)}, bf16[128,512]{1,0:T(8,128)(2,1)S(1)}, u32[]{:S(2)}, u32[]{:S(2)}) collective-permute-start(bf16[128,512]{1,0:T(8,128)(2,1)S(1)} %get-tuple-element.202), channel_id=1, source_target_pairs={{0,4},{4,0},{8,12},{12,8},{16,20},{20,16},{24,28},{28,24},{1,5},{5... | collective-permute-start | bytes 393224 | tf_op jit(solution)/shard_map/ppermute | solution.py:474
  55.5 7.0 %collective-permute-start.23 = (bf16[128,512]{1,0:T(8,128)(2,1)S(1)}, bf16[128,512]{1,0:T(8,128)(2,1)S(1)}, u32[]{:S(2)}, u32[]{:S(2)}) collective-permute-start(bf16[128,512]{1,0:T(8,128)(2,1)S(1)} %get-tuple-element.203), channel_id=1, source_target_pairs={{0,8},{4,12},{8,0},{12,4},{16,24},{20,28},{24,16},{28,20},{1,9},{5... | collective-permute-start | bytes 393224 | tf_op jit(solution)/shard_map/ppermute | solution.py:474
  55.6 7.9 %collective-permute-start.17 = (bf16[256,512]{1,0:T(8,128)(2,1)S(1)}, bf16[256,512]{1,0:T(8,128)(2,1)S(1)}, u32[]{:S(2)}, u32[]{:S(2)}) collective-permute-start(bf16[256,512]{1,0:T(8,128)(2,1)S(1)} %add_convert_fusion.4), channel_id=1, source_target_pairs={{0,2},{1,3},{2,0},{3,1},{4,6},{5,7},{6,4},{7,5},{8,10},{9,11},{10,... | collective-permute-start | bytes 786440 | tf_op jit(solution)/shard_map/ppermute | solution.py:474
  57.3 9.3 %collective-permute-start.21 = (bf16[256,512]{1,0:T(8,128)(2,1)S(1)}, bf16[256,512]{1,0:T(8,128)(2,1)S(1)}, u32[]{:S(2)}, u32[]{:S(2)}) collective-permute-start(bf16[256,512]{1,0:T(8,128)(2,1)S(1)} %add_convert_fusion.1.refs_3_), channel_id=1, source_target_pairs={{0,1},{1,0},{2,3},{3,2},{4,5},{5,4},{6,7},{7,6},{8,9},{9,8},{10,11... | collective-permute-start | bytes 786440 | tf_op jit(solution)/shard_map/ppermute | solution.py:474
  62.6 8.0 %collective-permute-start.24 = (bf16[256,512]{1,0:T(8,128)(2,1)S(1)}, bf16[256,512]{1,0:T(8,128)(2,1)S(1)}, u32[]{:S(2)}, u32[]{:S(2)}) collective-permute-start(bf16[256,512]{1,0:T(8,128)(2,1)S(1)} %maximum_select_fusion.refs_2_), channel_id=1, source_target_pairs={{0,4},{4,0},{8,12},{12,8},{16,20},{20,16},{24,28},{28,24},{1,5},{5... | collective-permute-start | bytes 786440 | tf_op jit(solution)/shard_map/ppermute | solution.py:474
  63.6 3.3 %collective-permute-start.18 = (bf16[256,512]{1,0:T(8,128)(2,1)S(1)}, bf16[256,512]{1,0:T(8,128)(2,1)S(1)}, u32[]{:S(2)}, u32[]{:S(2)}) collective-permute-start(bf16[256,512]{1,0:T(8,128)(2,1)S(1)} %add_convert_fusion.3.refs_1_), channel_id=1, source_target_pairs={{0,1},{1,0},{2,3},{3,2},{4,5},{5,4},{6,7},{7,6},{8,9},{9,8},{10,11... | collective-permute-start | bytes 786440 | tf_op jit(solution)/shard_map/ppermute | solution.py:474
  63.8 9.2 %collective-permute-start.26 = (bf16[256,512]{1,0:T(8,128)(2,1)S(1)}, bf16[256,512]{1,0:T(8,128)(2,1)S(1)}, u32[]{:S(2)}, u32[]{:S(2)}) collective-permute-start(bf16[256,512]{1,0:T(8,128)(2,1)S(1)} %maximum_select_fusion.1.refs_4_), channel_id=1, source_target_pairs={{0,8},{4,12},{8,0},{12,4},{16,24},{20,28},{24,16},{28,20},{1,9},{5... | collective-permute-start | bytes 786440 | tf_op jit(solution)/shard_map/ppermute | solution.py:474
  64.4 12.3 %collective-permute-start.33 = (bf16[144,512]{1,0:T(8,128)(2,1)S(1)}, bf16[144,512]{1,0:T(8,128)(2,1)S(1)}, u32[]{:S(2)}, u32[]{:S(2)}) collective-permute-start(bf16[144,512]{1,0:T(8,128)(2,1)S(1)} %add_convert_fusion.9.refs_2_), channel_id=1, source_target_pairs={{0,12},{4,8},{8,4},{12,0},{16,28},{20,24},{24,20},{28,16},{1,13},{... | collective-permute-start | bytes 442376 | tf_op jit(solution)/shard_map/ppermute | solution.py:474
  66.6 12.3 %collective-permute-start.32 = (bf16[144,512]{1,0:T(8,128)(2,1)S(1)}, bf16[144,512]{1,0:T(8,128)(2,1)S(1)}, u32[]{:S(2)}, u32[]{:S(2)}) collective-permute-start(bf16[144,512]{1,0:T(8,128)(2,1)S(1)} %add_convert_fusion.9.refs_2_), channel_id=1, source_target_pairs={{0,8},{4,12},{8,0},{12,4},{16,24},{20,28},{24,16},{28,20},{1,9},{5... | collective-permute-start | bytes 442376 | tf_op jit(solution)/shard_map/ppermute | solution.py:474
  66.9 11.9 %collective-permute-start.31 = (bf16[144,512]{1,0:T(8,128)(2,1)S(1)}, bf16[144,512]{1,0:T(8,128)(2,1)S(1)}, u32[]{:S(2)}, u32[]{:S(2)}) collective-permute-start(bf16[144,512]{1,0:T(8,128)(2,1)S(1)} %add_convert_fusion.9.refs_2_), channel_id=1, source_target_pairs={{0,4},{4,0},{8,12},{12,8},{16,20},{20,16},{24,28},{28,24},{1,5},{5... | collective-permute-start | bytes 442376 | tf_op jit(solution)/shard_map/ppermute | solution.py:474
